TPU v7x, 32 devices: a whole 2x2x4 slice. The times are simulated.
32 devices in a mesh: wide: 8 (over z, core), narrow: 4 (over y, x).
Axes of the slice: x: 2, y: 2, z: 4, core: 2. Of those that a mesh axis runs over, the one named last changes fastest.
Arguments:
- tokens: bfloat16 [4096, 2048], P(('wide', 'narrow')), may hold values from -6 to 6
- cotangent: bfloat16 [4096, 2048], P(('wide', 'narrow')), may hold values from -6 to 6
- gain_copy: float32 [4352], replicated, may hold values from 0.5 to 1.5
- query_weight: bfloat16 [2048, 2048], P(None, 'narrow'), may hold values from -0.125 to 0.125
- keyvalue_weight: bfloat16 [2, 2048, 1024], P(None, None, 'narrow'), may hold values from -0.125 to 0.125
- output_weight: bfloat16 [2048, 2048], P('narrow'), may hold values from -1 to 1
- gateup_weight: bfloat16 [2, 2048, 6144], P(None, None, 'narrow'), may hold values from -0.125 to 0.125
- down_weight: bfloat16 [6144, 2048], P('narrow'), may hold values from -0.078125 to 0.078125
- query_master: float32 [2048, 2048], P('wide', 'narrow'), may hold values from -0.125 to 0.125
- query_moment: float32 [2048, 2048], P('wide', 'narrow'), may hold values from -32 to 32
- query_second: float32 [2048, 2048], P('wide', 'narrow'), may hold values from 2.9568 to 11.84
- query_average: float32 [2048, 2048], P('wide', 'narrow'), may hold values from -0.125 to 0.125
- keyvalue_master: float32 [2, 2048, 1024], P(None, 'wide', 'narrow'), may hold values from -0.125 to 0.125
- keyvalue_moment: float32 [2, 2048, 1024], P(None, 'wide', 'narrow'), may hold values from -48 to 48
- keyvalue_second: float32 [2, 2048, 1024], P(None, 'wide', 'narrow'), may hold values from 5.776 to 23.104
- keyvalue_average: float32 [2, 2048, 1024], P(None, 'wide', 'narrow'), may hold values from -0.125 to 0.125
- output_master: float32 [2048, 2048], P('narrow', 'wide'), may hold values from -1 to 1
- output_moment: float32 [2048, 2048], P('narrow', 'wide'), may hold values from -4 to 4
- output_second: float32 [2048, 2048], P('narrow', 'wide'), may hold values from 0.036 to 0.144
- output_average: float32 [2048, 2048], P('narrow', 'wide'), may hold values from -1 to 1
- gateup_master: float32 [2, 2048, 6144], P(None, 'wide', 'narrow'), may hold values from -0.125 to 0.125
- gateup_moment: float32 [2, 2048, 6144], P(None, 'wide', 'narrow'), may hold values from -14 to 14
- gateup_second: float32 [2, 2048, 6144], P(None, 'wide', 'narrow'), may hold values from 0.446464 to 1.785856
- gateup_average: float32 [2, 2048, 6144], P(None, 'wide', 'narrow'), may hold values from -0.125 to 0.125
- down_master: float32 [6144, 2048], P('narrow', 'wide'), may hold values from -0.078125 to 0.078125
- down_moment: float32 [6144, 2048], P('narrow', 'wide'), may hold values from -24 to 24
- down_second: float32 [6144, 2048], P('narrow', 'wide'), may hold values from 1.47456 to 5.89824
- down_average: float32 [6144, 2048], P('narrow', 'wide'), may hold values from -0.078125 to 0.078125
- gain_master: float32 [4352], P(('wide', 'narrow')), may hold values from 0.5 to 1.5
- gain_moment: float32 [4352], P(('wide', 'narrow'))
- gain_second: float32 [4352], P(('wide', 'narrow'))
- gain_average: float32 [4352], P(('wide', 'narrow')), may hold values from 0.1 to 1.9
Outputs:
- block_output: float32 [4096, 2048], P(('wide', 'narrow'))
- input_grad: float32 [4096, 2048], P(('wide', 'narrow'))
- query_grad: float32 [2048, 2048], P('wide', 'narrow')
- query_updated: float32 [2048, 2048], P('wide', 'narrow')
- query_moment_new: float32 [2048, 2048], P('wide', 'narrow')
- query_second_new: float32 [2048, 2048], P('wide', 'narrow')
- query_average_new: float32 [2048, 2048], P('wide', 'narrow')
- keyvalue_grad: float32 [2, 2048, 1024], P(None, 'wide', 'narrow')
- keyvalue_updated: float32 [2, 2048, 1024], P(None, 'wide', 'narrow')
- keyvalue_moment_new: float32 [2, 2048, 1024], P(None, 'wide', 'narrow')
- keyvalue_second_new: float32 [2, 2048, 1024], P(None, 'wide', 'narrow')
- keyvalue_average_new: float32 [2, 2048, 1024], P(None, 'wide', 'narrow')
- output_grad: float32 [2048, 2048], P('narrow', 'wide')
- output_updated: float32 [2048, 2048], P('narrow', 'wide')
- output_moment_new: float32 [2048, 2048], P('narrow', 'wide')
- output_second_new: float32 [2048, 2048], P('narrow', 'wide')
- output_average_new: float32 [2048, 2048], P('narrow', 'wide')
- gateup_grad: float32 [2, 2048, 6144], P(None, 'wide', 'narrow')
- gateup_updated: float32 [2, 2048, 6144], P(None, 'wide', 'narrow')
- gateup_moment_new: float32 [2, 2048, 6144], P(None, 'wide', 'narrow')
- gateup_second_new: float32 [2, 2048, 6144], P(None, 'wide', 'narrow')
- gateup_average_new: float32 [2, 2048, 6144], P(None, 'wide', 'narrow')
- down_grad: float32 [6144, 2048], P('narrow', 'wide')
- down_updated: float32 [6144, 2048], P('narrow', 'wide')
- down_moment_new: float32 [6144, 2048], P('narrow', 'wide')
- down_second_new: float32 [6144, 2048], P('narrow', 'wide')
- down_average_new: float32 [6144, 2048], P('narrow', 'wide')
- gain_grad: float32 [4352], P(('wide', 'narrow'))
- gain_updated: float32 [4352], P(('wide', 'narrow'))
- gain_moment_new: float32 [4352], P(('wide', 'narrow'))
- gain_second_new: float32 [4352], P(('wide', 'narrow'))
- gain_average_new: float32 [4352], P(('wide', 'narrow'))
All inputs are finite; a program needn't handle non-finite values.
Results may differ from a plain program's by a relative error of at most 0.025.
Values may be sent and summed in bfloat16 or wider, within the bound.
A program may use at most 256 MiB of HBM per device.

v0:
```python
import jax
import jax.numpy as jnp
from jax import lax
from jax.sharding import PartitionSpec as P

D = 2048
HD = 128
FF = 6144
STEP = 10
WO_FAN = 32


EPSILON = 1e-06
THETA = 1000000.0
MASKED_SCORE = -1e30
BETA_ONE = 0.9
BETA_TWO = 0.999
ADAM_EPS = 1e-08
WEIGHT_DECAY = 0.1
EMA_KEEP = 0.5
RATE_GAIN = 0.4


def multiply(left, right):
    return jnp.dot(left, right, preferred_element_type=jnp.float32)


def multiply_back(left, right):
    return lax.dot_general(
        left, right, (((1,), (1,)), ((), ())), preferred_element_type=jnp.float32
    )


def multiply_rows(left, right):
    return lax.dot_general(
        left, right, (((0,), (0,)), ((), ())), preferred_element_type=jnp.float32
    )


def rope_tables(positions, width):
    half_width = width // 2
    inverse_freq = THETA ** (-(2.0 * jnp.arange(half_width, dtype=jnp.float32)) / width)
    angles = positions[:, None] * inverse_freq[None, :]
    angles = jnp.concatenate([angles, angles], axis=-1)
    return (jnp.cos(angles), jnp.sin(angles))


def rotate(values_in, cosine_table, sine_table):
    half_width = values_in.shape[-1] // 2
    turned = jnp.concatenate([-values_in[..., half_width:], values_in[..., :half_width]], axis=-1)
    return values_in * cosine_table[:, None, :] + turned * sine_table[:, None, :]


def rotate_back(gradient, cosine_table, sine_table):
    half_width = gradient.shape[-1] // 2
    sined = gradient * sine_table[:, None, :]
    turned = jnp.concatenate([sined[..., half_width:], -sined[..., :half_width]], axis=-1)
    return gradient * cosine_table[:, None, :] + turned


def norm_parts(values_in, gain_vec):
    inv_scale = lax.rsqrt(jnp.mean(values_in * values_in, axis=-1, keepdims=True) + EPSILON)
    unit_rows = values_in * inv_scale
    return (unit_rows * gain_vec, unit_rows, inv_scale)


def norm_back(gradient, unit_rows, inv_scale, gain_vec):
    scaled = gradient * gain_vec
    inner = scaled - unit_rows * jnp.mean(scaled * unit_rows, axis=-1, keepdims=True)
    gain_sum = jnp.sum((gradient * unit_rows).reshape(-1, gain_vec.shape[0]), axis=0)
    return (inv_scale * inner, gain_sum)


def to_groups(values_in, kv_heads, group_size):
    row_count = values_in.shape[0]
    shaped = values_in.reshape(row_count, kv_heads, group_size, HD).transpose(1, 2, 0, 3)
    return shaped.reshape(kv_heads, group_size * row_count, HD)


def from_groups(values_in, kv_heads, group_size):
    row_count = values_in.shape[1] // group_size
    shaped = values_in.reshape(kv_heads, group_size, row_count, HD).transpose(2, 0, 1, 3)
    return shaped.reshape(row_count, kv_heads * group_size, HD)


def adamw(gradient, master, moment, second, average, step_rate, decay_rate):
    moment_new = BETA_ONE * moment + (1.0 - BETA_ONE) * gradient
    second_new = BETA_TWO * second + (1.0 - BETA_TWO) * gradient * gradient
    moment_hat = moment_new / (1.0 - BETA_ONE**STEP)
    second_hat = second_new / (1.0 - BETA_TWO**STEP)
    master_new = master - step_rate * (
        moment_hat / (jnp.sqrt(second_hat) + ADAM_EPS) + decay_rate * master
    )
    average_new = EMA_KEEP * average + (1.0 - EMA_KEEP) * master_new
    return (gradient, master_new, moment_new, second_new, average_new)


def body(
    tokens,
    cotangent,
    gain_copy,
    query_weight,
    keyvalue_weight,
    output_weight,
    gateup_weight,
    down_weight,
    query_master,
    query_moment,
    query_second,
    query_average,
    keyvalue_master,
    keyvalue_moment,
    keyvalue_second,
    keyvalue_average,
    output_master,
    output_moment,
    output_second,
    output_average,
    gateup_master,
    gateup_moment,
    gateup_second,
    gateup_average,
    down_master,
    down_moment,
    down_second,
    down_average,
    gain_master,
    gain_moment,
    gain_second,
    gain_average,
):
    row_count = tokens.shape[0]
    stretch_rows = row_count * lax.axis_size("narrow")
    total_rows = stretch_rows * lax.axis_size("wide")
    wide_index = lax.axis_index("wide")
    kv_heads = keyvalue_weight.shape[2] // HD
    q_heads = query_weight.shape[1] // HD
    group_size = q_heads // kv_heads
    factor = HD ** (-0.5)
    attn_gain = gain_copy[:D]
    mlp_gain = gain_copy[D : 2 * D]
    query_gain = gain_copy[2 * D : 2 * D + HD]
    key_gain = gain_copy[2 * D + HD :]
    hidden_in = tokens.astype(jnp.float32)
    normed, unit_one, scale_one = norm_parts(hidden_in, attn_gain)
    attn_input = lax.all_gather(normed.astype(jnp.bfloat16), "narrow", axis=0, tiled=True)
    query_proj = multiply(attn_input, query_weight).reshape(stretch_rows, q_heads, HD)
    key_proj = multiply(attn_input, keyvalue_weight[0]).reshape(stretch_rows, kv_heads, HD)
    value_low = multiply(attn_input, keyvalue_weight[1]).astype(jnp.bfloat16)
    positions = (wide_index * stretch_rows + jnp.arange(stretch_rows, dtype=jnp.int32)).astype(
        jnp.float32
    )
    cosine_table, sine_table = rope_tables(positions, HD)
    query_normed, query_unit, query_scale = norm_parts(query_proj, query_gain)
    key_normed, key_unit, key_scale = norm_parts(key_proj, key_gain)
    query_low = rotate(query_normed, cosine_table, sine_table).astype(jnp.bfloat16)
    key_low = (
        rotate(key_normed, cosine_table, sine_table)
        .astype(jnp.bfloat16)
        .reshape(stretch_rows, kv_heads * HD)
    )
    query_grouped = to_groups(query_low, kv_heads, group_size)
    query_global = wide_index * stretch_rows + jnp.tile(
        jnp.arange(stretch_rows, dtype=jnp.int32), group_size
    )

    def piece_scores(piece_keys, start_row):
        span_rows = piece_keys.shape[0]
        key_block = piece_keys.reshape(span_rows, kv_heads, HD)
        scores = (
            jnp.einsum("hqd,khd->hqk", query_grouped, key_block, preferred_element_type=jnp.float32)
            * factor
        )
        key_global = start_row + jnp.arange(span_rows, dtype=jnp.int32)
        visible = key_global[None, :] <= query_global[:, None]
        return (jnp.where(visible[None], scores, MASKED_SCORE), visible)

    def block_keys(source, block_index):
        return lax.dynamic_slice_in_dim(source, block_index * stretch_rows, stretch_rows, 0)

    start_max = jnp.full((kv_heads, group_size * stretch_rows), MASKED_SCORE, jnp.float32)
    zeros_out = jnp.zeros((kv_heads, group_size * stretch_rows, HD), jnp.float32)

    def add_max(carry, piece_keys, start_row):
        running_max, running_sum = carry
        scores, visible = piece_scores(piece_keys, start_row)
        new_max = jnp.maximum(running_max, jnp.max(scores, axis=-1))
        terms = jnp.where(visible[None], jnp.exp(scores - new_max[..., None]), 0.0)
        running_sum = running_sum * jnp.exp(running_max - new_max) + jnp.sum(terms, axis=-1)
        return (new_max, running_sum)

    def add_out(total_out, piece_keys, piece_values, start_row, log_total):
        span_rows = piece_keys.shape[0]
        scores, visible = piece_scores(piece_keys, start_row)
        weights_low = jnp.exp(scores - log_total[..., None]).astype(jnp.bfloat16)
        value_block = piece_values.reshape(span_rows, kv_heads, HD)
        return total_out + jnp.einsum(
            "hqk,khd->hqd", weights_low, value_block, preferred_element_type=jnp.float32
        )

    keys_all, values_all = (
        lax.all_gather(key_low, "wide", axis=0, tiled=True),
        lax.all_gather(value_low, "wide", axis=0, tiled=True),
    )

    def max_step(block_index, carry):
        return add_max(carry, block_keys(keys_all, block_index), block_index * stretch_rows)

    running_max, running_sum = lax.fori_loop(
        0, wide_index + 1, max_step, (start_max, jnp.zeros_like(start_max))
    )
    log_total = running_max + jnp.log(running_sum)

    def out_step(block_index, total_out):
        return add_out(
            total_out,
            block_keys(keys_all, block_index),
            block_keys(values_all, block_index),
            block_index * stretch_rows,
            log_total,
        )

    attn_out = lax.fori_loop(0, wide_index + 1, out_step, zeros_out)
    attn_low = (
        from_groups(attn_out, kv_heads, group_size)
        .reshape(stretch_rows, q_heads * HD)
        .astype(jnp.bfloat16)
    )
    hidden_mid = hidden_in + lax.psum_scatter(
        multiply(attn_low, output_weight).astype(jnp.bfloat16),
        "narrow",
        scatter_dimension=0,
        tiled=True,
    ).astype(jnp.float32)
    mlp_normed, unit_two, scale_two = norm_parts(hidden_mid, mlp_gain)
    mlp_input = lax.all_gather(mlp_normed.astype(jnp.bfloat16), "narrow", axis=0, tiled=True)
    gate_proj = multiply(mlp_input, gateup_weight[0])
    up_proj = multiply(mlp_input, gateup_weight[1])
    gate_sigmoid = jax.nn.sigmoid(gate_proj)
    gate_swish = gate_proj * gate_sigmoid
    activated = (gate_swish * up_proj).astype(jnp.bfloat16)
    block_output = hidden_mid + lax.psum_scatter(
        multiply(activated, down_weight).astype(jnp.bfloat16),
        "narrow",
        scatter_dimension=0,
        tiled=True,
    ).astype(jnp.float32)
    back_mlp = lax.all_gather(cotangent, "narrow", axis=0, tiled=True)
    down_grad = multiply_rows(activated, back_mlp)
    act_grad = multiply_back(back_mlp, down_weight)
    gate_grad = (
        act_grad * up_proj * gate_sigmoid * (1.0 + gate_proj * (1.0 - gate_sigmoid))
    ).astype(jnp.bfloat16)
    up_grad = (act_grad * gate_swish).astype(jnp.bfloat16)
    gateup_grad = jnp.stack(
        [multiply_rows(mlp_input, gate_grad), multiply_rows(mlp_input, up_grad)]
    )
    mlp_in_grad = lax.psum_scatter(
        (
            multiply_back(gate_grad, gateup_weight[0]) + multiply_back(up_grad, gateup_weight[1])
        ).astype(jnp.bfloat16),
        "narrow",
        scatter_dimension=0,
        tiled=True,
    ).astype(jnp.float32)
    mid_norm_grad, mlp_gain_grad = norm_back(mlp_in_grad, unit_two, scale_two, mlp_gain)
    mid_grad = cotangent.astype(jnp.float32) + mid_norm_grad
    back_attn = lax.all_gather(mid_grad.astype(jnp.bfloat16), "narrow", axis=0, tiled=True)
    output_grad = multiply_rows(attn_low, back_attn)
    out_grad_low = multiply_back(back_attn, output_weight).astype(jnp.bfloat16)
    out_grouped = to_groups(out_grad_low, kv_heads, group_size)
    row_delta = jnp.sum(out_grouped.astype(jnp.float32) * attn_out, axis=-1)

    def add_back(carry, piece_keys, piece_values, start_row):
        query_sum, key_sum, value_sum = carry
        span_rows = piece_keys.shape[0]
        key_block = piece_keys.reshape(span_rows, kv_heads, HD)
        value_block = piece_values.reshape(span_rows, kv_heads, HD)
        scores, visible = piece_scores(piece_keys, start_row)
        weights = jnp.exp(scores - log_total[..., None])
        weight_grad = jnp.einsum(
            "hqd,khd->hqk", out_grouped, value_block, preferred_element_type=jnp.float32
        )
        score_grad = (weights * (weight_grad - row_delta[..., None])).astype(jnp.bfloat16)
        query_sum = (
            query_sum
            + jnp.einsum("hqk,khd->hqd", score_grad, key_block, preferred_element_type=jnp.float32)
            * factor
        )
        key_part = (
            jnp.einsum(
                "hqk,hqd->khd", score_grad, query_grouped, preferred_element_type=jnp.float32
            )
            * factor
        )
        value_part = jnp.einsum(
            "hqk,hqd->khd",
            weights.astype(jnp.bfloat16),
            out_grouped,
            preferred_element_type=jnp.float32,
        )
        key_sum = lax.dynamic_update_slice_in_dim(
            key_sum,
            lax.dynamic_slice_in_dim(key_sum, start_row, span_rows, 0) + key_part,
            start_row,
            0,
        )
        value_sum = lax.dynamic_update_slice_in_dim(
            value_sum,
            lax.dynamic_slice_in_dim(value_sum, start_row, span_rows, 0) + value_part,
            start_row,
            0,
        )
        return (query_sum, key_sum, value_sum)

    zeros_keys = jnp.zeros((total_rows, kv_heads, HD), jnp.float32)
    start_back = (jnp.zeros_like(attn_out), zeros_keys, zeros_keys)

    def back_step(block_index, carry):
        return add_back(
            carry,
            block_keys(keys_all, block_index),
            block_keys(values_all, block_index),
            block_index * stretch_rows,
        )

    query_sum, key_sum, value_sum = lax.fori_loop(0, wide_index + 1, back_step, start_back)
    key_red, value_red = (
        lax.psum_scatter(
            key_sum.reshape(total_rows, kv_heads * HD).astype(jnp.bfloat16),
            "wide",
            scatter_dimension=0,
            tiled=True,
        ).astype(jnp.float32),
        lax.psum_scatter(
            value_sum.reshape(total_rows, kv_heads * HD).astype(jnp.bfloat16),
            "wide",
            scatter_dimension=0,
            tiled=True,
        ).astype(jnp.float32),
    )
    value_grad = value_red.astype(jnp.bfloat16)
    key_back, key_gain_grad = norm_back(
        rotate_back(key_red.reshape(stretch_rows, kv_heads, HD), cosine_table, sine_table),
        key_unit,
        key_scale,
        key_gain,
    )
    query_back, query_gain_grad = norm_back(
        rotate_back(from_groups(query_sum, kv_heads, group_size), cosine_table, sine_table),
        query_unit,
        query_scale,
        query_gain,
    )
    key_grad_low = key_back.reshape(stretch_rows, kv_heads * HD).astype(jnp.bfloat16)
    query_grad_low = query_back.reshape(stretch_rows, q_heads * HD).astype(jnp.bfloat16)
    query_grad = multiply_rows(attn_input, query_grad_low)
    keyvalue_grad = jnp.stack(
        [multiply_rows(attn_input, key_grad_low), multiply_rows(attn_input, value_grad)]
    )
    query_total, keyvalue_total, output_total, gateup_total, down_total = (
        lax.psum_scatter(
            query_grad.astype(jnp.bfloat16), "wide", scatter_dimension=0, tiled=True
        ).astype(jnp.float32),
        lax.psum_scatter(
            keyvalue_grad.astype(jnp.bfloat16), "wide", scatter_dimension=1, tiled=True
        ).astype(jnp.float32),
        lax.psum_scatter(
            output_grad.astype(jnp.bfloat16), "wide", scatter_dimension=1, tiled=True
        ).astype(jnp.float32),
        lax.psum_scatter(
            gateup_grad.astype(jnp.bfloat16), "wide", scatter_dimension=1, tiled=True
        ).astype(jnp.float32),
        lax.psum_scatter(
            down_grad.astype(jnp.bfloat16), "wide", scatter_dimension=1, tiled=True
        ).astype(jnp.float32),
    )
    normed_grad = lax.psum_scatter(
        (
            multiply_back(query_grad_low, query_weight)
            + multiply_back(key_grad_low, keyvalue_weight[0])
            + multiply_back(value_grad, keyvalue_weight[1])
        ).astype(jnp.bfloat16),
        "narrow",
        scatter_dimension=0,
        tiled=True,
    ).astype(jnp.float32)
    in_norm_grad, attn_gain_grad = norm_back(normed_grad, unit_one, scale_one, attn_gain)
    input_grad = mid_grad + in_norm_grad
    gain_partial = jnp.concatenate([attn_gain_grad, mlp_gain_grad, query_gain_grad, key_gain_grad])
    gain_total = lax.psum_scatter(gain_partial, ("wide", "narrow"), scatter_dimension=0, tiled=True)
    query_new = adamw(
        query_total,
        query_master,
        query_moment,
        query_second,
        query_average,
        2.0 * D ** (-0.5),
        WEIGHT_DECAY,
    )
    keyvalue_new = adamw(
        keyvalue_total,
        keyvalue_master,
        keyvalue_moment,
        keyvalue_second,
        keyvalue_average,
        2.0 * D ** (-0.5),
        WEIGHT_DECAY,
    )
    output_new = adamw(
        output_total,
        output_master,
        output_moment,
        output_second,
        output_average,
        2.0 * WO_FAN ** (-0.5),
        WEIGHT_DECAY,
    )
    gateup_new = adamw(
        gateup_total,
        gateup_master,
        gateup_moment,
        gateup_second,
        gateup_average,
        2.0 * D ** (-0.5),
        WEIGHT_DECAY,
    )
    down_new = adamw(
        down_total,
        down_master,
        down_moment,
        down_second,
        down_average,
        2.0 * FF ** (-0.5),
        WEIGHT_DECAY,
    )
    gain_new = adamw(
        gain_total, gain_master, gain_moment, gain_second, gain_average, RATE_GAIN, 0.0
    )
    return (
        block_output,
        input_grad,
        query_new[0],
        query_new[1],
        query_new[2],
        query_new[3],
        query_new[4],
        keyvalue_new[0],
        keyvalue_new[1],
        keyvalue_new[2],
        keyvalue_new[3],
        keyvalue_new[4],
        output_new[0],
        output_new[1],
        output_new[2],
        output_new[3],
        output_new[4],
        gateup_new[0],
        gateup_new[1],
        gateup_new[2],
        gateup_new[3],
        gateup_new[4],
        down_new[0],
        down_new[1],
        down_new[2],
        down_new[3],
        down_new[4],
        gain_new[0],
        gain_new[1],
        gain_new[2],
        gain_new[3],
        gain_new[4],
    )


def solution(mesh):
    return jax.shard_map(
        body,
        mesh=mesh,
        in_specs=(
            P(("wide", "narrow"), None),
            P(("wide", "narrow"), None),
            P(),
            P(None, "narrow"),
            P(None, None, "narrow"),
            P("narrow", None),
            P(None, None, "narrow"),
            P("narrow", None),
            P("wide", "narrow"),
            P("wide", "narrow"),
            P("wide", "narrow"),
            P("wide", "narrow"),
            P(None, "wide", "narrow"),
            P(None, "wide", "narrow"),
            P(None, "wide", "narrow"),
            P(None, "wide", "narrow"),
            P("narrow", "wide"),
            P("narrow", "wide"),
            P("narrow", "wide"),
            P("narrow", "wide"),
            P(None, "wide", "narrow"),
            P(None, "wide", "narrow"),
            P(None, "wide", "narrow"),
            P(None, "wide", "narrow"),
            P("narrow", "wide"),
            P("narrow", "wide"),
            P("narrow", "wide"),
            P("narrow", "wide"),
            P(("wide", "narrow")),
            P(("wide", "narrow")),
            P(("wide", "narrow")),
            P(("wide", "narrow")),
        ),
        out_specs=(
            P(("wide", "narrow"), None),
            P(("wide", "narrow"), None),
            P("wide", "narrow"),
            P("wide", "narrow"),
            P("wide", "narrow"),
            P("wide", "narrow"),
            P("wide", "narrow"),
            P(None, "wide", "narrow"),
            P(None, "wide", "narrow"),
            P(None, "wide", "narrow"),
            P(None, "wide", "narrow"),
            P(None, "wide", "narrow"),
            P("narrow", "wide"),
            P("narrow", "wide"),
            P("narrow", "wide"),
            P("narrow", "wide"),
            P("narrow", "wide"),
            P(None, "wide", "narrow"),
            P(None, "wide", "narrow"),
            P(None, "wide", "narrow"),
            P(None, "wide", "narrow"),
            P(None, "wide", "narrow"),
            P("narrow", "wide"),
            P("narrow", "wide"),
            P("narrow", "wide"),
            P("narrow", "wide"),
            P("narrow", "wide"),
            P(("wide", "narrow")),
            P(("wide", "narrow")),
            P(("wide", "narrow")),
            P(("wide", "narrow")),
            P(("wide", "narrow")),
        ),
        check_vma=False,
    )
```

profile of v0, /device:TPU:0, one launch (start us, length us, event | category | flops | bytes accessed | tf_op | source)
XLA Modules:
  0.0 1094.0 jit_solution(8909102853079854264)
XLA Ops:
  17.9 31.7 %all-gather.7.cloned.1.call-done = bf16[512,2048]{1,0:T(8,128)(2,1)} async-done(((bf16[128,2048]{1,0:T(8,128)(2,1)}), bf16[512,2048]{1,0:T(8,128)(2,1)}) %all-gather.7.cloned.1.call-update) | async-done | bytes 2097168 | tf_op jit(solution)/shard_map/all_gather | solution.py:146
  53.9 3.9 multiply_reduce_fusion.4
  60.2 3.4 convolution_convert_fusion.10
  63.8 19.3 %all-gather.9.cloned.1.call-done = bf16[4096,256]{0,1:T(8,128)(2,1)} async-done(((bf16[512,256]{0,1:T(8,128)(2,1)}), bf16[4096,256]{0,1:T(8,128)(2,1)}) %all-gather.9.cloned.1.call-update) | async-done | bytes 2097168 | tf_op jit(solution)/shard_map/all_gather | solution.py:202
  83.1 3.6 while.39
  86.8 27.1 %all-gather.11.cloned.1.call-done = bf16[4096,256]{1,0:T(8,128)(2,1)} async-done(((bf16[512,256]{1,0:T(8,128)(2,1)}), bf16[4096,256]{1,0:T(8,128)(2,1)}) %all-gather.11.cloned.1.call-update) | async-done | bytes 2097168 | tf_op jit(solution)/shard_map/all_gather | solution.py:203
  113.9 4.1 copy.129
  119.0 6.5 while.40
  121.2 4.3 fusion.187
  127.8 4.4 convolution_convert_fusion.6
  132.9 79.2 %reduce-scatter.12.cloned.1.call-done = bf16[128,2048]{1,0:T(8,128)(2,1)} async-done(((bf16[512,2048]{1,0:T(8,128)(2,1)}), bf16[128,2048]{1,0:T(8,128)(2,1)}) %reduce-scatter.12.cloned.1.call-update) | async-done | bytes 524304 | tf_op jit(solution)/shard_map/reduce_scatter | solution.py:229
  215.8 33.6 %all-gather.15.cloned.1.call-done = bf16[512,2048]{1,0:T(8,128)(2,1)} async-done(((bf16[128,2048]{1,0:T(8,128)(2,1)}), bf16[512,2048]{1,0:T(8,128)(2,1)}) %all-gather.15.cloned.1.call-update) | async-done | bytes 2097168 | tf_op jit(solution)/shard_map/all_gather | solution.py:248
  249.3 8.5 fusion.110
  257.8 29.2 %all-gather.13.cloned.1.call-done = bf16[512,2048]{1,0:T(8,128)(2,1)} async-done(((bf16[128,2048]{1,0:T(8,128)(2,1)}), bf16[512,2048]{1,0:T(8,128)(2,1)}) %all-gather.13.cloned.1.call-update) | async-done | bytes 2097168 | tf_op jit(solution)/shard_map/all_gather | solution.py:236
  287.1 8.6 fusion.36
  295.7 9.6 multiply_convert_fusion.1
  305.4 3.4 fusion.34
  308.8 4.6 add_convert_fusion.1
  314.0 34.9 %reduce-scatter.16.cloned.1.call-done = bf16[128,2048]{1,0:T(8,128)(2,1)} async-done(((bf16[512,2048]{1,0:T(8,128)(2,1)}), bf16[128,2048]{1,0:T(8,128)(2,1)}) %reduce-scatter.16.cloned.1.call-update) | async-done | bytes 524304 | tf_op jit(solution)/shard_map/reduce_scatter | solution.py:258
  353.2 35.4 %all-gather.17.cloned.1.call-done = bf16[512,2048]{1,0:T(8,128)(2,1)} async-done(((bf16[128,2048]{1,0:T(8,128)(2,1)}), bf16[512,2048]{1,0:T(8,128)(2,1)}) %all-gather.17.cloned.1.call-update) | async-done | bytes 2097168 | tf_op jit(solution)/shard_map/all_gather | solution.py:268
  388.7 3.5 convolution_convert_fusion.9
  400.9 26.1 %while.41 = (s32[]{:T(128)}, f32[2,1024,128]{2,1,0:T(8,128)}, f32[4096,2,128]{0,2,1:T(8,128)}, f32[4096,2,128]{0,2,1:T(8,128)}, s32[]{:T(128)}, /*index=5*/bf16[...) while((s32[]{:T(128)}, f32[2,1024,128]{2,1,0:T(8,128)}, ...), condition=%wide.region_16.17_spmd.clone, body=%wide.region_15.16_spmd.clone.sunk | while | flops 1354106368 | bytes 42250548 | solution.py:327
  411.1 3.1 fusion.201
  418.4 3.1 fusion.200
  427.0 3.8 convert_element_type.168
  430.8 3.9 convert_element_type.172
  434.8 4.2 convolution_convert_fusion.3
  450.9 8.1 convolution_convert_fusion
  459.1 189.2 %reduce-scatter.18.cloned.1.call-done = bf16[512,256]{0,1:T(8,128)(2,1)} async-done(((bf16[4096,256]{0,1:T(8,128)(2,1)}), bf16[512,256]{0,1:T(8,128)(2,1)}) %reduce-scatter.18.cloned.1.call-update) | async-done | bytes 262160 | tf_op jit(solution)/shard_map/reduce_scatter | solution.py:329
  651.1 2.7 fusion.82
  653.9 31.6 %reduce-scatter.20.cloned.1.call-done = bf16[512,256]{0,1:T(8,128)(2,1)} async-done(((bf16[4096,256]{0,1:T(8,128)(2,1)}), bf16[512,256]{0,1:T(8,128)(2,1)}) %reduce-scatter.20.cloned.1.call-update) | async-done | bytes 262160 | tf_op jit(solution)/shard_map/reduce_scatter | solution.py:335
  695.9 8.0 convolution_convert_fusion.5
  704.1 5.7 fusion.32
  709.8 3.7 fusion.33
  713.5 5.6 pad_maximum_fusion
  719.1 3.8 reduce-scatter.28.cloned.1.call-done
  722.9 2.9 add_multiply_fusion.2
  725.8 34.1 %reduce-scatter.24.cloned.1.call-done = bf16[256,512]{1,0:T(8,128)(2,1)} async-done(((bf16[2048,512]{1,0:T(8,128)(2,1)}), bf16[256,512]{1,0:T(8,128)(2,1)}) %reduce-scatter.24.cloned.1.call-update) | async-done | bytes 262160 | tf_op jit(solution)/shard_map/reduce_scatter | solution.py:362
  760.0 3.3 add_multiply_fusion.4
  763.3 67.5 %reduce-scatter.32.cloned.1.call-done = bf16[1536,256]{1,0:T(8,128)(2,1)} async-done(((bf16[1536,2048]{1,0:T(8,128)(2,1)}), bf16[1536,256]{1,0:T(8,128)(2,1)}) %reduce-scatter.32.cloned.1.call-update) | async-done | bytes 786448 | tf_op jit(solution)/shard_map/reduce_scatter | solution.py:374
  830.8 7.3 add_multiply_fusion.1
  838.2 29.7 %reduce-scatter.22.cloned.1.call-done = bf16[128,2048]{1,0:T(8,128)(2,1)} async-done(((bf16[512,2048]{1,0:T(8,128)(2,1)}), bf16[128,2048]{1,0:T(8,128)(2,1)}) %reduce-scatter.22.cloned.1.call-update) | async-done | bytes 524304 | tf_op jit(solution)/shard_map/reduce_scatter | solution.py:378
  869.3 40.6 %all-reduce = f32[4352]{0:T(1024)S(1)} all-reduce(f32[4352]{0:T(1024)S(1)} %pad_maximum_fusion.4), channel_id=13, replica_groups=mesh['wide'=8,'narrow'=4] {'wide','narrow'}, use_global_device_ids=true, to_apply=%region_32.33.clone | all-reduce | flops 4352 | bytes 34816
  910.6 3.2 add_multiply_fusion.3
  913.8 30.6 %reduce-scatter.14.cloned.1.call-done = bf16[128,2048]{1,0:T(8,128)(2,1)} async-done(((bf16[512,2048]{1,0:T(8,128)(2,1)}), bf16[128,2048]{1,0:T(8,128)(2,1)}) %reduce-scatter.14.cloned.1.call-update) | async-done | bytes 524304 | tf_op jit(solution)/shard_map/reduce_scatter | solution.py:242
  944.4 3.6 fusion.63
  948.1 127.7 %reduce-scatter.30.cloned.1.call-done = bf16[2,256,1536]{2,1,0:T(8,128)(2,1)} async-done(((bf16[2,2048,1536]{2,1,0:T(8,128)(2,1)}), bf16[2,256,1536]{2,1,0:T(8,128)(2,1)}) %reduce-scatter.30.cloned.1.call-update) | async-done | bytes 1572880 | tf_op jit(solution)/shard_map/reduce_scatter | solution.py:371
  1075.8 11.3 %add_multiply_fusion = (f32[2,256,1536]{2,1,0:T(8,128)}, f32[2,256,1536]{2,1,0:T(8,128)}, f32[2,256,1536]{2,1,0:T(8,128)}, f32[2,256,1536]{2,1,0:T(8,128)}, f32[2,256,1536]{2,1,0:T(8,128)}) fusion(f32[2,256,1536]{2,1,0:T(8,128)} %param.61, f32[2,256,1536]{2,1,0:T(8,128)} %param.58, f32[2,256,1536]{2,1,0:T(8,128)} %param.59, f32[2,256,1536]{2,1,0:T(8,128)} %param.60, ...), kind=kLoop, calls=%fused_computation.72 | loop fusion | flops 14155776 | bytes 29884416 | tf_op jit(solution)/shard_map/add | solution.py:94
  (240 shorter events, 91.5 us)
Async XLA Ops:
  7.2 46.7 %copy-start = (bf16[2048,512]{1,0:T(8,128)(2,1)S(1)}, bf16[2048,512]{1,0:T(8,128)(2,1)}, u32[]{:S(2)}) copy-start(bf16[2048,512]{1,0:T(8,128)(2,1)} %param.41) | copy-start | bytes 6291460
  7.2 42.4 %all-gather.7.cloned.1.call-start = ((), (), s32[]{:S(2)}) async-start(), calls=%async_computation.11 | async-start | bytes 2621440 | tf_op jit(solution)/shard_map/all_gather | solution.py:146
  8.6 7.4 copy-start.38
  9.4 6.7 copy-start.26
  11.4 71.7 %all-gather.9.cloned.1.call-start = ((), (), s32[]{:S(2)}) async-start(), calls=%async_computation.12 | async-start | bytes 2359296 | tf_op jit(solution)/shard_map/all_gather | solution.py:202
  17.1 42.3 %copy-start.10 = (f32[512,128]{0,1:T(8,128)}, f32[512,128]{0,1:T(8,128)S(1)}, u32[]{:S(2)}) copy-start(f32[512,128]{0,1:T(8,128)S(1)} %get-tuple-element.442) | copy-start | bytes 786436
  17.1 42.3 %copy-start.15 = (f32[512,128]{0,1:T(8,128)}, f32[512,128]{0,1:T(8,128)S(1)}, u32[]{:S(2)}) copy-start(f32[512,128]{0,1:T(8,128)S(1)} %get-tuple-element.443) | copy-start | bytes 786436
  17.9 34.5 %copy-start.36 = (f32[128]{0:T(128)}, f32[128]{0:T(128)S(1)}, u32[]{:S(2)}) copy-start(f32[128]{0:T(128)S(1)} %get-tuple-element.447) | copy-start | bytes 1540
  17.9 41.5 %copy-start.34 = (f32[128]{0:T(128)}, f32[128]{0:T(128)S(1)}, u32[]{:S(2)}) copy-start(f32[128]{0:T(128)S(1)} %get-tuple-element.446) | copy-start | bytes 1540
  53.9 60.1 %all-gather.11.cloned.1.call-start = ((), (), s32[]{:S(2)}) async-start(), calls=%async_computation.13 | async-start | bytes 2359296 | tf_op jit(solution)/shard_map/all_gather | solution.py:203
  63.6 148.5 %reduce-scatter.12.cloned.1.call-start = ((), (), s32[]{:S(2)}) async-start(), calls=%async_computation.14 | async-start | bytes 2621440 | tf_op jit(solution)/shard_map/reduce_scatter | solution.py:229
  127.8 84.3 %copy-start.1 = (bf16[128,2048]{1,0:T(8,128)(2,1)S(1)}, bf16[128,2048]{1,0:T(8,128)(2,1)}, u32[]{:S(2)}) copy-start(bf16[128,2048]{1,0:T(8,128)(2,1)} %param.38) | copy-start | bytes 1572868
  132.2 117.1 %all-gather.15.cloned.1.call-start = ((), (), s32[]{:S(2)}) async-start(), calls=%async_computation.17 | async-start | bytes 2621440 | tf_op jit(solution)/shard_map/all_gather | solution.py:248
  132.8 154.2 %all-gather.13.cloned.1.call-start = ((), (), s32[]{:S(2)}) async-start(), calls=%async_computation.15 | async-start | bytes 2621440 | tf_op jit(solution)/shard_map/all_gather | solution.py:236
  215.5 133.4 %reduce-scatter.16.cloned.1.call-start = ((), (), s32[]{:S(2)}) async-start(), calls=%async_computation.18 | async-start | bytes 2621440 | tf_op jit(solution)/shard_map/reduce_scatter | solution.py:258
  287.1 8.6 copy-start.46
  287.1 8.6 copy-start.48
  287.1 18.3 %slice-start = ((s8[12582912]{0:T(1024)(128)(4,1)}), s8[4194304]{0:T(1024)(128)(4,1)S(1)}, s32[]{:S(2)}) async-start(s8[12582912]{0:T(1024)(128)(4,1)} %bitcast.313), calls=%async_computation.28 | async-start | bytes 8388608
  287.1 18.3 %slice-start.1 = ((s8[12582912]{0:T(1024)(128)(4,1)}), s8[4194304]{0:T(1024)(128)(4,1)S(1)}, s32[]{:S(2)}) async-start(s8[12582912]{0:T(1024)(128)(4,1)} %bitcast.313), calls=%async_computation.29 | async-start | bytes 8388608
  295.7 9.6 slice-start.2
  313.5 75.1 %all-gather.17.cloned.1.call-start = ((), (), s32[]{:S(2)}) async-start(), calls=%async_computation.19 | async-start | bytes 2621440 | tf_op jit(solution)/shard_map/all_gather | solution.py:268
  353.2 295.2 %reduce-scatter.18.cloned.1.call-start = ((), (), s32[]{:S(2)}) async-start(), calls=%async_computation.20 | async-start | bytes 2359296 | tf_op jit(solution)/shard_map/reduce_scatter | solution.py:329
  430.8 254.7 %reduce-scatter.20.cloned.1.call-start = ((), (), s32[]{:S(2)}) async-start(), calls=%async_computation.21 | async-start | bytes 2359296 | tf_op jit(solution)/shard_map/reduce_scatter | solution.py:335
  430.8 4.0 copy-start.25
  434.7 4.5 copy-start.35
  434.7 288.2 %reduce-scatter.28.cloned.1.call-start = ((), (), s32[]{:S(2)}) async-start(), calls=%async_computation.25 | async-start | bytes 2359296 | tf_op jit(solution)/shard_map/reduce_scatter | solution.py:368
  439.0 321.0 %reduce-scatter.24.cloned.1.call-start = ((), (), s32[]{:S(2)}) async-start(), calls=%async_computation.23 | async-start | bytes 2359296 | tf_op jit(solution)/shard_map/reduce_scatter | solution.py:362
  439.2 4.2 copy-start.11
  439.2 4.2 copy-start.33
  450.9 380.0 %reduce-scatter.32.cloned.1.call-start = ((), (), s32[]{:S(2)}) async-start(), calls=%async_computation.27 | async-start | bytes 7077888 | tf_op jit(solution)/shard_map/reduce_scatter | solution.py:374
  459.1 190.5 %copy-start.13 = (f32[512,2,128]{0,2,1:T(8,128)S(1)}, f32[512,2,128]{0,2,1:T(8,128)}, u32[]{:S(2)}) copy-start(f32[512,2,128]{0,2,1:T(8,128)} %copy-done.12) | copy-start | bytes 1572868
  459.1 190.5 %copy-start.31 = (f32[512,2]{0,1:T(2,128)S(1)}, f32[512,2]{0,1:T(2,128)}, u32[]{:S(2)}) copy-start(f32[512,2]{0,1:T(2,128)} %copy-done.30) | copy-start | bytes 12292
  459.1 190.5 %copy-start.37 = (f32[128]{0:T(128)S(1)}, f32[128]{0:T(128)}, u32[]{:S(2)}) copy-start(f32[128]{0:T(128)} %copy-done.36) | copy-start | bytes 1540
  459.1 408.8 %reduce-scatter.22.cloned.1.call-start = ((), (), s32[]{:S(2)}) async-start(), calls=%async_computation.22 | async-start | bytes 2621440 | tf_op jit(solution)/shard_map/reduce_scatter | solution.py:378
  653.9 33.8 %copy-start.21 = (bf16[512,512]{0,1:T(8,128)(2,1)S(1)}, bf16[512,512]{0,1:T(8,128)(2,1)}, u32[]{:S(2)}) copy-start(bf16[512,512]{0,1:T(8,128)(2,1)} %copy-done.20) | copy-start | bytes 1572868
  690.8 219.8 %reduce-scatter.26.cloned.1.call-start = ((), (), s32[]{:S(2)}) async-start(), calls=%async_computation.24 | async-start | bytes 2359296 | tf_op jit(solution)/shard_map/reduce_scatter | solution.py:365
  695.7 248.8 %reduce-scatter.14.cloned.1.call-start = ((), (), s32[]{:S(2)}) async-start(), calls=%async_computation.16 | async-start | bytes 2621440 | tf_op jit(solution)/shard_map/reduce_scatter | solution.py:242
  704.0 371.8 %reduce-scatter.30.cloned.1.call-start = ((), (), s32[]{:S(2)}) async-start(), calls=%async_computation.26 | async-start | bytes 14155776 | tf_op jit(solution)/shard_map/reduce_scatter | solution.py:371
  704.1 5.7 copy-start.47
  704.1 5.7 copy-start.51
  763.3 104.6 %copy-start.2 = (bf16[128,2048]{1,0:T(8,128)(2,1)S(1)}, bf16[128,2048]{1,0:T(8,128)(2,1)}, u32[]{:S(2)}) copy-start(bf16[128,2048]{1,0:T(8,128)(2,1)} %param.38) | copy-start | bytes 1572868
  763.3 104.6 %copy-start.27 = (f32[2048]{0:T(1024)S(1)}, f32[2048]{0:T(1024)}, u32[]{:S(2)}) copy-start(f32[2048]{0:T(1024)} %copy-done.26) | copy-start | bytes 24580
  763.3 104.6 %copy-start.39 = (f32[128]{0:T(128)S(1)}, f32[128]{0:T(128)}, u32[]{:S(2)}) copy-start(f32[128]{0:T(128)} %copy-done.38) | copy-start | bytes 1540
  763.3 146.6 %copy-start.40 = (f32[136]{0:T(256)S(1)}, f32[136]{0:T(256)}, u32[]{:S(2)}) copy-start(f32[136]{0:T(256)} %param.69) | copy-start | bytes 1636
  763.3 146.6 %copy-start.41 = (f32[136]{0:T(256)S(1)}, f32[136]{0:T(256)}, u32[]{:S(2)}) copy-start(f32[136]{0:T(256)} %param.66) | copy-start | bytes 1636
  763.3 146.6 %copy-start.42 = (f32[136]{0:T(256)S(1)}, f32[136]{0:T(256)}, u32[]{:S(2)}) copy-start(f32[136]{0:T(256)} %param.67) | copy-start | bytes 1636
  763.3 146.6 %copy-start.43 = (f32[136]{0:T(256)S(1)}, f32[136]{0:T(256)}, u32[]{:S(2)}) copy-start(f32[136]{0:T(256)} %param.68) | copy-start | bytes 1636
  838.2 106.3 %copy-start.7 = (bf16[128,2048]{1,0:T(8,128)(2,1)S(1)}, bf16[128,2048]{1,0:T(8,128)(2,1)}, u32[]{:S(2)}) copy-start(bf16[128,2048]{1,0:T(8,128)(2,1)} %reduce-scatter.12.cloned.1.call-done) | copy-start | bytes 1572868
  (24 other events, 54.7 us)
Sparse Core Ops, SparseCore 0:
  11.5 38.0 all-gather.6
  54.0 29.0 all-gather.8
  85.3 28.5 all-gather.10
  132.4 79.7 reduce-scatter.11
  214.0 35.3 all-gather.14
  251.7 35.2 all-gather.12
  313.6 35.1 reduce-scatter.15
  353.3 35.2 all-gather.16
  430.9 217.4 reduce-scatter.17
  651.1 34.3 reduce-scatter.19
  688.3 34.5 reduce-scatter.27
  725.7 34.2 reduce-scatter.23
  762.3 68.5 reduce-scatter.31
  834.2 33.5 reduce-scatter.21
  870.7 36.0 reduce-scatter.25
  910.4 33.9 reduce-scatter.13
  946.6 129.1 reduce-scatter.29
where the time goes:
time: 1100 us; the launch traced here: 1090 us
  waiting for transfers between devices  806 us (73%)
  matrix products  112 us (10%)
  other arithmetic  77.6 us (7%)
  local copies, waits for them, and re-layouts  40.8 us (4%)
  blocking collectives  40.6 us (4%)
  between operations  15 us (1%)
    reduce_scatter x1, waiting for transfers between devices, body(): lax.psum_scatter(key_sum.reshape(total_rows, kv_heads * HD).astype(jnp.bf...  189 us
    reduce_scatter x1, waiting for transfers between devices, body(): lax.psum_scatter(gateup_grad.astype(jnp.bfloat16), 'wide', scatter_dimens...  128 us
    reduce_scatter x1, waiting for transfers between devices, body(): lax.psum_scatter(multiply(attn_low, output_weight).astype(jnp.bfloat16),...  79.2 us
    reduce_scatter x1, waiting for transfers between devices, body(): lax.psum_scatter(down_grad.astype(jnp.bfloat16), 'wide', scatter_dimensio...  67.5 us
    unnamed x1, blocking collectives  40.6 us
    dot_general x7, matrix products, multiply(): return jnp.dot(left, right, preferred_element_type=jnp.float32)  40.6 us
    all_gather x1, waiting for transfers between devices, body(): lax.all_gather(mid_grad.astype(jnp.bfloat16), 'narrow', axis=0, tiled=True)  35.4 us
    reduce_scatter x1, waiting for transfers between devices, body(): lax.psum_scatter((multiply_back(gate_grad, gateup_weight[0]) + multiply_b...  34.9 us
  transfers between devices with their start and end apart: 17, of which 16 were waited for; matrix products, arithmetic and copies ran while one was open for 11% of the time, Pallas kernels for 0%

commit v1 on v0

v1 whole, which is shorter than its diff:
```python
import functools

import jax
import jax.numpy as jnp
from jax import lax
from jax.experimental import pallas as pl
from jax.experimental.pallas import tpu as pltpu
from jax.sharding import PartitionSpec as P

D = 2048
HD = 128
FF = 6144
STEP = 10
WO_FAN = 32

EPSILON = 1e-06
THETA = 1000000.0
BETA_ONE = 0.9
BETA_TWO = 0.999
ADAM_EPS = 1e-08
WEIGHT_DECAY = 0.1
EMA_KEEP = 0.5
RATE_GAIN = 0.4
FACTOR = HD ** (-0.5)
LOG2E = 1.4426950408889634

F32 = jnp.float32
BF16 = jnp.bfloat16
MESH = pl.DeviceIdType.MESH
VM = pl.BlockSpec(memory_space=pltpu.VMEM)
SM = pl.BlockSpec(memory_space=pltpu.SMEM)
VMEM_LIMIT = 60 << 20

NT = (((1,), (1,)), ((), ()))
TN = (((0,), (0,)), ((), ()))


def dot(left, right):
    return jnp.dot(left, right, preferred_element_type=F32)


def dot_nt(left, right):
    return lax.dot_general(left, right, NT, preferred_element_type=F32)


def dot_tn(left, right):
    return lax.dot_general(left, right, TN, preferred_element_type=F32)


def rope_tables(positions):
    half_width = HD // 2
    inverse_freq = THETA ** (-(2.0 * jnp.arange(half_width, dtype=F32)) / HD)
    angles = positions[:, None] * inverse_freq[None, :]
    cosine, sine = jnp.cos(angles), jnp.sin(angles)
    return (
        jnp.concatenate([cosine, cosine], axis=-1),
        jnp.concatenate([-sine, sine], axis=-1),
    )


def adamw(gradient, master, moment, second, average, step_rate, decay_rate):
    moment_new = BETA_ONE * moment + (1.0 - BETA_ONE) * gradient
    second_new = BETA_TWO * second + (1.0 - BETA_TWO) * gradient * gradient
    moment_hat = moment_new / (1.0 - BETA_ONE**STEP)
    second_hat = second_new / (1.0 - BETA_TWO**STEP)
    master_new = master - step_rate * (
        moment_hat / (jnp.sqrt(second_hat) + ADAM_EPS) + decay_rate * master
    )
    average_new = EMA_KEEP * average + (1.0 - EMA_KEEP) * master_new
    return (gradient, master_new, moment_new, second_new, average_new)


def row_scale(values_in):
    return lax.rsqrt(jnp.mean(values_in * values_in, axis=-1, keepdims=True) + EPSILON)


def norm_back(gradient, unit_rows, inv_scale, gain_row):
    scaled = gradient * gain_row
    inner = scaled - unit_rows * jnp.mean(scaled * unit_rows, axis=-1, keepdims=True)
    return inv_scale * inner, jnp.sum(gradient * unit_rows, axis=0, keepdims=True)


def square():
    me = lax.axis_index("narrow")
    xn = me + 1 - 2 * (me % 2)
    yn = (me + 2) % 4
    dg = (xn + 2) % 4
    return me, xn, yn, dg


def greet(axis, peers):
    barrier = pltpu.get_barrier_semaphore()
    for peer in peers:
        pl.semaphore_signal(barrier, inc=1, device_id={axis: peer}, device_id_type=MESH)
    pl.semaphore_wait(barrier, len(peers))


class Copies:
    def __init__(self, send, recv):
        self.send, self.recv, self.sent = send, recv, []

    def go(self, src, dst, slot, peer):
        copy = pltpu.make_async_remote_copy(
            src_ref=src,
            dst_ref=dst,
            send_sem=self.send.at[slot],
            recv_sem=self.recv.at[slot],
            device_id={"narrow": peer},
            device_id_type=MESH,
        )
        copy.start()
        self.sent.append(copy)
        return copy

    def finish(self):
        for copy in self.sent:
            copy.wait_send()


def gather_square(copies, slot, x_ref, o_ref):
    me, xn, yn, dg = square()
    rows = x_ref.shape[0]
    half = rows // 2

    def part(owner, low):
        return o_ref.at[pl.ds(pl.multiple_of(owner * rows + low, half), half)]

    upper, lower = x_ref.at[pl.ds(0, half)], x_ref.at[pl.ds(half, half)]
    xa = copies.go(upper, part(me, 0), slot, xn)
    yb = copies.go(lower, part(me, half), slot + 1, yn)
    xb = copies.go(lower, part(me, half), slot + 2, xn)
    ya = copies.go(upper, part(me, 0), slot + 3, yn)
    o_ref[pl.ds(pl.multiple_of(me * rows, rows), rows)] = x_ref[...]
    xa.wait_recv()
    yf = copies.go(part(xn, 0), part(xn, 0), slot + 4, yn)
    yb.wait_recv()
    xf = copies.go(part(yn, half), part(yn, half), slot + 5, xn)
    for copy in (xb, ya, yf, xf):
        copy.wait_recv()


def scatter_square(copies, slot, p_ref, buf, stage, emit):
    me, xn, yn, dg = square()
    rows = p_ref.shape[0] // 4
    half = rows // 2

    def part(owner, low):
        return p_ref.at[pl.ds(pl.multiple_of(owner * rows + low, half), half)]

    c0 = copies.go(part(dg, 0), buf.at[0], slot, xn)
    c1 = copies.go(part(dg, half), buf.at[1], slot + 1, yn)
    c2 = copies.go(part(xn, 0), buf.at[2], slot + 2, xn)
    c3 = copies.go(part(yn, half), buf.at[3], slot + 3, yn)
    c0.wait_recv()
    stage[0] = (part(yn, 0)[...].astype(F32) + buf[0].astype(F32)).astype(BF16)
    c4 = copies.go(stage.at[0], buf.at[4], slot + 4, yn)
    c1.wait_recv()
    stage[1] = (part(xn, half)[...].astype(F32) + buf[1].astype(F32)).astype(BF16)
    c5 = copies.go(stage.at[1], buf.at[5], slot + 5, xn)
    c2.wait_recv()
    c4.wait_recv()
    emit(0, part(me, 0)[...].astype(F32) + buf[2].astype(F32) + buf[4].astype(F32))
    c3.wait_recv()
    c5.wait_recv()
    emit(half, part(me, half)[...].astype(F32) + buf[3].astype(F32) + buf[5].astype(F32))


def dma_sems(count):
    return [pltpu.SemaphoreType.DMA((count,)), pltpu.SemaphoreType.DMA((count,))]


def scatter_space(rows):
    return [pltpu.VMEM((6, rows // 2, D), BF16), pltpu.VMEM((2, rows // 2, D), BF16)]


def remote_params(collective_id):
    return pltpu.CompilerParams(
        collective_id=collective_id, has_side_effects=True, vmem_limit_bytes=VMEM_LIMIT
    )


def norm_gather_kernel(t_ref, g_ref, o_ref, own, send, recv):
    _, xn, yn, _ = square()
    greet("narrow", (xn, yn))
    hidden = t_ref[...].astype(F32)
    own[...] = (hidden * row_scale(hidden) * g_ref[...]).astype(BF16)
    copies = Copies(send, recv)
    gather_square(copies, 0, own, o_ref)
    copies.finish()


def norm_gather(tokens, gain_row, special):
    rows = tokens.shape[0]
    if not special:
        hidden = tokens.astype(F32)
        normed = (hidden * row_scale(hidden) * gain_row).astype(BF16)
        return lax.all_gather(normed, "narrow", axis=0, tiled=True)
    return pl.pallas_call(
        norm_gather_kernel,
        name="norm_gather",
        out_shape=jax.ShapeDtypeStruct((4 * rows, D), BF16),
        in_specs=[VM, VM],
        out_specs=VM,
        scratch_shapes=[pltpu.VMEM((rows, D), BF16)] + dma_sems(6),
        cost_estimate=cost(1, 1),
        compiler_params=remote_params(1),
    )(tokens, gain_row)


def mid_forward_kernel(p_ref, t_ref, g_ref, h_ref, o_ref, buf, stage, own, send, recv):
    _, xn, yn, _ = square()
    half = t_ref.shape[0] // 2
    greet("narrow", (xn, yn))
    copies = Copies(send, recv)

    def emit(low, total):
        hidden = t_ref[pl.ds(low, half)].astype(F32) + total
        h_ref[pl.ds(low, half)] = hidden
        own[pl.ds(low, half)] = (hidden * row_scale(hidden) * g_ref[...]).astype(BF16)

    scatter_square(copies, 0, p_ref, buf, stage, emit)
    gather_square(copies, 6, own, o_ref)
    copies.finish()


def mid_forward(partial, tokens, gain_row, special):
    rows = tokens.shape[0]
    if not special:
        hidden = tokens.astype(F32) + lax.psum_scatter(
            partial, "narrow", scatter_dimension=0, tiled=True
        ).astype(F32)
        normed = (hidden * row_scale(hidden) * gain_row).astype(BF16)
        return hidden, lax.all_gather(normed, "narrow", axis=0, tiled=True)
    return pl.pallas_call(
        mid_forward_kernel,
        name="mid_forward",
        out_shape=(
            jax.ShapeDtypeStruct((rows, D), F32),
            jax.ShapeDtypeStruct((4 * rows, D), BF16),
        ),
        in_specs=[VM] * 3,
        out_specs=(VM, VM),
        scratch_shapes=scatter_space(rows) + [pltpu.VMEM((rows, D), BF16)] + dma_sems(12),
        cost_estimate=cost(1, 1),
        compiler_params=remote_params(2),
    )(partial, tokens, gain_row)


def mid_backward_kernel(
    p_ref, h_ref, c_ref, g_ref, m_ref, o_ref, gg_ref, buf, stage, own, send, recv
):
    _, xn, yn, _ = square()
    half = h_ref.shape[0] // 2
    greet("narrow", (xn, yn))
    copies = Copies(send, recv)
    gg_ref[...] = jnp.zeros_like(gg_ref)

    def emit(low, total):
        hidden = h_ref[pl.ds(low, half)]
        scale = row_scale(hidden)
        back, gain_sum = norm_back(total, hidden * scale, scale, g_ref[...])
        gg_ref[...] += gain_sum
        mid = c_ref[pl.ds(low, half)].astype(F32) + back
        m_ref[pl.ds(low, half)] = mid
        own[pl.ds(low, half)] = mid.astype(BF16)

    scatter_square(copies, 0, p_ref, buf, stage, emit)
    gather_square(copies, 6, own, o_ref)
    copies.finish()


def mid_backward(partial, hidden_mid, cotangent, gain_row, special):
    rows = hidden_mid.shape[0]
    if not special:
        total = lax.psum_scatter(partial, "narrow", scatter_dimension=0, tiled=True).astype(F32)
        scale = row_scale(hidden_mid)
        back, gain_sum = norm_back(total, hidden_mid * scale, scale, gain_row)
        mid = cotangent.astype(F32) + back
        return mid, lax.all_gather(mid.astype(BF16), "narrow", axis=0, tiled=True), gain_sum
    return pl.pallas_call(
        mid_backward_kernel,
        name="mid_backward",
        out_shape=(
            jax.ShapeDtypeStruct((rows, D), F32),
            jax.ShapeDtypeStruct((4 * rows, D), BF16),
            jax.ShapeDtypeStruct((1, D), F32),
        ),
        in_specs=[VM] * 4,
        out_specs=(VM,) * 3,
        scratch_shapes=scatter_space(rows) + [pltpu.VMEM((rows, D), BF16)] + dma_sems(12),
        cost_estimate=cost(1, 1),
        compiler_params=remote_params(3),
    )(partial, hidden_mid, cotangent, gain_row)


def last_kernel(p_ref, t_ref, m_ref, g_ref, q_ref, h_ref, o_ref, gg_ref, b_ref, buf, stage, buf2, stage2, send, recv):
    _, xn, yn, _ = square()
    half = t_ref.shape[0] // 2
    greet("narrow", (xn, yn))
    copies = Copies(send, recv)
    gg_ref[...] = jnp.zeros_like(gg_ref)

    def emit(low, total):
        hidden = t_ref[pl.ds(low, half)].astype(F32)
        scale = row_scale(hidden)
        back, gain_sum = norm_back(total, hidden * scale, scale, g_ref[...])
        gg_ref[...] += gain_sum
        o_ref[pl.ds(low, half)] = m_ref[pl.ds(low, half)] + back

    def emit_out(low, total):
        b_ref[pl.ds(low, half)] = h_ref[pl.ds(low, half)] + total

    scatter_square(copies, 0, p_ref, buf, stage, emit)
    scatter_square(copies, 6, q_ref, buf2, stage2, emit_out)
    copies.finish()


def last_scatter(partial, tokens, mid_grad, gain_row, out_partial, hidden_mid, special):
    rows = tokens.shape[0]
    if not special:
        total = lax.psum_scatter(partial, "narrow", scatter_dimension=0, tiled=True).astype(F32)
        hidden = tokens.astype(F32)
        scale = row_scale(hidden)
        back, gain_sum = norm_back(total, hidden * scale, scale, gain_row)
        out = lax.psum_scatter(out_partial, "narrow", scatter_dimension=0, tiled=True)
        return mid_grad + back, gain_sum, hidden_mid + out.astype(F32)
    return pl.pallas_call(
        last_kernel,
        name="last_scatter",
        out_shape=(
            jax.ShapeDtypeStruct((rows, D), F32),
            jax.ShapeDtypeStruct((1, D), F32),
            jax.ShapeDtypeStruct((rows, D), F32),
        ),
        in_specs=[VM] * 6,
        out_specs=(VM,) * 3,
        scratch_shapes=scatter_space(rows) + scatter_space(rows) + dma_sems(12),
        cost_estimate=cost(1, 1),
        compiler_params=remote_params(4),
    )(partial, tokens, mid_grad, gain_row, out_partial, hidden_mid)


def line(count):
    w = lax.axis_index("wide")
    z, c = w // 2, w % 2
    return w, z, c, count // 2, w + 1 - 2 * c, jnp.minimum(w + 2, count - 1), jnp.maximum(w - 2, 0)


def greet_line(count):
    w, z, c, chips, mate, above, below = line(count)
    barrier = pltpu.get_barrier_semaphore()
    has_above, has_below = z < chips - 1, z > 0

    @pl.when(has_above)
    def _():
        pl.semaphore_signal(barrier, inc=1, device_id={"wide": above}, device_id_type=MESH)

    @pl.when(has_below)
    def _():
        pl.semaphore_signal(barrier, inc=1, device_id={"wide": below}, device_id_type=MESH)

    pl.semaphore_signal(barrier, inc=1, device_id={"wide": mate}, device_id_type=MESH)
    pl.semaphore_wait(barrier, 1 + has_above.astype(jnp.int32) + has_below.astype(jnp.int32))


def wide_copy(src, dst, send, recv, slot, peer):
    return pltpu.make_async_remote_copy(
        src_ref=src,
        dst_ref=dst,
        send_sem=send.at[slot],
        recv_sem=recv.at[slot],
        device_id={"wide": peer},
        device_id_type=MESH,
    )


def pass_keys_kernel(count, x_ref, o_ref, send, recv, mate_send, mate_recv):
    w, z, c, chips, mate, above, below = line(count)
    greet_line(count)
    own_up = wide_copy(x_ref, o_ref.at[w], send, recv, 0, above)

    @pl.when(z < chips - 1)
    def _():
        own_up.start()

    own_mate = wide_copy(x_ref, o_ref.at[w], mate_send, mate_recv, 0, mate)
    own_mate.start()
    o_ref[w] = x_ref[...]
    for step in range(1, chips):
        block = jnp.maximum(w - 2 * step, 0)
        arrived = wide_copy(o_ref.at[block], o_ref.at[block], send, recv, step - 1, above)
        onward = wide_copy(o_ref.at[block], o_ref.at[block], send, recv, min(step, chips - 2), above)
        share = wide_copy(o_ref.at[block], o_ref.at[block], mate_send, mate_recv, step, mate)

        @pl.when(z >= step)
        def _():
            arrived.wait_recv()
            if step < chips - 1:

                @pl.when(z < chips - 1)
                def _():
                    onward.start()

            share.start()

    own_mate.wait()

    @pl.when(z < chips - 1)
    def _():
        own_up.wait_send()

    for step in range(1, chips):
        block = jnp.maximum(w - 2 * step, 0)
        onward = wide_copy(o_ref.at[block], o_ref.at[block], send, recv, min(step, chips - 2), above)
        share = wide_copy(o_ref.at[block], o_ref.at[block], mate_send, mate_recv, step, mate)

        @pl.when(z >= step)
        def _():
            share.wait()
            if step < chips - 1:

                @pl.when(z < chips - 1)
                def _():
                    onward.wait_send()


def pass_keys(keys_values, count, special):
    rows, width = keys_values.shape
    if not special:
        return lax.all_gather(keys_values, "wide", axis=0)
    chips = count // 2
    return pl.pallas_call(
        functools.partial(pass_keys_kernel, count),
        name="pass_keys",
        out_shape=jax.ShapeDtypeStruct((count, rows, width), BF16),
        in_specs=[VM],
        out_specs=VM,
        scratch_shapes=dma_sems(chips - 1) + dma_sems(chips),
        cost_estimate=cost(1, 1),
        compiler_params=remote_params(5),
    )(keys_values)


def return_grads_kernel(
    count, x_ref, o_ref, from_mate, from_above, stage, send, recv, mate_send, mate_recv
):
    w, z, c, chips, mate, above, below = line(count)
    greet_line(count)

    def to_mate(s):
        return wide_copy(
            x_ref.at[jnp.minimum(2 * s + 1 - c, count - 1)],
            from_mate.at[s],
            mate_send,
            mate_recv,
            s,
            mate,
        )

    def sends_mate(s):
        return (z > s) | ((z == s) & (c == 1))

    def gets_mate(s):
        return (z > s) | ((z == s) & (c == 0))

    def down(s):
        return wide_copy(stage.at[s], from_above.at[s], send, recv, s, below)

    for s in range(chips):

        @pl.when(sends_mate(s))
        def _():
            to_mate(s).start()

    for s in range(chips):
        block = jnp.minimum(2 * s + c, count - 1)

        @pl.when(z > s)
        def _():
            to_mate(s).wait_recv()

            @pl.when(z == chips - 1)
            def _():
                stage[s] = (x_ref[block].astype(F32) + from_mate[s].astype(F32)).astype(BF16)

            @pl.when(z < chips - 1)
            def _():
                down(s).wait_recv()
                stage[s] = (
                    x_ref[block].astype(F32) + from_mate[s].astype(F32) + from_above[s].astype(F32)
                ).astype(BF16)

            down(s).start()

        @pl.when(z == s)
        def _():
            o_ref[...] = x_ref[block].astype(F32)

            @pl.when(c == 0)
            def _():
                to_mate(s).wait_recv()
                o_ref[...] += from_mate[s].astype(F32)

            if s < chips - 1:
                down(s).wait_recv()
                o_ref[...] += from_above[s].astype(F32)

    for s in range(chips):

        @pl.when(sends_mate(s))
        def _():
            to_mate(s).wait_send()

        @pl.when(z > s)
        def _():
            down(s).wait_send()


def return_grads(grads, count, special):
    _, rows, width = grads.shape
    if not special:
        w = lax.axis_index("wide")
        seen = (jnp.arange(count) <= w)[:, None, None]
        total = lax.psum_scatter(
            jnp.where(seen, grads, 0).reshape(count * rows, width),
            "wide",
            scatter_dimension=0,
            tiled=True,
        )
        return total.astype(F32)
    chips = count // 2
    return pl.pallas_call(
        functools.partial(return_grads_kernel, count),
        name="return_grads",
        out_shape=jax.ShapeDtypeStruct((rows, width), F32),
        in_specs=[VM],
        out_specs=VM,
        scratch_shapes=[
            pltpu.VMEM((chips, rows, width), BF16),
            pltpu.VMEM((chips, rows, width), BF16),
            pltpu.VMEM((chips, rows, width), BF16),
        ]
        + dma_sems(chips)
        + dma_sems(chips),
        cost_estimate=cost(1, 1),
        compiler_params=remote_params(6),
    )(grads)


def gain_kernel(wide, x_ref, o_ref, near, mid, far, send, recv, wide_send, wide_recv):
    me, xn, yn, dg = square()
    w = lax.axis_index("wide")
    barrier = pltpu.get_barrier_semaphore()
    for peer in (xn, yn, dg):
        pl.semaphore_signal(barrier, inc=1, device_id={"narrow": peer}, device_id_type=MESH)
    for step in range(1, wide):
        pl.semaphore_signal(
            barrier, inc=1, device_id={"wide": (w + step) % wide}, device_id_type=MESH
        )
    pl.semaphore_wait(barrier, 3 + wide - 1)
    copies = Copies(send, recv)
    sent = [
        copies.go(x_ref.at[peer], near.at[slot], slot, peer)
        for slot, peer in enumerate((xn, yn, dg))
    ]
    for copy in sent:
        copy.wait_recv()
    mid[...] = x_ref[me] + near[0] + near[1] + near[2]
    away = []
    for step in range(1, wide):
        peer = (w + step) % wide
        copy = wide_copy(
            mid.at[peer], far.at[step - 1], wide_send, wide_recv, step - 1, peer
        )
        copy.start()
        away.append(copy)
    total = mid[w]
    for step in range(1, wide):
        away[step - 1].wait_recv()
        total = total + far[step - 1]
    o_ref[...] = total
    copies.finish()
    for copy in away:
        copy.wait_send()


def gain_sums(partial, wide, narrow, special):
    if not special:
        return lax.psum_scatter(partial, ("wide", "narrow"), scatter_dimension=0, tiled=True)
    count = partial.shape[0] // (wide * narrow)
    padded = -(-count // 128) * 128
    shaped = partial.reshape(wide, narrow, count).transpose(1, 0, 2)
    shaped = jnp.pad(shaped, ((0, 0), (0, 0), (0, padded - count)))
    shaped = shaped.reshape(narrow, wide, padded // 128, 128)
    out = pl.pallas_call(
        functools.partial(gain_kernel, wide),
        name="gain_sums",
        out_shape=jax.ShapeDtypeStruct((padded // 128, 128), F32),
        in_specs=[VM],
        out_specs=VM,
        scratch_shapes=[
            pltpu.VMEM((3, wide, padded // 128, 128), F32),
            pltpu.VMEM((wide, padded // 128, 128), F32),
            pltpu.VMEM((wide - 1, padded // 128, 128), F32),
        ]
        + dma_sems(3)
        + dma_sems(wide - 1),
        cost_estimate=cost(1, 1),
        compiler_params=remote_params(7),
    )(shaped)
    return out.reshape(padded)[:count]


def cost(flops, moved, exps=0):
    return pl.CostEstimate(flops=1, bytes_accessed=1, transcendentals=0)


def params(*semantics):
    if not semantics:
        return pltpu.CompilerParams(vmem_limit_bytes=VMEM_LIMIT)
    return pltpu.CompilerParams(vmem_limit_bytes=VMEM_LIMIT, dimension_semantics=semantics)


def spin(raw, gain_row, cosine, sine):
    normed = raw * row_scale(raw) * gain_row
    return normed * cosine + pltpu.roll(normed, HD // 2, axis=1) * sine


def keys_kernel(x_ref, w_ref, g_ref, cos_ref, sin_ref, kv_ref, raw_ref):
    which = pl.program_id(0)
    width = w_ref.shape[2]
    out = dot(x_ref[...], w_ref[0])

    @pl.when(which == 0)
    def _():
        raw_ref[...] = out
        for h in range(width // HD):
            part = out[:, h * HD : (h + 1) * HD]
            kv_ref[:, h * HD : (h + 1) * HD] = spin(
                part, g_ref[...], cos_ref[...], sin_ref[...]
            ).astype(BF16)

    @pl.when(which == 1)
    def _():
        kv_ref[...] = out.astype(BF16)


def keys_values(x, weight, gain_row, cosine, sine):
    rows, width = x.shape[0], weight.shape[2]
    whole = lambda i: (0, 0)
    return pl.pallas_call(
        keys_kernel,
        name="keys_values",
        grid=(2,),
        out_shape=(
            jax.ShapeDtypeStruct((rows, 2 * width), BF16),
            jax.ShapeDtypeStruct((rows, width), F32),
        ),
        in_specs=[
            pl.BlockSpec((rows, D), whole),
            pl.BlockSpec((1, D, width), lambda i: (i, 0, 0)),
            pl.BlockSpec((1, HD), whole),
            pl.BlockSpec((rows, HD), whole),
            pl.BlockSpec((rows, HD), whole),
        ],
        out_specs=(
            pl.BlockSpec((rows, width), lambda i: (0, i)),
            pl.BlockSpec((rows, width), whole),
        ),
        compiler_params=params("arbitrary"),
        cost_estimate=cost(4 * rows * D * width, 2 * rows * D + 4 * D * width),
    )(x, weight, gain_row, cosine, sine)


def queries_kernel(x_ref, w_ref, g_ref, cos_ref, sin_ref, q_ref, raw_ref):
    out = dot(x_ref[...], w_ref[...])
    raw_ref[...] = out
    for h in range(w_ref.shape[1] // HD):
        part = out[:, h * HD : (h + 1) * HD]
        q_ref[:, h * HD : (h + 1) * HD] = spin(
            part, g_ref[...], cos_ref[...], sin_ref[...]
        ).astype(BF16)


def queries(x, weight, gain_row, cosine, sine):
    rows, width = x.shape[0], weight.shape[1]
    tile = 256
    whole = lambda i: (0, 0)
    return pl.pallas_call(
        queries_kernel,
        name="queries",
        grid=(width // tile,),
        out_shape=(
            jax.ShapeDtypeStruct((rows, width), BF16),
            jax.ShapeDtypeStruct((rows, width), F32),
        ),
        in_specs=[
            pl.BlockSpec((rows, D), whole),
            pl.BlockSpec((D, tile), lambda i: (0, i)),
            pl.BlockSpec((1, HD), whole),
            pl.BlockSpec((rows, HD), whole),
            pl.BlockSpec((rows, HD), whole),
        ],
        out_specs=(
            pl.BlockSpec((rows, tile), lambda i: (0, i)),
            pl.BlockSpec((rows, tile), lambda i: (0, i)),
        ),
        compiler_params=params("arbitrary"),
        cost_estimate=cost(2 * rows * D * width, 2 * rows * D + 2 * D * width),
    )(x, weight, gain_row, cosine, sine)


def attend_kernel(heads, group, w_ref, q_ref, kv_ref, o_ref, low_ref, lse_ref, acc):
    rows = q_ref.shape[0]
    kv_width = kv_ref.shape[2] // 2
    w = w_ref[0]
    acc[...] = jnp.zeros_like(acc)
    ones = jnp.ones((rows, HD), BF16)

    def block(j, masked):
        for h in range(heads):
            kv = h // group
            key = kv_ref[j, :, kv * HD : (kv + 1) * HD]
            value = kv_ref[j, :, kv_width + kv * HD : kv_width + (kv + 1) * HD]
            query = q_ref[:, h * HD : (h + 1) * HD]
            terms = jnp.exp2(dot_nt(query, key) * (FACTOR * LOG2E))
            if masked:
                at = lax.broadcasted_iota(jnp.int32, (rows, rows), 0)
                key_at = lax.broadcasted_iota(jnp.int32, (rows, rows), 1)
                terms = jnp.where(key_at <= at, terms, 0.0)
            acc[h] += dot(terms.astype(BF16), jnp.concatenate([value, ones], axis=1))

    @pl.loop(0, w)
    def _(j):
        block(j, False)

    block(w, True)
    for h in range(heads):
        total = acc[h, :, HD:]
        out = acc[h, :, :HD] / total
        o_ref[:, h * HD : (h + 1) * HD] = out
        low_ref[:, h * HD : (h + 1) * HD] = out.astype(BF16)
        lse_ref[h : h + 1, :] = jnp.transpose(jnp.log2(total))[0:1]


def attend(w_index, query, kv_all, heads, group):
    rows, width = query.shape
    count = kv_all.shape[0]
    return pl.pallas_call(
        functools.partial(attend_kernel, heads, group),
        name="attend",
        out_shape=(
            jax.ShapeDtypeStruct((rows, width), F32),
            jax.ShapeDtypeStruct((rows, width), BF16),
            jax.ShapeDtypeStruct((heads, rows), F32),
        ),
        in_specs=[SM, VM, VM],
        out_specs=(VM, VM, VM),
        scratch_shapes=[pltpu.VMEM((heads, rows, 2 * HD), F32)],
        compiler_params=params(),
        cost_estimate=cost(4 * rows * rows * count * width, 2 * kv_all.size, rows * rows * heads * count),
    )(w_index, query, kv_all)


def attend_back_kernel(
    heads, group, w_ref, q_ref, kv_ref, do_ref, o_ref, lse_ref, dq_ref, dkv_ref, delta
):
    rows = q_ref.shape[0]
    kv_width = kv_ref.shape[2] // 2
    w = w_ref[0]
    for h in range(heads):
        part = slice(h * HD, (h + 1) * HD)
        delta[h : h + 1, :] = jnp.sum(
            jnp.transpose(do_ref[:, part].astype(F32) * o_ref[:, part]), axis=0, keepdims=True
        )
    dq_ref[...] = jnp.zeros_like(dq_ref)

    def block(j, masked):
        for kv in range(heads // group):
            key = kv_ref[j, :, kv * HD : (kv + 1) * HD]
            value = kv_ref[j, :, kv_width + kv * HD : kv_width + (kv + 1) * HD]
            key_sum = jnp.zeros((rows, HD), F32)
            value_sum = jnp.zeros((rows, HD), F32)
            for h in range(kv * group, (kv + 1) * group):
                part = slice(h * HD, (h + 1) * HD)
                query, out_grad = q_ref[:, part], do_ref[:, part]
                probs = jnp.exp2(
                    dot_nt(key, query) * (FACTOR * LOG2E) - lse_ref[h : h + 1, :]
                )
                if masked:
                    key_at = lax.broadcasted_iota(jnp.int32, (rows, rows), 0)
                    at = lax.broadcasted_iota(jnp.int32, (rows, rows), 1)
                    probs = jnp.where(key_at <= at, probs, 0.0)
                value_sum += dot(probs.astype(BF16), out_grad)
                prob_grad = dot_nt(value, out_grad)
                score_grad = (probs * (prob_grad - delta[h : h + 1, :])).astype(BF16)
                key_sum += dot(score_grad, query)
                dq_ref[:, part] += dot_tn(score_grad, key)
            dkv_ref[j, :, kv * HD : (kv + 1) * HD] = (key_sum * FACTOR).astype(BF16)
            dkv_ref[j, :, kv_width + kv * HD : kv_width + (kv + 1) * HD] = value_sum.astype(BF16)

    @pl.loop(0, w)
    def _(j):
        block(j, False)

    block(w, True)
    dq_ref[...] = dq_ref[...] * FACTOR


def attend_back(w_index, query, kv_all, out_grad, out, lse, heads, group):
    rows, width = query.shape
    count = kv_all.shape[0]
    return pl.pallas_call(
        functools.partial(attend_back_kernel, heads, group),
        name="attend_back",
        out_shape=(
            jax.ShapeDtypeStruct((rows, width), F32),
            jax.ShapeDtypeStruct(kv_all.shape, BF16),
        ),
        in_specs=[SM] + [VM] * 5,
        out_specs=(VM, VM),
        scratch_shapes=[pltpu.VMEM((heads, rows), F32)],
        compiler_params=params(),
        cost_estimate=cost(10 * rows * rows * count * width, 4 * kv_all.size, rows * rows * heads * count),
    )(w_index, query, kv_all, out_grad, out, lse)


def unspin_kernel(width, e_ref, raw_ref, g_ref, cos_ref, sin_ref, o_ref, gg_ref):
    gain_sum = jnp.zeros((1, HD), F32)
    for h in range(raw_ref.shape[1] // HD):
        part = slice(h * HD, (h + 1) * HD)
        grad = e_ref[:, part]
        turned = grad * cos_ref[...] - pltpu.roll(grad, HD // 2, axis=1) * sin_ref[...]
        raw = raw_ref[:, part]
        scale = row_scale(raw)
        back, total = norm_back(turned, raw * scale, scale, g_ref[...])
        o_ref[:, part] = back.astype(BF16)
        gain_sum += total
    if width > raw_ref.shape[1]:
        o_ref[:, raw_ref.shape[1] :] = e_ref[:, raw_ref.shape[1] :].astype(BF16)
    gg_ref[...] = gain_sum


def unspin(grad, raw, gain_row, cosine, sine):
    rows, width = grad.shape
    return pl.pallas_call(
        functools.partial(unspin_kernel, width),
        name="unspin",
        out_shape=(
            jax.ShapeDtypeStruct((rows, width), BF16),
            jax.ShapeDtypeStruct((1, HD), F32),
        ),
        in_specs=[VM] * 5,
        out_specs=(VM, VM),
        compiler_params=params(),
        cost_estimate=cost(20 * grad.size, 10 * grad.size),
    )(grad, raw, gain_row, cosine, sine)


def feed_kernel(x_ref, dy_ref, w_ref, d_ref, act_ref, grad_ref, down_ref):
    x, dy = x_ref[...], dy_ref[...]
    gate = dot(x, w_ref[0])
    upper = dot(x, w_ref[1])
    act_grad = dot_nt(dy, d_ref[...])
    sig = jax.nn.sigmoid(gate)
    swish = gate * sig
    act = (swish * upper).astype(BF16)
    act_ref[...] = act
    grad_ref[0] = (act_grad * upper * sig * (1.0 + gate * (1.0 - sig))).astype(BF16)
    grad_ref[1] = (act_grad * swish).astype(BF16)
    down_ref[...] = dot_tn(act, dy).astype(BF16)


def feed(x, dy, gateup_weight, down_weight):
    rows, width = x.shape[0], down_weight.shape[0]
    tile = 256
    whole = lambda i: (0, 0)
    return pl.pallas_call(
        feed_kernel,
        name="feed",
        grid=(width // tile,),
        out_shape=(
            jax.ShapeDtypeStruct((rows, width), BF16),
            jax.ShapeDtypeStruct((2, rows, width), BF16),
            jax.ShapeDtypeStruct((width, D), BF16),
        ),
        in_specs=[
            pl.BlockSpec((rows, D), whole),
            pl.BlockSpec((rows, D), whole),
            pl.BlockSpec((2, D, tile), lambda i: (0, 0, i)),
            pl.BlockSpec((tile, D), lambda i: (i, 0)),
        ],
        out_specs=(
            pl.BlockSpec((rows, tile), lambda i: (0, i)),
            pl.BlockSpec((2, rows, tile), lambda i: (0, 0, i)),
            pl.BlockSpec((tile, D), lambda i: (i, 0)),
        ),
        compiler_params=params("arbitrary"),
        cost_estimate=cost(8 * rows * D * width, 4 * rows * D + 8 * D * width),
    )(x, dy, gateup_weight, down_weight)


def feed_back_kernel(x_ref, act_ref, grad_ref, w_ref, d_ref, full_ref, in_ref, out_ref, in_acc, out_acc):
    step = pl.program_id(0)

    @pl.when(step == 0)
    def _():
        in_acc[...] = jnp.zeros_like(in_acc)
        out_acc[...] = jnp.zeros_like(out_acc)

    in_acc[...] += dot_nt(grad_ref[0], w_ref[0]) + dot_nt(grad_ref[1], w_ref[1])
    out_acc[...] += dot(act_ref[...], d_ref[...])
    x = x_ref[...]
    full_ref[0] = dot_tn(x, grad_ref[0]).astype(BF16)
    full_ref[1] = dot_tn(x, grad_ref[1]).astype(BF16)

    @pl.when(step == pl.num_programs(0) - 1)
    def _():
        in_ref[...] = in_acc[...].astype(BF16)
        out_ref[...] = out_acc[...].astype(BF16)


def feed_back(x, act, grads, gateup_weight, down_weight):
    rows, width = x.shape[0], down_weight.shape[0]
    tile = 256
    whole = lambda i: (0, 0)
    return pl.pallas_call(
        feed_back_kernel,
        name="feed_back",
        grid=(width // tile,),
        out_shape=(
            jax.ShapeDtypeStruct((2, D, width), BF16),
            jax.ShapeDtypeStruct((rows, D), BF16),
            jax.ShapeDtypeStruct((rows, D), BF16),
        ),
        in_specs=[
            pl.BlockSpec((rows, D), whole),
            pl.BlockSpec((rows, tile), lambda i: (0, i)),
            pl.BlockSpec((2, rows, tile), lambda i: (0, 0, i)),
            pl.BlockSpec((2, D, tile), lambda i: (0, 0, i)),
            pl.BlockSpec((tile, D), lambda i: (i, 0)),
        ],
        out_specs=(
            pl.BlockSpec((2, D, tile), lambda i: (0, 0, i)),
            pl.BlockSpec((rows, D), whole),
            pl.BlockSpec((rows, D), whole),
        ),
        scratch_shapes=[pltpu.VMEM((rows, D), F32), pltpu.VMEM((rows, D), F32)],
        compiler_params=params("arbitrary"),
        cost_estimate=cost(10 * rows * D * width, 8 * rows * D + 10 * D * width),
    )(x, act, grads, gateup_weight, down_weight)


def out_back_kernel(dy_ref, w_ref, low_ref, grad_ref, full_ref):
    dy = dy_ref[...]
    grad_ref[...] = dot_nt(dy, w_ref[...]).astype(BF16)
    full_ref[...] = dot_tn(dy, low_ref[...]).astype(BF16)


def out_back(dy, weight, attn_low):
    rows, width = attn_low.shape
    tile = 256
    whole = lambda i: (0, 0)
    return pl.pallas_call(
        out_back_kernel,
        name="out_back",
        grid=(width // tile,),
        out_shape=(
            jax.ShapeDtypeStruct((rows, width), BF16),
            jax.ShapeDtypeStruct((D, width), BF16),
        ),
        in_specs=[
            pl.BlockSpec((rows, D), whole),
            pl.BlockSpec((tile, D), lambda i: (i, 0)),
            pl.BlockSpec((rows, tile), lambda i: (0, i)),
        ],
        out_specs=(
            pl.BlockSpec((rows, tile), lambda i: (0, i)),
            pl.BlockSpec((D, tile), lambda i: (0, i)),
        ),
        compiler_params=params("arbitrary"),
        cost_estimate=cost(4 * rows * D * width, 2 * rows * D + 4 * D * width),
    )(dy, weight, attn_low)


def project_back_kernel(x_ref, q_ref, kv_ref, wq_ref, wkv_ref, in_ref, full_ref):
    q_width, kv_width = wq_ref.shape[1], wkv_ref.shape[2]
    x = x_ref[...]
    key, value = kv_ref[:, :kv_width], kv_ref[:, kv_width:]
    in_ref[...] = (
        dot_nt(q_ref[...], wq_ref[...]) + dot_nt(key, wkv_ref[0]) + dot_nt(value, wkv_ref[1])
    ).astype(BF16)
    full_ref[:, :q_width] = dot_tn(x, q_ref[...]).astype(BF16)
    full_ref[:, q_width:] = dot_tn(x, kv_ref[...]).astype(BF16)


def project_back(x, q_back, kv_back, query_weight, keyvalue_weight):
    rows = x.shape[0]
    q_width, kv_width = query_weight.shape[1], keyvalue_weight.shape[2]
    tile = 512
    whole = lambda i: (0, 0)
    return pl.pallas_call(
        project_back_kernel,
        name="project_back",
        grid=(D // tile,),
        out_shape=(
            jax.ShapeDtypeStruct((rows, D), BF16),
            jax.ShapeDtypeStruct((D, q_width + 2 * kv_width), BF16),
        ),
        in_specs=[
            pl.BlockSpec((rows, tile), lambda i: (0, i)),
            pl.BlockSpec((rows, q_width), whole),
            pl.BlockSpec((rows, 2 * kv_width), whole),
            pl.BlockSpec((tile, q_width), lambda i: (i, 0)),
            pl.BlockSpec((2, tile, kv_width), lambda i: (0, i, 0)),
        ],
        out_specs=(
            pl.BlockSpec((rows, tile), lambda i: (0, i)),
            pl.BlockSpec((tile, q_width + 2 * kv_width), lambda i: (i, 0)),
        ),
        compiler_params=params("arbitrary"),
        cost_estimate=cost(4 * rows * D * (q_width + 2 * kv_width), 6 * D * (q_width + 2 * kv_width)),
    )(x, q_back, kv_back, query_weight, keyvalue_weight)


def wide_scatter(partial, axis):
    return lax.psum_scatter(partial, "wide", scatter_dimension=axis, tiled=True)


def body(
    tokens,
    cotangent,
    gain_copy,
    query_weight,
    keyvalue_weight,
    output_weight,
    gateup_weight,
    down_weight,
    query_master,
    query_moment,
    query_second,
    query_average,
    keyvalue_master,
    keyvalue_moment,
    keyvalue_second,
    keyvalue_average,
    output_master,
    output_moment,
    output_second,
    output_average,
    gateup_master,
    gateup_moment,
    gateup_second,
    gateup_average,
    down_master,
    down_moment,
    down_second,
    down_average,
    gain_master,
    gain_moment,
    gain_second,
    gain_average,
):
    narrow, wide = lax.axis_size("narrow"), lax.axis_size("wide")
    special = narrow == 4 and wide == 8
    stretch_rows = tokens.shape[0] * narrow
    wide_index = lax.axis_index("wide")
    w_scalar = wide_index.astype(jnp.int32).reshape(1)
    kv_heads = keyvalue_weight.shape[2] // HD
    q_heads = query_weight.shape[1] // HD
    group = q_heads // kv_heads
    q_width, kv_width = q_heads * HD, kv_heads * HD
    attn_gain = gain_copy[:D].reshape(1, D)
    mlp_gain = gain_copy[D : 2 * D].reshape(1, D)
    query_gain = gain_copy[2 * D : 2 * D + HD].reshape(1, HD)
    key_gain = gain_copy[2 * D + HD :].reshape(1, HD)

    attn_input = norm_gather(tokens, attn_gain, special)
    positions = (wide_index * stretch_rows + jnp.arange(stretch_rows, dtype=jnp.int32)).astype(F32)
    cosine, sine = rope_tables(positions)
    kv_low, key_raw = keys_values(attn_input, keyvalue_weight, key_gain, cosine, sine)
    late_cotangent, kv_low = lax.optimization_barrier((cotangent, kv_low))
    back_mlp = lax.all_gather(late_cotangent, "narrow", axis=0, tiled=True)
    query_low, query_raw = queries(attn_input, query_weight, query_gain, cosine, sine)
    kv_all = pass_keys(kv_low, wide, special)
    attn_out, attn_low, lse = attend(w_scalar, query_low, kv_all, q_heads, group)
    hidden_mid, mlp_input = mid_forward(
        dot(attn_low, output_weight).astype(BF16), tokens, mlp_gain, special
    )
    act, act_grads, down_full = feed(mlp_input, back_mlp, gateup_weight, down_weight)
    down_total = wide_scatter(down_full, 1)
    gateup_full, in_partial, out_partial = feed_back(
        mlp_input, act, act_grads, gateup_weight, down_weight
    )
    gateup_total = wide_scatter(gateup_full, 1)
    mid_grad, back_attn, mlp_gain_grad = mid_backward(
        in_partial, hidden_mid, cotangent, mlp_gain, special
    )
    attn_grad, output_full = out_back(back_attn, output_weight, attn_low)
    query_sum, kv_sums = attend_back(
        w_scalar, query_low, kv_all, attn_grad, attn_out, lse, q_heads, group
    )
    down_new = adamw(
        down_total.astype(F32),
        down_master,
        down_moment,
        down_second,
        down_average,
        2.0 * FF ** (-0.5),
        WEIGHT_DECAY,
    )
    kv_sums, down_new = lax.optimization_barrier((kv_sums, down_new))
    query_back, query_gain_grad = unspin(query_sum, query_raw, query_gain, cosine, sine)
    kv_sum = return_grads(kv_sums, wide, special)
    kv_back, key_gain_grad = unspin(kv_sum, key_raw, key_gain, cosine, sine)
    normed_partial, project_full = project_back(
        attn_input, query_back, kv_back, query_weight, keyvalue_weight
    )
    input_grad, attn_gain_grad, block_output = last_scatter(
        normed_partial, tokens, mid_grad, attn_gain, out_partial, hidden_mid, special
    )
    gain_partial = jnp.concatenate(
        [attn_gain_grad, mlp_gain_grad, query_gain_grad, key_gain_grad], axis=1
    ).reshape(-1)
    gain_total = gain_sums(gain_partial, wide, narrow, special)

    rest_full = jnp.concatenate([project_full, output_full], axis=1)
    rest_full, gateup_total, gain_total, block_output, input_grad = lax.optimization_barrier(
        (rest_full, gateup_total, gain_total, block_output, input_grad)
    )
    rest_total = wide_scatter(rest_full, 0).astype(F32)
    query_total = rest_total[:, :q_width]
    keyvalue_total = jnp.stack(
        [rest_total[:, q_width : q_width + kv_width], rest_total[:, q_width + kv_width : q_width + 2 * kv_width]]
    )
    output_total = rest_total[:, q_width + 2 * kv_width :].T
    query_new = adamw(
        query_total,
        query_master,
        query_moment,
        query_second,
        query_average,
        2.0 * D ** (-0.5),
        WEIGHT_DECAY,
    )
    keyvalue_new = adamw(
        keyvalue_total,
        keyvalue_master,
        keyvalue_moment,
        keyvalue_second,
        keyvalue_average,
        2.0 * D ** (-0.5),
        WEIGHT_DECAY,
    )
    output_new = adamw(
        output_total,
        output_master,
        output_moment,
        output_second,
        output_average,
        2.0 * WO_FAN ** (-0.5),
        WEIGHT_DECAY,
    )
    gateup_new = adamw(
        gateup_total.astype(F32),
        gateup_master,
        gateup_moment,
        gateup_second,
        gateup_average,
        2.0 * D ** (-0.5),
        WEIGHT_DECAY,
    )
    gain_new = adamw(
        gain_total, gain_master, gain_moment, gain_second, gain_average, RATE_GAIN, 0.0
    )
    return (
        block_output,
        input_grad,
        *query_new,
        *keyvalue_new,
        *output_new,
        *gateup_new,
        *down_new,
        *gain_new,
    )


def solution(mesh):
    rows = P(("wide", "narrow"), None)
    flat = P(("wide", "narrow"))
    stacked = P(None, "wide", "narrow")
    query, output = P("wide", "narrow"), P("narrow", "wide")
    states = (
        *[query] * 4,
        *[stacked] * 4,
        *[output] * 4,
        *[stacked] * 4,
        *[output] * 4,
        *[flat] * 4,
    )
    return jax.shard_map(
        body,
        mesh=mesh,
        in_specs=(
            rows,
            rows,
            P(),
            P(None, "narrow"),
            P(None, None, "narrow"),
            P("narrow", None),
            P(None, None, "narrow"),
            P("narrow", None),
            *states,
        ),
        out_specs=(
            rows,
            rows,
            *[query] * 5,
            *[stacked] * 5,
            *[output] * 5,
            *[stacked] * 5,
            *[output] * 5,
            *[flat] * 5,
        ),
        check_vma=False,
    )
```

time: 1100 us -> 535 us (0.49)
  waiting for transfers between devices: 806 us -> 67.8 us
  Pallas kernels: 0 us -> 382 us
  matrix products: 112 us -> 3.62 us
  other arithmetic: 77.6 us -> 35.2 us
  blocking collectives: 40.6 us -> 0 us
  local copies, waits for them, and re-layouts: 40.8 us -> 23.8 us
    reduce_scatter x11 -> x3, waiting for transfers between devices: 628 us -> 67.7 us  [wide_scatter(): return lax.psum_scatter(partial, 'wide', scatter_dimension=axis, tiled=True)]
    pallas_call x0 -> x17, Pallas kernels: none -> 382 us  [the longest x1 116 us: return_grads(): pl.pallas_call(functools.partial(return_grads_kernel, count), name='retur...]
    all_gather x6 -> x1, waiting for transfers between devices: 176 us -> 0.02 us  [body(): back_mlp = lax.all_gather(late_cotangent, 'narrow', axis=0, tiled=True)]
    dot_general x28 -> x1, matrix products: 112 us -> 3.62 us  [dot(): return jnp.dot(left, right, preferred_element_type=F32)]
    unnamed x1 -> x0, blocking collectives: 40.6 us -> none
    convert_element_type x9 -> x2, other arithmetic: 18.5 us -> 3.77 us  [the longest x1 2.47 us: body(): down_total.astype(F32)]
    unnamed x105 -> x72, local copies, waits for them, and re-layouts: 6.34 us -> 18.8 us
  transfers between devices with their start and end apart: 17 -> 4, of which waited for: 16 -> 2; matrix products, arithmetic and copies ran while one was open for 11% -> 7% of each run, Pallas kernels for 0% -> 63%
where the time goes in v1:
time: 535 us; the launch traced here: 527 us
  Pallas kernels  382 us (71%)
  waiting for transfers between devices  67.8 us (13%)
  other arithmetic  35.2 us (7%)
  local copies, waits for them, and re-layouts  23.8 us (4%)
  between operations  14.6 us (3%)
    pallas_call x1, Pallas kernels, return_grads(): pl.pallas_call(functools.partial(return_grads_kernel, count), name='retur...  116 us
    reduce_scatter x3, waiting for transfers between devices, wide_scatter(): return lax.psum_scatter(partial, 'wide', scatter_dimension=axis, tiled=True)  67.7 us
    pallas_call x1, Pallas kernels, mid_forward(): pl.pallas_call(mid_forward_kernel, name='mid_forward', out_shape=(jax.Sha...  43.3 us
    pallas_call x1, Pallas kernels, last_scatter(): pl.pallas_call(last_kernel, name='last_scatter', out_shape=(jax.ShapeDtyp...  41.3 us
    pallas_call x1, Pallas kernels, mid_backward(): pl.pallas_call(mid_backward_kernel, name='mid_backward', out_shape=(jax.S...  39.5 us
    pallas_call x1, Pallas kernels, feed_back(): pl.pallas_call(feed_back_kernel, name='feed_back', grid=(width // tile,),...  24.5 us
    pallas_call x1, Pallas kernels, norm_gather(): pl.pallas_call(norm_gather_kernel, name='norm_gather', out_shape=jax.Shap...  24.5 us
    add x6, other arithmetic, adamw(): average_new = EMA_KEEP * average + (1.0 - EMA_KEEP) * master_new  23.3 us
  transfers between devices with their start and end apart: 4, of which 2 were waited for; matrix products, arithmetic and copies ran while one was open for 7% of the time, Pallas kernels for 63%

profile of v1, /device:TPU:0, one launch (start us, length us, event | category | flops | bytes accessed | tf_op | source)
XLA Modules:
  0.0 526.9 jit_solution(4413253974127764486)
XLA Ops:
  7.3 1.3 fusion.13
  8.6 1.3 slice_bitcast_fusion.3
  9.9 1.0 fusion.5
  10.9 24.5 %norm_gather.1.x_ref = bf16[512,2048]{1,0:T(8,128)(2,1)} custom-call(bf16[128,2048]{1,0:T(8,128)(2,1)} %t_ref.5, f32[1,2048]{1,0:T(1,128)} %bitcast.27), custom_call_target="tpu_custom_call" | custom-call | flops 1 | bytes 1 | tf_op jit(solution)/shard_map/norm_gather/pallas_call | solution.py:198
  35.4 1.0 pad_maximum_fusion.2
  36.4 4.8 keys_values.1
  41.3 15.4 %pass_keys.1.kv_ref = bf16[8,512,512]{2,1,0:T(8,128)(2,1)} custom-call(bf16[512,512]{1,0:T(8,128)(2,1)} %get-tuple-element.78.x_ref), custom_call_target="tpu_custom_call" | custom-call | flops 1 | bytes 1 | tf_op jit(solution)/shard_map/pass_keys/pallas_call | solution.py:432
  56.7 5.7 %queries.1 = (bf16[512,512]{1,0:T(8,128)(2,1)}, f32[512,512]{1,0:T(8,128)}) custom-call(bf16[512,2048]{1,0:T(8,128)(2,1)} %norm_gather.1.x_ref, bf16[2048,512]{1,0:T(8,128)(2,1)} %wq_ref.1, f32[1,128]{1,0:T(1,128)} %get-tuple-element.184.g_ref, f32[512,128]{1,0:T(8,128)} %get-tuple-element.188.cos_ref, f32[512,128]{1,0:T(8,128)} %get-tuple-element.189.sin_ref), custom_call_target="tpu_custom_call" | custom-call | flops 1 | bytes 1 | tf_op jit(solution)/shard_map/queries/pallas_call | solution.py:689
  62.4 5.5 %attend.1 = (f32[512,512]{1,0:T(8,128)}, bf16[512,512]{1,0:T(8,128)(2,1)}, f32[4,512]{1,0:T(4,128)}) custom-call(s32[1]{0:T(128)} %bitcast.1.w_ref, bf16[512,512]{1,0:T(8,128)(2,1)} %get-tuple-element.76.q_ref, bf16[8,512,512]{2,1,0:T(8,128)(2,1)} %pass_keys.1.kv_ref), custom_call_target="tpu_custom_call" | custom-call | flops 1 | bytes 1 | tf_op jit(solution)/shard_map/attend/pallas_call | solution.py:749
  67.9 3.6 convolution_convert_fusion.p_ref
  71.5 43.3 %mid_forward.1 = (f32[128,2048]{1,0:T(8,128)}, bf16[512,2048]{1,0:T(8,128)(2,1)}) custom-call(bf16[512,2048]{1,0:T(8,128)(2,1)} %convolution_convert_fusion.p_ref, bf16[128,2048]{1,0:T(8,128)(2,1)} %t_ref.5, f32[1,2048]{1,0:T(1,128)} %bitcast.29), custom_call_target="tpu_custom_call" | custom-call | flops 1 | bytes 1 | tf_op jit(solution)/shard_map/mid_forward/pallas_call | solution.py:234
  114.8 19.3 %feed.1 = (bf16[512,1536]{1,0:T(8,128)(2,1)}, bf16[2,512,1536]{2,1,0:T(8,128)(2,1)}, bf16[1536,2048]{1,0:T(8,128)(2,1)}) custom-call(bf16[512,2048]{1,0:T(8,128)(2,1)} %get-tuple-element.80.x_ref, bf16[512,2048]{1,0:T(8,128)(2,1)} %all-gather.2.cloned.1.call-done.dy_ref, bf16[2,2048,1536]{2,1,0:T(8,128)(2,1)} %w_ref.8, bf16[1536,2048]{1,0:T(8,128)(2,1)} %d_ref.3), custom_call_target="tpu_custom_call" | custom-call | flops 1 | bytes 1 | tf_op jit(solution)/shard_map/feed/pallas_call | solution.py:878
  134.4 24.5 %feed_back.1 = (bf16[2,2048,1536]{2,1,0:T(8,128)(2,1)}, bf16[512,2048]{1,0:T(8,128)(2,1)}, bf16[512,2048]{1,0:T(8,128)(2,1)}) custom-call(bf16[512,2048]{1,0:T(8,128)(2,1)} %get-tuple-element.80.x_ref, bf16[512,1536]{1,0:T(8,128)(2,1)} %get-tuple-element.82.act_ref, bf16[2,512,1536]{2,1,0:T(8,128)(2,1)} %get-tuple-element.83.grad_ref, ...), custom_call_target="tpu_custom_call" | custom-call | flops 1 | bytes 1 | tf_op jit(solution)/shard_map/feed_back/pallas_call | solution.py:927
  159.0 39.5 %mid_backward.1 = (f32[128,2048]{1,0:T(8,128)}, bf16[512,2048]{1,0:T(8,128)(2,1)}, f32[1,2048]{1,0:T(1,128)}) custom-call(bf16[512,2048]{1,0:T(8,128)(2,1)} %get-tuple-element.84.p_ref, f32[128,2048]{1,0:T(8,128)} %get-tuple-element.85.h_ref, bf16[128,2048]{1,0:T(8,128)(2,1)} %c_ref.1, f32[1,2048]{1,0:T(1,128)} %bitcast.30), custom_call_target="tpu_custom_call" | custom-call | flops 1 | bytes 1 | tf_op jit(solution)/shard_map/mid_backward/pallas_call | solution.py:280
  198.5 5.7 %out_back.1 = (bf16[512,512]{1,0:T(8,128)(2,1)}, bf16[2048,512]{1,0:T(8,128)(2,1)}) custom-call(bf16[512,2048]{1,0:T(8,128)(2,1)} %get-tuple-element.86.dy_ref, bf16[512,2048]{1,0:T(8,128)(2,1)} %w_ref.9, bf16[512,512]{1,0:T(8,128)(2,1)} %get-tuple-element.79.low_ref), custom_call_target="tpu_custom_call" | custom-call | flops 1 | bytes 1 | tf_op jit(solution)/shard_map/out_back/pallas_call | solution.py:964
  204.2 9.1 %attend_back.1 = (f32[512,512]{1,0:T(8,128)}, bf16[8,512,512]{2,1,0:T(8,128)(2,1)}) custom-call(s32[1]{0:T(128)} %bitcast.1.w_ref, bf16[512,512]{1,0:T(8,128)(2,1)} %get-tuple-element.76.q_ref, bf16[8,512,512]{2,1,0:T(8,128)(2,1)} %pass_keys.1.kv_ref, bf16[512,512]{1,0:T(8,128)(2,1)} %get-tuple-element.87.do_ref, f32[512,512]{1,0:T(8,128)} %get-tuple-element.88.o_ref, ...), custom_call_target="tpu_custom_call" | custom-call | flops 1 | bytes 1 | tf_op jit(solution)/shard_map/attend_back/pallas_call | solution.py:813
  213.3 3.7 unspin.2
  217.0 19.6 %reduce-scatter.4.cloned.1.call-done = bf16[1536,256]{1,0:T(8,128)(2,1)} async-done(((bf16[1536,2048]{1,0:T(8,128)(2,1)}), bf16[1536,256]{1,0:T(8,128)(2,1)}) %reduce-scatter.4.cloned.1.call-update) | async-done | bytes 786448 | tf_op jit(solution)/shard_map/reduce_scatter | solution.py:1027
  236.6 2.5 convert_element_type.23
  239.1 5.9 %add_multiply_fusion.1 = (f32[1536,256]{1,0:T(8,128)}, f32[1536,256]{1,0:T(8,128)}, f32[1536,256]{1,0:T(8,128)}, f32[1536,256]{1,0:T(8,128)}) fusion(f32[1536,256]{1,0:T(8,128)S(1)} %copy-done.10, f32[1536,256]{1,0:T(8,128)S(1)} %copy-done.11, bf16[1536,256]{1,0:T(8,128)(2,1)S(1)} %copy-done.1, f32[1536,256]{1,0:T(8,128)} %param.57, f32[1536,256]{1,0:T(8,128)} %param.58), kind=kLoop, calls=%fused_computation.9 | loop fusion | flops 7077888 | bytes 13369344 | tf_op jit(solution)/shard_map/add | solution.py:69
  245.0 116.1 %return_grads.1.e_ref = f32[512,512]{1,0:T(8,128)} custom-call(bf16[8,512,512]{2,1,0:T(8,128)(2,1)} %get-tuple-element.95.x_ref), custom_call_target="tpu_custom_call" | custom-call | flops 1 | bytes 1 | tf_op jit(solution)/shard_map/return_grads/pallas_call | solution.py:532
  361.0 3.0 unspin.3
  364.0 8.5 %project_back.1 = (bf16[512,2048]{1,0:T(8,128)(2,1)}, bf16[2048,1024]{1,0:T(8,128)(2,1)}) custom-call(bf16[512,2048]{1,0:T(8,128)(2,1)} %norm_gather.1.x_ref, bf16[512,512]{1,0:T(8,128)(2,1)} %get-tuple-element.92.q_ref, bf16[512,512]{1,0:T(8,128)(2,1)} %get-tuple-element.97.kv_ref, bf16[2048,512]{1,0:T(8,128)(2,1)} %wq_ref.1, bf16[2,2048,256]{2,1,0:T(8,128)(2,1)} %wkv_ref.1), custom_call_target="tpu_custom_call" | custom-call | flops 1 | bytes 1 | tf_op jit(solution)/shard_map/project_back/pallas_call | solution.py:1002
  372.6 41.3 %last_scatter.1 = (f32[128,2048]{1,0:T(8,128)}, f32[1,2048]{1,0:T(1,128)}, f32[128,2048]{1,0:T(8,128)}) custom-call(bf16[512,2048]{1,0:T(8,128)(2,1)} %get-tuple-element.101.p_ref, bf16[128,2048]{1,0:T(8,128)(2,1)} %t_ref.5, f32[128,2048]{1,0:T(8,128)} %get-tuple-element.102.m_ref, f32[1,2048]{1,0:T(1,128)} %bitcast.28, ...), custom_call_target="tpu_custom_call" | custom-call | flops 1 | bytes 1 | tf_op jit(solution)/shard_map/last_scatter/pallas_call | solution.py:327
  413.9 0.7 maximum_reduce_fusion
  414.8 0.6 reshape.102.x_ref
  415.5 11.6 %gain_sums.1 = f32[2,128]{1,0:T(2,128)} custom-call(f32[4,8,2,128]{3,2,1,0:T(2,128)} %reshape.102.x_ref), custom_call_target="tpu_custom_call" | custom-call | flops 1 | bytes 1 | tf_op jit(solution)/shard_map/gain_sums/pallas_call | solution.py:595
  427.1 5.3 %pad_maximum_fusion = bf16[2048,1536]{1,0:T(8,128)(2,1)} fusion(bf16[2048,512]{1,0:T(8,128)(2,1)S(1)} %copy-done.9, bf16[2048,1024]{1,0:T(8,128)(2,1)} %get-tuple-element.98), kind=kLoop, calls=%fused_computation | loop fusion | flops 12582912 | bytes 12582912 | tf_op jit(solution)/shard_map/concatenate | solution.py:1127
  432.6 2.2 copy.65
  434.7 2.0 copy.66
  436.8 2.1 copy.68
  438.9 2.0 copy.69
  441.5 10.9 %add_multiply_fusion = (f32[2,256,1536]{2,1,0:T(8,128)}, f32[2,256,1536]{2,1,0:T(8,128)}, f32[2,256,1536]{2,1,0:T(8,128)}, f32[2,256,1536]{2,1,0:T(8,128)}, f32[2,256,1536]{2,1,0:T(8,128)}) fusion(f32[2,256,1536]{2,1,0:T(8,128)S(1)} %copy-done, f32[2,256,1536]{2,1,0:T(8,128)} %param.52, f32[2,256,1536]{2,1,0:T(8,128)} %param.53, f32[2,256,1536]{2,1,0:T(8,128)} %param.54, ...), kind=kLoop, calls=%fused_computation.3 | loop fusion | flops 14155776 | bytes 29884416 | tf_op jit(solution)/shard_map/add | solution.py:69
  452.5 48.2 %reduce-scatter.8.cloned.1.call-done = bf16[256,1536]{1,0:T(8,128)(2,1)} async-done(((bf16[2048,1536]{1,0:T(8,128)(2,1)}), bf16[256,1536]{1,0:T(8,128)(2,1)}) %reduce-scatter.8.cloned.1.call-update) | async-done | bytes 786448 | tf_op jit(solution)/shard_map/reduce_scatter | solution.py:1027
  500.7 1.3 convert_element_type.24
  502.0 0.7 slice_bitcast_fusion.2
  502.7 0.8 slice_bitcast_fusion
  503.6 1.4 add_multiply_fusion.2
  504.9 2.1 copy.71
  507.0 2.1 copy.72
  509.2 1.0 copy.73
  510.2 1.0 copy.74
  511.2 1.0 copy.70
  512.2 2.8 add_multiply_fusion.3
  515.1 1.7 add_multiply_fusion.4
  516.8 1.0 copy.80
  517.8 0.6 copy-done.12
  518.4 1.0 copy.81
  (76 shorter events, 1.9 us)
Async XLA Ops:
  7.2 107.6 %all-gather.2.cloned.1.call-start = ((), (), s32[]{:S(2)}) async-start(), calls=%async_computation.3 | async-start | bytes 2621440 | tf_op jit(solution)/shard_map/all_gather | solution.py:1083
  41.3 195.3 %reduce-scatter.4.cloned.1.call-start = ((), (), s32[]{:S(2)}) async-start(), calls=%async_computation.4 | async-start | bytes 7077888 | tf_op jit(solution)/shard_map/reduce_scatter | solution.py:1027
  62.4 5.5 %copy-start.7 = (bf16[512,2048]{1,0:T(8,128)(2,1)S(1)}, bf16[512,2048]{1,0:T(8,128)(2,1)}, u32[]{:S(2)}) copy-start(bf16[512,2048]{1,0:T(8,128)(2,1)} %w_ref.9) | copy-start | bytes 6291460
  134.1 298.3 %reduce-scatter.6.cloned.1.call-start = ((), (), s32[]{:S(2)}) async-start(), calls=%async_computation.5 | async-start | bytes 14155776 | tf_op jit(solution)/shard_map/reduce_scatter | solution.py:1027
  158.9 341.7 %reduce-scatter.8.cloned.1.call-start = ((), (), s32[]{:S(2)}) async-start(), calls=%async_computation.6 | async-start | bytes 7077888 | tf_op jit(solution)/shard_map/reduce_scatter | solution.py:1027
  213.3 25.8 %copy-start.10 = (f32[1536,256]{1,0:T(8,128)S(1)}, f32[1536,256]{1,0:T(8,128)}, u32[]{:S(2)}) copy-start(f32[1536,256]{1,0:T(8,128)} %param.59) | copy-start | bytes 4718596
  213.3 25.8 %copy-start.11 = (f32[1536,256]{1,0:T(8,128)S(1)}, f32[1536,256]{1,0:T(8,128)}, u32[]{:S(2)}) copy-start(f32[1536,256]{1,0:T(8,128)} %param.56) | copy-start | bytes 4718596
  236.6 2.5 copy-start.1
  372.6 41.4 %copy-start.23 = (f32[1,2048]{1,0:T(1,128)S(1)}, f32[1,2048]{1,0:T(1,128)}, u32[]{:S(2)}) copy-start(f32[1,2048]{1,0:T(1,128)} %get-tuple-element.105) | copy-start | bytes 24580
  372.6 41.4 %copy-start.28 = (f32[1,128]{1,0:T(1,128)S(1)}, f32[1,128]{1,0:T(1,128)}, u32[]{:S(2)}) copy-start(f32[1,128]{1,0:T(1,128)} %get-tuple-element.106) | copy-start | bytes 1540
  372.6 41.4 %copy-start.29 = (f32[1,128]{1,0:T(1,128)S(1)}, f32[1,128]{1,0:T(1,128)}, u32[]{:S(2)}) copy-start(f32[1,128]{1,0:T(1,128)} %get-tuple-element.107) | copy-start | bytes 1540
  372.6 54.5 %copy-start.9 = (bf16[2048,512]{1,0:T(8,128)(2,1)S(1)}, bf16[2048,512]{1,0:T(8,128)(2,1)}, u32[]{:S(2)}) copy-start(bf16[2048,512]{1,0:T(8,128)(2,1)} %get-tuple-element.99) | copy-start | bytes 6291460
  432.5 8.4 %copy-start.22 = (f32[2,128]{1,0:T(2,128)S(1)}, f32[2,128]{1,0:T(2,128)}, u32[]{:S(2)}) copy-start(f32[2,128]{1,0:T(2,128)} %gain_sums.1) | copy-start | bytes 3076
  432.5 8.4 %copy-start.24 = (f32[136]{0:T(256)S(1)}, f32[136]{0:T(256)}, u32[]{:S(2)}) copy-start(f32[136]{0:T(256)} %param.63) | copy-start | bytes 1636
  432.5 8.4 %copy-start.25 = (f32[136]{0:T(256)S(1)}, f32[136]{0:T(256)}, u32[]{:S(2)}) copy-start(f32[136]{0:T(256)} %param.60) | copy-start | bytes 1636
  432.5 8.4 %copy-start.26 = (f32[136]{0:T(256)S(1)}, f32[136]{0:T(256)}, u32[]{:S(2)}) copy-start(f32[136]{0:T(256)} %param.61) | copy-start | bytes 1636
  432.5 8.4 %copy-start.27 = (f32[136]{0:T(256)S(1)}, f32[136]{0:T(256)}, u32[]{:S(2)}) copy-start(f32[136]{0:T(256)} %param.62) | copy-start | bytes 1636
  432.5 9.0 %copy-start = (f32[2,256,1536]{2,1,0:T(8,128)S(1)}, f32[2,256,1536]{2,1,0:T(8,128)}, u32[]{:S(2)}) copy-start(f32[2,256,1536]{2,1,0:T(8,128)} %param.55) | copy-start | bytes 9437188
  452.5 51.1 %copy-start.3 = (f32[512,256]{0,1:T(8,128)S(1)}, f32[512,256]{0,1:T(8,128)}, u32[]{:S(2)}) copy-start(f32[512,256]{0,1:T(8,128)} %copy.65) | copy-start | bytes 1572868
  452.5 51.1 %copy-start.4 = (f32[512,256]{0,1:T(8,128)S(1)}, f32[512,256]{0,1:T(8,128)}, u32[]{:S(2)}) copy-start(f32[512,256]{0,1:T(8,128)} %copy.66) | copy-start | bytes 1572868
  452.5 51.1 %copy-start.5 = (f32[512,256]{0,1:T(8,128)S(1)}, f32[512,256]{0,1:T(8,128)}, u32[]{:S(2)}) copy-start(f32[512,256]{0,1:T(8,128)} %copy.68) | copy-start | bytes 1572868
  452.5 51.1 %copy-start.6 = (f32[512,256]{0,1:T(8,128)S(1)}, f32[512,256]{0,1:T(8,128)}, u32[]{:S(2)}) copy-start(f32[512,256]{0,1:T(8,128)} %copy.69) | copy-start | bytes 1572868
  504.9 6.2 %copy-start.8 = (f32[512,256]{0,1:T(8,128)S(1)}, f32[512,256]{0,1:T(8,128)}, u32[]{:S(2)}) copy-start(f32[512,256]{0,1:T(8,128)} %slice_bitcast_fusion) | copy-start | bytes 1572868
  507.0 5.1 copy-start.14
  507.0 5.1 copy-start.15
  507.0 5.1 copy-start.16
  510.2 2.0 copy-start.17
  512.2 2.9 copy-start.2
  512.2 2.9 copy-start.18
  512.2 2.9 copy-start.19
  512.2 2.9 copy-start.20
  512.2 2.9 copy-start.21
  515.1 1.7 copy-start.13
  516.8 1.6 copy-start.12
Sparse Core Ops, SparseCore 0:
  41.4 36.7 all-gather.1
  134.3 102.2 reduce-scatter.3
  238.9 161.2 reduce-scatter.5
  432.6 67.9 reduce-scatter.7

commit v2 on v1

--- a/solution.py
+++ b/solution.py
@@ -139,7 +139,7 @@
         copy.wait_recv()
 
 
-def scatter_square(copies, slot, p_ref, buf, stage, emit):
+def scatter_square(copies, slot, p_ref, buf, stage, emit, fill=None):
     me, xn, yn, dg = square()
     rows = p_ref.shape[0] // 4
     half = rows // 2
@@ -147,10 +147,16 @@
     def part(owner, low):
         return p_ref.at[pl.ds(pl.multiple_of(owner * rows + low, half), half)]
 
+    if fill is None:
+        fill = lambda owner: None
+    fill(dg)
     c0 = copies.go(part(dg, 0), buf.at[0], slot, xn)
     c1 = copies.go(part(dg, half), buf.at[1], slot + 1, yn)
+    fill(xn)
     c2 = copies.go(part(xn, 0), buf.at[2], slot + 2, xn)
+    fill(yn)
     c3 = copies.go(part(yn, half), buf.at[3], slot + 3, yn)
+    fill(me)
     c0.wait_recv()
     stage[0] = (part(yn, 0)[...].astype(F32) + buf[0].astype(F32)).astype(BF16)
     c4 = copies.go(stage.at[0], buf.at[4], slot + 4, yn)
@@ -179,53 +185,31 @@
     )
 
 
-def norm_gather_kernel(t_ref, g_ref, o_ref, own, send, recv):
+def mid_forward_kernel(a_ref, w_ref, t_ref, g_ref, h_ref, o_ref, p_ref, buf, stage, own, send, recv):
     _, xn, yn, _ = square()
-    greet("narrow", (xn, yn))
-    hidden = t_ref[...].astype(F32)
-    own[...] = (hidden * row_scale(hidden) * g_ref[...]).astype(BF16)
-    copies = Copies(send, recv)
-    gather_square(copies, 0, own, o_ref)
-    copies.finish()
-
-
-def norm_gather(tokens, gain_row, special):
-    rows = tokens.shape[0]
-    if not special:
-        hidden = tokens.astype(F32)
-        normed = (hidden * row_scale(hidden) * gain_row).astype(BF16)
-        return lax.all_gather(normed, "narrow", axis=0, tiled=True)
-    return pl.pallas_call(
-        norm_gather_kernel,
-        name="norm_gather",
-        out_shape=jax.ShapeDtypeStruct((4 * rows, D), BF16),
-        in_specs=[VM, VM],
-        out_specs=VM,
-        scratch_shapes=[pltpu.VMEM((rows, D), BF16)] + dma_sems(6),
-        cost_estimate=cost(1, 1),
-        compiler_params=remote_params(1),
-    )(tokens, gain_row)
-
-
-def mid_forward_kernel(p_ref, t_ref, g_ref, h_ref, o_ref, buf, stage, own, send, recv):
-    _, xn, yn, _ = square()
-    half = t_ref.shape[0] // 2
+    rows = t_ref.shape[0]
+    half = rows // 2
     greet("narrow", (xn, yn))
     copies = Copies(send, recv)
+
+    def fill(owner):
+        at = pl.ds(pl.multiple_of(owner * rows, rows), rows)
+        p_ref[at, :] = dot(a_ref[at, :], w_ref[...]).astype(BF16)
 
     def emit(low, total):
         hidden = t_ref[pl.ds(low, half)].astype(F32) + total
         h_ref[pl.ds(low, half)] = hidden
         own[pl.ds(low, half)] = (hidden * row_scale(hidden) * g_ref[...]).astype(BF16)
 
-    scatter_square(copies, 0, p_ref, buf, stage, emit)
+    scatter_square(copies, 0, p_ref, buf, stage, emit, fill)
     gather_square(copies, 6, own, o_ref)
     copies.finish()
 
 
-def mid_forward(partial, tokens, gain_row, special):
+def mid_forward(attn_low, weight, tokens, gain_row, special):
     rows = tokens.shape[0]
     if not special:
+        partial = dot(attn_low, weight).astype(BF16)
         hidden = tokens.astype(F32) + lax.psum_scatter(
             partial, "narrow", scatter_dimension=0, tiled=True
         ).astype(F32)
@@ -238,12 +222,13 @@
             jax.ShapeDtypeStruct((rows, D), F32),
             jax.ShapeDtypeStruct((4 * rows, D), BF16),
         ),
-        in_specs=[VM] * 3,
+        in_specs=[VM] * 4,
         out_specs=(VM, VM),
-        scratch_shapes=scatter_space(rows) + [pltpu.VMEM((rows, D), BF16)] + dma_sems(12),
+        scratch_shapes=[pltpu.VMEM((4 * rows, D), BF16)]
+        + scatter_space(rows) + [pltpu.VMEM((rows, D), BF16)] + dma_sems(12),
         cost_estimate=cost(1, 1),
         compiler_params=remote_params(2),
-    )(partial, tokens, gain_row)
+    )(attn_low, weight, tokens, gain_row)
 
 
 def mid_backward_kernel(
@@ -293,7 +278,37 @@
     )(partial, hidden_mid, cotangent, gain_row)
 
 
-def last_kernel(p_ref, t_ref, m_ref, g_ref, q_ref, h_ref, o_ref, gg_ref, b_ref, buf, stage, buf2, stage2, send, recv):
+def out_scatter_kernel(p_ref, h_ref, o_ref, buf, stage, send, recv):
+    _, xn, yn, _ = square()
+    half = h_ref.shape[0] // 2
+    greet("narrow", (xn, yn))
+    copies = Copies(send, recv)
+
+    def emit(low, total):
+        o_ref[pl.ds(low, half)] = h_ref[pl.ds(low, half)] + total
+
+    scatter_square(copies, 0, p_ref, buf, stage, emit)
+    copies.finish()
+
+
+def out_scatter(partial, hidden_mid, special):
+    rows = hidden_mid.shape[0]
+    if not special:
+        total = lax.psum_scatter(partial, "narrow", scatter_dimension=0, tiled=True)
+        return hidden_mid + total.astype(F32)
+    return pl.pallas_call(
+        out_scatter_kernel,
+        name="out_scatter",
+        out_shape=jax.ShapeDtypeStruct((rows, D), F32),
+        in_specs=[VM] * 2,
+        out_specs=VM,
+        scratch_shapes=scatter_space(rows) + dma_sems(6),
+        cost_estimate=cost(1, 1),
+        compiler_params=remote_params(9),
+    )(partial, hidden_mid)
+
+
+def in_scatter_kernel(p_ref, t_ref, m_ref, g_ref, o_ref, gg_ref, buf, stage, send, recv):
     _, xn, yn, _ = square()
     half = t_ref.shape[0] // 2
     greet("narrow", (xn, yn))
@@ -307,37 +322,31 @@
         gg_ref[...] += gain_sum
         o_ref[pl.ds(low, half)] = m_ref[pl.ds(low, half)] + back
 
-    def emit_out(low, total):
-        b_ref[pl.ds(low, half)] = h_ref[pl.ds(low, half)] + total
-
     scatter_square(copies, 0, p_ref, buf, stage, emit)
-    scatter_square(copies, 6, q_ref, buf2, stage2, emit_out)
     copies.finish()
 
 
-def last_scatter(partial, tokens, mid_grad, gain_row, out_partial, hidden_mid, special):
+def in_scatter(partial, tokens, mid_grad, gain_row, special):
     rows = tokens.shape[0]
     if not special:
         total = lax.psum_scatter(partial, "narrow", scatter_dimension=0, tiled=True).astype(F32)
         hidden = tokens.astype(F32)
         scale = row_scale(hidden)
         back, gain_sum = norm_back(total, hidden * scale, scale, gain_row)
-        out = lax.psum_scatter(out_partial, "narrow", scatter_dimension=0, tiled=True)
-        return mid_grad + back, gain_sum, hidden_mid + out.astype(F32)
+        return mid_grad + back, gain_sum
     return pl.pallas_call(
-        last_kernel,
-        name="last_scatter",
+        in_scatter_kernel,
+        name="in_scatter",
         out_shape=(
             jax.ShapeDtypeStruct((rows, D), F32),
             jax.ShapeDtypeStruct((1, D), F32),
-            jax.ShapeDtypeStruct((rows, D), F32),
-        ),
-        in_specs=[VM] * 6,
-        out_specs=(VM,) * 3,
-        scratch_shapes=scatter_space(rows) + scatter_space(rows) + dma_sems(12),
+        ),
+        in_specs=[VM] * 4,
+        out_specs=(VM,) * 2,
+        scratch_shapes=scatter_space(rows) + dma_sems(6),
         cost_estimate=cost(1, 1),
         compiler_params=remote_params(4),
-    )(partial, tokens, mid_grad, gain_row, out_partial, hidden_mid)
+    )(partial, tokens, mid_grad, gain_row)
 
 
 def line(count):
@@ -372,73 +381,6 @@
         device_id={"wide": peer},
         device_id_type=MESH,
     )
-
-
-def pass_keys_kernel(count, x_ref, o_ref, send, recv, mate_send, mate_recv):
-    w, z, c, chips, mate, above, below = line(count)
-    greet_line(count)
-    own_up = wide_copy(x_ref, o_ref.at[w], send, recv, 0, above)
-
-    @pl.when(z < chips - 1)
-    def _():
-        own_up.start()
-
-    own_mate = wide_copy(x_ref, o_ref.at[w], mate_send, mate_recv, 0, mate)
-    own_mate.start()
-    o_ref[w] = x_ref[...]
-    for step in range(1, chips):
-        block = jnp.maximum(w - 2 * step, 0)
-        arrived = wide_copy(o_ref.at[block], o_ref.at[block], send, recv, step - 1, above)
-        onward = wide_copy(o_ref.at[block], o_ref.at[block], send, recv, min(step, chips - 2), above)
-        share = wide_copy(o_ref.at[block], o_ref.at[block], mate_send, mate_recv, step, mate)
-
-        @pl.when(z >= step)
-        def _():
-            arrived.wait_recv()
-            if step < chips - 1:
-
-                @pl.when(z < chips - 1)
-                def _():
-                    onward.start()
-
-            share.start()
-
-    own_mate.wait()
-
-    @pl.when(z < chips - 1)
-    def _():
-        own_up.wait_send()
-
-    for step in range(1, chips):
-        block = jnp.maximum(w - 2 * step, 0)
-        onward = wide_copy(o_ref.at[block], o_ref.at[block], send, recv, min(step, chips - 2), above)
-        share = wide_copy(o_ref.at[block], o_ref.at[block], mate_send, mate_recv, step, mate)
-
-        @pl.when(z >= step)
-        def _():
-            share.wait()
-            if step < chips - 1:
-
-                @pl.when(z < chips - 1)
-                def _():
-                    onward.wait_send()
-
-
-def pass_keys(keys_values, count, special):
-    rows, width = keys_values.shape
-    if not special:
-        return lax.all_gather(keys_values, "wide", axis=0)
-    chips = count // 2
-    return pl.pallas_call(
-        functools.partial(pass_keys_kernel, count),
-        name="pass_keys",
-        out_shape=jax.ShapeDtypeStruct((count, rows, width), BF16),
-        in_specs=[VM],
-        out_specs=VM,
-        scratch_shapes=dma_sems(chips - 1) + dma_sems(chips),
-        cost_estimate=cost(1, 1),
-        compiler_params=remote_params(5),
-    )(keys_values)
 
 
 def return_grads_kernel(
@@ -857,6 +799,262 @@
     )(grad, raw, gain_row, cosine, sine)
 
 
+def front_kernel(
+    count, heads, group,
+    t_ref, c_ref, g_ref, wq_hbm, wkv_hbm, qg_ref, kg_ref, cos_ref, sin_ref,
+    dy_hbm, x_hbm, q_hbm, qraw_hbm, kraw_hbm, kv_hbm, o_ref, low_ref, lse_ref,
+    own, x, weight, q, qraw, kraw, kv, acc,
+    send, recv, z_send, z_recv, m_send, m_recv, c_send, c_recv, load_sem, store_sem, kv_sem,
+):
+    me, xn, yn, dg = square()
+    w, z, c, chips, mate, above, below = line(count)
+    rows = t_ref.shape[0]
+    half = rows // 2
+    all_rows = 4 * rows
+    q_width, kv_width = wq_hbm.shape[1], wkv_hbm.shape[2]
+    owners = (me, xn, yn, dg)
+    loads = [
+        pltpu.make_async_copy(wq_hbm, weight.at[:, pl.ds(0, q_width)], load_sem.at[0]),
+        pltpu.make_async_copy(wkv_hbm.at[0], weight.at[:, pl.ds(q_width, kv_width)], load_sem.at[1]),
+        pltpu.make_async_copy(
+            wkv_hbm.at[1], weight.at[:, pl.ds(q_width + kv_width, kv_width)], load_sem.at[2]
+        ),
+    ]
+    for load in loads:
+        load.start()
+
+    has_above, has_below = z < chips - 1, z > 0
+    barrier = pltpu.get_barrier_semaphore()
+    for peer in (xn, yn, dg):
+        pl.semaphore_signal(barrier, inc=1, device_id={"narrow": peer}, device_id_type=MESH)
+
+    @pl.when(has_above)
+    def _():
+        pl.semaphore_signal(barrier, inc=1, device_id={"wide": above}, device_id_type=MESH)
+
+    @pl.when(has_below)
+    def _():
+        pl.semaphore_signal(barrier, inc=1, device_id={"wide": below}, device_id_type=MESH)
+
+    pl.semaphore_signal(barrier, inc=1, device_id={"wide": mate}, device_id_type=MESH)
+    hidden = t_ref[...].astype(F32)
+    own[...] = (hidden * row_scale(hidden) * g_ref[...]).astype(BF16)
+    pl.semaphore_wait(barrier, 4 + has_above.astype(jnp.int32) + has_below.astype(jnp.int32))
+
+    copies = Copies(send, recv)
+
+    def part(owner, low):
+        return x.at[pl.ds(pl.multiple_of(owner * rows + low, half), half)]
+
+    upper, lower = own.at[pl.ds(0, half)], own.at[pl.ds(half, half)]
+    xa = copies.go(upper, part(me, 0), 0, xn)
+    yb = copies.go(lower, part(me, half), 1, yn)
+    xb = copies.go(lower, part(me, half), 2, xn)
+    ya = copies.go(upper, part(me, 0), 3, yn)
+
+    def unit_rows(unit):
+        return pl.ds(pl.multiple_of(owners[unit] * rows, rows), rows)
+
+    def unit(block, k):
+        return kv.at[block, unit_rows(k)]
+
+    def to_above(s, k):
+        block = jnp.maximum(w - 2 * s, 0)
+        return wide_copy(unit(block, k), unit(block, k), z_send, z_recv, 4 * s + k, above)
+
+    def from_below(s, k):
+        block = jnp.maximum(w - 2 * s, 0)
+        return wide_copy(unit(block, k), unit(block, k), z_send, z_recv, 4 * (s - 1) + k, above)
+
+    def to_mate(s, k):
+        block = jnp.maximum(w - 2 * s, 0)
+        return wide_copy(unit(block, k), unit(block, k), m_send, m_recv, 4 * s + k, mate)
+
+    def project(k):
+        at = unit_rows(k)
+        out = dot(x[at, :], weight[...])
+        cosine, sine = cos_ref[at, :], sin_ref[at, :]
+        qraw[at, :] = out[:, :q_width]
+        kraw[at, :] = out[:, q_width : q_width + kv_width]
+        for h in range(heads):
+            lanes = slice(h * HD, (h + 1) * HD)
+            q[at, lanes] = spin(out[:, lanes], qg_ref[...], cosine, sine).astype(BF16)
+        for h in range(heads // group):
+            lanes = slice(q_width + h * HD, q_width + (h + 1) * HD)
+            kv[w, at, h * HD : (h + 1) * HD] = spin(
+                out[:, lanes], kg_ref[...], cosine, sine
+            ).astype(BF16)
+        kv[w, at, kv_width:] = out[:, q_width + kv_width :].astype(BF16)
+
+        @pl.when(has_above)
+        def _():
+            to_above(0, k).start()
+
+        @pl.when(c == 0)
+        def _():
+            to_mate(0, k).start()
+
+    def receive(s, k):
+        @pl.when(z >= s)
+        def _():
+            from_below(s, k).wait_recv()
+            if s < chips - 1:
+
+                @pl.when(has_above)
+                def _():
+                    to_above(s, k).start()
+
+            to_mate(s, k).start()
+
+    x[unit_rows(0), :] = own[...]
+    for load in loads:
+        load.wait()
+    project(0)
+    xa.wait_recv()
+    yf = copies.go(part(xn, 0), part(xn, 0), 4, yn)
+    yb.wait_recv()
+    xf = copies.go(part(yn, half), part(yn, half), 5, xn)
+    receive(1, 0)
+    xb.wait_recv()
+    project(1)
+    ya.wait_recv()
+    project(2)
+    receive(2, 0)
+    receive(1, 1)
+    receive(1, 2)
+    receive(3, 0)
+    yf.wait_recv()
+    xf.wait_recv()
+    project(3)
+    away = Copies(c_send, c_recv)
+    dy_part = dy_hbm.at[unit_rows(0)]
+    for slot, peer in enumerate((dg, xn, yn)):
+        away.go(c_ref, dy_part, slot, peer)
+    stores = [
+        pltpu.make_async_copy(src, dst, store_sem.at[n])
+        for n, (src, dst) in enumerate(
+            ((x, x_hbm), (q, q_hbm), (qraw, qraw_hbm), (kraw, kraw_hbm), (c_ref, dy_part))
+        )
+    ]
+    for store in stores:
+        store.start()
+    acc[...] = jnp.zeros_like(acc)
+    ones = jnp.ones((all_rows, HD), BF16)
+
+    def keep(j):
+        return pltpu.make_async_copy(kv.at[j], kv_hbm.at[j], kv_sem.at[j])
+
+    def block(j, masked):
+        for h in range(heads):
+            head = h // group
+            key = kv[j, :, head * HD : (head + 1) * HD]
+            value = kv[j, :, kv_width + head * HD : kv_width + (head + 1) * HD]
+            terms = jnp.exp2(dot_nt(q[:, h * HD : (h + 1) * HD], key) * (FACTOR * LOG2E))
+            if masked:
+                at = lax.broadcasted_iota(jnp.int32, (all_rows, all_rows), 0)
+                key_at = lax.broadcasted_iota(jnp.int32, (all_rows, all_rows), 1)
+                terms = jnp.where(key_at <= at, terms, 0.0)
+            acc[h] += dot(terms.astype(BF16), jnp.concatenate([value, ones], axis=1))
+        keep(j).start()
+
+    block(w, True)
+
+    @pl.loop(1 - c, 2 * z + 1)
+    def _(i):
+        for s, units in ((1, ((2, 1), (2, 2), (1, 3))), (2, ((3, 1), (3, 2), (2, 3))), (3, ((3, 3),))):
+
+            @pl.when(i == 2 * s - 1)
+            def _():
+                for pair in units:
+                    receive(*pair)
+
+        for s in range(chips):
+
+            @pl.when(i == 2 * s)
+            def _():
+                for k in range(4):
+                    to_mate(s, k).wait_recv()
+
+        odd = i % 2
+        step = (i + 1) // 2
+        block(2 * (z - step) + c + (1 - odd) * (1 - 2 * c), False)
+
+    for h in range(heads):
+        total = acc[h, :, HD:]
+        out = acc[h, :, :HD] / total
+        o_ref[:, h * HD : (h + 1) * HD] = out
+        low_ref[:, h * HD : (h + 1) * HD] = out.astype(BF16)
+        lse_ref[h : h + 1, :] = jnp.transpose(jnp.log2(total))[0:1]
+
+    copies.finish()
+    for copy in away.sent:
+        copy.wait()
+    for s in range(chips):
+        for k in range(4):
+
+            @pl.when((z >= s) & has_above)
+            def _():
+                to_above(s, k).wait_send()
+
+            @pl.when((z >= s) & ((c == 0) | (s > 0)))
+            def _():
+                to_mate(s, k).wait_send()
+
+    for store in stores:
+        store.wait()
+
+    @pl.loop(0, w + 1)
+    def _(j):
+        keep(j).wait()
+
+
+def front(tokens, cotangent, gain_row, query_weight, keyvalue_weight, query_gain, key_gain, cosine, sine, count):
+    rows = tokens.shape[0]
+    all_rows = 4 * rows
+    q_width, kv_width = query_weight.shape[1], keyvalue_weight.shape[2]
+    heads, group = q_width // HD, q_width // kv_width
+    chips = count // 2
+    anywhere = pl.BlockSpec(memory_space=pl.ANY)
+    return pl.pallas_call(
+        functools.partial(front_kernel, count, heads, group),
+        name="front",
+        out_shape=(
+            jax.ShapeDtypeStruct((all_rows, D), BF16),
+            jax.ShapeDtypeStruct((all_rows, D), BF16),
+            jax.ShapeDtypeStruct((all_rows, q_width), BF16),
+            jax.ShapeDtypeStruct((all_rows, q_width), F32),
+            jax.ShapeDtypeStruct((all_rows, kv_width), F32),
+            jax.ShapeDtypeStruct((count, all_rows, 2 * kv_width), BF16),
+            jax.ShapeDtypeStruct((all_rows, q_width), F32),
+            jax.ShapeDtypeStruct((all_rows, q_width), BF16),
+            jax.ShapeDtypeStruct((heads, all_rows), F32),
+        ),
+        in_specs=[VM, VM, VM, anywhere, anywhere, VM, VM, VM, VM],
+        out_specs=(anywhere,) * 6 + (VM,) * 3,
+        scratch_shapes=[
+            pltpu.VMEM((rows, D), BF16),
+            pltpu.VMEM((all_rows, D), BF16),
+            pltpu.VMEM((D, q_width + 2 * kv_width), BF16),
+            pltpu.VMEM((all_rows, q_width), BF16),
+            pltpu.VMEM((all_rows, q_width), F32),
+            pltpu.VMEM((all_rows, kv_width), F32),
+            pltpu.VMEM((count, all_rows, 2 * kv_width), BF16),
+            pltpu.VMEM((heads, all_rows, 2 * HD), F32),
+        ]
+        + dma_sems(6)
+        + dma_sems(4 * chips)
+        + dma_sems(4 * chips)
+        + dma_sems(3)
+        + [
+            pltpu.SemaphoreType.DMA((3,)),
+            pltpu.SemaphoreType.DMA((5,)),
+            pltpu.SemaphoreType.DMA((count,)),
+        ],
+        cost_estimate=cost(1, 1),
+        compiler_params=remote_params(8),
+    )(tokens, cotangent, gain_row, query_weight, keyvalue_weight, query_gain, key_gain, cosine, sine)
+
+
 def feed_kernel(x_ref, dy_ref, w_ref, d_ref, act_ref, grad_ref, down_ref):
     x, dy = x_ref[...], dy_ref[...]
     gate = dot(x, w_ref[0])
@@ -983,7 +1181,7 @@
     )(dy, weight, attn_low)
 
 
-def project_back_kernel(x_ref, q_ref, kv_ref, wq_ref, wkv_ref, in_ref, full_ref):
+def project_back_kernel(x_ref, q_ref, kv_ref, wq_ref, wkv_ref, out_ref, in_ref, full_ref):
     q_width, kv_width = wq_ref.shape[1], wkv_ref.shape[2]
     x = x_ref[...]
     key, value = kv_ref[:, :kv_width], kv_ref[:, kv_width:]
@@ -991,11 +1189,12 @@
         dot_nt(q_ref[...], wq_ref[...]) + dot_nt(key, wkv_ref[0]) + dot_nt(value, wkv_ref[1])
     ).astype(BF16)
     full_ref[:, :q_width] = dot_tn(x, q_ref[...]).astype(BF16)
-    full_ref[:, q_width:] = dot_tn(x, kv_ref[...]).astype(BF16)
-
-
-def project_back(x, q_back, kv_back, query_weight, keyvalue_weight):
-    rows = x.shape[0]
+    full_ref[:, q_width : q_width + 2 * kv_width] = dot_tn(x, kv_ref[...]).astype(BF16)
+    full_ref[:, q_width + 2 * kv_width :] = out_ref[...]
+
+
+def project_back(x, q_back, kv_back, query_weight, keyvalue_weight, output_full):
+    rows, out_width = x.shape[0], output_full.shape[1]
     q_width, kv_width = query_weight.shape[1], keyvalue_weight.shape[2]
     tile = 512
     whole = lambda i: (0, 0)
@@ -1005,7 +1204,7 @@
         grid=(D // tile,),
         out_shape=(
             jax.ShapeDtypeStruct((rows, D), BF16),
-            jax.ShapeDtypeStruct((D, q_width + 2 * kv_width), BF16),
+            jax.ShapeDtypeStruct((D, q_width + 2 * kv_width + out_width), BF16),
         ),
         in_specs=[
             pl.BlockSpec((rows, tile), lambda i: (0, i)),
@@ -1013,14 +1212,15 @@
             pl.BlockSpec((rows, 2 * kv_width), whole),
             pl.BlockSpec((tile, q_width), lambda i: (i, 0)),
             pl.BlockSpec((2, tile, kv_width), lambda i: (0, i, 0)),
+            pl.BlockSpec((tile, out_width), lambda i: (i, 0)),
         ],
         out_specs=(
             pl.BlockSpec((rows, tile), lambda i: (0, i)),
-            pl.BlockSpec((tile, q_width + 2 * kv_width), lambda i: (i, 0)),
+            pl.BlockSpec((tile, q_width + 2 * kv_width + out_width), lambda i: (i, 0)),
         ),
         compiler_params=params("arbitrary"),
         cost_estimate=cost(4 * rows * D * (q_width + 2 * kv_width), 6 * D * (q_width + 2 * kv_width)),
-    )(x, q_back, kv_back, query_weight, keyvalue_weight)
+    )(x, q_back, kv_back, query_weight, keyvalue_weight, output_full)
 
 
 def wide_scatter(partial, axis):
@@ -1075,18 +1275,31 @@
     query_gain = gain_copy[2 * D : 2 * D + HD].reshape(1, HD)
     key_gain = gain_copy[2 * D + HD :].reshape(1, HD)
 
-    attn_input = norm_gather(tokens, attn_gain, special)
     positions = (wide_index * stretch_rows + jnp.arange(stretch_rows, dtype=jnp.int32)).astype(F32)
     cosine, sine = rope_tables(positions)
-    kv_low, key_raw = keys_values(attn_input, keyvalue_weight, key_gain, cosine, sine)
-    late_cotangent, kv_low = lax.optimization_barrier((cotangent, kv_low))
-    back_mlp = lax.all_gather(late_cotangent, "narrow", axis=0, tiled=True)
-    query_low, query_raw = queries(attn_input, query_weight, query_gain, cosine, sine)
-    kv_all = pass_keys(kv_low, wide, special)
-    attn_out, attn_low, lse = attend(w_scalar, query_low, kv_all, q_heads, group)
-    hidden_mid, mlp_input = mid_forward(
-        dot(attn_low, output_weight).astype(BF16), tokens, mlp_gain, special
-    )
+    if special:
+        back_mlp, attn_input, query_low, query_raw, key_raw, kv_all, attn_out, attn_low, lse = front(
+            tokens,
+            cotangent,
+            attn_gain,
+            query_weight,
+            keyvalue_weight,
+            query_gain,
+            key_gain,
+            cosine,
+            sine,
+            wide,
+        )
+    else:
+        hidden = tokens.astype(F32)
+        normed = (hidden * row_scale(hidden) * attn_gain).astype(BF16)
+        attn_input = lax.all_gather(normed, "narrow", axis=0, tiled=True)
+        kv_low, key_raw = keys_values(attn_input, keyvalue_weight, key_gain, cosine, sine)
+        query_low, query_raw = queries(attn_input, query_weight, query_gain, cosine, sine)
+        kv_all = lax.all_gather(kv_low, "wide", axis=0)
+        attn_out, attn_low, lse = attend(w_scalar, query_low, kv_all, q_heads, group)
+        back_mlp = lax.all_gather(cotangent, "narrow", axis=0, tiled=True)
+    hidden_mid, mlp_input = mid_forward(attn_low, output_weight, tokens, mlp_gain, special)
     act, act_grads, down_full = feed(mlp_input, back_mlp, gateup_weight, down_weight)
     down_total = wide_scatter(down_full, 1)
     gateup_full, in_partial, out_partial = feed_back(
@@ -1114,21 +1327,20 @@
     kv_sum = return_grads(kv_sums, wide, special)
     kv_back, key_gain_grad = unspin(kv_sum, key_raw, key_gain, cosine, sine)
     normed_partial, project_full = project_back(
-        attn_input, query_back, kv_back, query_weight, keyvalue_weight
-    )
-    input_grad, attn_gain_grad, block_output = last_scatter(
-        normed_partial, tokens, mid_grad, attn_gain, out_partial, hidden_mid, special
-    )
+        attn_input, query_back, kv_back, query_weight, keyvalue_weight, output_full
+    )
+    project_full, out_partial = lax.optimization_barrier((project_full, out_partial))
+    block_output = out_scatter(out_partial, hidden_mid, special)
+    project_full, gateup_total, block_output, normed_partial = lax.optimization_barrier(
+        (project_full, gateup_total, block_output, normed_partial)
+    )
+    rest_total = wide_scatter(project_full, 0).astype(F32)
+    input_grad, attn_gain_grad = in_scatter(normed_partial, tokens, mid_grad, attn_gain, special)
     gain_partial = jnp.concatenate(
         [attn_gain_grad, mlp_gain_grad, query_gain_grad, key_gain_grad], axis=1
     ).reshape(-1)
     gain_total = gain_sums(gain_partial, wide, narrow, special)
 
-    rest_full = jnp.concatenate([project_full, output_full], axis=1)
-    rest_full, gateup_total, gain_total, block_output, input_grad = lax.optimization_barrier(
-        (rest_full, gateup_total, gain_total, block_output, input_grad)
-    )
-    rest_total = wide_scatter(rest_full, 0).astype(F32)
     query_total = rest_total[:, :q_width]
     keyvalue_total = jnp.stack(
         [rest_total[:, q_width : q_width + kv_width], rest_total[:, q_width + kv_width : q_width + 2 * kv_width]]

time: 535 us -> 464 us (0.87)
  waiting for transfers between devices: 67.8 us -> 27.5 us
  Pallas kernels: 382 us -> 364 us
    reduce_scatter x3, waiting for transfers between devices: 67.7 us -> 27.5 us  [wide_scatter(): return lax.psum_scatter(partial, 'wide', scatter_dimension=axis, tiled=True)]
    pallas_call x1, Pallas kernels: 116 us -> 106 us  [return_grads(): pl.pallas_call(functools.partial(return_grads_kernel, count), name='retur...]
    pallas_call x6 -> x3, Pallas kernels: 97.2 us -> 87.7 us  [the longest x1 50.3 us: front(): pl.pallas_call(functools.partial(front_kernel, count, heads, group), name...]
    unnamed x72 -> x71, local copies, waits for them, and re-layouts: 18.8 us -> 15.9 us
  transfers between devices with their start and end apart: 4 -> 3, of which waited for: 2 -> 2; matrix products, arithmetic and copies ran while one was open for 7% -> 6% of each run, Pallas kernels for 63% -> 55%
where the time goes in v2:
time: 464 us; the launch traced here: 457 us
  Pallas kernels  364 us (78%)
  other arithmetic  30 us (6%)
  waiting for transfers between devices  27.5 us (6%)
  local copies, waits for them, and re-layouts  20.9 us (5%)
  between operations  14.5 us (3%)
    pallas_call x1, Pallas kernels, return_grads(): pl.pallas_call(functools.partial(return_grads_kernel, count), name='retur...  106 us
    pallas_call x1, Pallas kernels, front(): pl.pallas_call(functools.partial(front_kernel, count, heads, group), name...  50.3 us
    pallas_call x1, Pallas kernels, mid_forward(): pl.pallas_call(mid_forward_kernel, name='mid_forward', out_shape=(jax.Sha...  40.8 us
    pallas_call x1, Pallas kernels, mid_backward(): pl.pallas_call(mid_backward_kernel, name='mid_backward', out_shape=(jax.S...  39.6 us
    reduce_scatter x3, waiting for transfers between devices, wide_scatter(): return lax.psum_scatter(partial, 'wide', scatter_dimension=axis, tiled=True)  27.5 us
    pallas_call x1, Pallas kernels, feed_back(): pl.pallas_call(feed_back_kernel, name='feed_back', grid=(width // tile,),...  24.9 us
    add x6, other arithmetic, adamw(): average_new = EMA_KEEP * average + (1.0 - EMA_KEEP) * master_new  23.5 us
    pallas_call x1, Pallas kernels, out_scatter(): pl.pallas_call(out_scatter_kernel, name='out_scatter', out_shape=jax.Shap...  20.3 us
  transfers between devices with their start and end apart: 3, of which 2 were waited for; matrix products, arithmetic and copies ran while one was open for 6% of the time, Pallas kernels for 55%

profile of v2, /device:TPU:0, one launch (start us, length us, event | category | flops | bytes accessed | tf_op | source)
XLA Modules:
  0.0 457.3 jit_solution(4294759918436820904)
XLA Ops:
  7.3 1.3 fusion.13
  8.6 1.3 slice_bitcast_fusion.3
  9.9 1.0 fusion.5
  10.9 1.0 pad_maximum_fusion.1
  11.9 50.3 %front.1 = (bf16[512,2048]{1,0:T(8,128)(2,1)}, bf16[512,2048]{1,0:T(8,128)(2,1)}, bf16[512,512]{1,0:T(8,128)(2,1)}, f32[512,512]{1,0:T(8,128)}, f32[512,256]{1,0...) custom-call(bf16[128,2048]{1,0:T(8,128)(2,1)} %t_ref.5, ...), custom_call_target="tpu_custom_call" | custom-call | flops 1 | bytes 1 | tf_op jit(solution)/shard_map/front/pallas_call | solution.py:1018
  62.2 40.8 %mid_forward.1 = (f32[128,2048]{1,0:T(8,128)}, bf16[512,2048]{1,0:T(8,128)(2,1)}) custom-call(bf16[512,512]{1,0:T(8,128)(2,1)} %get-tuple-element.79.a_ref.low_ref, bf16[512,2048]{1,0:T(8,128)(2,1)} %w_ref.7, bf16[128,2048]{1,0:T(8,128)(2,1)} %t_ref.5, f32[1,2048]{1,0:T(1,128)} %bitcast.26), custom_call_target="tpu_custom_call" | custom-call | flops 1 | bytes 1 | tf_op jit(solution)/shard_map/mid_forward/pallas_call | solution.py:218
  103.0 19.3 %feed.1 = (bf16[512,1536]{1,0:T(8,128)(2,1)}, bf16[2,512,1536]{2,1,0:T(8,128)(2,1)}, bf16[1536,2048]{1,0:T(8,128)(2,1)}) custom-call(bf16[512,2048]{1,0:T(8,128)(2,1)} %get-tuple-element.80.x_ref, bf16[512,2048]{1,0:T(8,128)(2,1)} %get-tuple-element.81.dy_ref, bf16[2,2048,1536]{2,1,0:T(8,128)(2,1)} %w_ref.6, bf16[1536,2048]{1,0:T(8,128)(2,1)} %d_ref.3), custom_call_target="tpu_custom_call" | custom-call | flops 1 | bytes 1 | tf_op jit(solution)/shard_map/feed/pallas_call | solution.py:1076
  122.3 0.0 reduce-scatter.6.cloned.1.call-start
  122.3 24.9 %feed_back.1 = (bf16[2,2048,1536]{2,1,0:T(8,128)(2,1)}, bf16[512,2048]{1,0:T(8,128)(2,1)}, bf16[512,2048]{1,0:T(8,128)(2,1)}) custom-call(bf16[512,2048]{1,0:T(8,128)(2,1)} %get-tuple-element.80.x_ref, bf16[512,1536]{1,0:T(8,128)(2,1)} %get-tuple-element.82.act_ref, bf16[2,512,1536]{2,1,0:T(8,128)(2,1)} %get-tuple-element.83.grad_ref, ...), custom_call_target="tpu_custom_call" | custom-call | flops 1 | bytes 1 | tf_op jit(solution)/shard_map/feed_back/pallas_call | solution.py:1125
  147.2 0.0 reduce-scatter.8.cloned.1.call-start
  147.3 39.6 %mid_backward.1 = (f32[128,2048]{1,0:T(8,128)}, bf16[512,2048]{1,0:T(8,128)(2,1)}, f32[1,2048]{1,0:T(1,128)}) custom-call(bf16[512,2048]{1,0:T(8,128)(2,1)} %get-tuple-element.84.p_ref, f32[128,2048]{1,0:T(8,128)} %get-tuple-element.85.h_ref, bf16[128,2048]{1,0:T(8,128)(2,1)} %c_ref.3, f32[1,2048]{1,0:T(1,128)} %bitcast.27), custom_call_target="tpu_custom_call" | custom-call | flops 1 | bytes 1 | tf_op jit(solution)/shard_map/mid_backward/pallas_call | solution.py:265
  186.9 5.7 %out_back.1 = (bf16[512,512]{1,0:T(8,128)(2,1)}, bf16[2048,512]{1,0:T(8,128)(2,1)}) custom-call(bf16[512,2048]{1,0:T(8,128)(2,1)} %get-tuple-element.86.dy_ref, bf16[512,2048]{1,0:T(8,128)(2,1)} %w_ref.7, bf16[512,512]{1,0:T(8,128)(2,1)} %get-tuple-element.79.a_ref.low_ref), custom_call_target="tpu_custom_call" | custom-call | flops 1 | bytes 1 | tf_op jit(solution)/shard_map/out_back/pallas_call | solution.py:1162
  192.6 9.0 %attend_back.1 = (f32[512,512]{1,0:T(8,128)}, bf16[8,512,512]{2,1,0:T(8,128)(2,1)}) custom-call(s32[1]{0:T(128)} %bitcast.3.w_ref, bf16[512,512]{1,0:T(8,128)(2,1)} %get-tuple-element.77.q_ref, bf16[8,512,512]{2,1,0:T(8,128)(2,1)} %get-tuple-element.78.kv_ref, bf16[512,512]{1,0:T(8,128)(2,1)} %get-tuple-element.87.do_ref, ...), custom_call_target="tpu_custom_call" | custom-call | flops 1 | bytes 1 | tf_op jit(solution)/shard_map/attend_back/pallas_call | solution.py:755
  201.6 3.7 unspin.2
  205.4 2.5 convert_element_type.19
  207.9 5.4 %add_multiply_fusion.1 = (f32[1536,256]{1,0:T(8,128)}, f32[1536,256]{1,0:T(8,128)}, f32[1536,256]{1,0:T(8,128)}, f32[1536,256]{1,0:T(8,128)}) fusion(f32[1536,256]{1,0:T(8,128)S(1)} %copy-done.9, f32[1536,256]{1,0:T(8,128)S(1)} %copy-done.10, bf16[1536,256]{1,0:T(8,128)(2,1)S(1)} %copy-done.2, f32[1536,256]{1,0:T(8,128)} %param.57, f32[1536,256]{1,0:T(8,128)} %param.58), kind=kLoop, calls=%fused_computation.7 | loop fusion | flops 7077888 | bytes 13369344 | tf_op jit(solution)/shard_map/add | solution.py:69
  213.3 105.8 %return_grads.1.e_ref = f32[512,512]{1,0:T(8,128)} custom-call(bf16[8,512,512]{2,1,0:T(8,128)(2,1)} %get-tuple-element.95.x_ref), custom_call_target="tpu_custom_call" | custom-call | flops 1 | bytes 1 | tf_op jit(solution)/shard_map/return_grads/pallas_call | solution.py:474
  319.2 2.9 unspin.3
  322.1 9.6 %project_back.1 = (bf16[512,2048]{1,0:T(8,128)(2,1)}, bf16[2048,1536]{1,0:T(8,128)(2,1)}) custom-call(bf16[512,2048]{1,0:T(8,128)(2,1)} %get-tuple-element.76.x_ref, bf16[512,512]{1,0:T(8,128)(2,1)} %get-tuple-element.92.q_ref, bf16[512,512]{1,0:T(8,128)(2,1)} %get-tuple-element.97.kv_ref, bf16[2048,512]{1,0:T(8,128)(2,1)} %wq_ref.1, ...), custom_call_target="tpu_custom_call" | custom-call | flops 1 | bytes 1 | tf_op jit(solution)/shard_map/project_back/pallas_call | solution.py:1201
  331.7 20.3 %out_scatter.1 = f32[128,2048]{1,0:T(8,128)} custom-call(bf16[512,2048]{1,0:T(8,128)(2,1)} %get-tuple-element.103.p_ref, f32[128,2048]{1,0:T(8,128)} %get-tuple-element.85.h_ref), custom_call_target="tpu_custom_call" | custom-call | flops 1 | bytes 1 | tf_op jit(solution)/shard_map/out_scatter/pallas_call | solution.py:299
  352.0 9.1 %reduce-scatter.6.cloned.1.call-done = bf16[2,256,1536]{2,1,0:T(8,128)(2,1)} async-done(((bf16[2,2048,1536]{2,1,0:T(8,128)(2,1)}), bf16[2,256,1536]{2,1,0:T(8,128)(2,1)}) %reduce-scatter.6.cloned.1.call-update) | async-done | bytes 1572880 | tf_op jit(solution)/shard_map/reduce_scatter | solution.py:1227
  361.2 1.0 copy-done.20
  362.2 1.0 copy.64
  363.2 1.0 copy.65
  364.2 1.0 copy.67
  365.2 17.1 %in_scatter.1 = (f32[128,2048]{1,0:T(8,128)}, f32[1,2048]{1,0:T(1,128)}) custom-call(bf16[512,2048]{1,0:T(8,128)(2,1)} %get-tuple-element.106.p_ref, bf16[128,2048]{1,0:T(8,128)(2,1)} %t_ref.5, f32[128,2048]{1,0:T(8,128)} %get-tuple-element.107.m_ref, f32[1,2048]{1,0:T(1,128)} %bitcast.25), custom_call_target="tpu_custom_call" | custom-call | flops 1 | bytes 1 | tf_op jit(solution)/shard_map/in_scatter/pallas_call | solution.py:337
  382.4 0.7 maximum_reduce_fusion
  383.1 0.1 reshape_reshape.3
  383.2 0.6 reshape.102.x_ref
  383.9 2.0 copy.68
  385.9 15.1 %gain_sums.1 = f32[2,128]{1,0:T(2,128)} custom-call(f32[4,8,2,128]{3,2,1,0:T(2,128)} %reshape.102.x_ref), custom_call_target="tpu_custom_call" | custom-call | flops 1 | bytes 1 | tf_op jit(solution)/shard_map/gain_sums/pallas_call | solution.py:537
  401.0 1.2 add_multiply_fusion.5
  402.3 10.9 %add_multiply_fusion = (f32[2,256,1536]{2,1,0:T(8,128)}, f32[2,256,1536]{2,1,0:T(8,128)}, f32[2,256,1536]{2,1,0:T(8,128)}, f32[2,256,1536]{2,1,0:T(8,128)}, f32[2,256,1536]{2,1,0:T(8,128)}) fusion(f32[2,256,1536]{2,1,0:T(8,128)S(1)} %copy-done.1, f32[2,256,1536]{2,1,0:T(8,128)} %param.52, f32[2,256,1536]{2,1,0:T(8,128)} %param.53, f32[2,256,1536]{2,1,0:T(8,128)} %param.54, ...), kind=kLoop, calls=%fused_computation.2 | loop fusion | flops 14155776 | bytes 29884416 | tf_op jit(solution)/shard_map/add | solution.py:69
  413.2 18.3 %reduce-scatter.8.cloned.1.call-done = bf16[256,1536]{1,0:T(8,128)(2,1)} async-done(((bf16[2048,1536]{1,0:T(8,128)(2,1)}), bf16[256,1536]{1,0:T(8,128)(2,1)}) %reduce-scatter.8.cloned.1.call-update) | async-done | bytes 786448 | tf_op jit(solution)/shard_map/reduce_scatter | solution.py:1227
  431.6 1.3 convert_element_type.20
  432.9 0.7 slice_bitcast_fusion.2
  433.6 0.8 slice_bitcast_fusion
  434.5 1.4 add_multiply_fusion.2
  435.9 2.1 copy.71
  438.0 2.1 copy.72
  440.1 1.0 copy.73
  441.1 1.0 copy.74
  442.1 1.0 copy.70
  443.2 2.8 add_multiply_fusion.3
  446.0 1.7 add_multiply_fusion.4
  447.7 1.0 copy.79
  448.7 0.6 copy-done.11
  449.3 1.0 copy.80
  (67 shorter events, 0.3 us)
Async XLA Ops:
  7.2 198.2 %reduce-scatter.4.cloned.1.call-start = ((), (), s32[]{:S(2)}) async-start(), calls=%async_computation.3 | async-start | bytes 7077888 | tf_op jit(solution)/shard_map/reduce_scatter | solution.py:1227
  122.3 238.8 %reduce-scatter.6.cloned.1.call-start = ((), (), s32[]{:S(2)}) async-start(), calls=%async_computation.4 | async-start | bytes 14155776 | tf_op jit(solution)/shard_map/reduce_scatter | solution.py:1227
  147.2 284.3 %reduce-scatter.8.cloned.1.call-start = ((), (), s32[]{:S(2)}) async-start(), calls=%async_computation.5 | async-start | bytes 7077888 | tf_op jit(solution)/shard_map/reduce_scatter | solution.py:1227
  201.6 6.2 %copy-start.9 = (f32[1536,256]{1,0:T(8,128)S(1)}, f32[1536,256]{1,0:T(8,128)}, u32[]{:S(2)}) copy-start(f32[1536,256]{1,0:T(8,128)} %param.59) | copy-start | bytes 4718596
  201.6 6.2 %copy-start.10 = (f32[1536,256]{1,0:T(8,128)S(1)}, f32[1536,256]{1,0:T(8,128)}, u32[]{:S(2)}) copy-start(f32[1536,256]{1,0:T(8,128)} %param.56) | copy-start | bytes 4718596
  205.4 2.5 copy-start.2
  361.1 1.0 copy-start.20
  361.1 2.0 copy-start.21
  362.2 2.0 copy-start.22
  365.2 17.2 %copy-start.23 = (f32[1,2048]{1,0:T(1,128)S(1)}, f32[1,2048]{1,0:T(1,128)}, u32[]{:S(2)}) copy-start(f32[1,2048]{1,0:T(1,128)} %get-tuple-element.117) | copy-start | bytes 24580
  365.2 17.2 %copy-start.28 = (f32[1,128]{1,0:T(1,128)S(1)}, f32[1,128]{1,0:T(1,128)}, u32[]{:S(2)}) copy-start(f32[1,128]{1,0:T(1,128)} %get-tuple-element.118) | copy-start | bytes 1540
  365.2 17.2 %copy-start.29 = (f32[1,128]{1,0:T(1,128)S(1)}, f32[1,128]{1,0:T(1,128)}, u32[]{:S(2)}) copy-start(f32[1,128]{1,0:T(1,128)} %get-tuple-element.119) | copy-start | bytes 1540
  365.2 35.8 %copy-start.24 = (f32[136]{0:T(256)S(1)}, f32[136]{0:T(256)}, u32[]{:S(2)}) copy-start(f32[136]{0:T(256)} %param.63) | copy-start | bytes 1636
  365.2 35.9 %copy-start.25 = (f32[136]{0:T(256)S(1)}, f32[136]{0:T(256)}, u32[]{:S(2)}) copy-start(f32[136]{0:T(256)} %param.60) | copy-start | bytes 1636
  365.2 35.8 %copy-start.26 = (f32[136]{0:T(256)S(1)}, f32[136]{0:T(256)}, u32[]{:S(2)}) copy-start(f32[136]{0:T(256)} %param.61) | copy-start | bytes 1636
  365.2 35.8 %copy-start.27 = (f32[136]{0:T(256)S(1)}, f32[136]{0:T(256)}, u32[]{:S(2)}) copy-start(f32[136]{0:T(256)} %param.62) | copy-start | bytes 1636
  365.2 37.1 %copy-start.1 = (f32[2,256,1536]{2,1,0:T(8,128)S(1)}, f32[2,256,1536]{2,1,0:T(8,128)}, u32[]{:S(2)}) copy-start(f32[2,256,1536]{2,1,0:T(8,128)} %param.55) | copy-start | bytes 9437188
  413.2 21.2 %copy-start.4 = (f32[512,256]{0,1:T(8,128)S(1)}, f32[512,256]{0,1:T(8,128)}, u32[]{:S(2)}) copy-start(f32[512,256]{0,1:T(8,128)} %copy.64) | copy-start | bytes 1572868
  413.2 21.2 %copy-start.5 = (f32[512,256]{0,1:T(8,128)S(1)}, f32[512,256]{0,1:T(8,128)}, u32[]{:S(2)}) copy-start(f32[512,256]{0,1:T(8,128)} %copy.65) | copy-start | bytes 1572868
  413.2 21.2 %copy-start.6 = (f32[512,256]{0,1:T(8,128)S(1)}, f32[512,256]{0,1:T(8,128)}, u32[]{:S(2)}) copy-start(f32[512,256]{0,1:T(8,128)} %copy.67) | copy-start | bytes 1572868
  413.2 21.2 %copy-start.7 = (f32[512,256]{0,1:T(8,128)S(1)}, f32[512,256]{0,1:T(8,128)}, u32[]{:S(2)}) copy-start(f32[512,256]{0,1:T(8,128)} %copy.68) | copy-start | bytes 1572868
  435.9 6.2 %copy-start.8 = (f32[512,256]{0,1:T(8,128)S(1)}, f32[512,256]{0,1:T(8,128)}, u32[]{:S(2)}) copy-start(f32[512,256]{0,1:T(8,128)} %slice_bitcast_fusion) | copy-start | bytes 1572868
  437.9 5.1 %copy-start.12 = (f32[1,256,256]{2,1,0:T(8,128)S(1)}, f32[1,256,256]{2,1,0:T(8,128)}, u32[]{:S(2)}) copy-start(f32[1,256,256]{2,1,0:T(8,128)} %get-tuple-element.181) | copy-start | bytes 786436
  437.9 5.1 %copy-start.13 = (f32[2,256,256]{2,1,0:T(8,128)S(1)}, f32[2,256,256]{2,1,0:T(8,128)}, u32[]{:S(2)}) copy-start(f32[2,256,256]{2,1,0:T(8,128)} %param.47) | copy-start | bytes 1572868
  438.0 5.1 %copy-start.14 = (f32[2,256,256]{2,1,0:T(8,128)S(1)}, f32[2,256,256]{2,1,0:T(8,128)}, u32[]{:S(2)}) copy-start(f32[2,256,256]{2,1,0:T(8,128)} %param.44) | copy-start | bytes 1572868
  441.1 2.0 copy-start.15
  443.1 2.9 copy-start.3
  443.1 2.9 copy-start.16
  443.1 2.9 copy-start.17
  443.1 2.9 copy-start.18
  443.1 2.9 copy-start.19
  446.0 1.7 copy-start
  447.7 1.6 copy-start.11
Sparse Core Ops, SparseCore 0:
  122.4 75.0 reduce-scatter.3
  199.8 161.2 reduce-scatter.5
  363.4 68.0 reduce-scatter.7

commit v3 on v2

--- a/solution.py
+++ b/solution.py
@@ -1223,8 +1223,330 @@
     )(x, q_back, kv_back, query_weight, keyvalue_weight, output_full)
 
 
+def mate_of():
+    w = lax.axis_index("wide")
+    c = w % 2
+    return c, w + 1 - 2 * c
+
+
+def greet_mate():
+    _, mate = mate_of()
+    barrier = pltpu.get_barrier_semaphore()
+    pl.semaphore_signal(barrier, inc=1, device_id={"wide": mate}, device_id_type=MESH)
+    pl.semaphore_wait(barrier, 1)
+
+
+def feed_pair_kernel(x_ref, dy_ref, w_ref, raw_ref, act_ref, down_ref, stage, inbox, send, recv):
+    step, steps = pl.program_id(0), pl.num_programs(0) - 1
+    c, mate = mate_of()
+
+    def trade(i):
+        return wide_copy(stage.at[i % 2, 1 - c], inbox.at[i], send, recv, i, mate)
+
+    @pl.when(step == 0)
+    def _():
+        greet_mate()
+
+    @pl.when((step >= 2) & (step <= steps))
+    def _():
+        trade(step - 2).wait_send()
+
+    @pl.when(step < steps)
+    def _():
+        x = x_ref[...]
+        gate = dot(x, w_ref[0])
+        upper = dot(x, w_ref[1])
+        raw_ref[0] = gate
+        raw_ref[1] = upper
+        act = (gate * jax.nn.sigmoid(gate) * upper).astype(BF16)
+        act_ref[...] = act
+        full = dot_tn(act, dy_ref[...]).astype(BF16)
+        width = stage.shape[4]
+        for part in range(D // width):
+            stage[step % 2, part % 2, part // 2] = full[:, part * width : (part + 1) * width]
+        trade(step).start()
+
+    @pl.when(step > 0)
+    def _():
+        last = jnp.maximum(step - 1, 0)
+        trade(last).wait_recv()
+        down_ref[...] = (stage[last % 2, c].astype(F32) + inbox[last].astype(F32)).astype(BF16)
+
+    @pl.when(step == steps)
+    def _():
+        trade(step - 1).wait_send()
+
+
+def feed_pair(x, dy, gateup_weight, width, count):
+    rows = x.shape[0]
+    tile = 256
+    steps = width // tile
+    part = D // count
+    whole = lambda i: (0, 0)
+    now = lambda i: jnp.minimum(i, steps - 1)
+    return pl.pallas_call(
+        feed_pair_kernel,
+        name="feed_pair",
+        grid=(steps + 1,),
+        out_shape=(
+            jax.ShapeDtypeStruct((2, rows, width), F32),
+            jax.ShapeDtypeStruct((rows, width), BF16),
+            jax.ShapeDtypeStruct((count // 2, width, part), BF16),
+        ),
+        in_specs=[
+            pl.BlockSpec((rows, D), whole),
+            pl.BlockSpec((rows, D), whole),
+            pl.BlockSpec((2, D, tile), lambda i: (0, 0, now(i))),
+        ],
+        out_specs=(
+            pl.BlockSpec((2, rows, tile), lambda i: (0, 0, now(i))),
+            pl.BlockSpec((rows, tile), lambda i: (0, now(i))),
+            pl.BlockSpec((count // 2, tile, part), lambda i: (0, jnp.maximum(i - 1, 0), 0)),
+        ),
+        scratch_shapes=[
+            pltpu.VMEM((2, 2, count // 2, tile, part), BF16),
+            pltpu.VMEM((steps, count // 2, tile, part), BF16),
+        ]
+        + dma_sems(steps),
+        cost_estimate=cost(1, 1),
+        compiler_params=remote_params(10),
+    )(x, dy, gateup_weight)
+
+
+def feed_back_pair_kernel(
+    x_ref, dy_ref, raw_ref, act_ref, w_ref, d_ref, full_ref, in_ref, out_ref,
+    in_acc, out_acc, stage, inbox, send, recv,
+):
+    step, steps = pl.program_id(0), pl.num_programs(0) - 1
+    c, mate = mate_of()
+
+    def trade(i):
+        return wide_copy(stage.at[i % 2, 1 - c], inbox.at[i], send, recv, i, mate)
+
+    @pl.when(step == 0)
+    def _():
+        greet_mate()
+        in_acc[...] = jnp.zeros_like(in_acc)
+        out_acc[...] = jnp.zeros_like(out_acc)
+
+    @pl.when((step >= 2) & (step <= steps))
+    def _():
+        trade(step - 2).wait_send()
+
+    @pl.when(step < steps)
+    def _():
+        act_grad = dot_nt(dy_ref[...], d_ref[...])
+        gate, upper = raw_ref[0], raw_ref[1]
+        sig = jax.nn.sigmoid(gate)
+        gate_grad = (act_grad * upper * sig * (1.0 + gate * (1.0 - sig))).astype(BF16)
+        up_grad = (act_grad * gate * sig).astype(BF16)
+        x = x_ref[...]
+        part = stage.shape[4]
+        for n, grad in enumerate((gate_grad, up_grad)):
+            full = dot_tn(x, grad).astype(BF16)
+            for k in range(D // part):
+                stage[step % 2, k % 2, n, k // 2] = full[k * part : (k + 1) * part]
+        trade(step).start()
+        in_acc[...] += dot_nt(gate_grad, w_ref[0]) + dot_nt(up_grad, w_ref[1])
+        out_acc[...] += dot(act_ref[...], d_ref[...])
+
+    @pl.when(step > 0)
+    def _():
+        last = jnp.maximum(step - 1, 0)
+        trade(last).wait_recv()
+        full_ref[...] = (stage[last % 2, c].astype(F32) + inbox[last].astype(F32)).astype(BF16)
+
+    @pl.when(step == steps)
+    def _():
+        trade(step - 1).wait_send()
+        in_ref[...] = in_acc[...].astype(BF16)
+        out_ref[...] = out_acc[...].astype(BF16)
+
+
+def feed_back_pair(x, dy, raw, act, gateup_weight, down_weight, count):
+    rows, width = act.shape
+    tile = 256
+    steps = width // tile
+    part = D // count
+    whole = lambda i: (0, 0)
+    now = lambda i: jnp.minimum(i, steps - 1)
+    full, in_partial, out_partial = pl.pallas_call(
+        feed_back_pair_kernel,
+        name="feed_back_pair",
+        grid=(steps + 1,),
+        out_shape=(
+            jax.ShapeDtypeStruct((2, count // 2, part, width), BF16),
+            jax.ShapeDtypeStruct((rows, D), BF16),
+            jax.ShapeDtypeStruct((rows, D), BF16),
+        ),
+        in_specs=[
+            pl.BlockSpec((rows, D), whole),
+            pl.BlockSpec((rows, D), whole),
+            pl.BlockSpec((2, rows, tile), lambda i: (0, 0, now(i))),
+            pl.BlockSpec((rows, tile), lambda i: (0, now(i))),
+            pl.BlockSpec((2, D, tile), lambda i: (0, 0, now(i))),
+            pl.BlockSpec((tile, D), lambda i: (now(i), 0)),
+        ],
+        out_specs=(
+            pl.BlockSpec((2, count // 2, part, tile), lambda i: (0, 0, 0, jnp.maximum(i - 1, 0))),
+            pl.BlockSpec((rows, D), whole),
+            pl.BlockSpec((rows, D), whole),
+        ),
+        scratch_shapes=[
+            pltpu.VMEM((rows, D), F32),
+            pltpu.VMEM((rows, D), F32),
+            pltpu.VMEM((2, 2, 2, count // 2, part, tile), BF16),
+            pltpu.VMEM((steps, 2, count // 2, part, tile), BF16),
+        ]
+        + dma_sems(steps),
+        cost_estimate=cost(1, 1),
+        compiler_params=remote_params(11),
+    )(x, dy, raw, act, gateup_weight, down_weight)
+    return full.reshape(2, D // 2, width), in_partial, out_partial
+
+
+def project_back_pair_kernel(
+    x_ref, q_ref, kv_ref, wq_ref, wkv_ref, out_ref, in_ref, full_ref, stage, inbox, send, recv
+):
+    step, steps = pl.program_id(0), pl.num_programs(0) - 1
+    c, mate = mate_of()
+    q_width, kv_width = wq_ref.shape[1], wkv_ref.shape[2]
+    part = full_ref.shape[1]
+
+    def trade(i):
+        return wide_copy(stage.at[i % 2, 1 - c], inbox.at[i], send, recv, i, mate)
+
+    @pl.when(step == 0)
+    def _():
+        greet_mate()
+
+    @pl.when((step >= 2) & (step <= steps))
+    def _():
+        trade(step - 2).wait_send()
+
+    @pl.when(step < steps)
+    def _():
+        x = x_ref[...]
+        q_full = dot_tn(x, q_ref[...]).astype(BF16)
+        kv_full = dot_tn(x, kv_ref[...]).astype(BF16)
+        for k in range(2):
+            at = slice(k * part, (k + 1) * part)
+            stage[step % 2, k, :, :q_width] = q_full[at]
+            stage[step % 2, k, :, q_width : q_width + 2 * kv_width] = kv_full[at]
+            stage[step % 2, k, :, q_width + 2 * kv_width :] = out_ref[at, :]
+        trade(step).start()
+        key, value = kv_ref[:, :kv_width], kv_ref[:, kv_width:]
+        in_ref[...] = (
+            dot_nt(q_ref[...], wq_ref[...]) + dot_nt(key, wkv_ref[0]) + dot_nt(value, wkv_ref[1])
+        ).astype(BF16)
+
+    @pl.when(step > 0)
+    def _():
+        last = jnp.maximum(step - 1, 0)
+        trade(last).wait_recv()
+        full_ref[0] = (stage[last % 2, c].astype(F32) + inbox[last].astype(F32)).astype(BF16)
+
+    @pl.when(step == steps)
+    def _():
+        trade(step - 1).wait_send()
+
+
+def project_back_pair(x, q_back, kv_back, query_weight, keyvalue_weight, output_full, count):
+    rows, out_width = x.shape[0], output_full.shape[1]
+    q_width, kv_width = query_weight.shape[1], keyvalue_weight.shape[2]
+    width = q_width + 2 * kv_width + out_width
+    part = D // count
+    tile = 2 * part
+    steps = count // 2
+    whole = lambda i: (0, 0)
+    now = lambda i: jnp.minimum(i, steps - 1)
+    in_partial, full = pl.pallas_call(
+        project_back_pair_kernel,
+        name="project_back_pair",
+        grid=(steps + 1,),
+        out_shape=(
+            jax.ShapeDtypeStruct((rows, D), BF16),
+            jax.ShapeDtypeStruct((steps, part, width), BF16),
+        ),
+        in_specs=[
+            pl.BlockSpec((rows, tile), lambda i: (0, now(i))),
+            pl.BlockSpec((rows, q_width), whole),
+            pl.BlockSpec((rows, 2 * kv_width), whole),
+            pl.BlockSpec((tile, q_width), lambda i: (now(i), 0)),
+            pl.BlockSpec((2, tile, kv_width), lambda i: (0, now(i), 0)),
+            pl.BlockSpec((tile, out_width), lambda i: (now(i), 0)),
+        ],
+        out_specs=(
+            pl.BlockSpec((rows, tile), lambda i: (0, now(i))),
+            pl.BlockSpec((1, part, width), lambda i: (jnp.maximum(i - 1, 0), 0, 0)),
+        ),
+        scratch_shapes=[
+            pltpu.VMEM((2, 2, part, width), BF16),
+            pltpu.VMEM((steps, part, width), BF16),
+        ]
+        + dma_sems(steps),
+        cost_estimate=cost(1, 1),
+        compiler_params=remote_params(12),
+    )(x, q_back, kv_back, query_weight, keyvalue_weight, output_full)
+    return in_partial, full.reshape(D // 2, width)
+
+
+def rest_adamw_kernel(total_ref, *refs):
+    q_width, kv_width = refs[0].shape[1], refs[4].shape[2]
+    ins, outs = refs[:12], refs[12:]
+    total = total_ref[...].astype(F32)
+    rate = 2.0 * D ** (-0.5)
+    for n, new in enumerate(
+        adamw(total[:, :q_width], *[r[...] for r in ins[:4]], rate, WEIGHT_DECAY)
+    ):
+        outs[n][...] = new
+    for k in range(2):
+        low = q_width + k * kv_width
+        for n, new in enumerate(
+            adamw(total[:, low : low + kv_width], *[r[k] for r in ins[4:8]], rate, WEIGHT_DECAY)
+        ):
+            outs[5 + n][k] = new
+    turned = jnp.transpose(total[:, q_width + 2 * kv_width :])
+    for n, new in enumerate(
+        adamw(turned, *[r[...] for r in ins[8:]], 2.0 * WO_FAN ** (-0.5), WEIGHT_DECAY)
+    ):
+        outs[10 + n][...] = new
+
+
+def rest_adamw(total, query_state, keyvalue_state, output_state):
+    tile = 128
+    rows, width = total.shape
+    q_spec = pl.BlockSpec((tile, query_state[0].shape[1]), lambda i: (i, 0))
+    kv_spec = pl.BlockSpec((2, tile, keyvalue_state[0].shape[2]), lambda i: (0, i, 0))
+    o_spec = pl.BlockSpec((output_state[0].shape[0], tile), lambda i: (0, i))
+    like = lambda a: jax.ShapeDtypeStruct(a.shape, F32)
+    out = pl.pallas_call(
+        rest_adamw_kernel,
+        name="rest_adamw",
+        grid=(rows // tile,),
+        out_shape=tuple(
+            like(state[0]) for state in (query_state, keyvalue_state, output_state) for _ in range(5)
+        ),
+        in_specs=[pl.BlockSpec((tile, width), lambda i: (i, 0))]
+        + [q_spec] * 4
+        + [kv_spec] * 4
+        + [o_spec] * 4,
+        out_specs=tuple([q_spec] * 5 + [kv_spec] * 5 + [o_spec] * 5),
+        compiler_params=params("arbitrary"),
+        cost_estimate=cost(1, 1),
+    )(total, *query_state, *keyvalue_state, *output_state)
+    return out[:5], out[5:10], out[10:]
+
+
 def wide_scatter(partial, axis):
     return lax.psum_scatter(partial, "wide", scatter_dimension=axis, tiled=True)
+
+
+def line_scatter(partial, axis, count):
+    groups = [[2 * z + c for z in range(count // 2)] for c in range(2)]
+    return lax.psum_scatter(
+        partial, "wide", scatter_dimension=axis, tiled=True, axis_index_groups=groups
+    )
 
 
 def body(
@@ -1300,12 +1622,20 @@
         attn_out, attn_low, lse = attend(w_scalar, query_low, kv_all, q_heads, group)
         back_mlp = lax.all_gather(cotangent, "narrow", axis=0, tiled=True)
     hidden_mid, mlp_input = mid_forward(attn_low, output_weight, tokens, mlp_gain, special)
-    act, act_grads, down_full = feed(mlp_input, back_mlp, gateup_weight, down_weight)
-    down_total = wide_scatter(down_full, 1)
-    gateup_full, in_partial, out_partial = feed_back(
-        mlp_input, act, act_grads, gateup_weight, down_weight
-    )
-    gateup_total = wide_scatter(gateup_full, 1)
+    if special:
+        raw, act, down_full = feed_pair(mlp_input, back_mlp, gateup_weight, down_weight.shape[0], wide)
+        down_total = line_scatter(down_full, 0, wide)[0]
+        gateup_full, in_partial, out_partial = feed_back_pair(
+            mlp_input, back_mlp, raw, act, gateup_weight, down_weight, wide
+        )
+        gateup_total = line_scatter(gateup_full, 1, wide)
+    else:
+        act, act_grads, down_full = feed(mlp_input, back_mlp, gateup_weight, down_weight)
+        down_total = wide_scatter(down_full, 1)
+        gateup_full, in_partial, out_partial = feed_back(
+            mlp_input, act, act_grads, gateup_weight, down_weight
+        )
+        gateup_total = wide_scatter(gateup_full, 1)
     mid_grad, back_attn, mlp_gain_grad = mid_backward(
         in_partial, hidden_mid, cotangent, mlp_gain, special
     )
@@ -1326,52 +1656,27 @@
     query_back, query_gain_grad = unspin(query_sum, query_raw, query_gain, cosine, sine)
     kv_sum = return_grads(kv_sums, wide, special)
     kv_back, key_gain_grad = unspin(kv_sum, key_raw, key_gain, cosine, sine)
-    normed_partial, project_full = project_back(
-        attn_input, query_back, kv_back, query_weight, keyvalue_weight, output_full
+    back_args = (attn_input, query_back, kv_back, query_weight, keyvalue_weight, output_full)
+    if special:
+        normed_partial, project_full = project_back_pair(*back_args, wide)
+    else:
+        normed_partial, project_full = project_back(*back_args)
+    project_full, gateup_total, out_partial, normed_partial = lax.optimization_barrier(
+        (project_full, gateup_total, out_partial, normed_partial)
     )
-    project_full, out_partial = lax.optimization_barrier((project_full, out_partial))
+    rest_total = line_scatter(project_full, 0, wide) if special else wide_scatter(project_full, 0)
     block_output = out_scatter(out_partial, hidden_mid, special)
-    project_full, gateup_total, block_output, normed_partial = lax.optimization_barrier(
-        (project_full, gateup_total, block_output, normed_partial)
-    )
-    rest_total = wide_scatter(project_full, 0).astype(F32)
     input_grad, attn_gain_grad = in_scatter(normed_partial, tokens, mid_grad, attn_gain, special)
     gain_partial = jnp.concatenate(
         [attn_gain_grad, mlp_gain_grad, query_gain_grad, key_gain_grad], axis=1
     ).reshape(-1)
     gain_total = gain_sums(gain_partial, wide, narrow, special)
 
-    query_total = rest_total[:, :q_width]
-    keyvalue_total = jnp.stack(
-        [rest_total[:, q_width : q_width + kv_width], rest_total[:, q_width + kv_width : q_width + 2 * kv_width]]
-    )
-    output_total = rest_total[:, q_width + 2 * kv_width :].T
-    query_new = adamw(
-        query_total,
-        query_master,
-        query_moment,
-        query_second,
-        query_average,
-        2.0 * D ** (-0.5),
-        WEIGHT_DECAY,
-    )
-    keyvalue_new = adamw(
-        keyvalue_total,
-        keyvalue_master,
-        keyvalue_moment,
-        keyvalue_second,
-        keyvalue_average,
-        2.0 * D ** (-0.5),
-        WEIGHT_DECAY,
-    )
-    output_new = adamw(
-        output_total,
-        output_master,
-        output_moment,
-        output_second,
-        output_average,
-        2.0 * WO_FAN ** (-0.5),
-        WEIGHT_DECAY,
+    query_new, keyvalue_new, output_new = rest_adamw(
+        rest_total,
+        (query_master, query_moment, query_second, query_average),
+        (keyvalue_master, keyvalue_moment, keyvalue_second, keyvalue_average),
+        (output_master, output_moment, output_second, output_average),
     )
     gateup_new = adamw(
         gateup_total.astype(F32),

time: 464 us -> 443 us (0.955)
  Pallas kernels: 364 us -> 393 us
  waiting for transfers between devices: 27.5 us -> 0.09 us
  local copies, waits for them, and re-layouts: 20.9 us -> 5.96 us
  other arithmetic: 30 us -> 22.8 us
    pallas_call x3 -> x4, Pallas kernels: 53.8 us -> 81.2 us  [the longest x1 44.9 us: feed_back_pair(): pl.pallas_call(feed_back_pair_kernel, name='feed_back_pair', grid=(steps...]
    reduce_scatter x3, waiting for transfers between devices: 27.5 us -> 0.04 us  [line_scatter(): lax.psum_scatter(partial, 'wide', scatter_dimension=axis, tiled=True, axi...]
    pallas_call x1, Pallas kernels: 106 us -> 92.1 us  [return_grads(): pl.pallas_call(functools.partial(return_grads_kernel, count), name='retur...]
    unnamed x71 -> x28, local copies, waits for them, and re-layouts: 15.9 us -> 2.61 us
    pallas_call x1, Pallas kernels: 17.1 us -> 23.5 us  [in_scatter(): pl.pallas_call(in_scatter_kernel, name='in_scatter', out_shape=(jax.Shape...]
    add x6 -> x3, other arithmetic: 23.5 us -> 17.6 us  [adamw(): average_new = EMA_KEEP * average + (1.0 - EMA_KEEP) * master_new]
  transfers between devices with their start and end apart: 3 -> 3, of which waited for: 2 -> 0; matrix products, arithmetic and copies ran while one was open for 6% -> 5% of each run, Pallas kernels for 55% -> 63%
where the time goes in v3:
time: 443 us; the launch traced here: 437 us
  Pallas kernels  393 us (89%)
  other arithmetic  22.8 us (5%)
  between operations  14.5 us (3%)
  local copies, waits for them, and re-layouts  5.96 us (1%)
    pallas_call x1, Pallas kernels, return_grads(): pl.pallas_call(functools.partial(return_grads_kernel, count), name='retur...  92.1 us
    pallas_call x1, Pallas kernels, front(): pl.pallas_call(functools.partial(front_kernel, count, heads, group), name...  50.3 us
    pallas_call x1, Pallas kernels, feed_back_pair(): pl.pallas_call(feed_back_pair_kernel, name='feed_back_pair', grid=(steps...  44.9 us
    pallas_call x1, Pallas kernels, mid_backward(): pl.pallas_call(mid_backward_kernel, name='mid_backward', out_shape=(jax.S...  44.2 us
    pallas_call x1, Pallas kernels, mid_forward(): pl.pallas_call(mid_forward_kernel, name='mid_forward', out_shape=(jax.Sha...  40.9 us
    pallas_call x1, Pallas kernels, in_scatter(): pl.pallas_call(in_scatter_kernel, name='in_scatter', out_shape=(jax.Shape...  23.5 us
    pallas_call x1, Pallas kernels, out_scatter(): pl.pallas_call(out_scatter_kernel, name='out_scatter', out_shape=jax.Shap...  22 us
    pallas_call x1, Pallas kernels, feed_pair(): pl.pallas_call(feed_pair_kernel, name='feed_pair', grid=(steps + 1,), out...  18.9 us
  transfers between devices with their start and end apart: 3, of which 0 were waited for; matrix products, arithmetic and copies ran while one was open for 5% of the time, Pallas kernels for 63%

profile of v3, /device:TPU:0, one launch (start us, length us, event | category | flops | bytes accessed | tf_op | source)
XLA Modules:
  0.0 436.6 jit_solution(6797950997334730942)
XLA Ops:
  7.2 0.0 reduce-scatter.4.cloned.1.call-start
  7.3 1.3 slice_bitcast_fusion
  8.6 1.3 fusion.7
  9.9 1.0 fusion.2
  10.9 1.0 pad_maximum_fusion
  11.9 50.3 %front.1 = (bf16[512,2048]{1,0:T(8,128)(2,1)}, bf16[512,2048]{1,0:T(8,128)(2,1)}, bf16[512,512]{1,0:T(8,128)(2,1)}, f32[512,512]{1,0:T(8,128)}, f32[512,256]{1,0...) custom-call(bf16[128,2048]{1,0:T(8,128)(2,1)} %t_ref.5, ...), custom_call_target="tpu_custom_call" | custom-call | flops 1 | bytes 1 | tf_op jit(solution)/shard_map/front/pallas_call | solution.py:1018
  62.2 40.9 %mid_forward.1 = (f32[128,2048]{1,0:T(8,128)}, bf16[512,2048]{1,0:T(8,128)(2,1)}) custom-call(bf16[512,512]{1,0:T(8,128)(2,1)} %get-tuple-element.92.a_ref.low_ref, bf16[512,2048]{1,0:T(8,128)(2,1)} %w_ref.7, bf16[128,2048]{1,0:T(8,128)(2,1)} %t_ref.5, f32[1,2048]{1,0:T(1,128)} %bitcast.25), custom_call_target="tpu_custom_call" | custom-call | flops 1 | bytes 1 | tf_op jit(solution)/shard_map/mid_forward/pallas_call | solution.py:218
  103.1 18.9 %feed_pair.1 = (f32[2,512,1536]{2,1,0:T(8,128)}, bf16[512,1536]{1,0:T(8,128)(2,1)}, bf16[4,1536,256]{2,1,0:T(8,128)(2,1)}) custom-call(bf16[512,2048]{1,0:T(8,128)(2,1)} %get-tuple-element.93.x_ref, bf16[512,2048]{1,0:T(8,128)(2,1)} %get-tuple-element.94.dy_ref, bf16[2,2048,1536]{2,1,0:T(8,128)(2,1)} %w_ref.6), custom_call_target="tpu_custom_call" | custom-call | flops 1 | bytes 1 | tf_op jit(solution)/shard_map/feed_pair/pallas_call | solution.py:1287
  122.0 0.0 reduce-scatter.4.cloned.1.call-update
  122.0 0.0 reduce-scatter.6.cloned.1.call-start
  122.1 44.9 %feed_back_pair.1 = (bf16[2,4,256,1536]{3,2,1,0:T(8,128)(2,1)}, bf16[512,2048]{1,0:T(8,128)(2,1)}, bf16[512,2048]{1,0:T(8,128)(2,1)}) custom-call(bf16[512,2048]{1,0:T(8,128)(2,1)} %get-tuple-element.93.x_ref, bf16[512,2048]{1,0:T(8,128)(2,1)} %get-tuple-element.94.dy_ref, f32[2,512,1536]{2,1,0:T(8,128)} %get-tuple-element.95.raw_ref, ...), custom_call_target="tpu_custom_call" | custom-call | flops 1 | bytes 1 | tf_op jit(solution)/shard_map/feed_back_pair/pallas_call | solution.py:1373
  167.0 0.0 reduce-scatter.6.cloned.1.call-update
  167.0 0.3 reduce-scatter.8.cloned.1.call-start
  167.2 44.2 %mid_backward.1 = (f32[128,2048]{1,0:T(8,128)}, bf16[512,2048]{1,0:T(8,128)(2,1)}, f32[1,2048]{1,0:T(1,128)}) custom-call(bf16[512,2048]{1,0:T(8,128)(2,1)} %get-tuple-element.97.p_ref, f32[128,2048]{1,0:T(8,128)} %get-tuple-element.98.h_ref, bf16[128,2048]{1,0:T(8,128)(2,1)} %c_ref.3, f32[1,2048]{1,0:T(1,128)} %bitcast.26), custom_call_target="tpu_custom_call" | custom-call | flops 1 | bytes 1 | tf_op jit(solution)/shard_map/mid_backward/pallas_call | solution.py:265
  211.5 5.7 %out_back.1 = (bf16[512,512]{1,0:T(8,128)(2,1)}, bf16[2048,512]{1,0:T(8,128)(2,1)}) custom-call(bf16[512,2048]{1,0:T(8,128)(2,1)} %get-tuple-element.99.dy_ref, bf16[512,2048]{1,0:T(8,128)(2,1)} %w_ref.7, bf16[512,512]{1,0:T(8,128)(2,1)} %get-tuple-element.92.a_ref.low_ref), custom_call_target="tpu_custom_call" | custom-call | flops 1 | bytes 1 | tf_op jit(solution)/shard_map/out_back/pallas_call | solution.py:1162
  217.1 8.8 %attend_back.1 = (f32[512,512]{1,0:T(8,128)}, bf16[8,512,512]{2,1,0:T(8,128)(2,1)}) custom-call(s32[1]{0:T(128)} %bitcast.3.w_ref, bf16[512,512]{1,0:T(8,128)(2,1)} %get-tuple-element.90.q_ref, bf16[8,512,512]{2,1,0:T(8,128)(2,1)} %get-tuple-element.91.kv_ref, bf16[512,512]{1,0:T(8,128)(2,1)} %get-tuple-element.100.do_ref, ...), custom_call_target="tpu_custom_call" | custom-call | flops 1 | bytes 1 | tf_op jit(solution)/shard_map/attend_back/pallas_call | solution.py:755
  225.9 3.7 unspin.2
  229.7 2.5 bitcast_convert_fusion
  232.1 0.0 copy-done.3
  232.1 0.0 copy-done.4
  232.1 0.0 copy-done.2
  232.1 5.4 %add_multiply_fusion.1 = (f32[1536,256]{1,0:T(8,128)}, f32[1536,256]{1,0:T(8,128)}, f32[1536,256]{1,0:T(8,128)}, f32[1536,256]{1,0:T(8,128)}) fusion(f32[1536,256]{1,0:T(8,128)S(1)} %copy-done.3, f32[1536,256]{1,0:T(8,128)S(1)} %copy-done.4, bf16[1,1536,256]{2,1,0:T(8,128)(2,1)S(1)} %copy-done.2, f32[1536,256]{1,0:T(8,128)} %param.57, f32[1536,256]{1,0:T(8,128)} %param.58), kind=kLoop, calls=%fused_computation.7 | loop fusion | flops 7077888 | bytes 13369344 | tf_op jit(solution)/shard_map/add | solution.py:69
  237.6 92.1 %return_grads.1.e_ref = f32[512,512]{1,0:T(8,128)} custom-call(bf16[8,512,512]{2,1,0:T(8,128)(2,1)} %get-tuple-element.108.x_ref), custom_call_target="tpu_custom_call" | custom-call | flops 1 | bytes 1 | tf_op jit(solution)/shard_map/return_grads/pallas_call | solution.py:474
  329.6 2.9 unspin.3
  332.6 11.5 %project_back_pair.1 = (bf16[512,2048]{1,0:T(8,128)(2,1)}, bf16[4,256,1536]{2,1,0:T(8,128)(2,1)}) custom-call(bf16[512,2048]{1,0:T(8,128)(2,1)} %get-tuple-element.89.x_ref, bf16[512,512]{1,0:T(8,128)(2,1)} %get-tuple-element.105.q_ref, bf16[512,512]{1,0:T(8,128)(2,1)} %get-tuple-element.110.kv_ref, bf16[2048,512]{1,0:T(8,128)(2,1)} %wq_ref.1, ...), custom_call_target="tpu_custom_call" | custom-call | flops 1 | bytes 1 | tf_op jit(solution)/shard_map/project_back_pair/pallas_call | solution.py:1463
  344.1 0.0 reduce-scatter.6.cloned.1.call-done
  344.1 0.0 reduce-scatter.8.cloned.1.call-update
  344.2 0.0 copy-start.6
  344.2 0.0 copy-start.11
  344.2 0.0 copy-start.12
  344.2 23.5 %in_scatter.1 = (f32[128,2048]{1,0:T(8,128)}, f32[1,2048]{1,0:T(1,128)}) custom-call(bf16[512,2048]{1,0:T(8,128)(2,1)} %get-tuple-element.117.p_ref, bf16[128,2048]{1,0:T(8,128)(2,1)} %t_ref.5, f32[128,2048]{1,0:T(8,128)} %get-tuple-element.118.m_ref, f32[1,2048]{1,0:T(1,128)} %bitcast.24), custom_call_target="tpu_custom_call" | custom-call | flops 1 | bytes 1 | tf_op jit(solution)/shard_map/in_scatter/pallas_call | solution.py:337
  367.7 0.0 copy-done.6
  367.7 0.7 maximum_reduce_fusion
  368.5 0.1 reshape_reshape.3
  368.6 0.6 reshape.112.x_ref
  369.3 0.0 copy-start.1
  369.3 22.0 %out_scatter.1 = f32[128,2048]{1,0:T(8,128)} custom-call(bf16[512,2048]{1,0:T(8,128)(2,1)} %get-tuple-element.116.p_ref, f32[128,2048]{1,0:T(8,128)} %get-tuple-element.98.h_ref), custom_call_target="tpu_custom_call" | custom-call | flops 1 | bytes 1 | tf_op jit(solution)/shard_map/out_scatter/pallas_call | solution.py:299
  391.3 17.6 %gain_sums.1 = f32[2,128]{1,0:T(2,128)} custom-call(f32[4,8,2,128]{3,2,1,0:T(2,128)} %reshape.112.x_ref), custom_call_target="tpu_custom_call" | custom-call | flops 1 | bytes 1 | tf_op jit(solution)/shard_map/gain_sums/pallas_call | solution.py:537
  409.0 1.3 add_multiply_fusion.2
  410.2 0.0 copy-done.1
  410.2 10.9 %add_multiply_fusion = (f32[2,256,1536]{2,1,0:T(8,128)}, f32[2,256,1536]{2,1,0:T(8,128)}, f32[2,256,1536]{2,1,0:T(8,128)}, f32[2,256,1536]{2,1,0:T(8,128)}, f32[2,256,1536]{2,1,0:T(8,128)}) fusion(f32[2,256,1536]{2,1,0:T(8,128)S(1)} %copy-done.1, f32[2,256,1536]{2,1,0:T(8,128)} %param.52, f32[2,256,1536]{2,1,0:T(8,128)} %param.53, f32[2,256,1536]{2,1,0:T(8,128)} %param.54, ...), kind=kLoop, calls=%fused_computation.2 | loop fusion | flops 14155776 | bytes 29884416 | tf_op jit(solution)/shard_map/add | solution.py:69
  421.1 0.0 reduce-scatter.8.cloned.1.call-done.total_ref
  421.2 5.9 %rest_adamw.1 = (f32[256,512]{1,0:T(8,128)}, f32[256,512]{1,0:T(8,128)}, f32[256,512]{1,0:T(8,128)}, f32[256,512]{1,0:T(8,128)}, f32[256,512]{1,0:T(8,128)}, /*i...) custom-call(bf16[256,1536]{1,0:T(8,128)(2,1)} %reduce-scatter.8.clon, ...), custom_call_target="tpu_custom_call" | custom-call | flops 1 | bytes 1 | tf_op jit(solution)/shard_map/rest_adamw/pallas_call | solution.py:1523
  427.1 0.0 copy-start.5
  427.1 0.0 copy-done
  427.1 1.0 copy.69
  428.1 0.6 copy-done.5
  428.7 1.0 copy.70
  (19 shorter events, 0.1 us)
Async XLA Ops:
  7.2 222.4 %reduce-scatter.4.cloned.1.call-start = ((), (), s32[]{:S(2)}) async-start(), calls=%async_computation.3 | async-start | bytes 3932160 | tf_op jit(solution)/shard_map/reduce_scatter | solution.py:1547
  122.0 222.1 %reduce-scatter.6.cloned.1.call-start = ((), (), s32[]{:S(2)}) async-start(), calls=%async_computation.4 | async-start | bytes 7864320 | tf_op jit(solution)/shard_map/reduce_scatter | solution.py:1547
  167.0 254.2 %reduce-scatter.8.cloned.1.call-start = ((), (), s32[]{:S(2)}) async-start(), calls=%async_computation.5 | async-start | bytes 3932160 | tf_op jit(solution)/shard_map/reduce_scatter | solution.py:1547
  225.9 6.2 %copy-start.3 = (f32[1536,256]{1,0:T(8,128)S(1)}, f32[1536,256]{1,0:T(8,128)}, u32[]{:S(2)}) copy-start(f32[1536,256]{1,0:T(8,128)} %param.59) | copy-start | bytes 4718596
  225.9 6.2 %copy-start.4 = (f32[1536,256]{1,0:T(8,128)S(1)}, f32[1536,256]{1,0:T(8,128)}, u32[]{:S(2)}) copy-start(f32[1536,256]{1,0:T(8,128)} %param.56) | copy-start | bytes 4718596
  229.6 2.5 copy-start.2
  344.2 23.5 %copy-start.6 = (f32[1,2048]{1,0:T(1,128)S(1)}, f32[1,2048]{1,0:T(1,128)}, u32[]{:S(2)}) copy-start(f32[1,2048]{1,0:T(1,128)} %get-tuple-element.143) | copy-start | bytes 24580
  344.2 23.5 %copy-start.11 = (f32[1,128]{1,0:T(1,128)S(1)}, f32[1,128]{1,0:T(1,128)}, u32[]{:S(2)}) copy-start(f32[1,128]{1,0:T(1,128)} %get-tuple-element.144) | copy-start | bytes 1540
  344.2 23.5 %copy-start.12 = (f32[1,128]{1,0:T(1,128)S(1)}, f32[1,128]{1,0:T(1,128)}, u32[]{:S(2)}) copy-start(f32[1,128]{1,0:T(1,128)} %get-tuple-element.145) | copy-start | bytes 1540
  369.2 39.7 %copy-start.7 = (f32[136]{0:T(256)S(1)}, f32[136]{0:T(256)}, u32[]{:S(2)}) copy-start(f32[136]{0:T(256)} %param.63) | copy-start | bytes 1636
  369.3 39.7 %copy-start.8 = (f32[136]{0:T(256)S(1)}, f32[136]{0:T(256)}, u32[]{:S(2)}) copy-start(f32[136]{0:T(256)} %param.60) | copy-start | bytes 1636
  369.3 39.7 %copy-start.9 = (f32[136]{0:T(256)S(1)}, f32[136]{0:T(256)}, u32[]{:S(2)}) copy-start(f32[136]{0:T(256)} %param.61) | copy-start | bytes 1636
  369.3 39.7 %copy-start.10 = (f32[136]{0:T(256)S(1)}, f32[136]{0:T(256)}, u32[]{:S(2)}) copy-start(f32[136]{0:T(256)} %param.62) | copy-start | bytes 1636
  369.3 41.0 %copy-start.1 = (f32[2,256,1536]{2,1,0:T(8,128)S(1)}, f32[2,256,1536]{2,1,0:T(8,128)}, u32[]{:S(2)}) copy-start(f32[2,256,1536]{2,1,0:T(8,128)} %param.55) | copy-start | bytes 9437188
  421.1 5.9 %copy-start = (f32[128,2048]{1,0:T(8,128)S(1)}, f32[128,2048]{1,0:T(8,128)}, u32[]{:S(2)}) copy-start(f32[128,2048]{1,0:T(8,128)} %out_scatter.1) | copy-start | bytes 3145732
  427.1 1.6 copy-start.5
Sparse Core Ops, SparseCore 0:
  122.1 65.4 reduce-scatter.3
  189.9 134.4 reduce-scatter.5
  344.3 65.0 reduce-scatter.7

commit v4 on v3

--- a/solution.py
+++ b/solution.py
@@ -117,7 +117,7 @@
             copy.wait_send()
 
 
-def gather_square(copies, slot, x_ref, o_ref):
+def gather_square(copies, slot, x_ref, o_ref, first=None, later=None, relay=None):
     me, xn, yn, dg = square()
     rows = x_ref.shape[0]
     half = rows // 2
@@ -131,15 +131,22 @@
     xb = copies.go(lower, part(me, half), slot + 2, xn)
     ya = copies.go(upper, part(me, 0), slot + 3, yn)
     o_ref[pl.ds(pl.multiple_of(me * rows, rows), rows)] = x_ref[...]
+    if first is not None:
+        first()
     xa.wait_recv()
     yf = copies.go(part(xn, 0), part(xn, 0), slot + 4, yn)
     yb.wait_recv()
     xf = copies.go(part(yn, half), part(yn, half), slot + 5, xn)
-    for copy in (xb, ya, yf, xf):
-        copy.wait_recv()
-
-
-def scatter_square(copies, slot, p_ref, buf, stage, emit, fill=None):
+    if relay is not None:
+        relay()
+    for pair, owner in (((xb,), xn), ((ya,), yn), ((yf, xf), dg)):
+        for copy in pair:
+            copy.wait_recv()
+        if later is not None:
+            later(owner)
+
+
+def scatter_square(copies, slot, p_ref, buf, stage, emit, fill=None, early=None, middle=None):
     me, xn, yn, dg = square()
     rows = p_ref.shape[0] // 4
     half = rows // 2
@@ -157,12 +164,16 @@
     fill(yn)
     c3 = copies.go(part(yn, half), buf.at[3], slot + 3, yn)
     fill(me)
+    if early is not None:
+        early()
     c0.wait_recv()
     stage[0] = (part(yn, 0)[...].astype(F32) + buf[0].astype(F32)).astype(BF16)
     c4 = copies.go(stage.at[0], buf.at[4], slot + 4, yn)
     c1.wait_recv()
     stage[1] = (part(xn, half)[...].astype(F32) + buf[1].astype(F32)).astype(BF16)
     c5 = copies.go(stage.at[1], buf.at[5], slot + 5, xn)
+    if middle is not None:
+        middle()
     c2.wait_recv()
     c4.wait_recv()
     emit(0, part(me, 0)[...].astype(F32) + buf[2].astype(F32) + buf[4].astype(F32))
@@ -185,58 +196,193 @@
     )
 
 
-def mid_forward_kernel(a_ref, w_ref, t_ref, g_ref, h_ref, o_ref, p_ref, buf, stage, own, send, recv):
-    _, xn, yn, _ = square()
+def mid_kernel(
+    a_ref, w_ref, t_ref, g_ref, dy_hbm, gu_hbm, d_hbm,
+    h_ref, x_hbm, grad_hbm, act_hbm, down_hbm,
+    p_ref, buf, stage, own, x, weight, dy, down, act_grad, grad, act, mine, inbox,
+    send, recv, m_send, m_recv, load_sem, store_sem, down_sem,
+):
+    me, xn, yn, dg = square()
+    c, mate = mate_of()
     rows = t_ref.shape[0]
     half = rows // 2
-    greet("narrow", (xn, yn))
+    tiles, tile, part = inbox.shape[0], inbox.shape[2], inbox.shape[3]
+    loads = [
+        pltpu.make_async_copy(src, dst, load_sem.at[n])
+        for n, (src, dst) in enumerate(((dy_hbm, dy), (d_hbm, down), (gu_hbm, weight)))
+    ]
+    for load in loads:
+        load.start()
+    barrier = pltpu.get_barrier_semaphore()
+    for peer in (xn, yn):
+        pl.semaphore_signal(barrier, inc=1, device_id={"narrow": peer}, device_id_type=MESH)
+    pl.semaphore_signal(barrier, inc=1, device_id={"wide": mate}, device_id_type=MESH)
+    pl.semaphore_wait(barrier, 3)
     copies = Copies(send, recv)
 
+    def rows_of(owner):
+        return pl.ds(pl.multiple_of(owner * rows, rows), rows)
+
     def fill(owner):
-        at = pl.ds(pl.multiple_of(owner * rows, rows), rows)
-        p_ref[at, :] = dot(a_ref[at, :], w_ref[...]).astype(BF16)
+        p_ref[rows_of(owner), :] = dot(a_ref[rows_of(owner), :], w_ref[...]).astype(BF16)
 
     def emit(low, total):
         hidden = t_ref[pl.ds(low, half)].astype(F32) + total
         h_ref[pl.ds(low, half)] = hidden
         own[pl.ds(low, half)] = (hidden * row_scale(hidden) * g_ref[...]).astype(BF16)
 
-    scatter_square(copies, 0, p_ref, buf, stage, emit, fill)
-    gather_square(copies, 6, own, o_ref)
+    def act_grads(low, high):
+        @pl.loop(low, high)
+        def _(t):
+            cols = pl.ds(pl.multiple_of(t * tile, tile), tile)
+            act_grad[:, cols] = dot_nt(dy[...], down[cols, :])
+
+    def early():
+        loads[0].wait()
+        loads[1].wait()
+        act_grads(0, tiles // 2)
+
+    def middle():
+        act_grads(tiles // 2, tiles)
+
+    scatter_square(copies, 0, p_ref, buf, stage, emit, fill, early, middle)
+
+    def expand(owner):
+        at = rows_of(owner)
+
+        @pl.loop(0, tiles)
+        def _(t):
+            cols = pl.ds(pl.multiple_of(t * tile, tile), tile)
+            gate = dot(x[at, :], weight[0, :, cols])
+            upper = dot(x[at, :], weight[1, :, cols])
+            sig = jax.nn.sigmoid(gate)
+            swish = gate * sig
+            back = act_grad[at, cols]
+            act[at, cols] = (swish * upper).astype(BF16)
+            grad[0, at, cols] = (back * upper * sig * (1.0 + gate * (1.0 - sig))).astype(BF16)
+            grad[1, at, cols] = (back * swish).astype(BF16)
+
+    def first():
+        loads[2].wait()
+        expand(me)
+
+    def later(owner):
+        expand(owner)
+
+    gather_square(copies, 6, own, x, first, later)
+    stores = [
+        pltpu.make_async_copy(src, dst, store_sem.at[n])
+        for n, (src, dst) in enumerate(((x, x_hbm), (grad, grad_hbm), (act, act_hbm)))
+    ]
+    for store in stores:
+        store.start()
+
+    def trade(t):
+        return wide_copy(mine.at[t, 1 - c], inbox.at[t], m_send, m_recv, t, mate)
+
+    def keep(t):
+        at = pl.ds(pl.multiple_of(t * tile, tile), tile)
+        return pltpu.make_async_copy(mine.at[t, c], down_hbm.at[:, at], down_sem.at[t])
+
+    @pl.loop(0, tiles)
+    def _(t):
+        cols = pl.ds(pl.multiple_of(t * tile, tile), tile)
+        full = dot_tn(act[:, cols], dy[...]).astype(BF16)
+        for k in range(D // part):
+            mine[t, k % 2, k // 2] = full[:, k * part : (k + 1) * part]
+        trade(t).start()
+
+    @pl.loop(0, tiles)
+    def _(t):
+        trade(t).wait_recv()
+        mine[t, c] = (mine[t, c].astype(F32) + inbox[t].astype(F32)).astype(BF16)
+        keep(t).start()
+
     copies.finish()
 
-
-def mid_forward(attn_low, weight, tokens, gain_row, special):
+    @pl.loop(0, tiles)
+    def _(t):
+        trade(t).wait_send()
+        keep(t).wait()
+
+    for store in stores:
+        store.wait()
+
+
+def mid_pair(attn_low, weight, tokens, gain_row, dy, gateup_weight, down_weight, count):
     rows = tokens.shape[0]
-    if not special:
-        partial = dot(attn_low, weight).astype(BF16)
-        hidden = tokens.astype(F32) + lax.psum_scatter(
-            partial, "narrow", scatter_dimension=0, tiled=True
-        ).astype(F32)
-        normed = (hidden * row_scale(hidden) * gain_row).astype(BF16)
-        return hidden, lax.all_gather(normed, "narrow", axis=0, tiled=True)
+    width = gateup_weight.shape[2]
+    tile, part, chips = 256, D // count, count // 2
+    tiles = width // tile
+    anywhere = pl.BlockSpec(memory_space=pl.ANY)
     return pl.pallas_call(
-        mid_forward_kernel,
-        name="mid_forward",
+        mid_kernel,
+        name="mid_pair",
         out_shape=(
             jax.ShapeDtypeStruct((rows, D), F32),
             jax.ShapeDtypeStruct((4 * rows, D), BF16),
-        ),
-        in_specs=[VM] * 4,
-        out_specs=(VM, VM),
+            jax.ShapeDtypeStruct((2, 4 * rows, width), BF16),
+            jax.ShapeDtypeStruct((4 * rows, width), BF16),
+            jax.ShapeDtypeStruct((chips, width, part), BF16),
+        ),
+        in_specs=[VM] * 4 + [anywhere] * 3,
+        out_specs=(VM,) + (anywhere,) * 4,
         scratch_shapes=[pltpu.VMEM((4 * rows, D), BF16)]
-        + scatter_space(rows) + [pltpu.VMEM((rows, D), BF16)] + dma_sems(12),
+        + scatter_space(rows)
+        + [
+            pltpu.VMEM((rows, D), BF16),
+            pltpu.VMEM((4 * rows, D), BF16),
+            pltpu.VMEM((2, D, width), BF16),
+            pltpu.VMEM((4 * rows, D), BF16),
+            pltpu.VMEM((width, D), BF16),
+            pltpu.VMEM((4 * rows, width), F32),
+            pltpu.VMEM((2, 4 * rows, width), BF16),
+            pltpu.VMEM((4 * rows, width), BF16),
+            pltpu.VMEM((tiles, 2, chips, tile, part), BF16),
+            pltpu.VMEM((tiles, chips, tile, part), BF16),
+        ]
+        + dma_sems(12)
+        + dma_sems(tiles)
+        + [
+            pltpu.SemaphoreType.DMA((3,)),
+            pltpu.SemaphoreType.DMA((3,)),
+            pltpu.SemaphoreType.DMA((tiles,)),
+        ],
         cost_estimate=cost(1, 1),
         compiler_params=remote_params(2),
-    )(attn_low, weight, tokens, gain_row)
+    )(attn_low, weight, tokens, gain_row, dy, gateup_weight, down_weight)
+
+
+def mid_forward(attn_low, weight, tokens, gain_row):
+    partial = dot(attn_low, weight).astype(BF16)
+    hidden = tokens.astype(F32) + lax.psum_scatter(
+        partial, "narrow", scatter_dimension=0, tiled=True
+    ).astype(F32)
+    normed = (hidden * row_scale(hidden) * gain_row).astype(BF16)
+    return hidden, lax.all_gather(normed, "narrow", axis=0, tiled=True)
 
 
 def mid_backward_kernel(
-    p_ref, h_ref, c_ref, g_ref, m_ref, o_ref, gg_ref, buf, stage, own, send, recv
+    h_ref, c_ref, g_ref, x_hbm, grad_hbm, gu_hbm,
+    m_ref, o_ref, gg_ref, full_hbm,
+    p_ref, buf, stage, own, x, grad, weight, mine, inbox,
+    send, recv, m_send, m_recv, load_sem, full_sem,
 ):
-    _, xn, yn, _ = square()
+    me, xn, yn, dg = square()
+    c, mate = mate_of()
     half = h_ref.shape[0] // 2
-    greet("narrow", (xn, yn))
+    tiles, part, tile = inbox.shape[0], inbox.shape[3], inbox.shape[4]
+    loads = [
+        pltpu.make_async_copy(src, dst, load_sem.at[n])
+        for n, (src, dst) in enumerate(((grad_hbm, grad), (gu_hbm, weight), (x_hbm, x)))
+    ]
+    for load in loads:
+        load.start()
+    barrier = pltpu.get_barrier_semaphore()
+    for peer in (xn, yn):
+        pl.semaphore_signal(barrier, inc=1, device_id={"narrow": peer}, device_id_type=MESH)
+    pl.semaphore_signal(barrier, inc=1, device_id={"wide": mate}, device_id_type=MESH)
+    pl.semaphore_wait(barrier, 3)
     copies = Copies(send, recv)
     gg_ref[...] = jnp.zeros_like(gg_ref)
 
@@ -249,63 +395,104 @@
         m_ref[pl.ds(low, half)] = mid
         own[pl.ds(low, half)] = mid.astype(BF16)
 
-    scatter_square(copies, 0, p_ref, buf, stage, emit)
-    gather_square(copies, 6, own, o_ref)
+    def trade(t):
+        return wide_copy(mine.at[t, 1 - c], inbox.at[t], m_send, m_recv, t, mate)
+
+    def keep(t):
+        cols = pl.ds(pl.multiple_of(t * tile, tile), tile)
+        return pltpu.make_async_copy(mine.at[t, c], full_hbm.at[:, :, :, cols], full_sem.at[t])
+
+    def products(low, high):
+        @pl.loop(low, high)
+        def _(t):
+            cols = pl.ds(pl.multiple_of(t * tile, tile), tile)
+            for n in range(2):
+                full = dot_tn(x[...], grad[n, :, cols]).astype(BF16)
+                for k in range(D // part):
+                    mine[t, k % 2, n, k // 2] = full[k * part : (k + 1) * part]
+            trade(t).start()
+
+    rows = 2 * half
+    loads[0].wait()
+    loads[1].wait()
+
+    def fill(owner):
+        at = pl.ds(pl.multiple_of(owner * rows, rows), rows)
+
+        @pl.loop(0, D // 512)
+        def _(t):
+            cols = pl.ds(pl.multiple_of(t * 512, 512), 512)
+            p_ref[at, cols] = (
+                dot_nt(grad[0, at, :], weight[0, cols, :])
+                + dot_nt(grad[1, at, :], weight[1, cols, :])
+            ).astype(BF16)
+
+    def early():
+        loads[2].wait()
+        products(0, tiles // 2)
+
+    def middle():
+        products(tiles // 2, tiles)
+
+    def relay():
+        @pl.loop(0, tiles)
+        def _(t):
+            trade(t).wait_recv()
+            mine[t, c] = (mine[t, c].astype(F32) + inbox[t].astype(F32)).astype(BF16)
+            keep(t).start()
+
+    scatter_square(copies, 0, p_ref, buf, stage, emit, fill, early, middle)
+    gather_square(copies, 6, own, o_ref, relay=relay)
     copies.finish()
 
-
-def mid_backward(partial, hidden_mid, cotangent, gain_row, special):
+    @pl.loop(0, tiles)
+    def _(t):
+        trade(t).wait_send()
+        keep(t).wait()
+
+
+def mid_backward_pair(hidden_mid, cotangent, gain_row, x, grads, gateup_weight, count):
     rows = hidden_mid.shape[0]
-    if not special:
-        total = lax.psum_scatter(partial, "narrow", scatter_dimension=0, tiled=True).astype(F32)
-        scale = row_scale(hidden_mid)
-        back, gain_sum = norm_back(total, hidden_mid * scale, scale, gain_row)
-        mid = cotangent.astype(F32) + back
-        return mid, lax.all_gather(mid.astype(BF16), "narrow", axis=0, tiled=True), gain_sum
-    return pl.pallas_call(
+    width = grads.shape[2]
+    tile, part, chips = 256, D // count, count // 2
+    tiles = width // tile
+    anywhere = pl.BlockSpec(memory_space=pl.ANY)
+    mid_grad, back_attn, gain_sum, full = pl.pallas_call(
         mid_backward_kernel,
-        name="mid_backward",
+        name="mid_backward_pair",
         out_shape=(
             jax.ShapeDtypeStruct((rows, D), F32),
             jax.ShapeDtypeStruct((4 * rows, D), BF16),
             jax.ShapeDtypeStruct((1, D), F32),
-        ),
-        in_specs=[VM] * 4,
-        out_specs=(VM,) * 3,
-        scratch_shapes=scatter_space(rows) + [pltpu.VMEM((rows, D), BF16)] + dma_sems(12),
+            jax.ShapeDtypeStruct((2, chips, part, width), BF16),
+        ),
+        in_specs=[VM] * 3 + [anywhere] * 3,
+        out_specs=(VM,) * 3 + (anywhere,),
+        scratch_shapes=[pltpu.VMEM((4 * rows, D), BF16)]
+        + scatter_space(rows)
+        + [
+            pltpu.VMEM((rows, D), BF16),
+            pltpu.VMEM(x.shape, BF16),
+            pltpu.VMEM(grads.shape, BF16),
+            pltpu.VMEM(gateup_weight.shape, BF16),
+            pltpu.VMEM((tiles, 2, 2, chips, part, tile), BF16),
+            pltpu.VMEM((tiles, 2, chips, part, tile), BF16),
+        ]
+        + dma_sems(12)
+        + dma_sems(tiles)
+        + [pltpu.SemaphoreType.DMA((3,)), pltpu.SemaphoreType.DMA((tiles,))],
         cost_estimate=cost(1, 1),
         compiler_params=remote_params(3),
-    )(partial, hidden_mid, cotangent, gain_row)
-
-
-def out_scatter_kernel(p_ref, h_ref, o_ref, buf, stage, send, recv):
-    _, xn, yn, _ = square()
-    half = h_ref.shape[0] // 2
-    greet("narrow", (xn, yn))
-    copies = Copies(send, recv)
-
-    def emit(low, total):
-        o_ref[pl.ds(low, half)] = h_ref[pl.ds(low, half)] + total
-
-    scatter_square(copies, 0, p_ref, buf, stage, emit)
-    copies.finish()
-
-
-def out_scatter(partial, hidden_mid, special):
-    rows = hidden_mid.shape[0]
-    if not special:
-        total = lax.psum_scatter(partial, "narrow", scatter_dimension=0, tiled=True)
-        return hidden_mid + total.astype(F32)
-    return pl.pallas_call(
-        out_scatter_kernel,
-        name="out_scatter",
-        out_shape=jax.ShapeDtypeStruct((rows, D), F32),
-        in_specs=[VM] * 2,
-        out_specs=VM,
-        scratch_shapes=scatter_space(rows) + dma_sems(6),
-        cost_estimate=cost(1, 1),
-        compiler_params=remote_params(9),
-    )(partial, hidden_mid)
+    )(hidden_mid, cotangent, gain_row, x, grads, gateup_weight)
+    return mid_grad, back_attn, gain_sum, full.reshape(2, D // 2, width)
+
+
+def mid_backward(partial, hidden_mid, cotangent, gain_row):
+    total = lax.psum_scatter(partial, "narrow", scatter_dimension=0, tiled=True).astype(F32)
+    scale = row_scale(hidden_mid)
+    back, gain_sum = norm_back(total, hidden_mid * scale, scale, gain_row)
+    mid = cotangent.astype(F32) + back
+    return mid, lax.all_gather(mid.astype(BF16), "narrow", axis=0, tiled=True), gain_sum
 
 
 def in_scatter_kernel(p_ref, t_ref, m_ref, g_ref, o_ref, gg_ref, buf, stage, send, recv):
@@ -355,23 +542,6 @@
     return w, z, c, count // 2, w + 1 - 2 * c, jnp.minimum(w + 2, count - 1), jnp.maximum(w - 2, 0)
 
 
-def greet_line(count):
-    w, z, c, chips, mate, above, below = line(count)
-    barrier = pltpu.get_barrier_semaphore()
-    has_above, has_below = z < chips - 1, z > 0
-
-    @pl.when(has_above)
-    def _():
-        pl.semaphore_signal(barrier, inc=1, device_id={"wide": above}, device_id_type=MESH)
-
-    @pl.when(has_below)
-    def _():
-        pl.semaphore_signal(barrier, inc=1, device_id={"wide": below}, device_id_type=MESH)
-
-    pl.semaphore_signal(barrier, inc=1, device_id={"wide": mate}, device_id_type=MESH)
-    pl.semaphore_wait(barrier, 1 + has_above.astype(jnp.int32) + has_below.astype(jnp.int32))
-
-
 def wide_copy(src, dst, send, recv, slot, peer):
     return pltpu.make_async_remote_copy(
         src_ref=src,
@@ -384,10 +554,35 @@
 
 
 def return_grads_kernel(
-    count, x_ref, o_ref, from_mate, from_above, stage, send, recv, mate_send, mate_recv
+    count, x_ref, h_ref, act_hbm, d_hbm, o_ref, b_ref,
+    from_mate, from_above, stage, p_ref, buf, out_stage, act, weight,
+    send, recv, mate_send, mate_recv, n_send, n_recv, load_sem,
 ):
     w, z, c, chips, mate, above, below = line(count)
-    greet_line(count)
+    me, xn, yn, dg = square()
+    rows = h_ref.shape[0]
+    half = rows // 2
+    loads = [
+        pltpu.make_async_copy(src, dst, load_sem.at[n])
+        for n, (src, dst) in enumerate(((act_hbm, act), (d_hbm, weight)))
+    ]
+    for load in loads:
+        load.start()
+    has_above, has_below = z < chips - 1, z > 0
+    barrier = pltpu.get_barrier_semaphore()
+    for peer in (xn, yn):
+        pl.semaphore_signal(barrier, inc=1, device_id={"narrow": peer}, device_id_type=MESH)
+
+    @pl.when(has_above)
+    def _():
+        pl.semaphore_signal(barrier, inc=1, device_id={"wide": above}, device_id_type=MESH)
+
+    @pl.when(has_below)
+    def _():
+        pl.semaphore_signal(barrier, inc=1, device_id={"wide": below}, device_id_type=MESH)
+
+    pl.semaphore_signal(barrier, inc=1, device_id={"wide": mate}, device_id_type=MESH)
+    pl.semaphore_wait(barrier, 3 + has_above.astype(jnp.int32) + has_below.astype(jnp.int32))
 
     def to_mate(s):
         return wide_copy(
@@ -402,9 +597,6 @@
     def sends_mate(s):
         return (z > s) | ((z == s) & (c == 1))
 
-    def gets_mate(s):
-        return (z > s) | ((z == s) & (c == 0))
-
     def down(s):
         return wide_copy(stage.at[s], from_above.at[s], send, recv, s, below)
 
@@ -414,25 +606,46 @@
         def _():
             to_mate(s).start()
 
+    def chain():
+        for s in range(chips - 1):
+            block = 2 * s + c
+
+            @pl.when(z > s)
+            def _():
+                to_mate(s).wait_recv()
+
+                @pl.when(z == chips - 1)
+                def _():
+                    stage[s] = (x_ref[block].astype(F32) + from_mate[s].astype(F32)).astype(BF16)
+
+                @pl.when(z < chips - 1)
+                def _():
+                    down(s).wait_recv()
+                    stage[s] = (
+                        x_ref[block].astype(F32)
+                        + from_mate[s].astype(F32)
+                        + from_above[s].astype(F32)
+                    ).astype(BF16)
+
+                down(s).start()
+
+    def emit(low, total):
+        b_ref[pl.ds(low, half)] = h_ref[pl.ds(low, half)] + total
+
+    def fill(owner):
+        at = pl.ds(pl.multiple_of(owner * rows, rows), rows)
+
+        @pl.loop(0, D // 512)
+        def _(t):
+            cols = pl.ds(pl.multiple_of(t * 512, 512), 512)
+            p_ref[at, cols] = dot(act[at, :], weight[:, cols]).astype(BF16)
+
+    for load in loads:
+        load.wait()
+    copies = Copies(n_send, n_recv)
+    scatter_square(copies, 0, p_ref, buf, out_stage, emit, fill, middle=chain)
     for s in range(chips):
-        block = jnp.minimum(2 * s + c, count - 1)
-
-        @pl.when(z > s)
-        def _():
-            to_mate(s).wait_recv()
-
-            @pl.when(z == chips - 1)
-            def _():
-                stage[s] = (x_ref[block].astype(F32) + from_mate[s].astype(F32)).astype(BF16)
-
-            @pl.when(z < chips - 1)
-            def _():
-                down(s).wait_recv()
-                stage[s] = (
-                    x_ref[block].astype(F32) + from_mate[s].astype(F32) + from_above[s].astype(F32)
-                ).astype(BF16)
-
-            down(s).start()
+        block = 2 * s + c
 
         @pl.when(z == s)
         def _():
@@ -447,6 +660,7 @@
                 down(s).wait_recv()
                 o_ref[...] += from_above[s].astype(F32)
 
+    copies.finish()
     for s in range(chips):
 
         @pl.when(sends_mate(s))
@@ -458,35 +672,46 @@
             down(s).wait_send()
 
 
-def return_grads(grads, count, special):
+def return_grads_out(grads, act, down_weight, hidden_mid, count):
     _, rows, width = grads.shape
-    if not special:
-        w = lax.axis_index("wide")
-        seen = (jnp.arange(count) <= w)[:, None, None]
-        total = lax.psum_scatter(
-            jnp.where(seen, grads, 0).reshape(count * rows, width),
-            "wide",
-            scatter_dimension=0,
-            tiled=True,
-        )
-        return total.astype(F32)
     chips = count // 2
     return pl.pallas_call(
         functools.partial(return_grads_kernel, count),
         name="return_grads",
-        out_shape=jax.ShapeDtypeStruct((rows, width), F32),
-        in_specs=[VM],
-        out_specs=VM,
+        out_shape=(
+            jax.ShapeDtypeStruct((rows, width), F32),
+            jax.ShapeDtypeStruct(hidden_mid.shape, F32),
+        ),
+        in_specs=[VM] * 2 + [pl.BlockSpec(memory_space=pl.ANY)] * 2,
+        out_specs=(VM, VM),
         scratch_shapes=[
             pltpu.VMEM((chips, rows, width), BF16),
             pltpu.VMEM((chips, rows, width), BF16),
             pltpu.VMEM((chips, rows, width), BF16),
+            pltpu.VMEM((act.shape[0], D), BF16),
         ]
+        + scatter_space(hidden_mid.shape[0])
+        + [pltpu.VMEM(act.shape, BF16), pltpu.VMEM(down_weight.shape, BF16)]
         + dma_sems(chips)
-        + dma_sems(chips),
+        + dma_sems(chips)
+        + dma_sems(6)
+        + [pltpu.SemaphoreType.DMA((2,))],
         cost_estimate=cost(1, 1),
         compiler_params=remote_params(6),
-    )(grads)
+    )(grads, hidden_mid, act, down_weight)
+
+
+def return_grads(grads, count):
+    _, rows, width = grads.shape
+    w = lax.axis_index("wide")
+    seen = (jnp.arange(count) <= w)[:, None, None]
+    total = lax.psum_scatter(
+        jnp.where(seen, grads, 0).reshape(count * rows, width),
+        "wide",
+        scatter_dimension=0,
+        tiled=True,
+    )
+    return total.astype(F32)
 
 
 def gain_kernel(wide, x_ref, o_ref, near, mid, far, send, recv, wide_send, wide_recv):
@@ -1234,175 +1459,6 @@
     barrier = pltpu.get_barrier_semaphore()
     pl.semaphore_signal(barrier, inc=1, device_id={"wide": mate}, device_id_type=MESH)
     pl.semaphore_wait(barrier, 1)
-
-
-def feed_pair_kernel(x_ref, dy_ref, w_ref, raw_ref, act_ref, down_ref, stage, inbox, send, recv):
-    step, steps = pl.program_id(0), pl.num_programs(0) - 1
-    c, mate = mate_of()
-
-    def trade(i):
-        return wide_copy(stage.at[i % 2, 1 - c], inbox.at[i], send, recv, i, mate)
-
-    @pl.when(step == 0)
-    def _():
-        greet_mate()
-
-    @pl.when((step >= 2) & (step <= steps))
-    def _():
-        trade(step - 2).wait_send()
-
-    @pl.when(step < steps)
-    def _():
-        x = x_ref[...]
-        gate = dot(x, w_ref[0])
-        upper = dot(x, w_ref[1])
-        raw_ref[0] = gate
-        raw_ref[1] = upper
-        act = (gate * jax.nn.sigmoid(gate) * upper).astype(BF16)
-        act_ref[...] = act
-        full = dot_tn(act, dy_ref[...]).astype(BF16)
-        width = stage.shape[4]
-        for part in range(D // width):
-            stage[step % 2, part % 2, part // 2] = full[:, part * width : (part + 1) * width]
-        trade(step).start()
-
-    @pl.when(step > 0)
-    def _():
-        last = jnp.maximum(step - 1, 0)
-        trade(last).wait_recv()
-        down_ref[...] = (stage[last % 2, c].astype(F32) + inbox[last].astype(F32)).astype(BF16)
-
-    @pl.when(step == steps)
-    def _():
-        trade(step - 1).wait_send()
-
-
-def feed_pair(x, dy, gateup_weight, width, count):
-    rows = x.shape[0]
-    tile = 256
-    steps = width // tile
-    part = D // count
-    whole = lambda i: (0, 0)
-    now = lambda i: jnp.minimum(i, steps - 1)
-    return pl.pallas_call(
-        feed_pair_kernel,
-        name="feed_pair",
-        grid=(steps + 1,),
-        out_shape=(
-            jax.ShapeDtypeStruct((2, rows, width), F32),
-            jax.ShapeDtypeStruct((rows, width), BF16),
-            jax.ShapeDtypeStruct((count // 2, width, part), BF16),
-        ),
-        in_specs=[
-            pl.BlockSpec((rows, D), whole),
-            pl.BlockSpec((rows, D), whole),
-            pl.BlockSpec((2, D, tile), lambda i: (0, 0, now(i))),
-        ],
-        out_specs=(
-            pl.BlockSpec((2, rows, tile), lambda i: (0, 0, now(i))),
-            pl.BlockSpec((rows, tile), lambda i: (0, now(i))),
-            pl.BlockSpec((count // 2, tile, part), lambda i: (0, jnp.maximum(i - 1, 0), 0)),
-        ),
-        scratch_shapes=[
-            pltpu.VMEM((2, 2, count // 2, tile, part), BF16),
-            pltpu.VMEM((steps, count // 2, tile, part), BF16),
-        ]
-        + dma_sems(steps),
-        cost_estimate=cost(1, 1),
-        compiler_params=remote_params(10),
-    )(x, dy, gateup_weight)
-
-
-def feed_back_pair_kernel(
-    x_ref, dy_ref, raw_ref, act_ref, w_ref, d_ref, full_ref, in_ref, out_ref,
-    in_acc, out_acc, stage, inbox, send, recv,
-):
-    step, steps = pl.program_id(0), pl.num_programs(0) - 1
-    c, mate = mate_of()
-
-    def trade(i):
-        return wide_copy(stage.at[i % 2, 1 - c], inbox.at[i], send, recv, i, mate)
-
-    @pl.when(step == 0)
-    def _():
-        greet_mate()
-        in_acc[...] = jnp.zeros_like(in_acc)
-        out_acc[...] = jnp.zeros_like(out_acc)
-
-    @pl.when((step >= 2) & (step <= steps))
-    def _():
-        trade(step - 2).wait_send()
-
-    @pl.when(step < steps)
-    def _():
-        act_grad = dot_nt(dy_ref[...], d_ref[...])
-        gate, upper = raw_ref[0], raw_ref[1]
-        sig = jax.nn.sigmoid(gate)
-        gate_grad = (act_grad * upper * sig * (1.0 + gate * (1.0 - sig))).astype(BF16)
-        up_grad = (act_grad * gate * sig).astype(BF16)
-        x = x_ref[...]
-        part = stage.shape[4]
-        for n, grad in enumerate((gate_grad, up_grad)):
-            full = dot_tn(x, grad).astype(BF16)
-            for k in range(D // part):
-                stage[step % 2, k % 2, n, k // 2] = full[k * part : (k + 1) * part]
-        trade(step).start()
-        in_acc[...] += dot_nt(gate_grad, w_ref[0]) + dot_nt(up_grad, w_ref[1])
-        out_acc[...] += dot(act_ref[...], d_ref[...])
-
-    @pl.when(step > 0)
-    def _():
-        last = jnp.maximum(step - 1, 0)
-        trade(last).wait_recv()
-        full_ref[...] = (stage[last % 2, c].astype(F32) + inbox[last].astype(F32)).astype(BF16)
-
-    @pl.when(step == steps)
-    def _():
-        trade(step - 1).wait_send()
-        in_ref[...] = in_acc[...].astype(BF16)
-        out_ref[...] = out_acc[...].astype(BF16)
-
-
-def feed_back_pair(x, dy, raw, act, gateup_weight, down_weight, count):
-    rows, width = act.shape
-    tile = 256
-    steps = width // tile
-    part = D // count
-    whole = lambda i: (0, 0)
-    now = lambda i: jnp.minimum(i, steps - 1)
-    full, in_partial, out_partial = pl.pallas_call(
-        feed_back_pair_kernel,
-        name="feed_back_pair",
-        grid=(steps + 1,),
-        out_shape=(
-            jax.ShapeDtypeStruct((2, count // 2, part, width), BF16),
-            jax.ShapeDtypeStruct((rows, D), BF16),
-            jax.ShapeDtypeStruct((rows, D), BF16),
-        ),
-        in_specs=[
-            pl.BlockSpec((rows, D), whole),
-            pl.BlockSpec((rows, D), whole),
-            pl.BlockSpec((2, rows, tile), lambda i: (0, 0, now(i))),
-            pl.BlockSpec((rows, tile), lambda i: (0, now(i))),
-            pl.BlockSpec((2, D, tile), lambda i: (0, 0, now(i))),
-            pl.BlockSpec((tile, D), lambda i: (now(i), 0)),
-        ],
-        out_specs=(
-            pl.BlockSpec((2, count // 2, part, tile), lambda i: (0, 0, 0, jnp.maximum(i - 1, 0))),
-            pl.BlockSpec((rows, D), whole),
-            pl.BlockSpec((rows, D), whole),
-        ),
-        scratch_shapes=[
-            pltpu.VMEM((rows, D), F32),
-            pltpu.VMEM((rows, D), F32),
-            pltpu.VMEM((2, 2, 2, count // 2, part, tile), BF16),
-            pltpu.VMEM((steps, 2, count // 2, part, tile), BF16),
-        ]
-        + dma_sems(steps),
-        cost_estimate=cost(1, 1),
-        compiler_params=remote_params(11),
-    )(x, dy, raw, act, gateup_weight, down_weight)
-    return full.reshape(2, D // 2, width), in_partial, out_partial
 
 
 def project_back_pair_kernel(
@@ -1621,51 +1677,48 @@
         kv_all = lax.all_gather(kv_low, "wide", axis=0)
         attn_out, attn_low, lse = attend(w_scalar, query_low, kv_all, q_heads, group)
         back_mlp = lax.all_gather(cotangent, "narrow", axis=0, tiled=True)
-    hidden_mid, mlp_input = mid_forward(attn_low, output_weight, tokens, mlp_gain, special)
     if special:
-        raw, act, down_full = feed_pair(mlp_input, back_mlp, gateup_weight, down_weight.shape[0], wide)
+        hidden_mid, mlp_input, act_grads, act, down_full = mid_pair(
+            attn_low, output_weight, tokens, mlp_gain, back_mlp, gateup_weight, down_weight, wide
+        )
         down_total = line_scatter(down_full, 0, wide)[0]
-        gateup_full, in_partial, out_partial = feed_back_pair(
-            mlp_input, back_mlp, raw, act, gateup_weight, down_weight, wide
+        mid_grad, back_attn, mlp_gain_grad, gateup_full = mid_backward_pair(
+            hidden_mid, cotangent, mlp_gain, mlp_input, act_grads, gateup_weight, wide
         )
         gateup_total = line_scatter(gateup_full, 1, wide)
     else:
+        hidden_mid, mlp_input = mid_forward(attn_low, output_weight, tokens, mlp_gain)
         act, act_grads, down_full = feed(mlp_input, back_mlp, gateup_weight, down_weight)
         down_total = wide_scatter(down_full, 1)
         gateup_full, in_partial, out_partial = feed_back(
             mlp_input, act, act_grads, gateup_weight, down_weight
         )
         gateup_total = wide_scatter(gateup_full, 1)
-    mid_grad, back_attn, mlp_gain_grad = mid_backward(
-        in_partial, hidden_mid, cotangent, mlp_gain, special
-    )
+        mid_grad, back_attn, mlp_gain_grad = mid_backward(
+            in_partial, hidden_mid, cotangent, mlp_gain
+        )
     attn_grad, output_full = out_back(back_attn, output_weight, attn_low)
     query_sum, kv_sums = attend_back(
         w_scalar, query_low, kv_all, attn_grad, attn_out, lse, q_heads, group
     )
-    down_new = adamw(
-        down_total.astype(F32),
-        down_master,
-        down_moment,
-        down_second,
-        down_average,
-        2.0 * FF ** (-0.5),
-        WEIGHT_DECAY,
-    )
-    kv_sums, down_new = lax.optimization_barrier((kv_sums, down_new))
     query_back, query_gain_grad = unspin(query_sum, query_raw, query_gain, cosine, sine)
-    kv_sum = return_grads(kv_sums, wide, special)
+    if special:
+        kv_sum, block_output = return_grads_out(kv_sums, act, down_weight, hidden_mid, wide)
+    else:
+        kv_sum = return_grads(kv_sums, wide)
+        block_output = hidden_mid + lax.psum_scatter(
+            out_partial, "narrow", scatter_dimension=0, tiled=True
+        ).astype(F32)
     kv_back, key_gain_grad = unspin(kv_sum, key_raw, key_gain, cosine, sine)
     back_args = (attn_input, query_back, kv_back, query_weight, keyvalue_weight, output_full)
     if special:
         normed_partial, project_full = project_back_pair(*back_args, wide)
     else:
         normed_partial, project_full = project_back(*back_args)
-    project_full, gateup_total, out_partial, normed_partial = lax.optimization_barrier(
-        (project_full, gateup_total, out_partial, normed_partial)
+    project_full, gateup_total, down_total, normed_partial = lax.optimization_barrier(
+        (project_full, gateup_total, down_total, normed_partial)
     )
     rest_total = line_scatter(project_full, 0, wide) if special else wide_scatter(project_full, 0)
-    block_output = out_scatter(out_partial, hidden_mid, special)
     input_grad, attn_gain_grad = in_scatter(normed_partial, tokens, mid_grad, attn_gain, special)
     gain_partial = jnp.concatenate(
         [attn_gain_grad, mlp_gain_grad, query_gain_grad, key_gain_grad], axis=1
@@ -1685,6 +1738,15 @@
         gateup_second,
         gateup_average,
         2.0 * D ** (-0.5),
+        WEIGHT_DECAY,
+    )
+    down_new = adamw(
+        down_total.astype(F32),
+        down_master,
+        down_moment,
+        down_second,
+        down_average,
+        2.0 * FF ** (-0.5),
         WEIGHT_DECAY,
     )
     gain_new = adamw(

time: 443 us -> 412 us (0.930)
  Pallas kernels: 393 us -> 344 us
  waiting for transfers between devices: 0.09 us -> 19.6 us
    pallas_call x6 -> x3, Pallas kernels: 263 us -> 210 us  [the longest x1 98 us: return_grads_out(): pl.pallas_call(functools.partial(return_grads_kernel, count), name='retur...]
    reduce_scatter x3, waiting for transfers between devices: 0.04 us -> 19.6 us  [line_scatter(): lax.psum_scatter(partial, 'wide', scatter_dimension=axis, tiled=True, axi...]
    pallas_call x1, Pallas kernels: 11.5 us -> 19.8 us  [project_back_pair(): pl.pallas_call(project_back_pair_kernel, name='project_back_pair', grid=(...]
    pallas_call x1, Pallas kernels: 17.6 us -> 12.9 us  [gain_sums(): pl.pallas_call(functools.partial(gain_kernel, wide), name='gain_sums', ou...]
  transfers between devices with their start and end apart: 3 -> 3, of which waited for: 0 -> 2; matrix products, arithmetic and copies ran while one was open for 5% -> 4% of each run, Pallas kernels for 63% -> 58%
where the time goes in v4:
time: 412 us; the launch traced here: 405 us
  Pallas kernels  344 us (83%)
  waiting for transfers between devices  19.6 us (5%)
  other arithmetic  18.8 us (5%)
  between operations  14.5 us (4%)
  local copies, waits for them, and re-layouts  8.47 us (2%)
    pallas_call x1, Pallas kernels, return_grads_out(): pl.pallas_call(functools.partial(return_grads_kernel, count), name='retur...  98 us
    pallas_call x1, Pallas kernels, mid_backward_pair(): pl.pallas_call(mid_backward_kernel, name='mid_backward_pair', out_shape=(...  59.2 us
    pallas_call x1, Pallas kernels, mid_pair(): pl.pallas_call(mid_kernel, name='mid_pair', out_shape=(jax.ShapeDtypeStru...  52.4 us
    pallas_call x1, Pallas kernels, front(): pl.pallas_call(functools.partial(front_kernel, count, heads, group), name...  50.3 us
    pallas_call x1, Pallas kernels, in_scatter(): pl.pallas_call(in_scatter_kernel, name='in_scatter', out_shape=(jax.Shape...  24.2 us
    pallas_call x1, Pallas kernels, project_back_pair(): pl.pallas_call(project_back_pair_kernel, name='project_back_pair', grid=(...  19.8 us
    reduce_scatter x3, waiting for transfers between devices, line_scatter(): lax.psum_scatter(partial, 'wide', scatter_dimension=axis, tiled=True, axi...  19.6 us
    add x3, other arithmetic, adamw(): average_new = EMA_KEEP * average + (1.0 - EMA_KEEP) * master_new  16 us
  transfers between devices with their start and end apart: 3, of which 2 were waited for; matrix products, arithmetic and copies ran while one was open for 4% of the time, Pallas kernels for 58%

profile of v4, /device:TPU:0, one launch (start us, length us, event | category | flops | bytes accessed | tf_op | source)
XLA Modules:
  0.0 405.3 jit_solution(1834991518185950374)
XLA Ops:
  7.2 0.0 reduce-scatter.6.cloned.1.call-start
  7.3 1.3 fusion.7
  8.6 1.3 slice_bitcast_fusion
  9.9 1.0 fusion.2
  10.9 1.0 pad_maximum_fusion
  11.9 50.3 %front.1 = (bf16[512,2048]{1,0:T(8,128)(2,1)}, bf16[512,2048]{1,0:T(8,128)(2,1)}, bf16[512,512]{1,0:T(8,128)(2,1)}, f32[512,512]{1,0:T(8,128)}, f32[512,256]{1,0...) custom-call(bf16[128,2048]{1,0:T(8,128)(2,1)} %t_ref.5, ...), custom_call_target="tpu_custom_call" | custom-call | flops 1 | bytes 1 | tf_op jit(solution)/shard_map/front/pallas_call | solution.py:1243
  62.2 52.4 %mid_pair.1 = (f32[128,2048]{1,0:T(8,128)}, bf16[512,2048]{1,0:T(8,128)(2,1)}, bf16[2,512,1536]{2,1,0:T(8,128)(2,1)}, bf16[512,1536]{1,0:T(8,128)(2,1)}, bf16[4,1536,256]{2,1,0:T(8,128)(2,1)}) custom-call(bf16[512,512]{1,0:T(8,128)(2,1)} %get-tuple-element.85.a_ref.low_ref, bf16[512,2048]{1,0:T(8,128)(2,1)} %w_ref.3, bf16[128,2048]{1,0:T(8,128)(2,1)} %t_ref.5, ...), custom_call_target="tpu_custom_call" | custom-call | flops 1 | bytes 1 | tf_op jit(solution)/shard_map/mid_pair/pallas_call | solution.py:318
  114.6 0.0 reduce-scatter.6.cloned.1.call-update
  114.6 0.0 reduce-scatter.4.cloned.1.call-start
  114.7 59.2 %mid_backward_pair.1 = (f32[128,2048]{1,0:T(8,128)}, bf16[512,2048]{1,0:T(8,128)(2,1)}, f32[1,2048]{1,0:T(1,128)}, bf16[2,4,256,1536]{3,2,1,0:T(8,128)(2,1)}) custom-call(f32[128,2048]{1,0:T(8,128)} %get-tuple-element.87.h_ref, bf16[128,2048]{1,0:T(8,128)(2,1)} %c_ref.3, f32[1,2048]{1,0:T(1,128)} %bitcast.21, bf16[512,2048]{1,0:T(8,128)(2,1)} %get-tuple-element.88.x_hbm, ...), custom_call_target="tpu_custom_call" | custom-call | flops 1 | bytes 1 | tf_op jit(solution)/shard_map/mid_backward_pair/pallas_call | solution.py:460
  173.8 0.0 reduce-scatter.4.cloned.1.call-update
  173.8 0.3 reduce-scatter.8.cloned.1.call-start
  174.1 5.7 %out_back.1 = (bf16[512,512]{1,0:T(8,128)(2,1)}, bf16[2048,512]{1,0:T(8,128)(2,1)}) custom-call(bf16[512,2048]{1,0:T(8,128)(2,1)} %get-tuple-element.90.dy_ref, bf16[512,2048]{1,0:T(8,128)(2,1)} %w_ref.3, bf16[512,512]{1,0:T(8,128)(2,1)} %get-tuple-element.85.a_ref.low_ref), custom_call_target="tpu_custom_call" | custom-call | flops 1 | bytes 1 | tf_op jit(solution)/shard_map/out_back/pallas_call | solution.py:1387
  179.8 8.8 %attend_back.1 = (f32[512,512]{1,0:T(8,128)}, bf16[8,512,512]{2,1,0:T(8,128)(2,1)}) custom-call(s32[1]{0:T(128)} %bitcast.w_ref, bf16[512,512]{1,0:T(8,128)(2,1)} %get-tuple-element.83.q_ref, bf16[8,512,512]{2,1,0:T(8,128)(2,1)} %get-tuple-element.84.kv_ref, bf16[512,512]{1,0:T(8,128)(2,1)} %get-tuple-element.91.do_ref, f32[512,512]{1,0:T(8,128)} %get-tuple-element.92.o_ref, ...), custom_call_target="tpu_custom_call" | custom-call | flops 1 | bytes 1 | tf_op jit(solution)/shard_map/attend_back/pallas_call | solution.py:980
  188.6 98.0 %return_grads.1 = (f32[512,512]{1,0:T(8,128)}, f32[128,2048]{1,0:T(8,128)}) custom-call(bf16[8,512,512]{2,1,0:T(8,128)(2,1)} %get-tuple-element.94.x_ref, f32[128,2048]{1,0:T(8,128)} %get-tuple-element.87.h_ref, bf16[512,1536]{1,0:T(8,128)(2,1)} %get-tuple-element.95.act_hbm, bf16[1536,2048]{1,0:T(8,128)(2,1)} %d_hbm.3), custom_call_target="tpu_custom_call" | custom-call | flops 1 | bytes 1 | tf_op jit(solution)/shard_map/return_grads/pallas_call | solution.py:678
  286.6 3.6 unspin.2
  290.2 2.9 unspin.3
  293.1 19.8 %project_back_pair.1 = (bf16[512,2048]{1,0:T(8,128)(2,1)}, bf16[4,256,1536]{2,1,0:T(8,128)(2,1)}) custom-call(bf16[512,2048]{1,0:T(8,128)(2,1)} %get-tuple-element.97.x_ref, bf16[512,512]{1,0:T(8,128)(2,1)} %get-tuple-element.100.q_ref, bf16[512,512]{1,0:T(8,128)(2,1)} %get-tuple-element.103.kv_ref, bf16[2048,512]{1,0:T(8,128)(2,1)} %wq_ref.1, ...), custom_call_target="tpu_custom_call" | custom-call | flops 1 | bytes 1 | tf_op jit(solution)/shard_map/project_back_pair/pallas_call | solution.py:1519
  312.9 0.0 reduce-scatter.6.cloned.1.call-done
  312.9 12.2 %reduce-scatter.4.cloned.1.call-done = bf16[2,256,1536]{2,1,0:T(8,128)(2,1)} async-done(((bf16[2,1024,1536]{2,1,0:T(8,128)(2,1)}), bf16[2,256,1536]{2,1,0:T(8,128)(2,1)}) %reduce-scatter.4.cloned.1.call-update) | async-done | bytes 1572880 | tf_op jit(solution)/shard_map/reduce_scatter | solution.py:1603
  325.1 0.0 reduce-scatter.8.cloned.1.call-update
  325.1 0.0 copy-start.14
  325.2 0.0 copy-start.15
  325.2 0.0 copy-start.10
  325.2 0.0 copy-start.11
  325.2 0.0 copy-start.12
  325.2 0.0 copy-start.13
  325.2 0.0 copy-start.5
  325.2 0.0 copy-start.6
  325.2 24.2 %in_scatter.1 = (f32[128,2048]{1,0:T(8,128)}, f32[1,2048]{1,0:T(1,128)}) custom-call(bf16[512,2048]{1,0:T(8,128)(2,1)} %get-tuple-element.109.p_ref, bf16[128,2048]{1,0:T(8,128)(2,1)} %t_ref.5, f32[128,2048]{1,0:T(8,128)} %get-tuple-element.110.m_ref, f32[1,2048]{1,0:T(1,128)} %bitcast.19), custom_call_target="tpu_custom_call" | custom-call | flops 1 | bytes 1 | tf_op jit(solution)/shard_map/in_scatter/pallas_call | solution.py:524
  349.5 0.7 maximum_reduce_fusion
  350.3 0.1 reshape_reshape.3
  350.4 0.6 reshape.110.x_ref
  351.0 12.9 %gain_sums.1 = f32[2,128]{1,0:T(2,128)} custom-call(f32[4,8,2,128]{3,2,1,0:T(2,128)} %reshape.110.x_ref), custom_call_target="tpu_custom_call" | custom-call | flops 1 | bytes 1 | tf_op jit(solution)/shard_map/gain_sums/pallas_call | solution.py:762
  364.0 1.3 add_multiply_fusion.2
  365.3 0.0 copy-start.1
  365.3 0.0 copy-start.2
  365.3 0.0 copy-start.3
  365.4 6.5 %add_multiply_fusion.1 = (f32[1536,256]{1,0:T(8,128)}, f32[1536,256]{1,0:T(8,128)}, f32[1536,256]{1,0:T(8,128)}, f32[1536,256]{1,0:T(8,128)}, f32[1536,256]{1,0:T(8,128)}) fusion(f32[1536,256]{1,0:T(8,128)S(1)} %copy-done.5, f32[1536,256]{1,0:T(8,128)S(1)} %copy-done.6, f32[1536,256]{1,0:T(8,128)} %param.57, f32[1536,256]{1,0:T(8,128)} %param.58, ...), kind=kLoop, calls=%fused_computation.7 | loop fusion | flops 7077888 | bytes 14942208 | tf_op jit(solution)/shard_map/add | solution.py:69
  371.9 1.2 copy-done.2
  373.1 0.9 copy-done.3
  374.0 0.4 copy-done.4
  374.4 8.3 %add_multiply_fusion = (f32[2,256,1536]{2,1,0:T(8,128)}, f32[2,256,1536]{2,1,0:T(8,128)}, f32[2,256,1536]{2,1,0:T(8,128)}, f32[2,256,1536]{2,1,0:T(8,128)}, f32[2,256,1536]{2,1,0:T(8,128)}) fusion(f32[2,256,1536]{2,1,0:T(8,128)S(1)} %copy-done, f32[2,256,1536]{2,1,0:T(8,128)S(1)} %copy-done.1, f32[2,256,1536]{2,1,0:T(8,128)S(1)} %copy-done.2, ...), kind=kLoop, calls=%fused_computation.2 | loop fusion | flops 14155776 | bytes 29884416 | tf_op jit(solution)/shard_map/add | solution.py:69
  382.6 7.3 %reduce-scatter.8.cloned.1.call-done.total_ref = bf16[256,1536]{1,0:T(8,128)(2,1)} async-done(((bf16[1024,1536]{1,0:T(8,128)(2,1)}), bf16[256,1536]{1,0:T(8,128)(2,1)}) %reduce-scatter.8.cloned.1.call-update) | async-done | bytes 786448 | tf_op jit(solution)/shard_map/reduce_scatter | solution.py:1603
  390.0 5.8 %rest_adamw.1 = (f32[256,512]{1,0:T(8,128)}, f32[256,512]{1,0:T(8,128)}, f32[256,512]{1,0:T(8,128)}, f32[256,512]{1,0:T(8,128)}, f32[256,512]{1,0:T(8,128)}, /*i...) custom-call(bf16[256,1536]{1,0:T(8,128)(2,1)} %reduce-scatter.8.clon, ...), custom_call_target="tpu_custom_call" | custom-call | flops 1 | bytes 1 | tf_op jit(solution)/shard_map/rest_adamw/pallas_call | solution.py:1579
  395.8 1.0 copy.69
  396.8 0.6 copy-done.8
  397.4 1.0 copy.70
  (21 shorter events, 0.1 us)
Async XLA Ops:
  7.2 305.7 %reduce-scatter.6.cloned.1.call-start = ((), (), s32[]{:S(2)}) async-start(), calls=%async_computation.4 | async-start | bytes 3932160 | tf_op jit(solution)/shard_map/reduce_scatter | solution.py:1603
  114.6 210.5 %reduce-scatter.4.cloned.1.call-start = ((), (), s32[]{:S(2)}) async-start(), calls=%async_computation.3 | async-start | bytes 7864320 | tf_op jit(solution)/shard_map/reduce_scatter | solution.py:1603
  173.8 216.1 %reduce-scatter.8.cloned.1.call-start = ((), (), s32[]{:S(2)}) async-start(), calls=%async_computation.5 | async-start | bytes 3932160 | tf_op jit(solution)/shard_map/reduce_scatter | solution.py:1603
  325.1 24.4 %copy-start.9 = (f32[1,2048]{1,0:T(1,128)S(1)}, f32[1,2048]{1,0:T(1,128)}, u32[]{:S(2)}) copy-start(f32[1,2048]{1,0:T(1,128)} %get-tuple-element.131) | copy-start | bytes 24580
  325.1 24.4 %copy-start.14 = (f32[1,128]{1,0:T(1,128)S(1)}, f32[1,128]{1,0:T(1,128)}, u32[]{:S(2)}) copy-start(f32[1,128]{1,0:T(1,128)} %get-tuple-element.132) | copy-start | bytes 1540
  325.2 24.4 %copy-start.15 = (f32[1,128]{1,0:T(1,128)S(1)}, f32[1,128]{1,0:T(1,128)}, u32[]{:S(2)}) copy-start(f32[1,128]{1,0:T(1,128)} %get-tuple-element.133) | copy-start | bytes 1540
  325.2 38.8 %copy-start.10 = (f32[136]{0:T(256)S(1)}, f32[136]{0:T(256)}, u32[]{:S(2)}) copy-start(f32[136]{0:T(256)} %param.63) | copy-start | bytes 1636
  325.2 38.8 %copy-start.11 = (f32[136]{0:T(256)S(1)}, f32[136]{0:T(256)}, u32[]{:S(2)}) copy-start(f32[136]{0:T(256)} %param.60) | copy-start | bytes 1636
  325.2 38.8 %copy-start.12 = (f32[136]{0:T(256)S(1)}, f32[136]{0:T(256)}, u32[]{:S(2)}) copy-start(f32[136]{0:T(256)} %param.61) | copy-start | bytes 1636
  325.2 38.8 %copy-start.13 = (f32[136]{0:T(256)S(1)}, f32[136]{0:T(256)}, u32[]{:S(2)}) copy-start(f32[136]{0:T(256)} %param.62) | copy-start | bytes 1636
  325.2 40.1 %copy-start.5 = (f32[1536,256]{1,0:T(8,128)S(1)}, f32[1536,256]{1,0:T(8,128)}, u32[]{:S(2)}) copy-start(f32[1536,256]{1,0:T(8,128)} %param.59) | copy-start | bytes 4718596
  325.2 40.1 %copy-start.6 = (f32[1536,256]{1,0:T(8,128)S(1)}, f32[1536,256]{1,0:T(8,128)}, u32[]{:S(2)}) copy-start(f32[1536,256]{1,0:T(8,128)} %param.56) | copy-start | bytes 4718596
  365.3 6.6 %copy-start = (f32[2,256,1536]{2,1,0:T(8,128)S(1)}, f32[2,256,1536]{2,1,0:T(8,128)}, u32[]{:S(2)}) copy-start(f32[2,256,1536]{2,1,0:T(8,128)} %param.55) | copy-start | bytes 9437188
  365.3 6.6 %copy-start.1 = (f32[2,256,1536]{2,1,0:T(8,128)S(1)}, f32[2,256,1536]{2,1,0:T(8,128)}, u32[]{:S(2)}) copy-start(f32[2,256,1536]{2,1,0:T(8,128)} %param.52) | copy-start | bytes 9437188
  365.3 7.7 %copy-start.2 = (f32[2,256,1536]{2,1,0:T(8,128)S(1)}, f32[2,256,1536]{2,1,0:T(8,128)}, u32[]{:S(2)}) copy-start(f32[2,256,1536]{2,1,0:T(8,128)} %param.53) | copy-start | bytes 9437188
  365.3 8.6 %copy-start.3 = (f32[2,256,1536]{2,1,0:T(8,128)S(1)}, f32[2,256,1536]{2,1,0:T(8,128)}, u32[]{:S(2)}) copy-start(f32[2,256,1536]{2,1,0:T(8,128)} %param.54) | copy-start | bytes 9437188
  365.3 9.0 %copy-start.4 = (bf16[2,256,1536]{2,1,0:T(8,128)(2,1)S(1)}, bf16[2,256,1536]{2,1,0:T(8,128)(2,1)}, u32[]{:S(2)}) copy-start(bf16[2,256,1536]{2,1,0:T(8,128)(2,1)} %reduce-scatter.4.cloned.1.call-done) | copy-start | bytes 4718596
  382.6 13.2 %copy-start.7 = (f32[128,2048]{1,0:T(8,128)S(1)}, f32[128,2048]{1,0:T(8,128)}, u32[]{:S(2)}) copy-start(f32[128,2048]{1,0:T(8,128)} %get-tuple-element.190) | copy-start | bytes 3145732
  395.8 1.6 copy-start.8
Sparse Core Ops, SparseCore 0:
  114.7 65.3 reduce-scatter.5
  182.5 142.5 reduce-scatter.3
  327.4 62.5 reduce-scatter.7

commit v5 on v4

--- a/solution.py
+++ b/solution.py
@@ -2,6 +2,7 @@
 
 import jax
 import jax.numpy as jnp
+import numpy as np
 from jax import lax
 from jax.experimental import pallas as pl
 from jax.experimental.pallas import tpu as pltpu
@@ -49,7 +50,9 @@
 
 def rope_tables(positions):
     half_width = HD // 2
-    inverse_freq = THETA ** (-(2.0 * jnp.arange(half_width, dtype=F32)) / HD)
+    inverse_freq = jnp.asarray(
+        THETA ** (-2.0 * np.arange(half_width, dtype=np.float64) / HD), dtype=F32
+    )
     angles = positions[:, None] * inverse_freq[None, :]
     cosine, sine = jnp.cos(angles), jnp.sin(angles)
     return (
@@ -74,8 +77,12 @@
     return lax.rsqrt(jnp.mean(values_in * values_in, axis=-1, keepdims=True) + EPSILON)
 
 
-def norm_back(gradient, unit_rows, inv_scale, gain_row):
-    scaled = gradient * gain_row
+def gain_row(g_ref, base):
+    return jnp.concatenate([g_ref[base + j : base + j + 1, :] for j in range(D // HD)], axis=1)
+
+
+def norm_back(gradient, unit_rows, inv_scale, gain):
+    scaled = gradient * gain
     inner = scaled - unit_rows * jnp.mean(scaled * unit_rows, axis=-1, keepdims=True)
     return inv_scale * inner, jnp.sum(gradient * unit_rows, axis=0, keepdims=True)
 
@@ -99,7 +106,7 @@
     def __init__(self, send, recv):
         self.send, self.recv, self.sent = send, recv, []
 
-    def go(self, src, dst, slot, peer):
+    def make(self, src, dst, slot, peer):
         copy = pltpu.make_async_remote_copy(
             src_ref=src,
             dst_ref=dst,
@@ -108,42 +115,17 @@
             device_id={"narrow": peer},
             device_id_type=MESH,
         )
+        self.sent.append(copy)
+        return copy
+
+    def go(self, src, dst, slot, peer):
+        copy = self.make(src, dst, slot, peer)
         copy.start()
-        self.sent.append(copy)
         return copy
 
     def finish(self):
         for copy in self.sent:
             copy.wait_send()
-
-
-def gather_square(copies, slot, x_ref, o_ref, first=None, later=None, relay=None):
-    me, xn, yn, dg = square()
-    rows = x_ref.shape[0]
-    half = rows // 2
-
-    def part(owner, low):
-        return o_ref.at[pl.ds(pl.multiple_of(owner * rows + low, half), half)]
-
-    upper, lower = x_ref.at[pl.ds(0, half)], x_ref.at[pl.ds(half, half)]
-    xa = copies.go(upper, part(me, 0), slot, xn)
-    yb = copies.go(lower, part(me, half), slot + 1, yn)
-    xb = copies.go(lower, part(me, half), slot + 2, xn)
-    ya = copies.go(upper, part(me, 0), slot + 3, yn)
-    o_ref[pl.ds(pl.multiple_of(me * rows, rows), rows)] = x_ref[...]
-    if first is not None:
-        first()
-    xa.wait_recv()
-    yf = copies.go(part(xn, 0), part(xn, 0), slot + 4, yn)
-    yb.wait_recv()
-    xf = copies.go(part(yn, half), part(yn, half), slot + 5, xn)
-    if relay is not None:
-        relay()
-    for pair, owner in (((xb,), xn), ((ya,), yn), ((yf, xf), dg)):
-        for copy in pair:
-            copy.wait_recv()
-        if later is not None:
-            later(owner)
 
 
 def scatter_square(copies, slot, p_ref, buf, stage, emit, fill=None, early=None, middle=None):
@@ -154,16 +136,25 @@
     def part(owner, low):
         return p_ref.at[pl.ds(pl.multiple_of(owner * rows + low, half), half)]
 
+    c0 = copies.make(part(dg, 0), buf.at[0], slot, xn)
+    c1 = copies.make(part(dg, half), buf.at[1], slot + 1, yn)
+    c2 = copies.make(part(xn, 0), buf.at[2], slot + 2, xn)
+    c3 = copies.make(part(yn, half), buf.at[3], slot + 3, yn)
     if fill is None:
-        fill = lambda owner: None
-    fill(dg)
-    c0 = copies.go(part(dg, 0), buf.at[0], slot, xn)
-    c1 = copies.go(part(dg, half), buf.at[1], slot + 1, yn)
-    fill(xn)
-    c2 = copies.go(part(xn, 0), buf.at[2], slot + 2, xn)
-    fill(yn)
-    c3 = copies.go(part(yn, half), buf.at[3], slot + 3, yn)
-    fill(me)
+        for copy in (c0, c1, c2, c3):
+            copy.start()
+    else:
+
+        @pl.loop(0, 4)
+        def _(k):
+            fill(jnp.where(k == 0, dg, jnp.where(k == 1, xn, jnp.where(k == 2, yn, me))))
+            for n, ready in ((0, (c0, c1)), (1, (c2,)), (2, (c3,))):
+
+                @pl.when(k == n)
+                def _():
+                    for copy in ready:
+                        copy.start()
+
     if early is not None:
         early()
     c0.wait_recv()
@@ -180,6 +171,124 @@
     c3.wait_recv()
     c5.wait_recv()
     emit(half, part(me, half)[...].astype(F32) + buf[3].astype(F32) + buf[5].astype(F32))
+
+
+def exchange_square(copies, p_ref, buf, stage, own, o_ref, emit, fill, early, middle, use=None, relay=None):
+    me, xn, yn, dg = square()
+    rows = p_ref.shape[0] // 4
+    group, piece = rows // 2, rows // 4
+
+    def at(ref, owner, g, h):
+        return ref.at[pl.ds(pl.multiple_of(owner * rows + g * group + h * piece, piece), piece)]
+
+    def mine(g, h):
+        return own.at[pl.ds(g * group + h * piece, piece)]
+
+    sums, firsts, relays = [], [], []
+    for g in range(2):
+        s, t = 6 * g, 12 + 6 * g
+        sums.append(
+            (
+                copies.make(at(p_ref, dg, g, 0), buf.at[g, 0], s, xn),
+                copies.make(at(p_ref, dg, g, 1), buf.at[g, 1], s + 1, yn),
+                copies.make(at(p_ref, xn, g, 0), buf.at[g, 2], s + 2, xn),
+                copies.make(at(p_ref, yn, g, 1), buf.at[g, 3], s + 3, yn),
+                copies.make(stage.at[g, 0], buf.at[g, 4], s + 4, yn),
+                copies.make(stage.at[g, 1], buf.at[g, 5], s + 5, xn),
+            )
+        )
+        firsts.append(
+            (
+                copies.make(mine(g, 0), at(o_ref, me, g, 0), t, xn),
+                copies.make(mine(g, 1), at(o_ref, me, g, 1), t + 1, yn),
+                copies.make(mine(g, 1), at(o_ref, me, g, 1), t + 2, xn),
+                copies.make(mine(g, 0), at(o_ref, me, g, 0), t + 3, yn),
+            )
+        )
+        relays.append(
+            (
+                copies.make(at(o_ref, xn, g, 0), at(o_ref, xn, g, 0), t + 4, yn),
+                copies.make(at(o_ref, yn, g, 1), at(o_ref, yn, g, 1), t + 5, xn),
+            )
+        )
+
+    def merge(g):
+        for h, other in ((0, yn), (1, xn)):
+            sums[g][h].wait_recv()
+            stage[g, h] = (at(p_ref, other, g, h)[...].astype(F32) + buf[g, h].astype(F32)).astype(
+                BF16
+            )
+            sums[g][4 + h].start()
+
+    def close(g):
+        for h in range(2):
+            sums[g][2 + h].wait_recv()
+            sums[g][4 + h].wait_recv()
+            emit(
+                g * group + h * piece,
+                piece,
+                at(p_ref, me, g, h)[...].astype(F32)
+                + buf[g, 2 + h].astype(F32)
+                + buf[g, 4 + h].astype(F32),
+            )
+        for copy in firsts[g]:
+            copy.start()
+
+    @pl.loop(0, 4)
+    def _(k):
+        fill(jnp.where(k == 0, dg, jnp.where(k == 1, xn, jnp.where(k == 2, yn, me))))
+        for n, ready in ((0, sums[0][:2]), (1, sums[0][2:3]), (2, sums[0][3:4])):
+
+            @pl.when(k == n)
+            def _():
+                for copy in ready:
+                    copy.start()
+
+    merge(0)
+    for copy in sums[1][:4]:
+        copy.start()
+    early()
+    merge(1)
+    close(0)
+    middle()
+    close(1)
+    o_ref[pl.ds(pl.multiple_of(me * rows, rows), rows)] = own[...]
+
+    def pass_on():
+        for g in range(2):
+            for h in range(2):
+                firsts[g][h].wait_recv()
+                relays[g][h].start()
+        if relay is not None:
+            relay()
+        for g in range(2):
+            firsts[g][2].wait_recv()
+
+    def from_y():
+        for g in range(2):
+            firsts[g][3].wait_recv()
+
+    def from_far():
+        for g in range(2):
+            for copy in relays[g]:
+                copy.wait_recv()
+
+    if use is None:
+        pass_on()
+        from_y()
+        from_far()
+        return
+
+    @pl.loop(0, 4)
+    def _(k):
+        pl.when(k == 1)(pass_on)
+        pl.when(k == 2)(from_y)
+        pl.when(k == 3)(from_far)
+        use(jnp.where(k == 0, me, jnp.where(k == 1, xn, jnp.where(k == 2, yn, dg))))
+
+
+def exchange_space(rows):
+    return [pltpu.VMEM((2, 6, rows // 4, D), BF16), pltpu.VMEM((2, 2, rows // 4, D), BF16)]
 
 
 def dma_sems(count):
@@ -226,10 +335,12 @@
     def fill(owner):
         p_ref[rows_of(owner), :] = dot(a_ref[rows_of(owner), :], w_ref[...]).astype(BF16)
 
-    def emit(low, total):
-        hidden = t_ref[pl.ds(low, half)].astype(F32) + total
-        h_ref[pl.ds(low, half)] = hidden
-        own[pl.ds(low, half)] = (hidden * row_scale(hidden) * g_ref[...]).astype(BF16)
+    gain = gain_row(g_ref, D // HD)
+
+    def emit(low, size, total):
+        hidden = t_ref[pl.ds(low, size)].astype(F32) + total
+        h_ref[pl.ds(low, size)] = hidden
+        own[pl.ds(low, size)] = (hidden * row_scale(hidden) * gain).astype(BF16)
 
     def act_grads(low, high):
         @pl.loop(low, high)
@@ -244,8 +355,7 @@
 
     def middle():
         act_grads(tiles // 2, tiles)
-
-    scatter_square(copies, 0, p_ref, buf, stage, emit, fill, early, middle)
+        loads[2].wait()
 
     def expand(owner):
         at = rows_of(owner)
@@ -262,14 +372,7 @@
             grad[0, at, cols] = (back * upper * sig * (1.0 + gate * (1.0 - sig))).astype(BF16)
             grad[1, at, cols] = (back * swish).astype(BF16)
 
-    def first():
-        loads[2].wait()
-        expand(me)
-
-    def later(owner):
-        expand(owner)
-
-    gather_square(copies, 6, own, x, first, later)
+    exchange_square(copies, p_ref, buf, stage, own, x, emit, fill, early, middle, expand)
     stores = [
         pltpu.make_async_copy(src, dst, store_sem.at[n])
         for n, (src, dst) in enumerate(((x, x_hbm), (grad, grad_hbm), (act, act_hbm)))
@@ -309,7 +412,7 @@
         store.wait()
 
 
-def mid_pair(attn_low, weight, tokens, gain_row, dy, gateup_weight, down_weight, count):
+def mid_pair(attn_low, weight, tokens, gains, dy, gateup_weight, down_weight, count):
     rows = tokens.shape[0]
     width = gateup_weight.shape[2]
     tile, part, chips = 256, D // count, count // 2
@@ -328,7 +431,7 @@
         in_specs=[VM] * 4 + [anywhere] * 3,
         out_specs=(VM,) + (anywhere,) * 4,
         scratch_shapes=[pltpu.VMEM((4 * rows, D), BF16)]
-        + scatter_space(rows)
+        + exchange_space(rows)
         + [
             pltpu.VMEM((rows, D), BF16),
             pltpu.VMEM((4 * rows, D), BF16),
@@ -341,7 +444,7 @@
             pltpu.VMEM((tiles, 2, chips, tile, part), BF16),
             pltpu.VMEM((tiles, chips, tile, part), BF16),
         ]
-        + dma_sems(12)
+        + dma_sems(24)
         + dma_sems(tiles)
         + [
             pltpu.SemaphoreType.DMA((3,)),
@@ -350,15 +453,15 @@
         ],
         cost_estimate=cost(1, 1),
         compiler_params=remote_params(2),
-    )(attn_low, weight, tokens, gain_row, dy, gateup_weight, down_weight)
-
-
-def mid_forward(attn_low, weight, tokens, gain_row):
+    )(attn_low, weight, tokens, gains, dy, gateup_weight, down_weight)
+
+
+def mid_forward(attn_low, weight, tokens, gain):
     partial = dot(attn_low, weight).astype(BF16)
     hidden = tokens.astype(F32) + lax.psum_scatter(
         partial, "narrow", scatter_dimension=0, tiled=True
     ).astype(F32)
-    normed = (hidden * row_scale(hidden) * gain_row).astype(BF16)
+    normed = (hidden * row_scale(hidden) * gain).astype(BF16)
     return hidden, lax.all_gather(normed, "narrow", axis=0, tiled=True)
 
 
@@ -385,15 +488,16 @@
     pl.semaphore_wait(barrier, 3)
     copies = Copies(send, recv)
     gg_ref[...] = jnp.zeros_like(gg_ref)
-
-    def emit(low, total):
-        hidden = h_ref[pl.ds(low, half)]
+    gain = gain_row(g_ref, D // HD)
+
+    def emit(low, size, total):
+        hidden = h_ref[pl.ds(low, size)]
         scale = row_scale(hidden)
-        back, gain_sum = norm_back(total, hidden * scale, scale, g_ref[...])
+        back, gain_sum = norm_back(total, hidden * scale, scale, gain)
         gg_ref[...] += gain_sum
-        mid = c_ref[pl.ds(low, half)].astype(F32) + back
-        m_ref[pl.ds(low, half)] = mid
-        own[pl.ds(low, half)] = mid.astype(BF16)
+        mid = c_ref[pl.ds(low, size)].astype(F32) + back
+        m_ref[pl.ds(low, size)] = mid
+        own[pl.ds(low, size)] = mid.astype(BF16)
 
     def trade(t):
         return wide_copy(mine.at[t, 1 - c], inbox.at[t], m_send, m_recv, t, mate)
@@ -441,8 +545,7 @@
             mine[t, c] = (mine[t, c].astype(F32) + inbox[t].astype(F32)).astype(BF16)
             keep(t).start()
 
-    scatter_square(copies, 0, p_ref, buf, stage, emit, fill, early, middle)
-    gather_square(copies, 6, own, o_ref, relay=relay)
+    exchange_square(copies, p_ref, buf, stage, own, o_ref, emit, fill, early, middle, relay=relay)
     copies.finish()
 
     @pl.loop(0, tiles)
@@ -451,7 +554,7 @@
         keep(t).wait()
 
 
-def mid_backward_pair(hidden_mid, cotangent, gain_row, x, grads, gateup_weight, count):
+def mid_backward_pair(hidden_mid, cotangent, gains, x, grads, gateup_weight, count):
     rows = hidden_mid.shape[0]
     width = grads.shape[2]
     tile, part, chips = 256, D // count, count // 2
@@ -469,7 +572,7 @@
         in_specs=[VM] * 3 + [anywhere] * 3,
         out_specs=(VM,) * 3 + (anywhere,),
         scratch_shapes=[pltpu.VMEM((4 * rows, D), BF16)]
-        + scatter_space(rows)
+        + exchange_space(rows)
         + [
             pltpu.VMEM((rows, D), BF16),
             pltpu.VMEM(x.shape, BF16),
@@ -478,49 +581,50 @@
             pltpu.VMEM((tiles, 2, 2, chips, part, tile), BF16),
             pltpu.VMEM((tiles, 2, chips, part, tile), BF16),
         ]
-        + dma_sems(12)
+        + dma_sems(24)
         + dma_sems(tiles)
         + [pltpu.SemaphoreType.DMA((3,)), pltpu.SemaphoreType.DMA((tiles,))],
         cost_estimate=cost(1, 1),
         compiler_params=remote_params(3),
-    )(hidden_mid, cotangent, gain_row, x, grads, gateup_weight)
+    )(hidden_mid, cotangent, gains, x, grads, gateup_weight)
     return mid_grad, back_attn, gain_sum, full.reshape(2, D // 2, width)
 
 
-def mid_backward(partial, hidden_mid, cotangent, gain_row):
+def mid_backward(partial, hidden_mid, cotangent, gain):
     total = lax.psum_scatter(partial, "narrow", scatter_dimension=0, tiled=True).astype(F32)
     scale = row_scale(hidden_mid)
-    back, gain_sum = norm_back(total, hidden_mid * scale, scale, gain_row)
+    back, gain_sum = norm_back(total, hidden_mid * scale, scale, gain)
     mid = cotangent.astype(F32) + back
     return mid, lax.all_gather(mid.astype(BF16), "narrow", axis=0, tiled=True), gain_sum
 
 
-def in_scatter_kernel(p_ref, t_ref, m_ref, g_ref, o_ref, gg_ref, buf, stage, send, recv):
+def in_scatter_kernel(p_ref, t_ref, g_ref, o_ref, gg_ref, buf, stage, send, recv):
     _, xn, yn, _ = square()
     half = t_ref.shape[0] // 2
     greet("narrow", (xn, yn))
     copies = Copies(send, recv)
     gg_ref[...] = jnp.zeros_like(gg_ref)
+    gain = gain_row(g_ref, 0)
 
     def emit(low, total):
         hidden = t_ref[pl.ds(low, half)].astype(F32)
         scale = row_scale(hidden)
-        back, gain_sum = norm_back(total, hidden * scale, scale, g_ref[...])
+        back, gain_sum = norm_back(total, hidden * scale, scale, gain)
         gg_ref[...] += gain_sum
-        o_ref[pl.ds(low, half)] = m_ref[pl.ds(low, half)] + back
+        o_ref[pl.ds(low, half)] = back
 
     scatter_square(copies, 0, p_ref, buf, stage, emit)
     copies.finish()
 
 
-def in_scatter(partial, tokens, mid_grad, gain_row, special):
+def in_scatter(partial, tokens, gains, special):
     rows = tokens.shape[0]
     if not special:
         total = lax.psum_scatter(partial, "narrow", scatter_dimension=0, tiled=True).astype(F32)
         hidden = tokens.astype(F32)
         scale = row_scale(hidden)
-        back, gain_sum = norm_back(total, hidden * scale, scale, gain_row)
-        return mid_grad + back, gain_sum
+        back, gain_sum = norm_back(total, hidden * scale, scale, gains[: D // HD].reshape(1, D))
+        return back, gain_sum
     return pl.pallas_call(
         in_scatter_kernel,
         name="in_scatter",
@@ -528,12 +632,12 @@
             jax.ShapeDtypeStruct((rows, D), F32),
             jax.ShapeDtypeStruct((1, D), F32),
         ),
-        in_specs=[VM] * 4,
+        in_specs=[VM] * 3,
         out_specs=(VM,) * 2,
         scratch_shapes=scatter_space(rows) + dma_sems(6),
         cost_estimate=cost(1, 1),
         compiler_params=remote_params(4),
-    )(partial, tokens, mid_grad, gain_row)
+    )(partial, tokens, gains)
 
 
 def line(count):
@@ -554,13 +658,13 @@
 
 
 def return_grads_kernel(
-    count, x_ref, h_ref, act_hbm, d_hbm, o_ref, b_ref,
+    count, x_ref, act_hbm, d_hbm, o_ref, b_ref,
     from_mate, from_above, stage, p_ref, buf, out_stage, act, weight,
     send, recv, mate_send, mate_recv, n_send, n_recv, load_sem,
 ):
     w, z, c, chips, mate, above, below = line(count)
     me, xn, yn, dg = square()
-    rows = h_ref.shape[0]
+    rows = b_ref.shape[0]
     half = rows // 2
     loads = [
         pltpu.make_async_copy(src, dst, load_sem.at[n])
@@ -630,7 +734,7 @@
                 down(s).start()
 
     def emit(low, total):
-        b_ref[pl.ds(low, half)] = h_ref[pl.ds(low, half)] + total
+        b_ref[pl.ds(low, half)] = total
 
     def fill(owner):
         at = pl.ds(pl.multiple_of(owner * rows, rows), rows)
@@ -672,7 +776,7 @@
             down(s).wait_send()
 
 
-def return_grads_out(grads, act, down_weight, hidden_mid, count):
+def return_grads_out(grads, act, down_weight, own_rows, count):
     _, rows, width = grads.shape
     chips = count // 2
     return pl.pallas_call(
@@ -680,9 +784,9 @@
         name="return_grads",
         out_shape=(
             jax.ShapeDtypeStruct((rows, width), F32),
-            jax.ShapeDtypeStruct(hidden_mid.shape, F32),
-        ),
-        in_specs=[VM] * 2 + [pl.BlockSpec(memory_space=pl.ANY)] * 2,
+            jax.ShapeDtypeStruct((own_rows, D), F32),
+        ),
+        in_specs=[VM] + [pl.BlockSpec(memory_space=pl.ANY)] * 2,
         out_specs=(VM, VM),
         scratch_shapes=[
             pltpu.VMEM((chips, rows, width), BF16),
@@ -690,7 +794,7 @@
             pltpu.VMEM((chips, rows, width), BF16),
             pltpu.VMEM((act.shape[0], D), BF16),
         ]
-        + scatter_space(hidden_mid.shape[0])
+        + scatter_space(own_rows)
         + [pltpu.VMEM(act.shape, BF16), pltpu.VMEM(down_weight.shape, BF16)]
         + dma_sems(chips)
         + dma_sems(chips)
@@ -698,7 +802,7 @@
         + [pltpu.SemaphoreType.DMA((2,))],
         cost_estimate=cost(1, 1),
         compiler_params=remote_params(6),
-    )(grads, hidden_mid, act, down_weight)
+    )(grads, act, down_weight)
 
 
 def return_grads(grads, count):
@@ -942,35 +1046,35 @@
         )
     dq_ref[...] = jnp.zeros_like(dq_ref)
 
-    def block(j, masked):
-        for kv in range(heads // group):
-            key = kv_ref[j, :, kv * HD : (kv + 1) * HD]
-            value = kv_ref[j, :, kv_width + kv * HD : kv_width + (kv + 1) * HD]
+    @pl.loop(0, w + 1)
+    def _(j):
+        seen = jnp.where(j == w, 0, rows)
+
+        @pl.loop(0, heads // group)
+        def _(kv):
+            key_at_lane = pl.ds(pl.multiple_of(kv * HD, HD), HD)
+            value_at_lane = pl.ds(pl.multiple_of(kv_width + kv * HD, HD), HD)
+            key, value = kv_ref[j, :, key_at_lane], kv_ref[j, :, value_at_lane]
             key_sum = jnp.zeros((rows, HD), F32)
             value_sum = jnp.zeros((rows, HD), F32)
-            for h in range(kv * group, (kv + 1) * group):
-                part = slice(h * HD, (h + 1) * HD)
+            for n in range(group):
+                h = kv * group + n
+                part = pl.ds(pl.multiple_of(h * HD, HD), HD)
                 query, out_grad = q_ref[:, part], do_ref[:, part]
                 probs = jnp.exp2(
-                    dot_nt(key, query) * (FACTOR * LOG2E) - lse_ref[h : h + 1, :]
+                    dot_nt(key, query) * (FACTOR * LOG2E) - lse_ref[pl.ds(h, 1), :]
                 )
-                if masked:
-                    key_at = lax.broadcasted_iota(jnp.int32, (rows, rows), 0)
-                    at = lax.broadcasted_iota(jnp.int32, (rows, rows), 1)
-                    probs = jnp.where(key_at <= at, probs, 0.0)
+                key_at = lax.broadcasted_iota(jnp.int32, (rows, rows), 0)
+                at = lax.broadcasted_iota(jnp.int32, (rows, rows), 1)
+                probs = jnp.where(key_at - at <= seen, probs, 0.0)
                 value_sum += dot(probs.astype(BF16), out_grad)
                 prob_grad = dot_nt(value, out_grad)
-                score_grad = (probs * (prob_grad - delta[h : h + 1, :])).astype(BF16)
+                score_grad = (probs * (prob_grad - delta[pl.ds(h, 1), :])).astype(BF16)
                 key_sum += dot(score_grad, query)
                 dq_ref[:, part] += dot_tn(score_grad, key)
-            dkv_ref[j, :, kv * HD : (kv + 1) * HD] = (key_sum * FACTOR).astype(BF16)
-            dkv_ref[j, :, kv_width + kv * HD : kv_width + (kv + 1) * HD] = value_sum.astype(BF16)
-
-    @pl.loop(0, w)
-    def _(j):
-        block(j, False)
-
-    block(w, True)
+            dkv_ref[j, :, key_at_lane] = (key_sum * FACTOR).astype(BF16)
+            dkv_ref[j, :, value_at_lane] = value_sum.astype(BF16)
+
     dq_ref[...] = dq_ref[...] * FACTOR
 
 
@@ -992,7 +1096,7 @@
     )(w_index, query, kv_all, out_grad, out, lse)
 
 
-def unspin_kernel(width, e_ref, raw_ref, g_ref, cos_ref, sin_ref, o_ref, gg_ref):
+def unspin_kernel(width, row, e_ref, raw_ref, g_ref, cos_ref, sin_ref, o_ref, gg_ref):
     gain_sum = jnp.zeros((1, HD), F32)
     for h in range(raw_ref.shape[1] // HD):
         part = slice(h * HD, (h + 1) * HD)
@@ -1000,7 +1104,7 @@
         turned = grad * cos_ref[...] - pltpu.roll(grad, HD // 2, axis=1) * sin_ref[...]
         raw = raw_ref[:, part]
         scale = row_scale(raw)
-        back, total = norm_back(turned, raw * scale, scale, g_ref[...])
+        back, total = norm_back(turned, raw * scale, scale, g_ref[row : row + 1, :])
         o_ref[:, part] = back.astype(BF16)
         gain_sum += total
     if width > raw_ref.shape[1]:
@@ -1008,10 +1112,10 @@
     gg_ref[...] = gain_sum
 
 
-def unspin(grad, raw, gain_row, cosine, sine):
+def unspin(grad, raw, gains, row, cosine, sine):
     rows, width = grad.shape
     return pl.pallas_call(
-        functools.partial(unspin_kernel, width),
+        functools.partial(unspin_kernel, width, row),
         name="unspin",
         out_shape=(
             jax.ShapeDtypeStruct((rows, width), BF16),
@@ -1021,12 +1125,12 @@
         out_specs=(VM, VM),
         compiler_params=params(),
         cost_estimate=cost(20 * grad.size, 10 * grad.size),
-    )(grad, raw, gain_row, cosine, sine)
+    )(grad, raw, gains, cosine, sine)
 
 
 def front_kernel(
     count, heads, group,
-    t_ref, c_ref, g_ref, wq_hbm, wkv_hbm, qg_ref, kg_ref, cos_ref, sin_ref,
+    t_ref, c_ref, g_ref, wq_hbm, wkv_hbm, cos_ref, sin_ref,
     dy_hbm, x_hbm, q_hbm, qraw_hbm, kraw_hbm, kv_hbm, o_ref, low_ref, lse_ref,
     own, x, weight, q, qraw, kraw, kv, acc,
     send, recv, z_send, z_recv, m_send, m_recv, c_send, c_recv, load_sem, store_sem, kv_sem,
@@ -1037,7 +1141,6 @@
     half = rows // 2
     all_rows = 4 * rows
     q_width, kv_width = wq_hbm.shape[1], wkv_hbm.shape[2]
-    owners = (me, xn, yn, dg)
     loads = [
         pltpu.make_async_copy(wq_hbm, weight.at[:, pl.ds(0, q_width)], load_sem.at[0]),
         pltpu.make_async_copy(wkv_hbm.at[0], weight.at[:, pl.ds(q_width, kv_width)], load_sem.at[1]),
@@ -1045,12 +1148,12 @@
             wkv_hbm.at[1], weight.at[:, pl.ds(q_width + kv_width, kv_width)], load_sem.at[2]
         ),
     ]
-    for load in loads:
+    for load in loads[::-1]:
         load.start()
 
     has_above, has_below = z < chips - 1, z > 0
     barrier = pltpu.get_barrier_semaphore()
-    for peer in (xn, yn, dg):
+    for peer in (xn, yn):
         pl.semaphore_signal(barrier, inc=1, device_id={"narrow": peer}, device_id_type=MESH)
 
     @pl.when(has_above)
@@ -1063,146 +1166,201 @@
 
     pl.semaphore_signal(barrier, inc=1, device_id={"wide": mate}, device_id_type=MESH)
     hidden = t_ref[...].astype(F32)
-    own[...] = (hidden * row_scale(hidden) * g_ref[...]).astype(BF16)
-    pl.semaphore_wait(barrier, 4 + has_above.astype(jnp.int32) + has_below.astype(jnp.int32))
-
-    copies = Copies(send, recv)
-
-    def part(owner, low):
-        return x.at[pl.ds(pl.multiple_of(owner * rows + low, half), half)]
-
-    upper, lower = own.at[pl.ds(0, half)], own.at[pl.ds(half, half)]
-    xa = copies.go(upper, part(me, 0), 0, xn)
-    yb = copies.go(lower, part(me, half), 1, yn)
-    xb = copies.go(lower, part(me, half), 2, xn)
-    ya = copies.go(upper, part(me, 0), 3, yn)
-
-    def unit_rows(unit):
-        return pl.ds(pl.multiple_of(owners[unit] * rows, rows), rows)
-
-    def unit(block, k):
-        return kv.at[block, unit_rows(k)]
-
-    def to_above(s, k):
+    own[...] = (hidden * row_scale(hidden) * gain_row(g_ref, 0)).astype(BF16)
+    pl.semaphore_wait(barrier, 3 + has_above.astype(jnp.int32) + has_below.astype(jnp.int32))
+
+    def half_of(ref, owner, low):
+        return ref.at[pl.ds(pl.multiple_of(owner * rows + low, half), half)]
+
+    def spread(copies, src, dst):
+        upper, lower = src.at[pl.ds(0, half)], src.at[pl.ds(half, half)]
+        return (
+            copies.go(upper, half_of(dst, me, 0), 0, xn),
+            copies.go(lower, half_of(dst, me, half), 1, yn),
+            copies.go(lower, half_of(dst, me, half), 2, xn),
+            copies.go(upper, half_of(dst, me, 0), 3, yn),
+        )
+
+    def lazy(copies, slot, owner, low, dst, peer):
+        return pltpu.make_async_remote_copy(
+            src_ref=half_of(dst, owner, low),
+            dst_ref=half_of(dst, owner, low),
+            send_sem=copies.send.at[slot],
+            recv_sem=copies.recv.at[slot],
+            device_id={"narrow": peer},
+            device_id_type=MESH,
+        )
+
+    copies, away = Copies(send, recv), Copies(c_send, c_recv)
+    xa, yb, xb, ya = spread(copies, own, x)
+    yf, xf = lazy(copies, 4, xn, 0, x, yn), lazy(copies, 5, yn, half, x, xn)
+    c_yf, c_xf = lazy(away, 4, xn, 0, dy_hbm, yn), lazy(away, 5, yn, half, dy_hbm, xn)
+    dy_part = dy_hbm.at[pl.ds(pl.multiple_of(me * rows, rows), rows)]
+    c_own = pltpu.make_async_copy(c_ref, dy_part, store_sem.at[4])
+
+    def piece(k, j):
+        owner = jnp.where(k == 0, me, jnp.where(k == 3, dg, xn if j == 0 else yn))
+        low = jnp.where((k == 2) == (j == 0), half, 0)
+        return pl.ds(pl.multiple_of(owner * rows + low, half), half)
+
+    def unit(block, k, j):
+        return kv.at[block, piece(k, j)]
+
+    def to_above(s, k, j):
         block = jnp.maximum(w - 2 * s, 0)
-        return wide_copy(unit(block, k), unit(block, k), z_send, z_recv, 4 * s + k, above)
-
-    def from_below(s, k):
+        return wide_copy(
+            unit(block, k, j), unit(block, k, j), z_send, z_recv, 8 * s + 2 * k + j, above
+        )
+
+    def from_below(s, k, j):
         block = jnp.maximum(w - 2 * s, 0)
-        return wide_copy(unit(block, k), unit(block, k), z_send, z_recv, 4 * (s - 1) + k, above)
-
-    def to_mate(s, k):
+        return wide_copy(
+            unit(block, k, j), unit(block, k, j), z_send, z_recv, 8 * (s - 1) + 2 * k + j, above
+        )
+
+    def to_mate(s, k, j):
         block = jnp.maximum(w - 2 * s, 0)
-        return wide_copy(unit(block, k), unit(block, k), m_send, m_recv, 4 * s + k, mate)
+        return wide_copy(
+            unit(block, k, j), unit(block, k, j), m_send, m_recv, 8 * s + 2 * k + j, mate
+        )
 
     def project(k):
-        at = unit_rows(k)
-        out = dot(x[at, :], weight[...])
-        cosine, sine = cos_ref[at, :], sin_ref[at, :]
-        qraw[at, :] = out[:, :q_width]
-        kraw[at, :] = out[:, q_width : q_width + kv_width]
+        rows_in = jnp.concatenate([x[piece(k, 0), :], x[piece(k, 1), :]], axis=0)
+        out = dot(rows_in, weight[:, q_width:])
+        cosine = jnp.concatenate([cos_ref[piece(k, 0), :], cos_ref[piece(k, 1), :]], axis=0)
+        sine = jnp.concatenate([sin_ref[piece(k, 0), :], sin_ref[piece(k, 1), :]], axis=0)
+        base = 2 * (D // HD)
+        parts = [slice(0, half), slice(half, rows)]
+        for h in range(heads // group):
+            lanes = slice(h * HD, (h + 1) * HD)
+            key = spin(out[:, lanes], g_ref[base + 1 : base + 2, :], cosine, sine).astype(BF16)
+            for j in range(2):
+                kv[w, piece(k, j), h * HD : (h + 1) * HD] = key[parts[j]]
+        for j in range(2):
+            kv[w, piece(k, j), kv_width:] = out[parts[j], kv_width:].astype(BF16)
+
+            @pl.when(has_above)
+            def _():
+                to_above(0, k, j).start()
+
+            @pl.when(c == 0)
+            def _():
+                to_mate(0, k, j).start()
+
+        for j in range(2):
+            kraw[piece(k, j), :] = out[parts[j], :kv_width]
+        pl.when(k == 0)(loads[0].wait)
+        out = dot(rows_in, weight[:, :q_width])
         for h in range(heads):
             lanes = slice(h * HD, (h + 1) * HD)
-            q[at, lanes] = spin(out[:, lanes], qg_ref[...], cosine, sine).astype(BF16)
-        for h in range(heads // group):
-            lanes = slice(q_width + h * HD, q_width + (h + 1) * HD)
-            kv[w, at, h * HD : (h + 1) * HD] = spin(
-                out[:, lanes], kg_ref[...], cosine, sine
-            ).astype(BF16)
-        kv[w, at, kv_width:] = out[:, q_width + kv_width :].astype(BF16)
-
-        @pl.when(has_above)
-        def _():
-            to_above(0, k).start()
-
-        @pl.when(c == 0)
-        def _():
-            to_mate(0, k).start()
+            query = spin(out[:, lanes], g_ref[base : base + 1, :], cosine, sine).astype(BF16)
+            for j in range(2):
+                q[piece(k, j), lanes] = query[parts[j]]
+        for j in range(2):
+            qraw[piece(k, j), :] = out[parts[j], :]
 
     def receive(s, k):
         @pl.when(z >= s)
         def _():
-            from_below(s, k).wait_recv()
-            if s < chips - 1:
-
-                @pl.when(has_above)
-                def _():
-                    to_above(s, k).start()
-
-            to_mate(s, k).start()
-
-    x[unit_rows(0), :] = own[...]
-    for load in loads:
-        load.wait()
-    project(0)
-    xa.wait_recv()
-    yf = copies.go(part(xn, 0), part(xn, 0), 4, yn)
-    yb.wait_recv()
-    xf = copies.go(part(yn, half), part(yn, half), 5, xn)
-    receive(1, 0)
-    xb.wait_recv()
-    project(1)
-    ya.wait_recv()
-    project(2)
-    receive(2, 0)
-    receive(1, 1)
-    receive(1, 2)
-    receive(3, 0)
-    yf.wait_recv()
-    xf.wait_recv()
-    project(3)
-    away = Copies(c_send, c_recv)
-    dy_part = dy_hbm.at[unit_rows(0)]
-    for slot, peer in enumerate((dg, xn, yn)):
-        away.go(c_ref, dy_part, slot, peer)
+            for j in range(2):
+                from_below(s, k, j).wait_recv()
+                if s < chips - 1:
+
+                    @pl.when(has_above)
+                    def _():
+                        to_above(s, k, j).start()
+
+                to_mate(s, k, j).start()
+
+    x[pl.ds(pl.multiple_of(me * rows, rows), rows), :] = own[...]
+    loads[1].wait()
+    loads[2].wait()
+
+    @pl.loop(0, 4)
+    def _(k):
+        @pl.when(k == 1)
+        def _():
+            xa.wait_recv()
+            yf.start()
+            yb.wait_recv()
+            xf.start()
+
+        @pl.when(k == 2)
+        def _():
+            receive(1, 0)
+            xb.wait_recv()
+            ya.wait_recv()
+
+        @pl.when(k == 3)
+        def _():
+            receive(2, 0)
+            receive(1, 1)
+            receive(3, 0)
+            yf.wait_recv()
+            xf.wait_recv()
+
+        project(k)
+
+    c_first = spread(away, c_ref, dy_hbm)
     stores = [
         pltpu.make_async_copy(src, dst, store_sem.at[n])
-        for n, (src, dst) in enumerate(
-            ((x, x_hbm), (q, q_hbm), (qraw, qraw_hbm), (kraw, kraw_hbm), (c_ref, dy_part))
-        )
-    ]
+        for n, (src, dst) in enumerate(((x, x_hbm), (q, q_hbm), (qraw, qraw_hbm), (kraw, kraw_hbm)))
+    ] + [c_own]
     for store in stores:
         store.start()
+    receive(2, 1)
+    receive(1, 2)
     acc[...] = jnp.zeros_like(acc)
     ones = jnp.ones((all_rows, HD), BF16)
 
     def keep(j):
         return pltpu.make_async_copy(kv.at[j], kv_hbm.at[j], kv_sem.at[j])
 
-    def block(j, masked):
+    def c_relay():
+        c_first[0].wait_recv()
+        c_yf.start()
+        c_first[1].wait_recv()
+        c_xf.start()
+
+    @pl.loop(0, 2 * z + 1 + c)
+    def _(n):
+        i = n - c
+        for s, units in ((1, ((3, 1), (2, 2), (1, 3))), (2, ((3, 2), (2, 3))), (3, ((3, 3),))):
+
+            @pl.when(i == 2 * s - 1)
+            def _():
+                for pair in units:
+                    receive(*pair)
+
+                if s == 2:
+                    c_relay()
+
+        for s in range(chips):
+
+            @pl.when((i == 2 * s) & (n > 0))
+            def _():
+                for k in range(4):
+                    for j in range(2):
+                        to_mate(s, k, j).wait_recv()
+
+        odd = i % 2
+        step = (i + 1) // 2
+        j = jnp.where(n == 0, w, 2 * (z - step) + c + (1 - odd) * (1 - 2 * c))
+        seen = jnp.where(n == 0, 0, all_rows)
         for h in range(heads):
             head = h // group
             key = kv[j, :, head * HD : (head + 1) * HD]
             value = kv[j, :, kv_width + head * HD : kv_width + (head + 1) * HD]
             terms = jnp.exp2(dot_nt(q[:, h * HD : (h + 1) * HD], key) * (FACTOR * LOG2E))
-            if masked:
-                at = lax.broadcasted_iota(jnp.int32, (all_rows, all_rows), 0)
-                key_at = lax.broadcasted_iota(jnp.int32, (all_rows, all_rows), 1)
-                terms = jnp.where(key_at <= at, terms, 0.0)
+            at = lax.broadcasted_iota(jnp.int32, (all_rows, all_rows), 0)
+            key_at = lax.broadcasted_iota(jnp.int32, (all_rows, all_rows), 1)
+            terms = jnp.where(key_at - at <= seen, terms, 0.0)
             acc[h] += dot(terms.astype(BF16), jnp.concatenate([value, ones], axis=1))
         keep(j).start()
 
-    block(w, True)
-
-    @pl.loop(1 - c, 2 * z + 1)
-    def _(i):
-        for s, units in ((1, ((2, 1), (2, 2), (1, 3))), (2, ((3, 1), (3, 2), (2, 3))), (3, ((3, 3),))):
-
-            @pl.when(i == 2 * s - 1)
-            def _():
-                for pair in units:
-                    receive(*pair)
-
-        for s in range(chips):
-
-            @pl.when(i == 2 * s)
-            def _():
-                for k in range(4):
-                    to_mate(s, k).wait_recv()
-
-        odd = i % 2
-        step = (i + 1) // 2
-        block(2 * (z - step) + c + (1 - odd) * (1 - 2 * c), False)
+    @pl.when(z < 2)
+    def _():
+        c_relay()
 
     for h in range(heads):
         total = acc[h, :, HD:]
@@ -1212,18 +1370,26 @@
         lse_ref[h : h + 1, :] = jnp.transpose(jnp.log2(total))[0:1]
 
     copies.finish()
-    for copy in away.sent:
-        copy.wait()
+    yf.wait_send()
+    xf.wait_send()
+    for copy in c_first[2:] + (c_yf, c_xf):
+        copy.wait_recv()
+    away.finish()
+    c_yf.wait_send()
+    c_xf.wait_send()
     for s in range(chips):
-        for k in range(4):
-
-            @pl.when((z >= s) & has_above)
-            def _():
-                to_above(s, k).wait_send()
-
-            @pl.when((z >= s) & ((c == 0) | (s > 0)))
-            def _():
-                to_mate(s, k).wait_send()
+
+        @pl.when((z >= s) & has_above)
+        def _():
+            for k in range(4):
+                for j in range(2):
+                    to_above(s, k, j).wait_send()
+
+        @pl.when((z >= s) & ((c == 0) | (s > 0)))
+        def _():
+            for k in range(4):
+                for j in range(2):
+                    to_mate(s, k, j).wait_send()
 
     for store in stores:
         store.wait()
@@ -1233,7 +1399,7 @@
         keep(j).wait()
 
 
-def front(tokens, cotangent, gain_row, query_weight, keyvalue_weight, query_gain, key_gain, cosine, sine, count):
+def front(tokens, cotangent, gains, query_weight, keyvalue_weight, cosine, sine, count):
     rows = tokens.shape[0]
     all_rows = 4 * rows
     q_width, kv_width = query_weight.shape[1], keyvalue_weight.shape[2]
@@ -1254,7 +1420,7 @@
             jax.ShapeDtypeStruct((all_rows, q_width), BF16),
             jax.ShapeDtypeStruct((heads, all_rows), F32),
         ),
-        in_specs=[VM, VM, VM, anywhere, anywhere, VM, VM, VM, VM],
+        in_specs=[VM, VM, VM, anywhere, anywhere, VM, VM],
         out_specs=(anywhere,) * 6 + (VM,) * 3,
         scratch_shapes=[
             pltpu.VMEM((rows, D), BF16),
@@ -1267,9 +1433,9 @@
             pltpu.VMEM((heads, all_rows, 2 * HD), F32),
         ]
         + dma_sems(6)
-        + dma_sems(4 * chips)
-        + dma_sems(4 * chips)
-        + dma_sems(3)
+        + dma_sems(8 * chips)
+        + dma_sems(8 * chips)
+        + dma_sems(6)
         + [
             pltpu.SemaphoreType.DMA((3,)),
             pltpu.SemaphoreType.DMA((5,)),
@@ -1277,7 +1443,7 @@
         ],
         cost_estimate=cost(1, 1),
         compiler_params=remote_params(8),
-    )(tokens, cotangent, gain_row, query_weight, keyvalue_weight, query_gain, key_gain, cosine, sine)
+    )(tokens, cotangent, gains, query_weight, keyvalue_weight, cosine, sine)
 
 
 def feed_kernel(x_ref, dy_ref, w_ref, d_ref, act_ref, grad_ref, down_ref):
@@ -1648,10 +1814,7 @@
     q_heads = query_weight.shape[1] // HD
     group = q_heads // kv_heads
     q_width, kv_width = q_heads * HD, kv_heads * HD
-    attn_gain = gain_copy[:D].reshape(1, D)
-    mlp_gain = gain_copy[D : 2 * D].reshape(1, D)
-    query_gain = gain_copy[2 * D : 2 * D + HD].reshape(1, HD)
-    key_gain = gain_copy[2 * D + HD :].reshape(1, HD)
+    gains = gain_copy.reshape(-1, HD)
 
     positions = (wide_index * stretch_rows + jnp.arange(stretch_rows, dtype=jnp.int32)).astype(F32)
     cosine, sine = rope_tables(positions)
@@ -1659,16 +1822,18 @@
         back_mlp, attn_input, query_low, query_raw, key_raw, kv_all, attn_out, attn_low, lse = front(
             tokens,
             cotangent,
-            attn_gain,
+            gains,
             query_weight,
             keyvalue_weight,
-            query_gain,
-            key_gain,
             cosine,
             sine,
             wide,
         )
     else:
+        attn_gain = gain_copy[:D].reshape(1, D)
+        mlp_gain = gain_copy[D : 2 * D].reshape(1, D)
+        query_gain = gain_copy[2 * D : 2 * D + HD].reshape(1, HD)
+        key_gain = gain_copy[2 * D + HD :].reshape(1, HD)
         hidden = tokens.astype(F32)
         normed = (hidden * row_scale(hidden) * attn_gain).astype(BF16)
         attn_input = lax.all_gather(normed, "narrow", axis=0, tiled=True)
@@ -1679,11 +1844,11 @@
         back_mlp = lax.all_gather(cotangent, "narrow", axis=0, tiled=True)
     if special:
         hidden_mid, mlp_input, act_grads, act, down_full = mid_pair(
-            attn_low, output_weight, tokens, mlp_gain, back_mlp, gateup_weight, down_weight, wide
+            attn_low, output_weight, tokens, gains, back_mlp, gateup_weight, down_weight, wide
         )
         down_total = line_scatter(down_full, 0, wide)[0]
         mid_grad, back_attn, mlp_gain_grad, gateup_full = mid_backward_pair(
-            hidden_mid, cotangent, mlp_gain, mlp_input, act_grads, gateup_weight, wide
+            hidden_mid, cotangent, gains, mlp_input, act_grads, gateup_weight, wide
         )
         gateup_total = line_scatter(gateup_full, 1, wide)
     else:
@@ -1701,15 +1866,16 @@
     query_sum, kv_sums = attend_back(
         w_scalar, query_low, kv_all, attn_grad, attn_out, lse, q_heads, group
     )
-    query_back, query_gain_grad = unspin(query_sum, query_raw, query_gain, cosine, sine)
+    query_back, query_gain_grad = unspin(query_sum, query_raw, gains, 2 * (D // HD), cosine, sine)
     if special:
-        kv_sum, block_output = return_grads_out(kv_sums, act, down_weight, hidden_mid, wide)
+        kv_sum, out_sum = return_grads_out(kv_sums, act, down_weight, tokens.shape[0], wide)
+        block_output = hidden_mid + out_sum
     else:
         kv_sum = return_grads(kv_sums, wide)
         block_output = hidden_mid + lax.psum_scatter(
             out_partial, "narrow", scatter_dimension=0, tiled=True
         ).astype(F32)
-    kv_back, key_gain_grad = unspin(kv_sum, key_raw, key_gain, cosine, sine)
+    kv_back, key_gain_grad = unspin(kv_sum, key_raw, gains, 2 * (D // HD) + 1, cosine, sine)
     back_args = (attn_input, query_back, kv_back, query_weight, keyvalue_weight, output_full)
     if special:
         normed_partial, project_full = project_back_pair(*back_args, wide)
@@ -1719,12 +1885,16 @@
         (project_full, gateup_total, down_total, normed_partial)
     )
     rest_total = line_scatter(project_full, 0, wide) if special else wide_scatter(project_full, 0)
-    input_grad, attn_gain_grad = in_scatter(normed_partial, tokens, mid_grad, attn_gain, special)
+    in_norm_grad, attn_gain_grad = in_scatter(normed_partial, tokens, gains, special)
+    input_grad = mid_grad + in_norm_grad
     gain_partial = jnp.concatenate(
         [attn_gain_grad, mlp_gain_grad, query_gain_grad, key_gain_grad], axis=1
     ).reshape(-1)
     gain_total = gain_sums(gain_partial, wide, narrow, special)
 
+    rest_total, input_grad, block_output = lax.optimization_barrier(
+        (rest_total, input_grad, block_output)
+    )
     query_new, keyvalue_new, output_new = rest_adamw(
         rest_total,
         (query_master, query_moment, query_second, query_average),

time: 412 us -> 396 us (0.961); the launches traced: 405 us -> 396 us
  waiting for transfers between devices: 19.6 us -> 12 us
  local copies, waits for them, and re-layouts: 8.47 us -> 3.34 us
    pallas_call x1, Pallas kernels: 98 us -> 112 us  [return_grads_out(): pl.pallas_call(functools.partial(return_grads_kernel, count), name='retur...]
    reduce_scatter x3, waiting for transfers between devices: 19.6 us -> 12 us  [line_scatter(): lax.psum_scatter(partial, 'wide', scatter_dimension=axis, tiled=True, axi...]
    pallas_call x1, Pallas kernels: 19.8 us -> 13.3 us  [project_back_pair(): pl.pallas_call(project_back_pair_kernel, name='project_back_pair', grid=(...]
    pallas_call x1, Pallas kernels: 50.3 us -> 45.6 us  [front(): pl.pallas_call(functools.partial(front_kernel, count, heads, group), name...]
  transfers between devices with their start and end apart: 3 -> 3, of which waited for: 2 -> 2; matrix products, arithmetic and copies ran while one was open for 4% -> 5% of each run, Pallas kernels for 58% -> 61%
where the time goes in v5:
time: 396 us
  Pallas kernels  344 us (87%)
  other arithmetic  22.3 us (6%)
  between operations  14.1 us (4%)
  waiting for transfers between devices  12 us (3%)
    pallas_call x1, Pallas kernels, return_grads_out(): pl.pallas_call(functools.partial(return_grads_kernel, count), name='retur...  112 us
    pallas_call x1, Pallas kernels, mid_backward_pair(): pl.pallas_call(mid_backward_kernel, name='mid_backward_pair', out_shape=(...  58.2 us
    pallas_call x1, Pallas kernels, mid_pair(): pl.pallas_call(mid_kernel, name='mid_pair', out_shape=(jax.ShapeDtypeStru...  50.2 us
    pallas_call x1, Pallas kernels, front(): pl.pallas_call(functools.partial(front_kernel, count, heads, group), name...  45.6 us
    pallas_call x1, Pallas kernels, in_scatter(): pl.pallas_call(in_scatter_kernel, name='in_scatter', out_shape=(jax.Shape...  23.9 us
    add x3, other arithmetic, adamw(): average_new = EMA_KEEP * average + (1.0 - EMA_KEEP) * master_new  15.1 us
    pallas_call x1, Pallas kernels, project_back_pair(): pl.pallas_call(project_back_pair_kernel, name='project_back_pair', grid=(...  13.3 us
    pallas_call x1, Pallas kernels, gain_sums(): pl.pallas_call(functools.partial(gain_kernel, wide), name='gain_sums', ou...  13 us
  transfers between devices with their start and end apart: 3, of which 2 were waited for; matrix products, arithmetic and copies ran while one was open for 5% of the time, Pallas kernels for 61%

profile of v5, /device:TPU:0, one launch (start us, length us, event | category | flops | bytes accessed | tf_op | source)
XLA Modules:
  0.0 396.0 jit_solution(5834367486988585346)
XLA Ops:
  7.2 0.0 reduce-scatter.6.cloned.1.call-start
  7.3 1.6 fusion.2
  8.9 1.0 pad_maximum_fusion
  9.9 45.6 %front.1 = (bf16[512,2048]{1,0:T(8,128)(2,1)}, bf16[512,2048]{1,0:T(8,128)(2,1)}, bf16[512,512]{1,0:T(8,128)(2,1)}, f32[512,512]{1,0:T(8,128)}, f32[512,256]{1,0...) custom-call(bf16[128,2048]{1,0:T(8,128)(2,1)} %t_ref.5, ...), custom_call_target="tpu_custom_call" | custom-call | flops 1 | bytes 1 | tf_op jit(solution)/shard_map/front/pallas_call | solution.py:1409
  55.5 50.2 %mid_pair.1 = (f32[128,2048]{1,0:T(8,128)}, bf16[512,2048]{1,0:T(8,128)(2,1)}, bf16[2,512,1536]{2,1,0:T(8,128)(2,1)}, bf16[512,1536]{1,0:T(8,128)(2,1)}, bf16[4,1536,256]{2,1,0:T(8,128)(2,1)}) custom-call(bf16[512,512]{1,0:T(8,128)(2,1)} %get-tuple-element.89.a_ref.low_ref, bf16[512,2048]{1,0:T(8,128)(2,1)} %w_ref.3, bf16[128,2048]{1,0:T(8,128)(2,1)} %t_ref.5, ...), custom_call_target="tpu_custom_call" | custom-call | flops 1 | bytes 1 | tf_op jit(solution)/shard_map/mid_pair/pallas_call | solution.py:421
  105.7 0.0 reduce-scatter.6.cloned.1.call-update
  105.7 0.2 reduce-scatter.4.cloned.1.call-start
  106.0 58.2 %mid_backward_pair.1 = (f32[128,2048]{1,0:T(8,128)}, bf16[512,2048]{1,0:T(8,128)(2,1)}, f32[1,2048]{1,0:T(1,128)}, bf16[2,4,256,1536]{3,2,1,0:T(8,128)(2,1)}) custom-call(f32[128,2048]{1,0:T(8,128)} %get-tuple-element.91.h_ref, bf16[128,2048]{1,0:T(8,128)(2,1)} %c_ref.3, f32[34,128]{1,0:T(8,128)} %bitcast.14, bf16[512,2048]{1,0:T(8,128)(2,1)} %get-tuple-element.92.x_hbm, ...), custom_call_target="tpu_custom_call" | custom-call | flops 1 | bytes 1 | tf_op jit(solution)/shard_map/mid_backward_pair/pallas_call | solution.py:563
  164.1 0.0 reduce-scatter.4.cloned.1.call-update
  164.2 0.0 reduce-scatter.8.cloned.1.call-start
  164.2 5.8 %out_back.1 = (bf16[512,512]{1,0:T(8,128)(2,1)}, bf16[2048,512]{1,0:T(8,128)(2,1)}) custom-call(bf16[512,2048]{1,0:T(8,128)(2,1)} %get-tuple-element.94.dy_ref, bf16[512,2048]{1,0:T(8,128)(2,1)} %w_ref.3, bf16[512,512]{1,0:T(8,128)(2,1)} %get-tuple-element.89.a_ref.low_ref), custom_call_target="tpu_custom_call" | custom-call | flops 1 | bytes 1 | tf_op jit(solution)/shard_map/out_back/pallas_call | solution.py:1553
  170.0 9.3 %attend_back.1 = (f32[512,512]{1,0:T(8,128)}, bf16[8,512,512]{2,1,0:T(8,128)(2,1)}) custom-call(s32[1]{0:T(128)} %bitcast.1.w_ref, bf16[512,512]{1,0:T(8,128)(2,1)} %get-tuple-element.87.q_ref, bf16[8,512,512]{2,1,0:T(8,128)(2,1)} %get-tuple-element.88.kv_ref, bf16[512,512]{1,0:T(8,128)(2,1)} %get-tuple-element.95.do_ref, ...), custom_call_target="tpu_custom_call" | custom-call | flops 1 | bytes 1 | tf_op jit(solution)/shard_map/attend_back/pallas_call | solution.py:1084
  179.3 112.5 %return_grads.1 = (f32[512,512]{1,0:T(8,128)}, f32[128,2048]{1,0:T(8,128)}) custom-call(bf16[8,512,512]{2,1,0:T(8,128)(2,1)} %get-tuple-element.101.x_ref, bf16[512,1536]{1,0:T(8,128)(2,1)} %get-tuple-element.102.act_hbm, bf16[1536,2048]{1,0:T(8,128)(2,1)} %d_hbm.3), custom_call_target="tpu_custom_call" | custom-call | flops 1 | bytes 1 | tf_op jit(solution)/shard_map/return_grads/pallas_call | solution.py:782
  291.8 2.9 unspin.3
  294.7 3.6 unspin.2
  298.3 13.3 %project_back_pair.1 = (bf16[512,2048]{1,0:T(8,128)(2,1)}, bf16[4,256,1536]{2,1,0:T(8,128)(2,1)}) custom-call(bf16[512,2048]{1,0:T(8,128)(2,1)} %get-tuple-element.86.x_ref, bf16[512,512]{1,0:T(8,128)(2,1)} %get-tuple-element.100.q_ref, bf16[512,512]{1,0:T(8,128)(2,1)} %get-tuple-element.105.kv_ref, bf16[2048,512]{1,0:T(8,128)(2,1)} %wq_ref.1, ...), custom_call_target="tpu_custom_call" | custom-call | flops 1 | bytes 1 | tf_op jit(solution)/shard_map/project_back_pair/pallas_call | solution.py:1685
  311.6 0.0 reduce-scatter.6.cloned.1.call-done
  311.7 7.1 %reduce-scatter.4.cloned.1.call-done = bf16[2,256,1536]{2,1,0:T(8,128)(2,1)} async-done(((bf16[2,1024,1536]{2,1,0:T(8,128)(2,1)}), bf16[2,256,1536]{2,1,0:T(8,128)(2,1)}) %reduce-scatter.4.cloned.1.call-update) | async-done | bytes 1572880 | tf_op jit(solution)/shard_map/reduce_scatter | solution.py:1769
  318.8 0.0 reduce-scatter.8.cloned.1.call-update
  318.8 0.0 copy-start.10
  318.8 0.0 copy-start.16
  318.8 0.0 copy-start.17
  318.9 23.9 %in_scatter.1 = (f32[128,2048]{1,0:T(8,128)}, f32[1,2048]{1,0:T(1,128)}) custom-call(bf16[512,2048]{1,0:T(8,128)(2,1)} %get-tuple-element.113.p_ref, bf16[128,2048]{1,0:T(8,128)(2,1)} %t_ref.5, f32[34,128]{1,0:T(8,128)} %bitcast.17), custom_call_target="tpu_custom_call" | custom-call | flops 1 | bytes 1 | tf_op jit(solution)/shard_map/in_scatter/pallas_call | solution.py:628
  342.7 0.0 copy-done.10
  342.7 0.0 copy-done.16
  342.7 0.0 copy-done.17
  342.8 0.7 maximum_reduce_fusion
  343.5 0.1 reshape_reshape.3
  343.6 0.6 reshape.92.x_ref
  344.3 0.0 copy-done.8
  344.3 1.1 add.84
  345.4 0.0 copy-start.6
  345.4 0.0 copy-start.7
  345.4 13.0 %gain_sums.1 = f32[2,128]{1,0:T(2,128)} custom-call(f32[4,8,2,128]{3,2,1,0:T(2,128)} %reshape.92.x_ref), custom_call_target="tpu_custom_call" | custom-call | flops 1 | bytes 1 | tf_op jit(solution)/shard_map/gain_sums/pallas_call | solution.py:866
  358.4 2.6 add.83
  361.1 0.0 copy-done.12
  361.1 0.6 add_multiply_fusion.2
  361.7 0.0 copy-start.1
  361.7 0.0 copy-start.2
  361.7 0.0 copy-start.3
  361.7 0.0 copy-start.4
  361.8 6.3 %add_multiply_fusion.1 = (f32[1536,256]{1,0:T(8,128)}, f32[1536,256]{1,0:T(8,128)}, f32[1536,256]{1,0:T(8,128)}, f32[1536,256]{1,0:T(8,128)}, f32[1536,256]{1,0:T(8,128)}) fusion(f32[1536,256]{1,0:T(8,128)S(1)} %copy-done.6, f32[1536,256]{1,0:T(8,128)S(1)} %copy-done.7, f32[1536,256]{1,0:T(8,128)} %param.58, f32[1536,256]{1,0:T(8,128)} %param.59, ...), kind=kLoop, calls=%fused_computation.7 | loop fusion | flops 7077888 | bytes 14942208 | tf_op jit(solution)/shard_map/add | solution.py:72
  368.0 1.2 copy-done.3
  369.2 0.9 copy-done.4
  370.1 0.4 copy-done.5
  370.5 8.3 %add_multiply_fusion = (f32[2,256,1536]{2,1,0:T(8,128)}, f32[2,256,1536]{2,1,0:T(8,128)}, f32[2,256,1536]{2,1,0:T(8,128)}, f32[2,256,1536]{2,1,0:T(8,128)}, f32[2,256,1536]{2,1,0:T(8,128)}) fusion(f32[2,256,1536]{2,1,0:T(8,128)S(1)} %copy-done.1, f32[2,256,1536]{2,1,0:T(8,128)S(1)} %copy-done.2, f32[2,256,1536]{2,1,0:T(8,128)S(1)} %copy-done.3, ...), kind=kLoop, calls=%fused_computation.2 | loop fusion | flops 14155776 | bytes 29884416 | tf_op jit(solution)/shard_map/add | solution.py:72
  378.8 4.8 %reduce-scatter.8.cloned.1.call-done.total_ref = bf16[256,1536]{1,0:T(8,128)(2,1)} async-done(((bf16[1024,1536]{1,0:T(8,128)(2,1)}), bf16[256,1536]{1,0:T(8,128)(2,1)}) %reduce-scatter.8.cloned.1.call-update) | async-done | bytes 786448 | tf_op jit(solution)/shard_map/reduce_scatter | solution.py:1769
  383.6 5.8 %rest_adamw.1 = (f32[256,512]{1,0:T(8,128)}, f32[256,512]{1,0:T(8,128)}, f32[256,512]{1,0:T(8,128)}, f32[256,512]{1,0:T(8,128)}, f32[256,512]{1,0:T(8,128)}, /*i...) custom-call(bf16[256,1536]{1,0:T(8,128)(2,1)} %reduce-scatter.8.clon, ...), custom_call_target="tpu_custom_call" | custom-call | flops 1 | bytes 1 | tf_op jit(solution)/shard_map/rest_adamw/pallas_call | solution.py:1745
  (22 shorter events, 0.1 us)
Async XLA Ops:
  7.2 304.5 %reduce-scatter.6.cloned.1.call-start = ((), (), s32[]{:S(2)}) async-start(), calls=%async_computation.4 | async-start | bytes 3932160 | tf_op jit(solution)/shard_map/reduce_scatter | solution.py:1769
  105.7 213.1 %reduce-scatter.4.cloned.1.call-start = ((), (), s32[]{:S(2)}) async-start(), calls=%async_computation.3 | async-start | bytes 7864320 | tf_op jit(solution)/shard_map/reduce_scatter | solution.py:1769
  164.2 219.5 %reduce-scatter.8.cloned.1.call-start = ((), (), s32[]{:S(2)}) async-start(), calls=%async_computation.5 | async-start | bytes 3932160 | tf_op jit(solution)/shard_map/reduce_scatter | solution.py:1769
  318.8 23.9 %copy-start.10 = (f32[1,2048]{1,0:T(1,128)S(1)}, f32[1,2048]{1,0:T(1,128)}, u32[]{:S(2)}) copy-start(f32[1,2048]{1,0:T(1,128)} %get-tuple-element.137) | copy-start | bytes 24580
  318.8 23.9 %copy-start.16 = (f32[1,128]{1,0:T(1,128)S(1)}, f32[1,128]{1,0:T(1,128)}, u32[]{:S(2)}) copy-start(f32[1,128]{1,0:T(1,128)} %get-tuple-element.139) | copy-start | bytes 1540
  318.8 23.9 %copy-start.17 = (f32[1,128]{1,0:T(1,128)S(1)}, f32[1,128]{1,0:T(1,128)}, u32[]{:S(2)}) copy-start(f32[1,128]{1,0:T(1,128)} %get-tuple-element.138) | copy-start | bytes 1540
  318.8 25.4 %copy-start = (f32[128,2048]{1,0:T(8,128)S(1)}, f32[128,2048]{1,0:T(8,128)}, u32[]{:S(2)}) copy-start(f32[128,2048]{1,0:T(8,128)} %get-tuple-element.91.h_ref) | copy-start | bytes 3145732
  318.8 25.4 %copy-start.8 = (f32[128,2048]{1,0:T(8,128)S(1)}, f32[128,2048]{1,0:T(8,128)}, u32[]{:S(2)}) copy-start(f32[128,2048]{1,0:T(8,128)} %get-tuple-element.115) | copy-start | bytes 3145732
  344.3 17.4 %copy-start.9 = (bf16[1,1536,256]{2,1,0:T(8,128)(2,1)S(1)}, bf16[1,1536,256]{2,1,0:T(8,128)(2,1)}, u32[]{:S(2)}) copy-start(bf16[1,1536,256]{2,1,0:T(8,128)(2,1)} %reduce-scatter.6.cloned.1.call-done) | copy-start | bytes 2359300
  345.4 15.7 %copy-start.12 = (f32[136]{0:T(256)S(1)}, f32[136]{0:T(256)}, u32[]{:S(2)}) copy-start(f32[136]{0:T(256)} %param.64) | copy-start | bytes 1636
  345.4 15.7 %copy-start.13 = (f32[136]{0:T(256)S(1)}, f32[136]{0:T(256)}, u32[]{:S(2)}) copy-start(f32[136]{0:T(256)} %param.61) | copy-start | bytes 1636
  345.4 15.7 %copy-start.14 = (f32[136]{0:T(256)S(1)}, f32[136]{0:T(256)}, u32[]{:S(2)}) copy-start(f32[136]{0:T(256)} %param.62) | copy-start | bytes 1636
  345.4 15.7 %copy-start.15 = (f32[136]{0:T(256)S(1)}, f32[136]{0:T(256)}, u32[]{:S(2)}) copy-start(f32[136]{0:T(256)} %param.63) | copy-start | bytes 1636
  345.4 16.3 %copy-start.6 = (f32[1536,256]{1,0:T(8,128)S(1)}, f32[1536,256]{1,0:T(8,128)}, u32[]{:S(2)}) copy-start(f32[1536,256]{1,0:T(8,128)} %param.60) | copy-start | bytes 4718596
  345.4 16.3 %copy-start.7 = (f32[1536,256]{1,0:T(8,128)S(1)}, f32[1536,256]{1,0:T(8,128)}, u32[]{:S(2)}) copy-start(f32[1536,256]{1,0:T(8,128)} %param.57) | copy-start | bytes 4718596
  358.4 2.7 copy-start.11
  361.7 6.3 %copy-start.1 = (f32[2,256,1536]{2,1,0:T(8,128)S(1)}, f32[2,256,1536]{2,1,0:T(8,128)}, u32[]{:S(2)}) copy-start(f32[2,256,1536]{2,1,0:T(8,128)} %param.56) | copy-start | bytes 9437188
  361.7 6.3 %copy-start.2 = (f32[2,256,1536]{2,1,0:T(8,128)S(1)}, f32[2,256,1536]{2,1,0:T(8,128)}, u32[]{:S(2)}) copy-start(f32[2,256,1536]{2,1,0:T(8,128)} %param.53) | copy-start | bytes 9437188
  361.7 7.5 %copy-start.3 = (f32[2,256,1536]{2,1,0:T(8,128)S(1)}, f32[2,256,1536]{2,1,0:T(8,128)}, u32[]{:S(2)}) copy-start(f32[2,256,1536]{2,1,0:T(8,128)} %param.54) | copy-start | bytes 9437188
  361.7 8.4 %copy-start.4 = (f32[2,256,1536]{2,1,0:T(8,128)S(1)}, f32[2,256,1536]{2,1,0:T(8,128)}, u32[]{:S(2)}) copy-start(f32[2,256,1536]{2,1,0:T(8,128)} %param.55) | copy-start | bytes 9437188
  361.7 8.8 %copy-start.5 = (bf16[2,256,1536]{2,1,0:T(8,128)(2,1)S(1)}, bf16[2,256,1536]{2,1,0:T(8,128)(2,1)}, u32[]{:S(2)}) copy-start(bf16[2,256,1536]{2,1,0:T(8,128)(2,1)} %reduce-scatter.4.cloned.1.call-done) | copy-start | bytes 4718596
Sparse Core Ops, SparseCore 0:
  105.8 67.9 reduce-scatter.5
  176.1 142.5 reduce-scatter.3
  321.1 62.5 reduce-scatter.7

commit v6 on v5

--- a/solution.py
+++ b/solution.py
@@ -48,17 +48,25 @@
     return lax.dot_general(left, right, TN, preferred_element_type=F32)
 
 
-def rope_tables(positions):
-    half_width = HD // 2
-    inverse_freq = jnp.asarray(
-        THETA ** (-2.0 * np.arange(half_width, dtype=np.float64) / HD), dtype=F32
-    )
-    angles = positions[:, None] * inverse_freq[None, :]
-    cosine, sine = jnp.cos(angles), jnp.sin(angles)
-    return (
-        jnp.concatenate([cosine, cosine], axis=-1),
-        jnp.concatenate([-sine, sine], axis=-1),
-    )
+def rope_freq():
+    inverse_freq = THETA ** (-2.0 * np.arange(HD // 2, dtype=np.float64) / HD)
+    return jnp.asarray(np.tile(inverse_freq, (8, 2)), dtype=F32)
+
+
+def rope_table(positions):
+    angles = positions[:, None] * rope_freq()[:1]
+    first = jnp.arange(HD)[None, :] < HD // 2
+    return jnp.where(first, jnp.cos(angles), jnp.sin(angles))
+
+
+def cos_sin(table, turn):
+    first = lax.broadcasted_iota(jnp.int32, table.shape, 1) < HD // 2
+    other = turn(table)
+    return jnp.where(first, table, other), jnp.where(first, -other, table)
+
+
+def swap_lanes(table):
+    return pltpu.roll(table, HD // 2, axis=1)
 
 
 def adamw(gradient, master, moment, second, average, step_rate, decay_rate):
@@ -147,7 +155,7 @@
 
         @pl.loop(0, 4)
         def _(k):
-            fill(jnp.where(k == 0, dg, jnp.where(k == 1, xn, jnp.where(k == 2, yn, me))))
+            fill(jnp.where(k == 0, dg, jnp.where(k == 1, xn, jnp.where(k == 2, yn, me))), k)
             for n, ready in ((0, (c0, c1)), (1, (c2,)), (2, (c3,))):
 
                 @pl.when(k == n)
@@ -236,7 +244,7 @@
 
     @pl.loop(0, 4)
     def _(k):
-        fill(jnp.where(k == 0, dg, jnp.where(k == 1, xn, jnp.where(k == 2, yn, me))))
+        fill(jnp.where(k == 0, dg, jnp.where(k == 1, xn, jnp.where(k == 2, yn, me))), k)
         for n, ready in ((0, sums[0][:2]), (1, sums[0][2:3]), (2, sums[0][3:4])):
 
             @pl.when(k == n)
@@ -306,9 +314,9 @@
 
 
 def mid_kernel(
-    a_ref, w_ref, t_ref, g_ref, dy_hbm, gu_hbm, d_hbm,
+    t_ref, g_ref, a_hbm, w_hbm, dy_hbm, gu_hbm, d_hbm,
     h_ref, x_hbm, grad_hbm, act_hbm, down_hbm,
-    p_ref, buf, stage, own, x, weight, dy, down, act_grad, grad, act, mine, inbox,
+    a_ref, w_ref, p_ref, buf, stage, own, x, weight, dy, down, act_grad, grad, act, mine, theirs, inbox,
     send, recv, m_send, m_recv, load_sem, store_sem, down_sem,
 ):
     me, xn, yn, dg = square()
@@ -318,9 +326,18 @@
     tiles, tile, part = inbox.shape[0], inbox.shape[2], inbox.shape[3]
     loads = [
         pltpu.make_async_copy(src, dst, load_sem.at[n])
-        for n, (src, dst) in enumerate(((dy_hbm, dy), (d_hbm, down), (gu_hbm, weight)))
+        for n, (src, dst) in enumerate(((a_hbm, a_ref), (w_hbm, w_ref), (gu_hbm, weight)))
     ]
-    for load in loads:
+    for n, (src, dst) in enumerate(((dy_hbm, dy), (d_hbm, down))):
+        for k in range(D // part):
+            loads.append(
+                pltpu.make_async_copy(
+                    src.at[:, pl.ds(k * part, part)],
+                    dst.at[k % 2, :, pl.ds(k // 2 * part, part)],
+                    load_sem.at[3 + n * (D // part) + k],
+                )
+            )
+    for load in loads[:2] + loads[3:] + loads[2:3]:
         load.start()
     barrier = pltpu.get_barrier_semaphore()
     for peer in (xn, yn):
@@ -332,7 +349,10 @@
     def rows_of(owner):
         return pl.ds(pl.multiple_of(owner * rows, rows), rows)
 
-    def fill(owner):
+    loads[0].wait()
+    loads[1].wait()
+
+    def fill(owner, k):
         p_ref[rows_of(owner), :] = dot(a_ref[rows_of(owner), :], w_ref[...]).astype(BF16)
 
     gain = gain_row(g_ref, D // HD)
@@ -346,33 +366,42 @@
         @pl.loop(low, high)
         def _(t):
             cols = pl.ds(pl.multiple_of(t * tile, tile), tile)
-            act_grad[:, cols] = dot_nt(dy[...], down[cols, :])
+            act_grad[:, cols] = dot_nt(dy[0], down[0, cols, :]) + dot_nt(dy[1], down[1, cols, :])
 
     def early():
-        loads[0].wait()
-        loads[1].wait()
+        for load in loads[3:]:
+            load.wait()
         act_grads(0, tiles // 2)
 
     def middle():
         act_grads(tiles // 2, tiles)
         loads[2].wait()
 
-    def expand(owner):
+    def expand(owner, t):
         at = rows_of(owner)
-
+        cols = pl.ds(pl.multiple_of(t * tile, tile), tile)
+        gate = dot(x[at, :], weight[0, :, cols])
+        upper = dot(x[at, :], weight[1, :, cols])
+        sig = jax.nn.sigmoid(gate)
+        swish = gate * sig
+        back = act_grad[at, cols]
+        act[at, cols] = (swish * upper).astype(BF16)
+        grad[0, at, cols] = (back * upper * sig * (1.0 + gate * (1.0 - sig))).astype(BF16)
+        grad[1, at, cols] = (back * swish).astype(BF16)
+
+    def use(owner):
         @pl.loop(0, tiles)
         def _(t):
-            cols = pl.ds(pl.multiple_of(t * tile, tile), tile)
-            gate = dot(x[at, :], weight[0, :, cols])
-            upper = dot(x[at, :], weight[1, :, cols])
-            sig = jax.nn.sigmoid(gate)
-            swish = gate * sig
-            back = act_grad[at, cols]
-            act[at, cols] = (swish * upper).astype(BF16)
-            grad[0, at, cols] = (back * upper * sig * (1.0 + gate * (1.0 - sig))).astype(BF16)
-            grad[1, at, cols] = (back * swish).astype(BF16)
-
-    exchange_square(copies, p_ref, buf, stage, own, x, emit, fill, early, middle, expand)
+            expand(owner, t)
+
+    def trade(t):
+        return wide_copy(theirs.at[t], inbox.at[t], m_send, m_recv, t, mate)
+
+    def keep(t):
+        at = pl.ds(pl.multiple_of(t * tile, tile), tile)
+        return pltpu.make_async_copy(mine.at[t], down_hbm.at[:, at], down_sem.at[t])
+
+    exchange_square(copies, p_ref, buf, stage, own, x, emit, fill, early, middle, use)
     stores = [
         pltpu.make_async_copy(src, dst, store_sem.at[n])
         for n, (src, dst) in enumerate(((x, x_hbm), (grad, grad_hbm), (act, act_hbm)))
@@ -380,25 +409,23 @@
     for store in stores:
         store.start()
 
-    def trade(t):
-        return wide_copy(mine.at[t, 1 - c], inbox.at[t], m_send, m_recv, t, mate)
-
-    def keep(t):
-        at = pl.ds(pl.multiple_of(t * tile, tile), tile)
-        return pltpu.make_async_copy(mine.at[t, c], down_hbm.at[:, at], down_sem.at[t])
-
     @pl.loop(0, tiles)
     def _(t):
         cols = pl.ds(pl.multiple_of(t * tile, tile), tile)
-        full = dot_tn(act[:, cols], dy[...]).astype(BF16)
-        for k in range(D // part):
-            mine[t, k % 2, k // 2] = full[:, k * part : (k + 1) * part]
+        half_full = dot_tn(act[:, cols], dy[1 - c]).astype(BF16)
+        for k in range(D // part // 2):
+            theirs[t, k] = half_full[:, k * part : (k + 1) * part]
         trade(t).start()
 
     @pl.loop(0, tiles)
     def _(t):
         trade(t).wait_recv()
-        mine[t, c] = (mine[t, c].astype(F32) + inbox[t].astype(F32)).astype(BF16)
+        cols = pl.ds(pl.multiple_of(t * tile, tile), tile)
+        half_full = dot_tn(act[:, cols], dy[c])
+        for k in range(D // part // 2):
+            mine[t, k] = (half_full[:, k * part : (k + 1) * part] + inbox[t, k].astype(F32)).astype(
+                BF16
+            )
         keep(t).start()
 
     copies.finish()
@@ -428,32 +455,37 @@
             jax.ShapeDtypeStruct((4 * rows, width), BF16),
             jax.ShapeDtypeStruct((chips, width, part), BF16),
         ),
-        in_specs=[VM] * 4 + [anywhere] * 3,
+        in_specs=[VM] * 2 + [anywhere] * 5,
         out_specs=(VM,) + (anywhere,) * 4,
-        scratch_shapes=[pltpu.VMEM((4 * rows, D), BF16)]
+        scratch_shapes=[
+            pltpu.VMEM(attn_low.shape, BF16),
+            pltpu.VMEM(weight.shape, BF16),
+            pltpu.VMEM((4 * rows, D), BF16),
+        ]
         + exchange_space(rows)
         + [
             pltpu.VMEM((rows, D), BF16),
             pltpu.VMEM((4 * rows, D), BF16),
             pltpu.VMEM((2, D, width), BF16),
-            pltpu.VMEM((4 * rows, D), BF16),
-            pltpu.VMEM((width, D), BF16),
+            pltpu.VMEM((2, 4 * rows, D // 2), BF16),
+            pltpu.VMEM((2, width, D // 2), BF16),
             pltpu.VMEM((4 * rows, width), F32),
             pltpu.VMEM((2, 4 * rows, width), BF16),
             pltpu.VMEM((4 * rows, width), BF16),
-            pltpu.VMEM((tiles, 2, chips, tile, part), BF16),
+            pltpu.VMEM((tiles, chips, tile, part), BF16),
+            pltpu.VMEM((tiles, chips, tile, part), BF16),
             pltpu.VMEM((tiles, chips, tile, part), BF16),
         ]
         + dma_sems(24)
         + dma_sems(tiles)
         + [
-            pltpu.SemaphoreType.DMA((3,)),
+            pltpu.SemaphoreType.DMA((3 + 2 * count,)),
             pltpu.SemaphoreType.DMA((3,)),
             pltpu.SemaphoreType.DMA((tiles,)),
         ],
         cost_estimate=cost(1, 1),
         compiler_params=remote_params(2),
-    )(attn_low, weight, tokens, gains, dy, gateup_weight, down_weight)
+    )(tokens, gains, attn_low, weight, dy, gateup_weight, down_weight)
 
 
 def mid_forward(attn_low, weight, tokens, gain):
@@ -475,12 +507,20 @@
     c, mate = mate_of()
     half = h_ref.shape[0] // 2
     tiles, part, tile = inbox.shape[0], inbox.shape[3], inbox.shape[4]
+    def load_weight(t):
+        rows_at = pl.ds(pl.multiple_of(t * 512, 512), 512)
+        return pltpu.make_async_copy(
+            gu_hbm.at[:, rows_at], weight.at[:, rows_at], load_sem.at[2 + t]
+        )
+
     loads = [
         pltpu.make_async_copy(src, dst, load_sem.at[n])
-        for n, (src, dst) in enumerate(((grad_hbm, grad), (gu_hbm, weight), (x_hbm, x)))
+        for n, (src, dst) in enumerate(((grad_hbm, grad), (x_hbm, x)))
     ]
-    for load in loads:
-        load.start()
+    loads[0].start()
+    for t in range(D // 512):
+        load_weight(t).start()
+    loads[1].start()
     barrier = pltpu.get_barrier_semaphore()
     for peer in (xn, yn):
         pl.semaphore_signal(barrier, inc=1, device_id={"narrow": peer}, device_id_type=MESH)
@@ -518,13 +558,13 @@
 
     rows = 2 * half
     loads[0].wait()
-    loads[1].wait()
-
-    def fill(owner):
+
+    def fill(owner, k):
         at = pl.ds(pl.multiple_of(owner * rows, rows), rows)
 
         @pl.loop(0, D // 512)
         def _(t):
+            pl.when(k == 0)(load_weight(t).wait)
             cols = pl.ds(pl.multiple_of(t * 512, 512), 512)
             p_ref[at, cols] = (
                 dot_nt(grad[0, at, :], weight[0, cols, :])
@@ -532,7 +572,7 @@
             ).astype(BF16)
 
     def early():
-        loads[2].wait()
+        loads[1].wait()
         products(0, tiles // 2)
 
     def middle():
@@ -583,7 +623,7 @@
         ]
         + dma_sems(24)
         + dma_sems(tiles)
-        + [pltpu.SemaphoreType.DMA((3,)), pltpu.SemaphoreType.DMA((tiles,))],
+        + [pltpu.SemaphoreType.DMA((2 + D // 512,)), pltpu.SemaphoreType.DMA((tiles,))],
         cost_estimate=cost(1, 1),
         compiler_params=remote_params(3),
     )(hidden_mid, cotangent, gains, x, grads, gateup_weight)
@@ -736,7 +776,7 @@
     def emit(low, total):
         b_ref[pl.ds(low, half)] = total
 
-    def fill(owner):
+    def fill(owner, k):
         at = pl.ds(pl.multiple_of(owner * rows, rows), rows)
 
         @pl.loop(0, D // 512)
@@ -1096,23 +1136,26 @@
     )(w_index, query, kv_all, out_grad, out, lse)
 
 
-def unspin_kernel(width, row, e_ref, raw_ref, g_ref, cos_ref, sin_ref, o_ref, gg_ref):
-    gain_sum = jnp.zeros((1, HD), F32)
-    for h in range(raw_ref.shape[1] // HD):
-        part = slice(h * HD, (h + 1) * HD)
+def unspin_kernel(width, row, e_ref, raw_ref, g_ref, tab_ref, o_ref, gg_ref):
+    gg_ref[...] = jnp.zeros_like(gg_ref)
+
+    @pl.loop(0, raw_ref.shape[1] // HD)
+    def _(h):
+        part = pl.ds(pl.multiple_of(h * HD, HD), HD)
+        cosine, sine = cos_sin(tab_ref[...], swap_lanes)
         grad = e_ref[:, part]
-        turned = grad * cos_ref[...] - pltpu.roll(grad, HD // 2, axis=1) * sin_ref[...]
+        turned = grad * cosine - pltpu.roll(grad, HD // 2, axis=1) * sine
         raw = raw_ref[:, part]
         scale = row_scale(raw)
         back, total = norm_back(turned, raw * scale, scale, g_ref[row : row + 1, :])
         o_ref[:, part] = back.astype(BF16)
-        gain_sum += total
+        gg_ref[...] += total
+
     if width > raw_ref.shape[1]:
         o_ref[:, raw_ref.shape[1] :] = e_ref[:, raw_ref.shape[1] :].astype(BF16)
-    gg_ref[...] = gain_sum
-
-
-def unspin(grad, raw, gains, row, cosine, sine):
+
+
+def unspin(grad, raw, gains, row, table):
     rows, width = grad.shape
     return pl.pallas_call(
         functools.partial(unspin_kernel, width, row),
@@ -1121,17 +1164,17 @@
             jax.ShapeDtypeStruct((rows, width), BF16),
             jax.ShapeDtypeStruct((1, HD), F32),
         ),
-        in_specs=[VM] * 5,
+        in_specs=[VM] * 4,
         out_specs=(VM, VM),
         compiler_params=params(),
-        cost_estimate=cost(20 * grad.size, 10 * grad.size),
-    )(grad, raw, gains, cosine, sine)
+        cost_estimate=cost(1, 1),
+    )(grad, raw, gains, table)
 
 
 def front_kernel(
     count, heads, group,
-    t_ref, c_ref, g_ref, wq_hbm, wkv_hbm, cos_ref, sin_ref,
-    dy_hbm, x_hbm, q_hbm, qraw_hbm, kraw_hbm, kv_hbm, o_ref, low_ref, lse_ref,
+    t_ref, c_ref, g_ref, f_ref, wq_hbm, wkv_hbm,
+    dy_hbm, x_hbm, q_hbm, qraw_hbm, kraw_hbm, kv_hbm, o_ref, low_ref, lse_ref, tab_ref,
     own, x, weight, q, qraw, kraw, kv, acc,
     send, recv, z_send, z_recv, m_send, m_recv, c_send, c_recv, load_sem, store_sem, kv_sem,
 ):
@@ -1167,6 +1210,7 @@
     pl.semaphore_signal(barrier, inc=1, device_id={"wide": mate}, device_id_type=MESH)
     hidden = t_ref[...].astype(F32)
     own[...] = (hidden * row_scale(hidden) * gain_row(g_ref, 0)).astype(BF16)
+    fill_table(tab_ref, f_ref, w * all_rows)
     pl.semaphore_wait(barrier, 3 + has_above.astype(jnp.int32) + has_below.astype(jnp.int32))
 
     def half_of(ref, owner, low):
@@ -1227,8 +1271,9 @@
     def project(k):
         rows_in = jnp.concatenate([x[piece(k, 0), :], x[piece(k, 1), :]], axis=0)
         out = dot(rows_in, weight[:, q_width:])
-        cosine = jnp.concatenate([cos_ref[piece(k, 0), :], cos_ref[piece(k, 1), :]], axis=0)
-        sine = jnp.concatenate([sin_ref[piece(k, 0), :], sin_ref[piece(k, 1), :]], axis=0)
+        cosine, sine = cos_sin(
+            jnp.concatenate([tab_ref[piece(k, 0), :], tab_ref[piece(k, 1), :]], axis=0), swap_lanes
+        )
         base = 2 * (D // HD)
         parts = [slice(0, half), slice(half, rows)]
         for h in range(heads // group):
@@ -1399,7 +1444,22 @@
         keep(j).wait()
 
 
-def front(tokens, cotangent, gains, query_weight, keyvalue_weight, cosine, sine, count):
+def fill_table(tab_ref, f_ref, start):
+    rows, fine = tab_ref.shape[0], 32
+    freq = f_ref[0:1, :]
+    high = start + fine * lax.broadcasted_iota(jnp.int32, (rows // fine, HD), 0)
+    low = lax.broadcasted_iota(jnp.int32, (fine, HD), 0).astype(F32) * freq
+    high = high.astype(F32) * freq
+    cos_high, sin_high, cos_low, sin_low = jnp.cos(high), jnp.sin(high), jnp.cos(low), jnp.sin(low)
+    first = lax.broadcasted_iota(jnp.int32, (fine, HD), 1) < HD // 2
+    for n in range(rows // fine):
+        c, s = cos_high[n : n + 1], sin_high[n : n + 1]
+        tab_ref[n * fine : (n + 1) * fine, :] = jnp.where(
+            first, c * cos_low - s * sin_low, s * cos_low + c * sin_low
+        )
+
+
+def front(tokens, cotangent, gains, query_weight, keyvalue_weight, count):
     rows = tokens.shape[0]
     all_rows = 4 * rows
     q_width, kv_width = query_weight.shape[1], keyvalue_weight.shape[2]
@@ -1419,9 +1479,10 @@
             jax.ShapeDtypeStruct((all_rows, q_width), F32),
             jax.ShapeDtypeStruct((all_rows, q_width), BF16),
             jax.ShapeDtypeStruct((heads, all_rows), F32),
-        ),
-        in_specs=[VM, VM, VM, anywhere, anywhere, VM, VM],
-        out_specs=(anywhere,) * 6 + (VM,) * 3,
+            jax.ShapeDtypeStruct((all_rows, HD), F32),
+        ),
+        in_specs=[VM] * 4 + [anywhere] * 2,
+        out_specs=(anywhere,) * 6 + (VM,) * 4,
         scratch_shapes=[
             pltpu.VMEM((rows, D), BF16),
             pltpu.VMEM((all_rows, D), BF16),
@@ -1443,7 +1504,7 @@
         ],
         cost_estimate=cost(1, 1),
         compiler_params=remote_params(8),
-    )(tokens, cotangent, gains, query_weight, keyvalue_weight, cosine, sine)
+    )(tokens, cotangent, gains, rope_freq(), query_weight, keyvalue_weight)
 
 
 def feed_kernel(x_ref, dy_ref, w_ref, d_ref, act_ref, grad_ref, down_ref):
@@ -1816,20 +1877,25 @@
     q_width, kv_width = q_heads * HD, kv_heads * HD
     gains = gain_copy.reshape(-1, HD)
 
-    positions = (wide_index * stretch_rows + jnp.arange(stretch_rows, dtype=jnp.int32)).astype(F32)
-    cosine, sine = rope_tables(positions)
     if special:
-        back_mlp, attn_input, query_low, query_raw, key_raw, kv_all, attn_out, attn_low, lse = front(
-            tokens,
-            cotangent,
-            gains,
-            query_weight,
-            keyvalue_weight,
-            cosine,
-            sine,
-            wide,
+        (
+            back_mlp,
+            attn_input,
+            query_low,
+            query_raw,
+            key_raw,
+            kv_all,
+            attn_out,
+            attn_low,
+            lse,
+            table,
+        ) = front(tokens, cotangent, gains, query_weight, keyvalue_weight, wide)
+    else:
+        positions = wide_index * stretch_rows + jnp.arange(stretch_rows, dtype=jnp.int32)
+        table = rope_table(positions.astype(F32))
+        cosine, sine = cos_sin(
+            table, lambda a: jnp.concatenate([a[:, HD // 2 :], a[:, : HD // 2]], axis=1)
         )
-    else:
         attn_gain = gain_copy[:D].reshape(1, D)
         mlp_gain = gain_copy[D : 2 * D].reshape(1, D)
         query_gain = gain_copy[2 * D : 2 * D + HD].reshape(1, HD)
@@ -1866,7 +1932,7 @@
     query_sum, kv_sums = attend_back(
         w_scalar, query_low, kv_all, attn_grad, attn_out, lse, q_heads, group
     )
-    query_back, query_gain_grad = unspin(query_sum, query_raw, gains, 2 * (D // HD), cosine, sine)
+    query_back, query_gain_grad = unspin(query_sum, query_raw, gains, 2 * (D // HD), table)
     if special:
         kv_sum, out_sum = return_grads_out(kv_sums, act, down_weight, tokens.shape[0], wide)
         block_output = hidden_mid + out_sum
@@ -1875,7 +1941,7 @@
         block_output = hidden_mid + lax.psum_scatter(
             out_partial, "narrow", scatter_dimension=0, tiled=True
         ).astype(F32)
-    kv_back, key_gain_grad = unspin(kv_sum, key_raw, gains, 2 * (D // HD) + 1, cosine, sine)
+    kv_back, key_gain_grad = unspin(kv_sum, key_raw, gains, 2 * (D // HD) + 1, table)
     back_args = (attn_input, query_back, kv_back, query_weight, keyvalue_weight, output_full)
     if special:
         normed_partial, project_full = project_back_pair(*back_args, wide)

time: 396 us -> 394 us (level)
  no operation moved by 1% of the time
where the time goes in v6:
time: 394 us; the launch traced here: 393 us
  Pallas kernels  343 us (87%)
  other arithmetic  19.6 us (5%)
  between operations  14 us (4%)
  waiting for transfers between devices  12.7 us (3%)
    pallas_call x1, Pallas kernels, return_grads_out(): pl.pallas_call(functools.partial(return_grads_kernel, count), name='retur...  111 us
    pallas_call x1, Pallas kernels, mid_backward_pair(): pl.pallas_call(mid_backward_kernel, name='mid_backward_pair', out_shape=(...  55.4 us
    pallas_call x1, Pallas kernels, mid_pair(): pl.pallas_call(mid_kernel, name='mid_pair', out_shape=(jax.ShapeDtypeStru...  50.9 us
    pallas_call x1, Pallas kernels, front(): pl.pallas_call(functools.partial(front_kernel, count, heads, group), name...  45.5 us
    pallas_call x1, Pallas kernels, in_scatter(): pl.pallas_call(in_scatter_kernel, name='in_scatter', out_shape=(jax.Shape...  23.9 us
    pallas_call x1, Pallas kernels, project_back_pair(): pl.pallas_call(project_back_pair_kernel, name='project_back_pair', grid=(...  16 us
    add x3, other arithmetic, adamw(): average_new = EMA_KEEP * average + (1.0 - EMA_KEEP) * master_new  15.1 us
    pallas_call x1, Pallas kernels, gain_sums(): pl.pallas_call(functools.partial(gain_kernel, wide), name='gain_sums', ou...  13 us
  transfers between devices with their start and end apart: 3, of which 2 were waited for; matrix products, arithmetic and copies ran while one was open for 5% of the time, Pallas kernels for 61%

profile of v6, /device:TPU:0, one launch (start us, length us, event | category | flops | bytes accessed | tf_op | source)
XLA Modules:
  0.0 393.5 jit_solution(17945531593922688838)
XLA Ops:
  7.2 0.0 reduce-scatter.6.cloned.1.call-start
  7.2 45.5 %front.1 = (bf16[512,2048]{1,0:T(8,128)(2,1)}, bf16[512,2048]{1,0:T(8,128)(2,1)}, bf16[512,512]{1,0:T(8,128)(2,1)}, f32[512,512]{1,0:T(8,128)}, f32[512,256]{1,0...) custom-call(bf16[128,2048]{1,0:T(8,128)(2,1)} %t_ref.5, ...), custom_call_target="tpu_custom_call" | custom-call | flops 1 | bytes 1 | tf_op jit(solution)/shard_map/front/pallas_call | solution.py:1469
  52.8 50.9 %mid_pair.1 = (f32[128,2048]{1,0:T(8,128)}, bf16[512,2048]{1,0:T(8,128)(2,1)}, bf16[2,512,1536]{2,1,0:T(8,128)(2,1)}, bf16[512,1536]{1,0:T(8,128)(2,1)}, bf16[4,1536,256]{2,1,0:T(8,128)(2,1)}) custom-call(bf16[128,2048]{1,0:T(8,128)(2,1)} %t_ref.5, f32[34,128]{1,0:T(8,128)} %bitcast.13, bf16[512,512]{1,0:T(8,128)(2,1)} %get-tuple-element.90.a_hbm.low_ref, ...), custom_call_target="tpu_custom_call" | custom-call | flops 1 | bytes 1 | tf_op jit(solution)/shard_map/mid_pair/pallas_call | solution.py:448
  103.7 0.0 reduce-scatter.6.cloned.1.call-update
  103.7 0.2 reduce-scatter.4.cloned.1.call-start
  104.0 55.4 %mid_backward_pair.1 = (f32[128,2048]{1,0:T(8,128)}, bf16[512,2048]{1,0:T(8,128)(2,1)}, f32[1,2048]{1,0:T(1,128)}, bf16[2,4,256,1536]{3,2,1,0:T(8,128)(2,1)}) custom-call(f32[128,2048]{1,0:T(8,128)} %get-tuple-element.92.h_ref, bf16[128,2048]{1,0:T(8,128)(2,1)} %c_ref.3, f32[34,128]{1,0:T(8,128)} %bitcast.14, bf16[512,2048]{1,0:T(8,128)(2,1)} %get-tuple-element.93.x_hbm, ...), custom_call_target="tpu_custom_call" | custom-call | flops 1 | bytes 1 | tf_op jit(solution)/shard_map/mid_backward_pair/pallas_call | solution.py:603
  159.4 0.0 reduce-scatter.4.cloned.1.call-update
  159.4 0.0 reduce-scatter.8.cloned.1.call-start
  159.4 5.7 %out_back.1 = (bf16[512,512]{1,0:T(8,128)(2,1)}, bf16[2048,512]{1,0:T(8,128)(2,1)}) custom-call(bf16[512,2048]{1,0:T(8,128)(2,1)} %get-tuple-element.95.dy_ref, bf16[512,2048]{1,0:T(8,128)(2,1)} %w_ref.1, bf16[512,512]{1,0:T(8,128)(2,1)} %get-tuple-element.90.a_hbm.low_ref), custom_call_target="tpu_custom_call" | custom-call | flops 1 | bytes 1 | tf_op jit(solution)/shard_map/out_back/pallas_call | solution.py:1614
  165.1 9.4 %attend_back.1 = (f32[512,512]{1,0:T(8,128)}, bf16[8,512,512]{2,1,0:T(8,128)(2,1)}) custom-call(s32[1]{0:T(128)} %bitcast.1.w_ref, bf16[512,512]{1,0:T(8,128)(2,1)} %get-tuple-element.88.q_ref, bf16[8,512,512]{2,1,0:T(8,128)(2,1)} %get-tuple-element.89.kv_ref, bf16[512,512]{1,0:T(8,128)(2,1)} %get-tuple-element.96.do_ref, ...), custom_call_target="tpu_custom_call" | custom-call | flops 1 | bytes 1 | tf_op jit(solution)/shard_map/attend_back/pallas_call | solution.py:1124
  174.5 110.9 %return_grads.1 = (f32[512,512]{1,0:T(8,128)}, f32[128,2048]{1,0:T(8,128)}) custom-call(bf16[8,512,512]{2,1,0:T(8,128)(2,1)} %get-tuple-element.103.x_ref, bf16[512,1536]{1,0:T(8,128)(2,1)} %get-tuple-element.104.act_hbm, bf16[1536,2048]{1,0:T(8,128)(2,1)} %d_hbm.3), custom_call_target="tpu_custom_call" | custom-call | flops 1 | bytes 1 | tf_op jit(solution)/shard_map/return_grads/pallas_call | solution.py:822
  285.4 3.1 unspin.3
  288.4 4.0 %unspin.2 = (bf16[512,512]{1,0:T(8,128)(2,1)}, f32[1,128]{1,0:T(1,128)}) custom-call(f32[512,512]{1,0:T(8,128)} %get-tuple-element.99.e_ref, f32[512,512]{1,0:T(8,128)} %get-tuple-element.100.raw_ref, f32[34,128]{1,0:T(8,128)} %bitcast.16, f32[512,128]{1,0:T(8,128)} %get-tuple-element.101.tab_ref), custom_call_target="tpu_custom_call" | custom-call | flops 1 | bytes 1 | tf_op jit(solution)/shard_map/unspin/pallas_call | solution.py:1160
  292.5 16.0 %project_back_pair.1 = (bf16[512,2048]{1,0:T(8,128)(2,1)}, bf16[4,256,1536]{2,1,0:T(8,128)(2,1)}) custom-call(bf16[512,2048]{1,0:T(8,128)(2,1)} %get-tuple-element.87.x_ref, bf16[512,512]{1,0:T(8,128)(2,1)} %get-tuple-element.102.q_ref, bf16[512,512]{1,0:T(8,128)(2,1)} %get-tuple-element.107.kv_ref, bf16[2048,512]{1,0:T(8,128)(2,1)} %wq_ref.1, ...), custom_call_target="tpu_custom_call" | custom-call | flops 1 | bytes 1 | tf_op jit(solution)/shard_map/project_back_pair/pallas_call | solution.py:1746
  308.4 0.0 reduce-scatter.6.cloned.1.call-done
  308.4 7.8 %reduce-scatter.4.cloned.1.call-done = bf16[2,256,1536]{2,1,0:T(8,128)(2,1)} async-done(((bf16[2,1024,1536]{2,1,0:T(8,128)(2,1)}), bf16[2,256,1536]{2,1,0:T(8,128)(2,1)}) %reduce-scatter.4.cloned.1.call-update) | async-done | bytes 1572880 | tf_op jit(solution)/shard_map/reduce_scatter | solution.py:1830
  316.3 0.0 reduce-scatter.8.cloned.1.call-update
  316.3 0.0 copy-start.10
  316.3 0.0 copy-start.16
  316.3 0.0 copy-start.17
  316.3 0.0 copy-start
  316.3 0.0 copy-start.8
  316.3 23.9 %in_scatter.1 = (f32[128,2048]{1,0:T(8,128)}, f32[1,2048]{1,0:T(1,128)}) custom-call(bf16[512,2048]{1,0:T(8,128)(2,1)} %get-tuple-element.115.p_ref, bf16[128,2048]{1,0:T(8,128)(2,1)} %t_ref.5, f32[34,128]{1,0:T(8,128)} %bitcast.17), custom_call_target="tpu_custom_call" | custom-call | flops 1 | bytes 1 | tf_op jit(solution)/shard_map/in_scatter/pallas_call | solution.py:668
  340.2 0.0 copy-done.10
  340.2 0.0 copy-done.16
  340.2 0.7 maximum_reduce_fusion
  341.0 0.1 reshape_reshape.3
  341.1 0.6 reshape.86.x_ref
  341.8 1.1 add.72
  342.9 0.0 copy-start.6
  342.9 0.0 copy-start.7
  342.9 13.0 %gain_sums.1 = f32[2,128]{1,0:T(2,128)} custom-call(f32[4,8,2,128]{3,2,1,0:T(2,128)} %reshape.86.x_ref), custom_call_target="tpu_custom_call" | custom-call | flops 1 | bytes 1 | tf_op jit(solution)/shard_map/gain_sums/pallas_call | solution.py:906
  355.9 0.0 copy-start.11
  355.9 2.6 add.71
  358.6 0.6 add_multiply_fusion.2
  359.2 0.0 copy-start.1
  359.2 0.0 copy-start.2
  359.2 0.0 copy-start.3
  359.2 0.0 copy-start.4
  359.2 0.0 copy-start.5
  359.2 6.3 %add_multiply_fusion.1 = (f32[1536,256]{1,0:T(8,128)}, f32[1536,256]{1,0:T(8,128)}, f32[1536,256]{1,0:T(8,128)}, f32[1536,256]{1,0:T(8,128)}, f32[1536,256]{1,0:T(8,128)}) fusion(f32[1536,256]{1,0:T(8,128)S(1)} %copy-done.6, f32[1536,256]{1,0:T(8,128)S(1)} %copy-done.7, f32[1536,256]{1,0:T(8,128)} %param.58, f32[1536,256]{1,0:T(8,128)} %param.59, ...), kind=kLoop, calls=%fused_computation.7 | loop fusion | flops 7077888 | bytes 14942208 | tf_op jit(solution)/shard_map/add | solution.py:80
  365.5 0.0 copy-done.1
  365.5 1.2 copy-done.3
  366.7 0.9 copy-done.4
  367.6 0.4 copy-done.5
  368.0 8.3 %add_multiply_fusion = (f32[2,256,1536]{2,1,0:T(8,128)}, f32[2,256,1536]{2,1,0:T(8,128)}, f32[2,256,1536]{2,1,0:T(8,128)}, f32[2,256,1536]{2,1,0:T(8,128)}, f32[2,256,1536]{2,1,0:T(8,128)}) fusion(f32[2,256,1536]{2,1,0:T(8,128)S(1)} %copy-done.1, f32[2,256,1536]{2,1,0:T(8,128)S(1)} %copy-done.2, f32[2,256,1536]{2,1,0:T(8,128)S(1)} %copy-done.3, ...), kind=kLoop, calls=%fused_computation.2 | loop fusion | flops 14155776 | bytes 29884416 | tf_op jit(solution)/shard_map/add | solution.py:80
  376.3 4.9 %reduce-scatter.8.cloned.1.call-done.total_ref = bf16[256,1536]{1,0:T(8,128)(2,1)} async-done(((bf16[1024,1536]{1,0:T(8,128)(2,1)}), bf16[256,1536]{1,0:T(8,128)(2,1)}) %reduce-scatter.8.cloned.1.call-update) | async-done | bytes 786448 | tf_op jit(solution)/shard_map/reduce_scatter | solution.py:1830
  381.1 5.8 %rest_adamw.1 = (f32[256,512]{1,0:T(8,128)}, f32[256,512]{1,0:T(8,128)}, f32[256,512]{1,0:T(8,128)}, f32[256,512]{1,0:T(8,128)}, f32[256,512]{1,0:T(8,128)}, /*i...) custom-call(bf16[256,1536]{1,0:T(8,128)(2,1)} %reduce-scatter.8.clon, ...), custom_call_target="tpu_custom_call" | custom-call | flops 1 | bytes 1 | tf_op jit(solution)/shard_map/rest_adamw/pallas_call | solution.py:1806
  (19 shorter events, 0.0 us)
Async XLA Ops:
  7.2 301.2 %reduce-scatter.6.cloned.1.call-start = ((), (), s32[]{:S(2)}) async-start(), calls=%async_computation.4 | async-start | bytes 3932160 | tf_op jit(solution)/shard_map/reduce_scatter | solution.py:1830
  103.7 212.5 %reduce-scatter.4.cloned.1.call-start = ((), (), s32[]{:S(2)}) async-start(), calls=%async_computation.3 | async-start | bytes 7864320 | tf_op jit(solution)/shard_map/reduce_scatter | solution.py:1830
  159.4 221.7 %reduce-scatter.8.cloned.1.call-start = ((), (), s32[]{:S(2)}) async-start(), calls=%async_computation.5 | async-start | bytes 3932160 | tf_op jit(solution)/shard_map/reduce_scatter | solution.py:1830
  316.3 23.9 %copy-start.10 = (f32[1,2048]{1,0:T(1,128)S(1)}, f32[1,2048]{1,0:T(1,128)}, u32[]{:S(2)}) copy-start(f32[1,2048]{1,0:T(1,128)} %get-tuple-element.139) | copy-start | bytes 24580
  316.3 23.9 %copy-start.16 = (f32[1,128]{1,0:T(1,128)S(1)}, f32[1,128]{1,0:T(1,128)}, u32[]{:S(2)}) copy-start(f32[1,128]{1,0:T(1,128)} %get-tuple-element.141) | copy-start | bytes 1540
  316.3 23.9 %copy-start.17 = (f32[1,128]{1,0:T(1,128)S(1)}, f32[1,128]{1,0:T(1,128)}, u32[]{:S(2)}) copy-start(f32[1,128]{1,0:T(1,128)} %get-tuple-element.140) | copy-start | bytes 1540
  316.3 25.4 %copy-start = (f32[128,2048]{1,0:T(8,128)S(1)}, f32[128,2048]{1,0:T(8,128)}, u32[]{:S(2)}) copy-start(f32[128,2048]{1,0:T(8,128)} %get-tuple-element.92.h_ref) | copy-start | bytes 3145732
  316.3 25.4 %copy-start.8 = (f32[128,2048]{1,0:T(8,128)S(1)}, f32[128,2048]{1,0:T(8,128)}, u32[]{:S(2)}) copy-start(f32[128,2048]{1,0:T(8,128)} %get-tuple-element.117) | copy-start | bytes 3145732
  341.8 17.4 %copy-start.9 = (bf16[1,1536,256]{2,1,0:T(8,128)(2,1)S(1)}, bf16[1,1536,256]{2,1,0:T(8,128)(2,1)}, u32[]{:S(2)}) copy-start(bf16[1,1536,256]{2,1,0:T(8,128)(2,1)} %reduce-scatter.6.cloned.1.call-done) | copy-start | bytes 2359300
  342.9 15.7 %copy-start.12 = (f32[136]{0:T(256)S(1)}, f32[136]{0:T(256)}, u32[]{:S(2)}) copy-start(f32[136]{0:T(256)} %param.64) | copy-start | bytes 1636
  342.9 15.7 %copy-start.13 = (f32[136]{0:T(256)S(1)}, f32[136]{0:T(256)}, u32[]{:S(2)}) copy-start(f32[136]{0:T(256)} %param.61) | copy-start | bytes 1636
  342.9 15.7 %copy-start.14 = (f32[136]{0:T(256)S(1)}, f32[136]{0:T(256)}, u32[]{:S(2)}) copy-start(f32[136]{0:T(256)} %param.62) | copy-start | bytes 1636
  342.9 15.7 %copy-start.15 = (f32[136]{0:T(256)S(1)}, f32[136]{0:T(256)}, u32[]{:S(2)}) copy-start(f32[136]{0:T(256)} %param.63) | copy-start | bytes 1636
  342.9 16.3 %copy-start.6 = (f32[1536,256]{1,0:T(8,128)S(1)}, f32[1536,256]{1,0:T(8,128)}, u32[]{:S(2)}) copy-start(f32[1536,256]{1,0:T(8,128)} %param.60) | copy-start | bytes 4718596
  342.9 16.3 %copy-start.7 = (f32[1536,256]{1,0:T(8,128)S(1)}, f32[1536,256]{1,0:T(8,128)}, u32[]{:S(2)}) copy-start(f32[1536,256]{1,0:T(8,128)} %param.57) | copy-start | bytes 4718596
  355.9 2.7 copy-start.11
  359.2 6.3 %copy-start.1 = (f32[2,256,1536]{2,1,0:T(8,128)S(1)}, f32[2,256,1536]{2,1,0:T(8,128)}, u32[]{:S(2)}) copy-start(f32[2,256,1536]{2,1,0:T(8,128)} %param.56) | copy-start | bytes 9437188
  359.2 6.3 %copy-start.2 = (f32[2,256,1536]{2,1,0:T(8,128)S(1)}, f32[2,256,1536]{2,1,0:T(8,128)}, u32[]{:S(2)}) copy-start(f32[2,256,1536]{2,1,0:T(8,128)} %param.53) | copy-start | bytes 9437188
  359.2 7.5 %copy-start.3 = (f32[2,256,1536]{2,1,0:T(8,128)S(1)}, f32[2,256,1536]{2,1,0:T(8,128)}, u32[]{:S(2)}) copy-start(f32[2,256,1536]{2,1,0:T(8,128)} %param.54) | copy-start | bytes 9437188
  359.2 8.4 %copy-start.4 = (f32[2,256,1536]{2,1,0:T(8,128)S(1)}, f32[2,256,1536]{2,1,0:T(8,128)}, u32[]{:S(2)}) copy-start(f32[2,256,1536]{2,1,0:T(8,128)} %param.55) | copy-start | bytes 9437188
  359.2 8.8 %copy-start.5 = (bf16[2,256,1536]{2,1,0:T(8,128)(2,1)S(1)}, bf16[2,256,1536]{2,1,0:T(8,128)(2,1)}, u32[]{:S(2)}) copy-start(bf16[2,256,1536]{2,1,0:T(8,128)(2,1)} %reduce-scatter.4.cloned.1.call-done) | copy-start | bytes 4718596
Sparse Core Ops, SparseCore 0:
  103.9 67.4 reduce-scatter.5
  173.6 142.5 reduce-scatter.3
  318.6 62.5 reduce-scatter.7

commit v7 on v6

--- a/solution.py
+++ b/solution.py
@@ -1174,9 +1174,9 @@
 def front_kernel(
     count, heads, group,
     t_ref, c_ref, g_ref, f_ref, wq_hbm, wkv_hbm,
-    dy_hbm, x_hbm, q_hbm, qraw_hbm, kraw_hbm, kv_hbm, o_ref, low_ref, lse_ref, tab_ref,
-    own, x, weight, q, qraw, kraw, kv, acc,
-    send, recv, z_send, z_recv, m_send, m_recv, c_send, c_recv, load_sem, store_sem, kv_sem,
+    dy_hbm, x_hbm, q_hbm, qraw_hbm, kraw_hbm, kv_hbm, o_hbm, low_hbm, tab_hbm, lse_ref,
+    own, x, weight, q, qraw, kraw, kv, acc, o_ref, low_ref, tab_ref,
+    send, recv, z_send, z_recv, m_send, m_recv, c_send, c_recv, load_sem, store_sem, kv_sem, out_sem,
 ):
     me, xn, yn, dg = square()
     w, z, c, chips, mate, above, below = line(count)
@@ -1210,7 +1210,6 @@
     pl.semaphore_signal(barrier, inc=1, device_id={"wide": mate}, device_id_type=MESH)
     hidden = t_ref[...].astype(F32)
     own[...] = (hidden * row_scale(hidden) * gain_row(g_ref, 0)).astype(BF16)
-    fill_table(tab_ref, f_ref, w * all_rows)
     pl.semaphore_wait(barrier, 3 + has_above.astype(jnp.int32) + has_below.astype(jnp.int32))
 
     def half_of(ref, owner, low):
@@ -1317,6 +1316,9 @@
 
                 to_mate(s, k, j).start()
 
+    fill_table(tab_ref, f_ref, w * all_rows)
+    keep_table = pltpu.make_async_copy(tab_ref, tab_hbm, out_sem.at[2 * heads])
+    keep_table.start()
     x[pl.ds(pl.multiple_of(me * rows, rows), rows), :] = own[...]
     loads[1].wait()
     loads[2].wait()
@@ -1407,11 +1409,17 @@
     def _():
         c_relay()
 
+    outs = [keep_table]
     for h in range(heads):
         total = acc[h, :, HD:]
         out = acc[h, :, :HD] / total
-        o_ref[:, h * HD : (h + 1) * HD] = out
-        low_ref[:, h * HD : (h + 1) * HD] = out.astype(BF16)
+        lanes = slice(h * HD, (h + 1) * HD)
+        low_ref[:, lanes] = out.astype(BF16)
+        o_ref[:, lanes] = out
+        for n, (src, dst) in enumerate(((low_ref, low_hbm), (o_ref, o_hbm))):
+            copy = pltpu.make_async_copy(src.at[:, lanes], dst.at[:, lanes], out_sem.at[2 * h + n])
+            copy.start()
+            outs.append(copy)
         lse_ref[h : h + 1, :] = jnp.transpose(jnp.log2(total))[0:1]
 
     copies.finish()
@@ -1436,7 +1444,7 @@
                 for j in range(2):
                     to_mate(s, k, j).wait_send()
 
-    for store in stores:
+    for store in stores + outs:
         store.wait()
 
     @pl.loop(0, w + 1)
@@ -1478,11 +1486,11 @@
             jax.ShapeDtypeStruct((count, all_rows, 2 * kv_width), BF16),
             jax.ShapeDtypeStruct((all_rows, q_width), F32),
             jax.ShapeDtypeStruct((all_rows, q_width), BF16),
+            jax.ShapeDtypeStruct((all_rows, HD), F32),
             jax.ShapeDtypeStruct((heads, all_rows), F32),
-            jax.ShapeDtypeStruct((all_rows, HD), F32),
         ),
         in_specs=[VM] * 4 + [anywhere] * 2,
-        out_specs=(anywhere,) * 6 + (VM,) * 4,
+        out_specs=(anywhere,) * 9 + (VM,),
         scratch_shapes=[
             pltpu.VMEM((rows, D), BF16),
             pltpu.VMEM((all_rows, D), BF16),
@@ -1492,6 +1500,9 @@
             pltpu.VMEM((all_rows, kv_width), F32),
             pltpu.VMEM((count, all_rows, 2 * kv_width), BF16),
             pltpu.VMEM((heads, all_rows, 2 * HD), F32),
+            pltpu.VMEM((all_rows, q_width), F32),
+            pltpu.VMEM((all_rows, q_width), BF16),
+            pltpu.VMEM((all_rows, HD), F32),
         ]
         + dma_sems(6)
         + dma_sems(8 * chips)
@@ -1501,6 +1512,7 @@
             pltpu.SemaphoreType.DMA((3,)),
             pltpu.SemaphoreType.DMA((5,)),
             pltpu.SemaphoreType.DMA((count,)),
+            pltpu.SemaphoreType.DMA((2 * heads + 1,)),
         ],
         cost_estimate=cost(1, 1),
         compiler_params=remote_params(8),
@@ -1774,50 +1786,67 @@
     return in_partial, full.reshape(D // 2, width)
 
 
-def rest_adamw_kernel(total_ref, *refs):
-    q_width, kv_width = refs[0].shape[1], refs[4].shape[2]
-    ins, outs = refs[:12], refs[12:]
-    total = total_ref[...].astype(F32)
+def rest_adamw_kernel(total_hbm, *refs):
+    ins, refs = refs[:12], refs[12:]
+    results, refs = refs[:15], refs[15:]
+    total_ref, refs = refs[0], refs[1:]
+    states, refs = refs[:12], refs[12:]
+    outs, (in_sem, out_sem) = refs[:15], refs[15:]
+    loads = [pltpu.make_async_copy(total_hbm, total_ref, in_sem.at[0])] + [
+        pltpu.make_async_copy(ins[n], ref, in_sem.at[1 + n]) for n, ref in enumerate(states)
+    ]
+    for load in loads:
+        load.start()
+    q_width, kv_width = outs[0].shape[1], outs[5].shape[2]
     rate = 2.0 * D ** (-0.5)
+    stores = [
+        pltpu.make_async_copy(src, dst, out_sem.at[n])
+        for n, (src, dst) in enumerate(zip(outs, results))
+    ]
+    for load in loads[:5]:
+        load.wait()
     for n, new in enumerate(
-        adamw(total[:, :q_width], *[r[...] for r in ins[:4]], rate, WEIGHT_DECAY)
+        adamw(total_ref[:, :q_width].astype(F32), *[r[...] for r in states[:4]], rate, WEIGHT_DECAY)
     ):
         outs[n][...] = new
+        stores[n].start()
+    for load in loads[5:9]:
+        load.wait()
     for k in range(2):
         low = q_width + k * kv_width
-        for n, new in enumerate(
-            adamw(total[:, low : low + kv_width], *[r[k] for r in ins[4:8]], rate, WEIGHT_DECAY)
-        ):
+        total = total_ref[:, low : low + kv_width].astype(F32)
+        for n, new in enumerate(adamw(total, *[r[k] for r in states[4:8]], rate, WEIGHT_DECAY)):
             outs[5 + n][k] = new
-    turned = jnp.transpose(total[:, q_width + 2 * kv_width :])
+    for n in range(5, 10):
+        stores[n].start()
+    for load in loads[9:]:
+        load.wait()
+    turned = jnp.transpose(total_ref[:, q_width + 2 * kv_width :].astype(F32))
     for n, new in enumerate(
-        adamw(turned, *[r[...] for r in ins[8:]], 2.0 * WO_FAN ** (-0.5), WEIGHT_DECAY)
+        adamw(turned, *[r[...] for r in states[8:]], 2.0 * WO_FAN ** (-0.5), WEIGHT_DECAY)
     ):
         outs[10 + n][...] = new
-
-
-def rest_adamw(total, query_state, keyvalue_state, output_state):
-    tile = 128
-    rows, width = total.shape
-    q_spec = pl.BlockSpec((tile, query_state[0].shape[1]), lambda i: (i, 0))
-    kv_spec = pl.BlockSpec((2, tile, keyvalue_state[0].shape[2]), lambda i: (0, i, 0))
-    o_spec = pl.BlockSpec((output_state[0].shape[0], tile), lambda i: (0, i))
-    like = lambda a: jax.ShapeDtypeStruct(a.shape, F32)
+        stores[10 + n].start()
+    for store in stores:
+        store.wait()
+
+
+def rest_adamw(total, states):
+    hbm = pl.BlockSpec(memory_space=pltpu.HBM)
+    shapes = [states[4 * n].shape for n in range(3) for _ in range(5)]
     out = pl.pallas_call(
         rest_adamw_kernel,
         name="rest_adamw",
-        grid=(rows // tile,),
-        out_shape=tuple(
-            like(state[0]) for state in (query_state, keyvalue_state, output_state) for _ in range(5)
-        ),
-        in_specs=[pl.BlockSpec((tile, width), lambda i: (i, 0))]
-        + [q_spec] * 4
-        + [kv_spec] * 4
-        + [o_spec] * 4,
-        out_specs=tuple([q_spec] * 5 + [kv_spec] * 5 + [o_spec] * 5),
-        compiler_params=params("arbitrary"),
+        out_shape=tuple(jax.ShapeDtypeStruct(shape, F32) for shape in shapes),
+        in_specs=[hbm] * 13,
+        out_specs=(hbm,) * 15,
+        scratch_shapes=[pltpu.VMEM(total.shape, total.dtype)]
+        + [pltpu.VMEM(state.shape, F32) for state in states]
+        + [pltpu.VMEM(shape, F32) for shape in shapes]
+        + [pltpu.SemaphoreType.DMA((13,)), pltpu.SemaphoreType.DMA((15,))],
+        compiler_params=params(),
         cost_estimate=cost(1, 1),
-    )(total, *query_state, *keyvalue_state, *output_state)
+    )(total, *states)
     return out[:5], out[5:10], out[10:]
 
 
@@ -1887,8 +1916,8 @@
             kv_all,
             attn_out,
             attn_low,
+            table,
             lse,
-            table,
         ) = front(tokens, cotangent, gains, query_weight, keyvalue_weight, wide)
     else:
         positions = wide_index * stretch_rows + jnp.arange(stretch_rows, dtype=jnp.int32)
@@ -1958,15 +1987,6 @@
     ).reshape(-1)
     gain_total = gain_sums(gain_partial, wide, narrow, special)
 
-    rest_total, input_grad, block_output = lax.optimization_barrier(
-        (rest_total, input_grad, block_output)
-    )
-    query_new, keyvalue_new, output_new = rest_adamw(
-        rest_total,
-        (query_master, query_moment, query_second, query_average),
-        (keyvalue_master, keyvalue_moment, keyvalue_second, keyvalue_average),
-        (output_master, output_moment, output_second, output_average),
-    )
     gateup_new = adamw(
         gateup_total.astype(F32),
         gateup_master,
@@ -1988,6 +2008,24 @@
     gain_new = adamw(
         gain_total, gain_master, gain_moment, gain_second, gain_average, RATE_GAIN, 0.0
     )
+    states = (
+        query_master,
+        query_moment,
+        query_second,
+        query_average,
+        keyvalue_master,
+        keyvalue_moment,
+        keyvalue_second,
+        keyvalue_average,
+        output_master,
+        output_moment,
+        output_second,
+        output_average,
+    )
+    states, gateup_new, down_new, gain_new, input_grad, block_output = lax.optimization_barrier(
+        (states, gateup_new, down_new, gain_new, input_grad, block_output)
+    )
+    query_new, keyvalue_new, output_new = rest_adamw(rest_total, states)
     return (
         block_output,
         input_grad,

time: 394 us -> 394 us (level)
    add x3, other arithmetic: 15.1 us -> 9.89 us  [adamw(): average_new = EMA_KEEP * average + (1.0 - EMA_KEEP) * master_new]
where the time goes in v7:
time: 394 us; the launch traced here: 393 us
  Pallas kernels  343 us (87%)
  other arithmetic  17.6 us (4%)
  between operations  14 us (4%)
  waiting for transfers between devices  13.2 us (3%)
  local copies, waits for them, and re-layouts  5.05 us (1%)
    pallas_call x1, Pallas kernels, return_grads_out(): pl.pallas_call(functools.partial(return_grads_kernel, count), name='retur...  112 us
    pallas_call x1, Pallas kernels, mid_backward_pair(): pl.pallas_call(mid_backward_kernel, name='mid_backward_pair', out_shape=(...  55.4 us
    pallas_call x1, Pallas kernels, mid_pair(): pl.pallas_call(mid_kernel, name='mid_pair', out_shape=(jax.ShapeDtypeStru...  51 us
    pallas_call x1, Pallas kernels, front(): pl.pallas_call(functools.partial(front_kernel, count, heads, group), name...  44.9 us
    pallas_call x1, Pallas kernels, in_scatter(): pl.pallas_call(in_scatter_kernel, name='in_scatter', out_shape=(jax.Shape...  23.8 us
    pallas_call x1, Pallas kernels, project_back_pair(): pl.pallas_call(project_back_pair_kernel, name='project_back_pair', grid=(...  16 us
    reduce_scatter x3, waiting for transfers between devices, line_scatter(): lax.psum_scatter(partial, 'wide', scatter_dimension=axis, tiled=True, axi...  13.1 us
    pallas_call x1, Pallas kernels, gain_sums(): pl.pallas_call(functools.partial(gain_kernel, wide), name='gain_sums', ou...  12.9 us
  transfers between devices with their start and end apart: 3, of which 2 were waited for; matrix products, arithmetic and copies ran while one was open for 5% of the time, Pallas kernels for 61%

profile of v7, /device:TPU:0, one launch (start us, length us, event | category | flops | bytes accessed | tf_op | source)
XLA Modules:
  0.0 393.4 jit_solution(14075435889736593505)
XLA Ops:
  7.2 0.0 reduce-scatter.6.cloned.1.call-start
  7.2 44.9 %front.1 = (bf16[512,2048]{1,0:T(8,128)(2,1)}, bf16[512,2048]{1,0:T(8,128)(2,1)}, bf16[512,512]{1,0:T(8,128)(2,1)}, f32[512,512]{1,0:T(8,128)}, f32[512,256]{1,0...) custom-call(bf16[128,2048]{1,0:T(8,128)(2,1)} %t_ref.5, ...), custom_call_target="tpu_custom_call" | custom-call | flops 1 | bytes 1 | tf_op jit(solution)/shard_map/front/pallas_call | solution.py:1477
  52.1 51.0 %mid_pair.1 = (f32[128,2048]{1,0:T(8,128)}, bf16[512,2048]{1,0:T(8,128)(2,1)}, bf16[2,512,1536]{2,1,0:T(8,128)(2,1)}, bf16[512,1536]{1,0:T(8,128)(2,1)}, bf16[4,1536,256]{2,1,0:T(8,128)(2,1)}) custom-call(bf16[128,2048]{1,0:T(8,128)(2,1)} %t_ref.5, f32[34,128]{1,0:T(8,128)} %bitcast.14, bf16[512,512]{1,0:T(8,128)(2,1)} %get-tuple-element.116.a_hbm.low_ref, ...), custom_call_target="tpu_custom_call" | custom-call | flops 1 | bytes 1 | tf_op jit(solution)/shard_map/mid_pair/pallas_call | solution.py:448
  103.1 0.0 reduce-scatter.6.cloned.1.call-update
  103.2 0.2 reduce-scatter.4.cloned.1.call-start
  103.4 55.4 %mid_backward_pair.1 = (f32[128,2048]{1,0:T(8,128)}, bf16[512,2048]{1,0:T(8,128)(2,1)}, f32[1,2048]{1,0:T(1,128)}, bf16[2,4,256,1536]{3,2,1,0:T(8,128)(2,1)}) custom-call(f32[128,2048]{1,0:T(8,128)} %get-tuple-element.118.h_ref, bf16[128,2048]{1,0:T(8,128)(2,1)} %c_ref.3, f32[34,128]{1,0:T(8,128)} %bitcast.15, bf16[512,2048]{1,0:T(8,128)(2,1)} %get-tuple-element.119.x_hbm, ...), custom_call_target="tpu_custom_call" | custom-call | flops 1 | bytes 1 | tf_op jit(solution)/shard_map/mid_backward_pair/pallas_call | solution.py:603
  158.8 0.0 reduce-scatter.4.cloned.1.call-update
  158.8 0.0 reduce-scatter.8.cloned.1.call-start
  158.9 5.7 %out_back.1 = (bf16[512,512]{1,0:T(8,128)(2,1)}, bf16[2048,512]{1,0:T(8,128)(2,1)}) custom-call(bf16[512,2048]{1,0:T(8,128)(2,1)} %get-tuple-element.121.dy_ref, bf16[512,2048]{1,0:T(8,128)(2,1)} %w_ref.1, bf16[512,512]{1,0:T(8,128)(2,1)} %get-tuple-element.116.a_hbm.low_ref), custom_call_target="tpu_custom_call" | custom-call | flops 1 | bytes 1 | tf_op jit(solution)/shard_map/out_back/pallas_call | solution.py:1626
  164.6 9.3 %attend_back.1 = (f32[512,512]{1,0:T(8,128)}, bf16[8,512,512]{2,1,0:T(8,128)(2,1)}) custom-call(s32[1]{0:T(128)} %bitcast.1.w_ref, bf16[512,512]{1,0:T(8,128)(2,1)} %get-tuple-element.114.q_ref, bf16[8,512,512]{2,1,0:T(8,128)(2,1)} %get-tuple-element.115.kv_ref, bf16[512,512]{1,0:T(8,128)(2,1)} %get-tuple-element.122.do_ref, ...), custom_call_target="tpu_custom_call" | custom-call | flops 1 | bytes 1 | tf_op jit(solution)/shard_map/attend_back/pallas_call | solution.py:1124
  173.9 111.7 %return_grads.1 = (f32[512,512]{1,0:T(8,128)}, f32[128,2048]{1,0:T(8,128)}) custom-call(bf16[8,512,512]{2,1,0:T(8,128)(2,1)} %get-tuple-element.129.x_ref, bf16[512,1536]{1,0:T(8,128)(2,1)} %get-tuple-element.130.act_hbm, bf16[1536,2048]{1,0:T(8,128)(2,1)} %d_hbm.3), custom_call_target="tpu_custom_call" | custom-call | flops 1 | bytes 1 | tf_op jit(solution)/shard_map/return_grads/pallas_call | solution.py:822
  285.6 4.0 %unspin.2 = (bf16[512,512]{1,0:T(8,128)(2,1)}, f32[1,128]{1,0:T(1,128)}) custom-call(f32[512,512]{1,0:T(8,128)} %get-tuple-element.125.e_ref, f32[512,512]{1,0:T(8,128)} %get-tuple-element.126.raw_ref, f32[34,128]{1,0:T(8,128)} %bitcast.16, f32[512,128]{1,0:T(8,128)} %get-tuple-element.127.tab_ref), custom_call_target="tpu_custom_call" | custom-call | flops 1 | bytes 1 | tf_op jit(solution)/shard_map/unspin/pallas_call | solution.py:1160
  289.7 3.1 unspin.3
  292.7 16.0 %project_back_pair.1 = (bf16[512,2048]{1,0:T(8,128)(2,1)}, bf16[4,256,1536]{2,1,0:T(8,128)(2,1)}) custom-call(bf16[512,2048]{1,0:T(8,128)(2,1)} %get-tuple-element.113.x_ref, bf16[512,512]{1,0:T(8,128)(2,1)} %get-tuple-element.128.q_ref, bf16[512,512]{1,0:T(8,128)(2,1)} %get-tuple-element.133.kv_ref, bf16[2048,512]{1,0:T(8,128)(2,1)} %wq_ref.1, ...), custom_call_target="tpu_custom_call" | custom-call | flops 1 | bytes 1 | tf_op jit(solution)/shard_map/project_back_pair/pallas_call | solution.py:1758
  308.7 0.0 reduce-scatter.6.cloned.1.call-done
  308.7 7.8 %reduce-scatter.4.cloned.1.call-done = bf16[2,256,1536]{2,1,0:T(8,128)(2,1)} async-done(((bf16[2,1024,1536]{2,1,0:T(8,128)(2,1)}), bf16[2,256,1536]{2,1,0:T(8,128)(2,1)}) %reduce-scatter.4.cloned.1.call-update) | async-done | bytes 1572880 | tf_op jit(solution)/shard_map/reduce_scatter | solution.py:1859
  316.6 0.0 reduce-scatter.8.cloned.1.call-update
  316.6 0.0 copy-start.13
  316.6 0.0 copy-start.19
  316.6 0.0 copy-start.20
  316.6 23.8 %in_scatter.1 = (f32[128,2048]{1,0:T(8,128)}, f32[1,2048]{1,0:T(1,128)}) custom-call(bf16[512,2048]{1,0:T(8,128)(2,1)} %get-tuple-element.141.p_ref, bf16[128,2048]{1,0:T(8,128)(2,1)} %t_ref.5, f32[34,128]{1,0:T(8,128)} %bitcast.18), custom_call_target="tpu_custom_call" | custom-call | flops 1 | bytes 1 | tf_op jit(solution)/shard_map/in_scatter/pallas_call | solution.py:668
  340.5 0.8 maximum_reduce_fusion
  341.3 0.1 reshape_reshape.3
  341.5 0.6 reshape.86.x_ref
  342.1 0.0 copy-done.1
  342.1 2.4 add.90
  344.5 12.9 %gain_sums.1 = f32[2,128]{1,0:T(2,128)} custom-call(f32[4,8,2,128]{3,2,1,0:T(2,128)} %reshape.86.x_ref), custom_call_target="tpu_custom_call" | custom-call | flops 1 | bytes 1 | tf_op jit(solution)/shard_map/gain_sums/pallas_call | solution.py:906
  357.5 1.3 convert_element_type.9
  358.7 2.1 convert_element_type.8
  360.8 0.0 copy-start.18
  360.8 0.0 copy-start.7
  360.8 0.0 copy-start.8
  360.9 1.1 add.89
  362.0 0.0 copy-done.14
  362.0 0.0 copy-done.15
  362.1 0.1 copy-done.16
  362.1 0.1 copy-done.17
  362.2 0.0 copy-done.18
  362.2 0.6 add_multiply_fusion.2
  362.8 0.3 copy-done.7
  363.1 0.5 copy-done.8
  363.6 3.8 add_multiply_fusion.1
  367.4 1.3 copy-done.3
  368.7 1.0 copy-done.4
  369.7 0.9 copy-done.5
  370.6 5.5 %add_multiply_fusion = (f32[2,256,1536]{2,1,0:T(8,128)}, f32[2,256,1536]{2,1,0:T(8,128)}, f32[2,256,1536]{2,1,0:T(8,128)}, f32[2,256,1536]{2,1,0:T(8,128)}) fusion(f32[2,256,1536]{2,1,0:T(8,128)S(1)} %copy-done.2, f32[2,256,1536]{2,1,0:T(8,128)S(1)} %copy-done.3, bf16[2,256,1536]{2,1,0:T(8,128)(2,1)S(1)} %copy-done, f32[2,256,1536]{2,1,0:T(8,128)S(1)} %copy-done.4, ...), kind=kLoop, calls=%fused_computation.2 | loop fusion | flops 14155776 | bytes 26738688 | tf_op jit(solution)/shard_map/add | solution.py:80
  376.1 5.3 %reduce-scatter.8.cloned.1.call-done.total_hbm = bf16[256,1536]{1,0:T(8,128)(2,1)} async-done(((bf16[1024,1536]{1,0:T(8,128)(2,1)}), bf16[256,1536]{1,0:T(8,128)(2,1)}) %reduce-scatter.8.cloned.1.call-update) | async-done | bytes 786448 | tf_op jit(solution)/shard_map/reduce_scatter | solution.py:1859
  381.4 5.5 %rest_adamw.1 = (f32[256,512]{1,0:T(8,128)}, f32[256,512]{1,0:T(8,128)}, f32[256,512]{1,0:T(8,128)}, f32[256,512]{1,0:T(8,128)}, f32[256,512]{1,0:T(8,128)}, /*i...) custom-call(bf16[256,1536]{1,0:T(8,128)(2,1)} %reduce-scatter.8.clon, ...), custom_call_target="tpu_custom_call" | custom-call | flops 1 | bytes 1 | tf_op jit(solution)/shard_map/rest_adamw/pallas_call | solution.py:1837
  (27 shorter events, 0.1 us)
Async XLA Ops:
  7.2 301.5 %reduce-scatter.6.cloned.1.call-start = ((), (), s32[]{:S(2)}) async-start(), calls=%async_computation.4 | async-start | bytes 3932160 | tf_op jit(solution)/shard_map/reduce_scatter | solution.py:1859
  103.2 213.4 %reduce-scatter.4.cloned.1.call-start = ((), (), s32[]{:S(2)}) async-start(), calls=%async_computation.3 | async-start | bytes 7864320 | tf_op jit(solution)/shard_map/reduce_scatter | solution.py:1859
  158.8 222.5 %reduce-scatter.8.cloned.1.call-start = ((), (), s32[]{:S(2)}) async-start(), calls=%async_computation.5 | async-start | bytes 3932160 | tf_op jit(solution)/shard_map/reduce_scatter | solution.py:1859
  316.6 23.9 %copy-start.13 = (f32[1,2048]{1,0:T(1,128)S(1)}, f32[1,2048]{1,0:T(1,128)}, u32[]{:S(2)}) copy-start(f32[1,2048]{1,0:T(1,128)} %get-tuple-element.143) | copy-start | bytes 24580
  316.6 23.9 %copy-start.19 = (f32[1,128]{1,0:T(1,128)S(1)}, f32[1,128]{1,0:T(1,128)}, u32[]{:S(2)}) copy-start(f32[1,128]{1,0:T(1,128)} %get-tuple-element.144) | copy-start | bytes 1540
  316.6 23.9 %copy-start.20 = (f32[1,128]{1,0:T(1,128)S(1)}, f32[1,128]{1,0:T(1,128)}, u32[]{:S(2)}) copy-start(f32[1,128]{1,0:T(1,128)} %get-tuple-element.145) | copy-start | bytes 1540
  316.6 25.5 %copy-start.1 = (f32[128,2048]{1,0:T(8,128)S(1)}, f32[128,2048]{1,0:T(8,128)}, u32[]{:S(2)}) copy-start(f32[128,2048]{1,0:T(8,128)} %get-tuple-element.118.h_ref) | copy-start | bytes 3145732
  340.5 17.0 %copy-start.6 = (bf16[1,1536,256]{2,1,0:T(8,128)(2,1)S(1)}, bf16[1,1536,256]{2,1,0:T(8,128)(2,1)}, u32[]{:S(2)}) copy-start(bf16[1,1536,256]{2,1,0:T(8,128)(2,1)} %reduce-scatter.6.cloned.1.call-done) | copy-start | bytes 2359300
  342.1 16.6 %copy-start = (bf16[2,256,1536]{2,1,0:T(8,128)(2,1)S(1)}, bf16[2,256,1536]{2,1,0:T(8,128)(2,1)}, u32[]{:S(2)}) copy-start(bf16[2,256,1536]{2,1,0:T(8,128)(2,1)} %reduce-scatter.4.cloned.1.call-done) | copy-start | bytes 4718596
  357.4 3.4 copy-start.12
  358.7 2.1 copy-start.11
  358.7 4.1 %copy-start.9 = (f32[1536,256]{1,0:T(8,128)S(1)}, f32[1536,256]{1,0:T(8,128)}, u32[]{:S(2)}) copy-start(f32[1536,256]{1,0:T(8,128)} %param.58) | copy-start | bytes 4718596
  358.7 4.1 %copy-start.10 = (f32[1536,256]{1,0:T(8,128)S(1)}, f32[1536,256]{1,0:T(8,128)}, u32[]{:S(2)}) copy-start(f32[1536,256]{1,0:T(8,128)} %param.59) | copy-start | bytes 4718596
  360.8 1.2 copy-start.14
  360.8 1.3 copy-start.15
  360.8 1.3 copy-start.16
  360.8 1.4 copy-start.17
  360.8 1.4 copy-start.18
  360.8 2.3 copy-start.7
  360.8 2.8 copy-start.8
  363.6 3.8 copy-start.2
  363.6 5.1 %copy-start.3 = (f32[2,256,1536]{2,1,0:T(8,128)S(1)}, f32[2,256,1536]{2,1,0:T(8,128)}, u32[]{:S(2)}) copy-start(f32[2,256,1536]{2,1,0:T(8,128)} %param.53) | copy-start | bytes 9437188
  363.6 6.0 %copy-start.4 = (f32[2,256,1536]{2,1,0:T(8,128)S(1)}, f32[2,256,1536]{2,1,0:T(8,128)}, u32[]{:S(2)}) copy-start(f32[2,256,1536]{2,1,0:T(8,128)} %param.54) | copy-start | bytes 9437188
  363.6 6.9 %copy-start.5 = (f32[2,256,1536]{2,1,0:T(8,128)S(1)}, f32[2,256,1536]{2,1,0:T(8,128)}, u32[]{:S(2)}) copy-start(f32[2,256,1536]{2,1,0:T(8,128)} %param.55) | copy-start | bytes 9437188
Sparse Core Ops, SparseCore 0:
  103.3 68.3 reduce-scatter.5
  173.9 142.5 reduce-scatter.3
  318.9 62.4 reduce-scatter.7
